TPU v7x, 256 devices: a whole 4x4x8 slice. The times are simulated.
256 devices in a mesh: col: 8 (over y_lo, x), row: 32 (over z, y_hi, core).
Axes of the slice: x: 4, y: 4 (y_hi: 2, y_lo: 2; y = y_hi * 2 + y_lo), z: 8, core: 2. Of those that a mesh axis runs over, the one named last changes fastest.
Arguments:
- images: bfloat16 [256, 16, 16, 1536], P(('col', 'row')), may hold values from -6 to 6
- hidden_cot: bfloat16 [256, 256, 3072], P(('col', 'row')), may hold values from -6 to 6
- residual_cot: bfloat16 [256, 16, 16, 1536], P(('col', 'row')), may hold values from -6 to 6
- w_up: bfloat16 [1536, 3072], replicated, may hold values from -0.15625 to 0.15625
- b_up: float32 [3072], replicated, may hold values from -3 to 3
- ln_gain: float32 [1536], replicated, may hold values from 0.1 to 1.9
- ln_bias: float32 [1536], replicated, may hold values from -3 to 3
- dw_weight: float32 [49, 1536], replicated, may hold values from -0.875 to 0.875
- dw_bias: float32 [1536], replicated, may hold values from -3 to 3
Outputs:
- grad_input: bfloat16 [256, 16, 16, 1536], P(('col', 'row'))
- grad_w_up: float32 [1536, 3072], P(('col', 'row'))
- grad_b_up: float32 [3072], replicated
- grad_ln_gain: float32 [1536], replicated
- grad_ln_bias: float32 [1536], replicated
- grad_dw_weight: float32 [49, 1536], replicated
- grad_dw_bias: float32 [1536], replicated
All inputs are finite; a program needn't handle non-finite values.
Results may differ from a plain program's by a relative error of at most 0.007.
Values may be sent and summed in bfloat16 or wider, within the bound.
No kernel may reach another device: no remote copies, remote signals or barrier semaphores. Data moves between devices by JAX's collectives and lax.ppermute only.
A program may use at most 128 MiB of HBM per device.

v0:
```python
import jax
import jax.numpy as jnp
from jax import lax
from jax.sharding import PartitionSpec as P


def depthwise(padded, dw_weight, side_cells):
    running = jnp.zeros(padded.shape[:1] + (side_cells, side_cells, padded.shape[3]), jnp.float32)
    for tap_row in range(7):
        for tap_col in range(7):
            running = (
                running
                + padded[:, tap_row : tap_row + side_cells, tap_col : tap_col + side_cells, :]
                * dw_weight[tap_row * 7 + tap_col]
            )
    return running


def local_backward(
    images, hidden_cot, residual_cot, w_up, b_up, ln_gain, ln_bias, dw_weight, dw_bias
):
    side_cells = images.shape[1]
    feat_width = images.shape[3]
    padded = jnp.pad(images.astype(jnp.float32), ((0, 0), (3, 3), (3, 3), (0, 0)))
    conv_out = depthwise(padded, dw_weight, side_cells) + dw_bias
    centred = conv_out - jnp.mean(conv_out, axis=-1, keepdims=True)
    inv_sigma = lax.rsqrt(jnp.mean(centred * centred, axis=-1, keepdims=True) + 1e-06)
    unit_vals = centred * inv_sigma
    normed = (unit_vals * ln_gain + ln_bias).astype(jnp.bfloat16).reshape(-1, feat_width)
    pre_act = jnp.dot(normed, w_up, preferred_element_type=jnp.float32) + b_up
    gelu_slope = (
        0.5 * (1.0 + lax.erf(pre_act * 0.7071067811865476))
        + pre_act * jnp.exp(-0.5 * pre_act * pre_act) * 0.3989422804014327
    )
    pre_grad = (hidden_cot.reshape(pre_act.shape).astype(jnp.float32) * gelu_slope).astype(
        jnp.bfloat16
    )
    normed_grad = lax.dot_general(
        pre_grad, w_up, (((1,), (1,)), ((), ())), preferred_element_type=jnp.float32
    )
    unit_flat = unit_vals.reshape(-1, feat_width)
    grad_gain = jnp.sum(normed_grad * unit_flat, axis=0)
    grad_shift = jnp.sum(normed_grad, axis=0)
    grad_bias_up = jnp.sum(pre_grad.astype(jnp.float32), axis=0)
    unit_grad = (normed_grad * ln_gain).reshape(unit_vals.shape)
    conv_grad = inv_sigma * (
        unit_grad
        - jnp.mean(unit_grad, axis=-1, keepdims=True)
        - unit_vals * jnp.mean(unit_grad * unit_vals, axis=-1, keepdims=True)
    )
    grad_conv_bias = jnp.sum(conv_grad, axis=(0, 1, 2))
    tap_sums = []
    for tap_row in range(7):
        for tap_col in range(7):
            window = padded[:, tap_row : tap_row + side_cells, tap_col : tap_col + side_cells, :]
            tap_sums.append(jnp.sum(conv_grad * window, axis=(0, 1, 2)))
    grad_filter = jnp.stack(tap_sums)
    grad_padded = jnp.pad(conv_grad, ((0, 0), (3, 3), (3, 3), (0, 0)))
    input_grad = residual_cot.astype(jnp.float32)
    for tap_row in range(7):
        for tap_col in range(7):
            input_grad = (
                input_grad
                + grad_padded[
                    :,
                    6 - tap_row : 6 - tap_row + side_cells,
                    6 - tap_col : 6 - tap_col + side_cells,
                    :,
                ]
                * dw_weight[tap_row * 7 + tap_col]
            )
    return (
        input_grad.astype(jnp.bfloat16),
        normed,
        pre_grad,
        (grad_bias_up, grad_gain, grad_shift, grad_filter, grad_conv_bias),
    )


def per_device(images, hidden_cot, residual_cot, w_up, b_up, ln_gain, ln_bias, dw_weight, dw_bias):
    feat_width = images.shape[3]
    devices_col = lax.axis_size("col")
    devices_row = lax.axis_size("row")
    inverse_count = 1.0 / (images.shape[0] * devices_col * devices_row)
    grad_input, normed, pre_grad, smalls = local_backward(
        images, hidden_cot, residual_cot, w_up, b_up, ln_gain, ln_bias, dw_weight, dw_bias
    )
    owned_width = feat_width // (devices_col * devices_row)
    permuted = (
        normed.reshape(-1, devices_col, devices_row, owned_width)
        .transpose(0, 2, 1, 3)
        .reshape(-1, feat_width)
    )
    row_owned = lax.psum_scatter(
        lax.dot_general(
            permuted, pre_grad, (((0,), (0,)), ((), ())), preferred_element_type=jnp.float32
        ),
        "row",
        scatter_dimension=0,
        tiled=True,
    )
    owned = lax.psum_scatter(row_owned, "col", scatter_dimension=0, tiled=True)
    grad_bias_up, grad_gain, grad_shift, grad_filter, grad_conv_bias = smalls
    summed = lax.psum(
        (grad_bias_up, grad_gain, grad_shift, grad_filter, grad_conv_bias), ("col", "row")
    )
    return (
        grad_input,
        owned * inverse_count,
        summed[0] * inverse_count,
        summed[1] * inverse_count,
        summed[2] * inverse_count,
        summed[3] * inverse_count,
        summed[4] * inverse_count,
    )


def solution(mesh):
    placed = (
        P(("col", "row"), None, None, None),
        P(("col", "row"), None, None),
        P(("col", "row"), None, None, None),
        P(),
        P(),
        P(),
        P(),
        P(),
        P(),
    )
    return jax.shard_map(
        per_device,
        mesh=mesh,
        in_specs=placed,
        out_specs=(
            P(("col", "row"), None, None, None),
            P(("col", "row"), None),
            P(),
            P(),
            P(),
            P(),
            P(),
        ),
        check_vma=False,
    )
```

profile of v0, /device:TPU:1, one launch (start us, length us, event | category | flops | bytes accessed | tf_op | source)
XLA Modules:
  0.0 405.1 jit_solution(8692546717174346875)
XLA Ops:
  8.0 0.0 reduce-scatter.4.cloned.1.call-start
  8.0 1.3 slice_reduce_fusion.46
  9.4 1.9 slice_reduce_fusion.48
  11.2 1.9 slice_reduce_fusion.47
  13.1 1.3 convert_element_type.28
  14.5 13.2 %fusion.109 = (f32[16,16]{1,0:T(8,128)S(1)}, f32[1,16,16,1536]{3,2,1,0:T(8,128)S(1)}) fusion(f32[1536]{0:T(1024)} %param.17, f32[1536]{0:T(1024)S(1)} %get-tuple-element.118, f32[1536]{0:T(1024)S(1)} %get-tuple-element.119, f32[1536]{0:T(1024)S(1)} %get-tuple-element.72, f32[1536]{0:T(1024)S(1)} %get-tuple-element.73, f32[1536]{0:T(1024)S(1)} %get-tuple-element.74, ...), kind=kLoop, calls=%fused_computation.323 | loop fusion | flops 38928128 | bytes 3453952 | tf_op jit(solution)/shard_map/reduce_sum | solution.py:26
  27.7 0.3 multiply_reduce_fusion.50
  28.0 0.4 copy-done.9
  28.4 0.0 copy-done.10
  28.4 1.8 add_convert_fusion
  30.2 7.7 %copy.18 = bf16[1,16,16,1536]{2,1,3,0:T(8,128)(2,1)} copy(bf16[1,16,16,1536]{3,2,1,0:T(8,128)(2,1)} %get-tuple-element.127) | data formatting | bytes 1572864 | tf_op jit(solution)/shard_map/convert_element_type | solution.py:29
  37.9 8.1 %reshape_reshape.3 = bf16[256,8,32,6]{0,3,2,1:T(8,128)(2,1)S(1)} reshape(bf16[1,16,16,1536]{2,1,3,0:T(8,128)(2,1)} %copy.18) | data formatting | bytes 1572864 | tf_op jit(solution)/shard_map/reshape;reshape | solution.py:90
  46.0 1.1 copy.19
  47.1 1.5 reshape.247
  48.6 7.1 %convert_reduce_fusion = (f32[3072]{0:T(1024)}, bf16[256,3072]{1,0:T(8,128)(2,1)S(1)}) fusion(f32[3072]{0:T(1024)} %param.13, bf16[256,1536]{1,0:T(8,128)(2,1)S(1)} %bitcast.29, bf16[1536,3072]{1,0:T(8,128)(2,1)} %param.12, bf16[1,256,3072]{2,1,0:T(8,128)(2,1)} %param.10), kind=kOutput, calls=%fused_computation.104 | convolution fusion | flops 2426926080 | bytes 13393920 | tf_op jit(solution)/shard_map/dot_general | solution.py:30
  55.7 1.2 copy-done.5
  56.8 7.9 %fusion.110 = f32[1536,3072]{1,0:T(8,128)} fusion(bf16[256,1536]{0,1:T(8,128)(2,1)S(1)} %reshape.247, bf16[256,3072]{1,0:T(8,128)(2,1)S(1)} %get-tuple-element.134), kind=kOutput, calls=%fused_computation.324 | convolution fusion | flops 2415919104 | bytes 21233664 | tf_op jit(solution)/shard_map/dot_general | solution.py:95
  64.7 0.0 reduce-scatter.4.cloned.1.call-update
  64.7 0.2 all-reduce.7.cloned.1.call-start
  65.0 1.1 copy-done
  66.1 8.7 %fusion.107 = (f32[1536]{0:T(1024)}, f32[1536]{0:T(1024)}, f32[256]{0:T(256)S(1)}, f32[256,1536]{1,0:T(8,128)}) fusion(f32[1,16,16,1536]{3,2,1,0:T(8,128)S(1)} %copy-done, f32[1536]{0:T(1024)} %param.14, bf16[256,3072]{1,0:T(8,128)(2,1)} %copy-done.5, bf16[1536,3072]{1,0:T(8,128)(2,1)} %param.12), kind=kOutput, calls=%fused_computation.321 | convolution fusion | flops 2417881856 | bytes 14175232 | tf_op jit(solution)/shard_map/dot_general | solution.py:38
  74.8 0.6 broadcast_multiply_fusion.8
  75.4 1.4 div.17
  76.8 1.8 multiply_reduce_fusion.49
  78.5 0.1 copy-done.1
  78.6 0.5 copy-done.2
  79.1 4.8 %multiply_reduce_fusion = (f32[1536]{0:T(1024)S(1)}, f32[1536]{0:T(1024)S(1)}, f32[1536]{0:T(1024)S(1)}, f32[1536]{0:T(1024)S(1)}, f32[1536]{0:T(1024)S(1)}, /*i...) fusion(f32[1,16,16,1536]{3,2,1,0:T(8,128)S(1)} %convert_element, ...), kind=kLoop, calls=%fused_computation.205 | loop fusion | flops 15700992 | bytes 6405120 | tf_op jit(solution)/shard_map/reduce_sum | solution.py:56
  83.9 0.6 stack.198
  84.5 0.6 stack.197
  85.1 0.6 stack.196
  85.7 0.6 stack.195
  86.3 0.6 stack.194
  86.9 0.6 stack.193
  87.5 0.6 stack.192
  88.1 0.6 stack.191
  88.7 0.6 stack.190
  89.3 0.6 stack.189
  89.9 0.6 stack.188
  90.5 0.6 stack.187
  91.1 0.6 stack.186
  91.7 0.6 stack.185
  92.3 0.6 stack.184
  92.9 0.6 stack.183
  93.5 0.6 stack.182
  94.1 0.6 stack.181
  94.7 3.7 multiply_reduce_fusion.18
  98.4 0.6 stack.180
  99.0 2.5 fusion.106
  101.9 7.9 %stack.199 = f32[49,1536]{1,0:T(8,128)} concatenate(f32[1,1536]{1,0:T(1,128)S(1)} %stack.150, f32[1,1536]{1,0:T(1,128)S(1)} %stack.151, f32[1,1536]{1,0:T(1,128)S(1)} %stack.152, f32[1,1536]{1,0:T(1,128)S(1)} %stack.153, f32[1,1536]{1,0:T(1,128)S(1)} %stack.154, f32[1,1536]{1,0:T(1,128)S(1)} %stack.155, f32[1,1536]{1,0:T(1,128)S(1)} %stack.156, f32[1,1536]{1,0:T(1,128)S(1)} %stack.157, ...), dimensions={0} | concatenate | bytes 602112 | tf_op jit(solution)/shard_map/stack | solution.py:57
  109.8 0.0 all-reduce.7.cloned.1.call-update
  109.9 11.6 %fusion.100 = bf16[1,16,16,1536]{3,2,1,0:T(8,128)(2,1)} fusion(f32[1,16,16,1536]{3,2,1,0:T(8,128)S(1)} %get-tuple-element.124, bf16[1,16,16,1536]{3,2,1,0:T(8,128)(2,1)S(1)} %copy-done.6, f32[1536]{0:T(1024)S(1)} %get-tuple-element.118, f32[1536]{0:T(1024)S(1)} %get-tuple-element.119, f32[1536]{0:T(1024)S(1)} %get-tuple-element.72, ...), kind=kLoop, calls=%fused_computation.198 | loop fusion | flops 39321600 | bytes 3446784 | tf_op jit(solution)/shard_map/convert_element_type | solution.py:73
  121.4 88.9 %all-reduce.4 = (f32[3072]{0:T(1024)S(1)}, f32[1536]{0:T(1024)S(1)}, f32[1536]{0:T(1024)S(1)}, f32[1536]{0:T(1024)S(1)}) all-reduce(f32[3072]{0:T(1024)S(1)} %copy-done.8, f32[1536]{0:T(1024)S(1)} %copy-done.12, f32[1536]{0:T(1024)S(1)} %copy-done.11, f32[1536]{0:T(1024)S(1)} %get-tuple-element.55), channel_id=1, replica_groups=mesh['col'=8,'row'=32] {'col','row'}, use_global_device_ids=true, to_apply=%region_7.8 | all-reduce | flops 7680 | bytes 61440 | tf_op jit(solution)/shard_map/psum | solution.py:104
  210.4 0.6 broadcast_multiply_fusion.2
  211.0 0.6 broadcast_multiply_fusion.5
  211.6 0.6 dynamic-slice.4
  212.8 0.6 broadcast_multiply_fusion.3
  213.4 88.9 %reduce-scatter.4.cloned.1.call-done = f32[48,3072]{1,0:T(8,128)} async-done(((f32[1536,3072]{1,0:T(8,128)}), f32[48,3072]{1,0:T(8,128)}) %reduce-scatter.4.cloned.1.call-update) | async-done | bytes 589840 | tf_op jit(solution)/shard_map/reduce_scatter | solution.py:94
  302.4 20.3 %fusion = f32[8,3072]{1,0:T(8,128)S(1)} fusion(f32[48,3072]{1,0:T(8,128)} %reduce-scatter.4.cloned.1.call-done), kind=kCustom, calls=%all-reduce-scatter | all-reduce-scatter fusion | flops 196609 | bytes 689152
  322.7 2.4 collective-permute-start
  325.2 2.7 collective-permute-start.1
  327.9 67.0 %all-reduce.7.cloned.1.call-done = f32[49,1536]{1,0:T(8,128)} async-done(((f32[49,1536]{1,0:T(8,128)}), f32[49,1536]{1,0:T(8,128)}) %all-reduce.7.cloned.1.call-update) | async-done | bytes 301072 | tf_op jit(solution)/shard_map/psum | solution.py:104
  394.9 1.7 broadcast_multiply_fusion.1
  396.6 0.3 concatenate
  397.0 0.7 dynamic-slice_multiply_fusion
  (58 shorter events, 0.3 us)
Async XLA Ops:
  8.0 294.4 %reduce-scatter.4.cloned.1.call-start = ((), (), s32[]{:S(2)}) async-start(), calls=%async_computation.1 | async-start | bytes 19464192 | tf_op jit(solution)/shard_map/reduce_scatter | solution.py:94
  27.7 0.7 copy-start.9
  27.7 0.7 copy-start.10
  47.1 1.5 copy-start.3
  55.7 1.2 copy-start.5
  64.7 1.4 copy-start
  64.7 330.1 %all-reduce.7.cloned.1.call-start = ((), (), s32[]{:S(2)}) async-start(), calls=%async_computation.2 | async-start | bytes 688128 | tf_op jit(solution)/shard_map/psum | solution.py:104
  76.7 1.9 copy-start.1
  76.7 2.4 copy-start.2
  76.7 2.4 copy-start.7
  94.7 4.3 %copy-start.4 = (bf16[1,16,16,1536]{3,2,1,0:T(8,128)(2,1)S(1)}, bf16[1,16,16,1536]{3,2,1,0:T(8,128)(2,1)}, u32[]{:S(2)}) copy-start(bf16[1,16,16,1536]{3,2,1,0:T(8,128)(2,1)} %param.9) | copy-start | bytes 2359300
  101.5 8.4 %copy-start.6 = (bf16[1,16,16,1536]{3,2,1,0:T(8,128)(2,1)S(1)}, bf16[1,16,16,1536]{3,2,1,0:T(8,128)(2,1)}, u32[]{:S(2)}) copy-start(bf16[1,16,16,1536]{3,2,1,0:T(8,128)(2,1)} %param.11) | copy-start | bytes 2359300
  109.8 11.6 %copy-start.8 = (f32[3072]{0:T(1024)S(1)}, f32[3072]{0:T(1024)}, u32[]{:S(2)}) copy-start(f32[3072]{0:T(1024)} %get-tuple-element.133) | copy-start | bytes 36868
  109.8 11.6 %copy-start.11 = (f32[1536]{0:T(1024)S(1)}, f32[1536]{0:T(1024)}, u32[]{:S(2)}) copy-start(f32[1536]{0:T(1024)} %get-tuple-element.69) | copy-start | bytes 18436
  109.9 11.6 %copy-start.12 = (f32[1536]{0:T(1024)S(1)}, f32[1536]{0:T(1024)}, u32[]{:S(2)}) copy-start(f32[1536]{0:T(1024)} %get-tuple-element.70) | copy-start | bytes 18436
  109.9 101.7 %copy-start.13 = (u32[256]{0:T(256)S(1)}, u32[256]{0:T(256)}, u32[]{:S(2)}) copy-start(u32[256]{0:T(256)} %constant.36) | copy-start | bytes 3076
  322.7 73.9 %collective-permute-start = (f32[8,3072]{1,0:T(8,128)S(1)}, f32[8,3072]{1,0:T(8,128)S(1)}, u32[]{:S(2)}, u32[]{:S(2)}) collective-permute-start(f32[8,3072]{1,0:T(8,128)S(1)} %fusion), channel_id=1, source_target_pairs={{0,32},{32,64},{64,96},{96,128},{128,160},{160,192},{192,224},{1,3... | collective-permute-start | bytes 294920
  325.2 71.4 %collective-permute-start.1 = (f32[6,3072]{1,0:T(8,128)S(1)}, f32[6,3072]{1,0:T(8,128)S(1)}, u32[]{:S(2)}, u32[]{:S(2)}) collective-permute-start(f32[6,3072]{1,0:T(8,128)S(1)} %slice.680), channel_id=1, source_target_pairs={{0,64},{32,96},{64,128},{96,160},{128,192},{160,224},{1,65},{33,97... | collective-permute-start | bytes 221192
Sparse Core Ops, SparseCore 0:
  64.9 237.4 reduce-scatter.3
Sparse Core Ops, SparseCore 1:
  109.9 284.9 all-reduce.6
where the time goes:
time: 406 us; the launch traced here: 405 us
  waiting for transfers between devices  156 us (38%)
  blocking collectives  109 us (27%)
  local copies, waits for them, and re-layouts  48.5 us (12%)
  other arithmetic  45.6 us (11%)
  matrix products  23.7 us (6%)
  between operations  16.6 us (4%)
  starting transfers between devices  5.41 us (1%)
    reduce_scatter x1, waiting for transfers between devices, per_device(): lax.psum_scatter(lax.dot_general(permuted, pre_grad, (((0,), (0,)), ((),...  88.9 us
    psum x1, blocking collectives, per_device(): lax.psum((grad_bias_up, grad_gain, grad_shift, grad_filter, grad_conv_bia...  88.9 us
    psum x1, waiting for transfers between devices, per_device(): lax.psum((grad_bias_up, grad_gain, grad_shift, grad_filter, grad_conv_bia...  67 us
    unnamed x1, blocking collectives  20.3 us
    another operation x50, local copies, waits for them, and re-layouts, local_backward(): grad_filter = jnp.stack(tap_sums)  19.4 us
    reduce_sum x1, other arithmetic, local_backward(): centred = conv_out - jnp.mean(conv_out, axis=-1, keepdims=True)  13.2 us
    convert_element_type x1, other arithmetic, local_backward(): input_grad.astype(jnp.bfloat16)  11.6 us
    dot_general x1, matrix products, local_backward(): lax.dot_general(pre_grad, w_up, (((1,), (1,)), ((), ())), preferred_eleme...  8.71 us
  transfers between devices with their start and end apart: 4, of which 2 were waited for; matrix products, arithmetic and copies ran while one was open for 19% of the time, Pallas kernels for 0%

commit v1 on v0

v1 whole, which is shorter than its diff:
```python
import jax
import jax.numpy as jnp
import numpy as np
from jax import lax
from jax.experimental import pallas as pl
from jax.experimental.pallas import tpu as pltpu
from jax.sharding import Mesh
from jax.sharding import PartitionSpec as P

LANES = 128
EDGE = 8
VMEM_LIMIT = 60 * 1024 * 1024


def conv_norm_kernel(
    image_ref, taps_ref, bias_ref, gain_ref, shift_ref, order_ref,
    unit_ref, sigma_ref, normed_ref, turned_ref, padded, conv,
):
    side, feat = image_ref.shape[1], image_ref.shape[3]
    blank = jnp.zeros((side, EDGE, LANES), jnp.float32)
    padded[:, 0:EDGE, :] = blank
    padded[:, EDGE + side : EDGE + side + EDGE, :] = blank

    @pl.loop(0, feat // LANES)
    def _(block):
        lanes = pl.ds(pl.multiple_of(block * LANES, LANES), LANES)
        padded[:, EDGE : EDGE + side, :] = image_ref[0, :, :, lanes].astype(jnp.float32)
        start = jnp.broadcast_to(bias_ref[:, lanes], (side, LANES))
        sums = [start] * side
        for tap_col in range(7):
            weights = [
                jnp.broadcast_to(taps_ref[pl.ds(7 * tap_row + tap_col, 1), lanes], (side, LANES))
                for tap_row in range(7)
            ]
            for source in range(side):
                cells = padded[source, EDGE - 3 + tap_col : EDGE - 3 + tap_col + side, :]
                for tap_row in range(7):
                    target = source + 3 - tap_row
                    if 0 <= target < side:
                        sums[target] = sums[target] + cells * weights[tap_row]
        for row in range(side):
            conv[row * side : (row + 1) * side, lanes] = sums[row]

    @pl.loop(0, side)
    def _(row):
        cells = pl.ds(pl.multiple_of(row * side, side), side)
        values = conv[cells, :]
        centred = values - jnp.mean(values, axis=-1, keepdims=True)
        inv_sigma = lax.rsqrt(jnp.mean(centred * centred, axis=-1, keepdims=True) + 1e-06)
        unit = centred * inv_sigma
        unit_ref[cells, :] = unit
        sigma_ref[cells, :] = jnp.broadcast_to(inv_sigma, (side, LANES))
        normed_ref[cells, :] = (unit * gain_ref[...] + shift_ref[...]).astype(jnp.bfloat16)

    width = order_ref.shape[0]
    rows = turned_ref.shape[3]
    for group in range(feat // width):
        y_lo, pair = divmod(group, 2)
        turned = lax.dot_general(
            order_ref[...],
            normed_ref[:, group * width : (group + 1) * width],
            (((1,), (1,)), ((), ())),
            preferred_element_type=jnp.float32,
        ).astype(jnp.bfloat16)
        for within in range(2):
            for y_hi in range(2):
                first = (within * 2 + y_hi) * rows
                turned_ref[2 * pair + within, y_hi, y_lo] = turned[first : first + rows]


def channel_order(rows, along_z):
    width = 4 * rows
    owned = rows // along_z
    target = np.arange(width).reshape(2, along_z, 2, owned).transpose(0, 2, 1, 3).reshape(-1)
    return jnp.asarray(np.eye(width, dtype=np.float32)[target], jnp.bfloat16)


def conv_norm(image, taps, bias, gain, shift, along_z):
    side, feat = image.shape[1], image.shape[3]
    cells = side * side
    rows = feat // 16
    order = channel_order(rows, along_z)
    return pl.pallas_call(
        conv_norm_kernel,
        name="conv_norm",
        out_shape=(
            jax.ShapeDtypeStruct((cells, feat), jnp.float32),
            jax.ShapeDtypeStruct((cells, LANES), jnp.float32),
            jax.ShapeDtypeStruct((cells, feat), jnp.bfloat16),
            jax.ShapeDtypeStruct((4, 2, 2, rows, cells), jnp.bfloat16),
        ),
        scratch_shapes=[
            pltpu.VMEM((side, side + 2 * EDGE, LANES), jnp.float32),
            pltpu.VMEM((cells, feat), jnp.float32),
        ],
        compiler_params=pltpu.CompilerParams(vmem_limit_bytes=VMEM_LIMIT),
        cost_estimate=pl.CostEstimate(flops=2 * 49 * cells * feat, bytes_accessed=cells * feat * 8, transcendentals=0),
    )(image, taps, bias.reshape(1, -1), gain.reshape(1, -1), shift.reshape(1, -1), order)


def slope_kernel(half_ref, normed_ref, w_ref, b_ref, cot_ref, grad_ref, sums_ref):
    pre_act = jnp.dot(normed_ref[...], w_ref[...], preferred_element_type=jnp.float32) + b_ref[...]
    slope = 0.5 * (1.0 + lax.erf(pre_act * 0.7071067811865476)) + pre_act * jnp.exp(
        -0.5 * pre_act * pre_act
    ) * 0.3989422804014327
    pre_grad = (cot_ref[0].astype(jnp.float32) * slope).astype(jnp.bfloat16)
    grad_ref[...] = pre_grad
    sums_ref[...] = jnp.sum(pre_grad.astype(jnp.float32), axis=0, keepdims=True)


def gelu_grad(half, normed, w_up, b_up, cot, width=512):
    cells, feat = normed.shape
    hid = w_up.shape[1] // 2
    steps = hid // width

    def block(i, half_ref):
        return half_ref[0] * steps + i

    return pl.pallas_call(
        slope_kernel,
        name="gelu_grad",
        grid_spec=pltpu.PrefetchScalarGridSpec(
            num_scalar_prefetch=1,
            grid=(steps,),
            in_specs=[
                pl.BlockSpec((cells, feat), lambda i, h: (0, 0)),
                pl.BlockSpec((feat, width), lambda i, h: (0, block(i, h))),
                pl.BlockSpec((1, width), lambda i, h: (0, block(i, h))),
                pl.BlockSpec((1, cells, width), lambda i, h: (0, 0, block(i, h))),
            ],
            out_specs=[
                pl.BlockSpec((cells, width), lambda i, h: (0, i)),
                pl.BlockSpec((1, width), lambda i, h: (0, i)),
            ],
        ),
        out_shape=(
            jax.ShapeDtypeStruct((cells, hid), jnp.bfloat16),
            jax.ShapeDtypeStruct((1, hid), jnp.float32),
        ),
        compiler_params=pltpu.CompilerParams(vmem_limit_bytes=VMEM_LIMIT),
        cost_estimate=pl.CostEstimate(
            flops=2 * cells * feat * hid, bytes_accessed=2 * feat * hid, transcendentals=2 * cells * hid
        ),
    )(half, normed, w_up, b_up.reshape(1, -1), cot)


def norm_grad_kernel(
    half_ref, near_ref, far_ref, w_ref, unit_ref, sigma_ref, gain_ref,
    conv_ref, gain_sum_ref, shift_sum_ref, total,
):
    step = pl.program_id(0)
    half_steps = pl.num_programs(0) // 2

    @pl.when(step == 0)
    def _():
        total[...] = jnp.zeros_like(total)

    dims = (((1,), (1,)), ((), ()))

    @pl.when(step < half_steps)
    def _():
        total[...] += lax.dot_general(near_ref[...], w_ref[...], dims, preferred_element_type=jnp.float32)

    @pl.when(step >= half_steps)
    def _():
        total[...] += lax.dot_general(far_ref[...], w_ref[...], dims, preferred_element_type=jnp.float32)

    @pl.when(step == pl.num_programs(0) - 1)
    def _():
        feat = total.shape[1]
        gain_sum_ref[...] = jnp.zeros_like(gain_sum_ref)
        shift_sum_ref[...] = jnp.zeros_like(shift_sum_ref)

        @pl.loop(0, total.shape[0] // 16)
        def _(row):
            cells = pl.ds(pl.multiple_of(row * 16, 16), 16)
            grad = total[cells, :]
            unit = unit_ref[cells, :]
            gain_sum_ref[...] += jnp.sum(grad * unit, axis=0, keepdims=True)
            shift_sum_ref[...] += jnp.sum(grad, axis=0, keepdims=True)
            unit_grad = grad * gain_ref[...]
            first = jnp.sum(unit_grad, axis=-1, keepdims=True) * (1.0 / feat)
            second = jnp.sum(unit_grad * unit, axis=-1, keepdims=True) * (1.0 / feat)
            conv_ref[cells, :] = sigma_ref[cells, 0:1] * (unit_grad - first - unit * second)


def norm_grad(half, near, far, w_up, unit, sigma, gain, width=512):
    cells, feat = unit.shape
    hid = w_up.shape[1]
    steps = hid // width
    hs = steps // 2

    def block(i, half_ref):
        return lax.rem(half_ref[0] * hs + i, steps)

    return pl.pallas_call(
        norm_grad_kernel,
        name="norm_grad",
        grid_spec=pltpu.PrefetchScalarGridSpec(
            num_scalar_prefetch=1,
            grid=(steps,),
            in_specs=[
                pl.BlockSpec((cells, width), lambda i, h: (0, jnp.minimum(i, hs - 1))),
                pl.BlockSpec((cells, width), lambda i, h: (0, jnp.maximum(i - hs, 0))),
                pl.BlockSpec((feat, width), lambda i, h: (0, block(i, h))),
                pl.BlockSpec((cells, feat), lambda i, h: (0, 0)),
                pl.BlockSpec((cells, LANES), lambda i, h: (0, 0)),
                pl.BlockSpec((1, feat), lambda i, h: (0, 0)),
            ],
            out_specs=[
                pl.BlockSpec((cells, feat), lambda i, h: (0, 0)),
                pl.BlockSpec((1, feat), lambda i, h: (0, 0)),
                pl.BlockSpec((1, feat), lambda i, h: (0, 0)),
            ],
            scratch_shapes=[pltpu.VMEM((cells, feat), jnp.float32)],
        ),
        out_shape=(
            jax.ShapeDtypeStruct((cells, feat), jnp.float32),
            jax.ShapeDtypeStruct((1, feat), jnp.float32),
            jax.ShapeDtypeStruct((1, feat), jnp.float32),
        ),
        compiler_params=pltpu.CompilerParams(vmem_limit_bytes=VMEM_LIMIT),
        cost_estimate=pl.CostEstimate(
            flops=2 * cells * feat * hid, bytes_accessed=2 * feat * hid + 8 * cells * feat, transcendentals=0
        ),
    )(half, near, far, w_up, unit, sigma, gain.reshape(1, -1))


def conv_grad_kernel(grad_ref, image_ref, res_ref, taps_ref, out_ref, tap_sum_ref, bias_sum_ref, padded, image):
    side = image_ref.shape[1]
    blank = jnp.zeros((side, EDGE, LANES), jnp.float32)
    padded[:, 0:EDGE, :] = blank
    padded[:, EDGE + side : EDGE + side + EDGE, :] = blank
    image[...] = image_ref[0].astype(jnp.float32)
    bias_sum = jnp.zeros((side, LANES), jnp.float32)
    for row in range(side):
        cells = grad_ref[row * side : (row + 1) * side, :]
        padded[row, EDGE : EDGE + side, :] = cells
        bias_sum = bias_sum + cells
    bias_sum_ref[...] = jnp.sum(bias_sum, axis=0, keepdims=True)
    sums = [res_ref[0, row].astype(jnp.float32) for row in range(side)]
    for turn_col in range(7):
        weights = [
            jnp.broadcast_to(
                taps_ref[pl.ds(7 * (6 - turn_row) + 6 - turn_col, 1), :], (side, LANES)
            )
            for turn_row in range(7)
        ]
        parts = [jnp.zeros((8, LANES), jnp.float32) for _ in range(7)]
        for source in range(side):
            cells = padded[source, EDGE - 3 + turn_col : EDGE - 3 + turn_col + side, :]
            for turn_row in range(7):
                target = source + 3 - turn_row
                if 0 <= target < side:
                    sums[target] = sums[target] + cells * weights[turn_row]
                    product = cells * image[target]
                    parts[turn_row] = parts[turn_row] + (product[:8] + product[8:])
        for turn_row in range(7):
            tap = 7 * (6 - turn_row) + 6 - turn_col
            tap_sum_ref[tap : tap + 1, :] = jnp.sum(parts[turn_row], axis=0, keepdims=True)
    for row in range(side):
        out_ref[0, row] = sums[row].astype(jnp.bfloat16)


def conv_backward(grad, image, residual, taps):
    side, feat = image.shape[1], image.shape[3]
    cells = side * side
    picture = pl.BlockSpec((1, side, side, LANES), lambda i: (0, 0, 0, i))
    return pl.pallas_call(
        conv_grad_kernel,
        name="conv_backward",
        grid=(feat // LANES,),
        in_specs=[
            pl.BlockSpec((cells, LANES), lambda i: (0, i)),
            picture,
            picture,
            pl.BlockSpec((49, LANES), lambda i: (0, i)),
        ],
        out_specs=[
            picture,
            pl.BlockSpec((49, LANES), lambda i: (0, i)),
            pl.BlockSpec((1, LANES), lambda i: (0, i)),
        ],
        out_shape=(
            jax.ShapeDtypeStruct(image.shape, jnp.bfloat16),
            jax.ShapeDtypeStruct((49, feat), jnp.float32),
            jax.ShapeDtypeStruct((1, feat), jnp.float32),
        ),
        scratch_shapes=[
            pltpu.VMEM((side, side + 2 * EDGE, LANES), jnp.float32),
            pltpu.VMEM((side, side, LANES), jnp.float32),
        ],
        compiler_params=pltpu.CompilerParams(vmem_limit_bytes=VMEM_LIMIT),
        cost_estimate=pl.CostEstimate(flops=4 * 49 * cells * feat, bytes_accessed=cells * feat * 10, transcendentals=0),
    )(grad, image, residual, taps)


def product_kernel(near_t_ref, far_t_ref, near_ref, far_ref, out_ref):
    out_ref[0] = (
        jnp.dot(near_t_ref[0], near_ref[...], preferred_element_type=jnp.float32)
        + jnp.dot(far_t_ref[0], far_ref[...], preferred_element_type=jnp.float32)
    ).astype(jnp.bfloat16)


def product(near_t, far_t, near, far):
    blocks, rows, cells = near_t.shape
    columns = near.shape[1]
    left = pl.BlockSpec((1, rows, cells), lambda i: (i, 0, 0))
    right = pl.BlockSpec((cells, columns), lambda i: (0, 0))
    return pl.pallas_call(
        product_kernel,
        name="product",
        grid=(blocks,),
        in_specs=[left, left, right, right],
        out_specs=pl.BlockSpec((1, rows, columns), lambda i: (i, 0, 0)),
        out_shape=jax.ShapeDtypeStruct((blocks, rows, columns), jnp.bfloat16),
        compiler_params=pltpu.CompilerParams(vmem_limit_bytes=VMEM_LIMIT),
        cost_estimate=pl.CostEstimate(
            flops=4 * blocks * rows * cells * columns, bytes_accessed=2 * blocks * rows * columns, transcendentals=0
        ),
    )(near_t, far_t, near, far)


def per_device(images, hidden_cot, residual_cot, w_up, b_up, ln_gain, ln_bias, dw_weight, dw_bias):
    feat, hid = w_up.shape
    everyone = ("y_lo", "x", "z", "y_hi", "core")
    along_z = lax.axis_size("z")
    devices = 1
    for name in everyone:
        devices *= lax.axis_size(name)
    inverse_count = 1.0 / (images.shape[0] * devices)
    mine = lax.axis_index("core").astype(jnp.int32).reshape(1)
    swap = [(0, 1), (1, 0)]

    unit, sigma, normed, turned = conv_norm(images, dw_weight, dw_bias, ln_gain, ln_bias, along_z)
    far_turned = lax.ppermute(turned, "core", swap)
    away, away_sums = gelu_grad(1 - mine, normed, w_up, b_up, hidden_cot)
    far = lax.ppermute(away, "core", swap)
    near, near_sums = gelu_grad(mine, normed, w_up, b_up, hidden_cot)
    cells = normed.shape[0]
    partial = product(turned.reshape(4, -1, cells), far_turned.reshape(4, -1, cells), near, far)

    by_x = lax.psum_scatter(partial.reshape(feat, -1), "x", scatter_dimension=0, tiled=True)
    by_y = lax.psum_scatter(by_x, ("y_hi", "y_lo"), scatter_dimension=0, tiled=True)
    pieces = 2 * along_z
    last = lax.all_to_all(by_y.reshape(pieces, -1, LANES), ("z", "core"), 0, 0, tiled=True)
    last = last.astype(jnp.float32).reshape(along_z, 2, feat // devices, hid // 2)
    owned = jnp.sum(last, axis=0).transpose(1, 0, 2).reshape(feat // devices, hid) * inverse_count

    conv_grad, gain_sum, shift_sum = norm_grad(mine, near, away, w_up, unit, sigma, ln_gain)
    grad_input, tap_sums, bias_sum = conv_backward(conv_grad, images, residual_cot, dw_weight)
    first = jnp.where(mine == 0, near_sums, away_sums)
    second = jnp.where(mine == 0, away_sums, near_sums)
    used = 49 + 3 + hid // feat
    rows = -(-used // 64) * 64
    small = jnp.concatenate(
        [
            tap_sums,
            gain_sum,
            shift_sum,
            bias_sum,
            first.reshape(-1, feat),
            second.reshape(-1, feat),
            jnp.zeros((rows - used, feat), jnp.float32),
        ],
        axis=0,
    )
    small = lax.all_to_all(small.reshape(devices, 1, -1), everyone, 0, 0, tiled=True)
    small = jnp.sum(small, axis=0, keepdims=True) * inverse_count
    small = lax.all_to_all(
        jnp.broadcast_to(small, (devices, 1, small.shape[2])), everyone, 0, 0, tiled=True
    ).reshape(rows, feat)
    return (
        grad_input,
        owned,
        small[52:used].reshape(hid),
        small[49],
        small[50],
        small[:49],
        small[51],
    )


def solution(mesh):
    x, z = 4, mesh.devices.size // 32
    split = Mesh(mesh.devices.reshape(2, x, z, 2, 2), ("y_lo", "x", "z", "y_hi", "core"))
    images = P(("y_lo", "x", "z", "y_hi", "core"))
    return jax.shard_map(
        per_device,
        mesh=split,
        in_specs=(images, images, images, P(), P(), P(), P(), P(), P()),
        out_specs=(images, images, P(), P(), P(), P(), P()),
        check_vma=False,
    )
```

time: 406 us -> 206 us (0.51)
  blocking collectives: 109 us -> 28.6 us
  waiting for transfers between devices: 156 us -> 78.7 us
  Pallas kernels: 0 us -> 52.3 us
  other arithmetic: 45.6 us -> 1.04 us
  local copies, waits for them, and re-layouts: 48.5 us -> 14.8 us
  matrix products: 23.7 us -> 0 us
  starting transfers between devices: 5.41 us -> 15.3 us
    psum x1 -> x0, blocking collectives: 88.9 us -> none  [per_device(): lax.psum((grad_bias_up, grad_gain, grad_shift, grad_filter, grad_conv_bia...]
    psum x1 -> x0, waiting for transfers between devices: 67 us -> none  [per_device(): lax.psum((grad_bias_up, grad_gain, grad_shift, grad_filter, grad_conv_bia...]
    pallas_call x0 -> x6, Pallas kernels: none -> 52.3 us  [the longest x1 12.4 us: conv_backward(): pl.pallas_call(conv_grad_kernel, name='conv_backward', grid=(feat // LANE...]
    reduce_scatter x1 -> x2, waiting for transfers between devices: 88.9 us -> 54.9 us  [the longest x1 54.8 us: per_device(): lax.psum_scatter(partial.reshape(feat, -1), 'x', scatter_dimension=0, til...]
    all_to_all x0 -> x1, blocking collectives: none -> 28.6 us  [per_device(): lax.all_to_all(small.reshape(devices, 1, -1), everyone, 0, 0, tiled=True)]
    another operation x51 -> x0, local copies, waits for them, and re-layouts: 27.5 us -> none  [the longest x50 19.4 us: local_backward(): grad_filter = jnp.stack(tap_sums)]
    reduce_sum x6 -> x2, other arithmetic: 26.2 us -> 0.37 us  [the longest x1 0.31 us: per_device(): small = jnp.sum(small, axis=0, keepdims=True) * inverse_count]
    all_to_all x0 -> x2, waiting for transfers between devices: none -> 23.8 us  [the longest x1 15.4 us: per_device(): lax.all_to_all(jnp.broadcast_to(small, (devices, 1, small.shape[2])), eve...]
  transfers between devices with their start and end apart: 4 -> 6, of which waited for: 2 -> 3; matrix products, arithmetic and copies ran while one was open for 19% -> 5% of each run, Pallas kernels for 0% -> 17%
where the time goes in v1:
time: 206 us; the launch traced here: 205 us
  waiting for transfers between devices  78.7 us (38%)
  Pallas kernels  52.3 us (25%)
  blocking collectives  28.6 us (14%)
  starting transfers between devices  15.3 us (7%)
  local copies, waits for them, and re-layouts  14.8 us (7%)
  between operations  14.2 us (7%)
    reduce_scatter x1, waiting for transfers between devices, per_device(): lax.psum_scatter(partial.reshape(feat, -1), 'x', scatter_dimension=0, til...  54.8 us
    all_to_all x1, blocking collectives, per_device(): lax.all_to_all(small.reshape(devices, 1, -1), everyone, 0, 0, tiled=True)  28.6 us
    all_to_all x1, waiting for transfers between devices, per_device(): lax.all_to_all(jnp.broadcast_to(small, (devices, 1, small.shape[2])), eve...  15.4 us
    pallas_call x1, Pallas kernels, conv_backward(): pl.pallas_call(conv_grad_kernel, name='conv_backward', grid=(feat // LANE...  12.4 us
    pallas_call x1, Pallas kernels, norm_grad(): pl.pallas_call(norm_grad_kernel, name='norm_grad', grid_spec=pltpu.Prefet...  11.4 us
    pallas_call x2, Pallas kernels, gelu_grad(): pl.pallas_call(slope_kernel, name='gelu_grad', grid_spec=pltpu.PrefetchSc...  11.3 us
    pallas_call x1, Pallas kernels, conv_norm(): pl.pallas_call(conv_norm_kernel, name='conv_norm', out_shape=(jax.ShapeDt...  10.9 us
    all_to_all x1, waiting for transfers between devices, per_device(): lax.all_to_all(by_y.reshape(pieces, -1, LANES), ('z', 'core'), 0, 0, tile...  8.43 us
  transfers between devices with their start and end apart: 6, of which 3 were waited for; matrix products, arithmetic and copies ran while one was open for 5% of the time, Pallas kernels for 17%

profile of v1, /device:TPU:1, one launch (start us, length us, event | category | flops | bytes accessed | tf_op | source)
XLA Modules:
  0.0 205.1 jit_solution(9775019873233111064)
XLA Ops:
  7.2 0.0 reduce-scatter.3.cloned.1.call-start
  7.2 1.3 reshape.81.bias_ref
  8.5 1.3 reshape.82.gain_ref
  9.8 1.3 reshape.83.shift_ref
  11.1 10.9 %conv_norm.1 = (f32[256,1536]{1,0:T(8,128)}, f32[256,128]{1,0:T(8,128)}, bf16[256,1536]{1,0:T(8,128)(2,1)}, bf16[4,2,2,96,256]{4,3,2,1,0:T(8,128)(2,1)}) custom-call(bf16[1,16,16,1536]{3,2,1,0:T(8,128)(2,1)} %image_ref.3, f32[49,1536]{1,0:T(8,128)} %taps_ref.3, f32[1,1536]{1,0:T(1,128)} %reshape.81.bias_ref, f32[1,1536]{1,0:T(1,128)} %reshape.82.gain_ref, ...), custom_call_target="tpu_custom_call" | custom-call | flops 38535168 | bytes 3145728 | tf_op jit(solution)/shard_map/conv_norm/pallas_call | solution.py:83
  22.0 3.2 %collective-permute-start = (bf16[4,2,2,96,256]{4,3,2,1,0:T(8,128)(2,1)}, bf16[4,2,2,96,256]{4,3,2,1,0:T(8,128)(2,1)S(1)}, u32[]{:S(2)}, u32[]{:S(2)}) collective-permute-start(bf16[4,2,2,96,256]{4,3,2,1,0:T(8,128)(2,1)} %get-tuple-element.28), channel_id=1, source_target_pairs={{0,1},{1,0},{2,3},{3,2},{4,5},{5,4},{6,7},{7,6},{8,9},{9,8},{10,11... | collective-permute-start | bytes 2359304 | tf_op jit(solution)/shard_map/ppermute | solution.py:336
  25.2 5.6 %gelu_grad.3 = (bf16[256,1536]{1,0:T(8,128)(2,1)}, f32[1,1536]{1,0:T(1,128)}) custom-call(s32[1]{0:T(128)S(6)} %sub.3.half_ref, bf16[256,1536]{1,0:T(8,128)(2,1)} %get-tuple-element.21.normed_ref, bf16[1536,3072]{1,0:T(8,128)(2,1)} %w_ref.5, f32[1,3072]{1,0:T(1,128)} %bitcast.12, bf16[1,256,3072]{2,1,0:T(8,128)(2,1)} %cot_ref.3), custom_call_target="tpu_custom_call" | custom-call | flops 1207959552 | bytes 4718592 | tf_op jit(solution)/shard_map/gelu_grad/pallas_call | solution.py:119
  30.8 0.0 collective-permute-start.1
  30.9 5.7 %gelu_grad.2 = (bf16[256,1536]{1,0:T(8,128)(2,1)}, f32[1,1536]{1,0:T(1,128)}) custom-call(s32[1]{0:T(128)} %bitcast.half_ref, bf16[256,1536]{1,0:T(8,128)(2,1)} %get-tuple-element.21.normed_ref, bf16[1536,3072]{1,0:T(8,128)(2,1)} %w_ref.5, f32[1,3072]{1,0:T(1,128)} %bitcast.13, bf16[1,256,3072]{2,1,0:T(8,128)(2,1)} %cot_ref.3), custom_call_target="tpu_custom_call" | custom-call | flops 1207959552 | bytes 4718592 | tf_op jit(solution)/shard_map/gelu_grad/pallas_call | solution.py:119
  36.5 0.0 collective-permute-done
  36.5 0.0 copy-start.4
  36.6 0.0 collective-permute-done.1.far_ref
  36.6 0.0 copy-start.5
  36.6 0.8 copy-done.4
  37.4 0.3 copy-done.5
  37.7 6.4 %product.1 = bf16[4,384,1536]{2,1,0:T(8,128)(2,1)} custom-call(bf16[4,384,256]{2,1,0:T(8,128)(2,1)} %bitcast.15, bf16[4,384,256]{2,1,0:T(8,128)(2,1)} %bitcast.16, bf16[256,1536]{1,0:T(8,128)(2,1)} %get-tuple-element.22.near_ref, bf16[256,1536]{1,0:T(8,128)(2,1)} %copy-done.5), custom_call_target="tpu_custom_call" | custom-call | flops 2415919104 | bytes 4718592 | tf_op jit(solution)/shard_map/product/pallas_call | solution.py:310
  44.2 0.0 reduce-scatter.3.cloned.1.call-update
  44.2 0.0 reduce-scatter.5.cloned.1.call-start
  44.3 54.8 %reduce-scatter.3.cloned.1.call-done = bf16[384,1536]{1,0:T(8,128)(2,1)} async-done(((bf16[1536,1536]{1,0:T(8,128)(2,1)}), bf16[384,1536]{1,0:T(8,128)(2,1)}) %reduce-scatter.3.cloned.1.call-update) | async-done | bytes 1179664 | tf_op jit(solution)/shard_map/reduce_scatter | solution.py:343
  99.1 0.0 reduce-scatter.5.cloned.1.call-update
  99.1 11.4 %norm_grad.1 = (f32[256,1536]{1,0:T(8,128)}, f32[1,1536]{1,0:T(1,128)}, f32[1,1536]{1,0:T(1,128)}) custom-call(s32[1]{0:T(128)} %bitcast.half_ref, bf16[256,1536]{1,0:T(8,128)(2,1)} %get-tuple-element.22.near_ref, bf16[256,1536]{1,0:T(8,128)(2,1)} %get-tuple-element.23.far_ref, bf16[1536,3072]{1,0:T(8,128)(2,1)} %w_ref.5, ...), custom_call_target="tpu_custom_call" | custom-call | flops 2415919104 | bytes 12582912 | tf_op jit(solution)/shard_map/norm_grad/pallas_call | solution.py:196
  110.5 0.0 copy-start.2
  110.5 0.0 copy-start.3
  110.5 0.0 copy-start
  110.5 0.0 copy-start.1
  110.5 12.4 %conv_backward.1 = (bf16[1,16,16,1536]{3,2,1,0:T(8,128)(2,1)}, f32[49,1536]{1,0:T(8,128)}, f32[1,1536]{1,0:T(1,128)}) custom-call(f32[256,1536]{1,0:T(8,128)} %get-tuple-element.26.grad_ref, bf16[1,16,16,1536]{3,2,1,0:T(8,128)(2,1)} %image_ref.3, bf16[1,16,16,1536]{3,2,1,0:T(8,128)(2,1)} %res_ref.1, f32[49,1536]{1,0:T(8,128)} %taps_ref.3), custom_call_target="tpu_custom_call" | custom-call | flops 77070336 | bytes 3932160 | tf_op jit(solution)/shard_map/conv_backward/pallas_call | solution.py:269
  122.9 0.0 copy-done.2
  122.9 0.0 copy-done.3
  122.9 0.0 copy-done
  122.9 0.0 copy-done.1
  123.0 1.9 concatenate.3
  124.9 0.5 reshape.95
  125.4 28.6 %all_to_all.15 = f32[256,1,384]{2,1,0:T(1,128)S(1)} all-to-all(f32[256,1,384]{2,1,0:T(1,128)S(1)} %reshape.95), channel_id=1, replica_groups=mesh['y_lo'=2,'x'=4,'z'=8,'y_hi'=2,'core'=2] {'y_lo','x','z','y_hi','core'}, dimensions={0} | all-to-all | bytes 786432 | tf_op jit(solution)/shard_map/all_to_all | solution.py:368
  154.0 0.3 reduce_sum.19
  154.3 0.9 broadcast_in_dim.22
  155.3 6.8 %all-to-all-start.2 = ((f32[256,1,384]{2,1,0:T(1,128)}), f32[256,1,384]{2,1,0:T(1,128)S(1)}, u32[]{:S(2)}, u32[]{:S(2)}) async-start(f32[256,1,384]{2,1,0:T(1,128)} %broadcast_in_dim.22), calls=%async_computation.4 | async-start | bytes 786432 | tf_op jit(solution)/shard_map/all_to_all | solution.py:370
  162.1 0.0 reduce-scatter.5.cloned.1.call-done
  162.1 2.0 reshape.88
  164.2 15.4 %all-to-all-done.2 = f32[256,1,384]{2,1,0:T(1,128)S(1)} async-done(((f32[256,1,384]{2,1,0:T(1,128)}), f32[256,1,384]{2,1,0:T(1,128)S(1)}, u32[]{:S(2)}, u32[]{:S(2)}) %all-to-all-start.2) | async-done | bytes 393248 | tf_op jit(solution)/shard_map/all_to_all | solution.py:370
  179.6 5.2 %all-to-all-start = ((bf16[16,72,128]{2,1,0:T(8,128)(2,1)}), bf16[16,72,128]{2,1,0:T(8,128)(2,1)S(1)}, u32[]{:S(2)}, u32[]{:S(2)}) async-start(bf16[16,72,128]{2,1,0:T(8,128)(2,1)} %reshape.88), calls=%async_computation.2 | async-start | bytes 589824 | tf_op jit(solution)/shard_map/all_to_all | solution.py:346
  184.7 0.1 slice_reduce_fusion.1
  184.8 0.6 squeeze.9
  185.4 0.6 squeeze.10
  186.0 0.8 slice_reduce_fusion
  186.8 0.8 slice.26
  187.5 0.6 squeeze.11
  188.1 0.6 slice.28
  188.8 8.4 %all-to-all-done = bf16[16,72,128]{2,1,0:T(8,128)(2,1)S(1)} async-done(((bf16[16,72,128]{2,1,0:T(8,128)(2,1)}), bf16[16,72,128]{2,1,0:T(8,128)(2,1)S(1)}, u32[]{:S(2)}, u32[]{:S(2)}) %all-to-all-start) | async-done | bytes 294944 | tf_op jit(solution)/shard_map/all_to_all | solution.py:346
  197.2 0.3 reshape.94
  197.5 0.1 reduce_sum.18
  197.6 0.7 broadcast_multiply_fusion
  (3 shorter events, 0.0 us)
Async XLA Ops:
  7.2 91.9 %reduce-scatter.3.cloned.1.call-start = ((), (), s32[]{:S(2)}) async-start(), calls=%async_computation.5 | async-start | bytes 5898240 | tf_op jit(solution)/shard_map/reduce_scatter | solution.py:343
  22.0 14.6 %collective-permute-start = (bf16[4,2,2,96,256]{4,3,2,1,0:T(8,128)(2,1)}, bf16[4,2,2,96,256]{4,3,2,1,0:T(8,128)(2,1)S(1)}, u32[]{:S(2)}, u32[]{:S(2)}) collective-permute-start(bf16[4,2,2,96,256]{4,3,2,1,0:T(8,128)(2,1)} %get-tuple-element.28), channel_id=1, source_target_pairs={{0,1},{1,0},{2,3},{3,2},{4,5},{5,4},{6,7},{7,6},{8,9},{9,8},{10,11... | collective-permute-start | bytes 2359304 | tf_op jit(solution)/shard_map/ppermute | solution.py:336
  30.8 5.7 %collective-permute-start.1 = (bf16[256,1536]{1,0:T(8,128)(2,1)}, bf16[256,1536]{1,0:T(8,128)(2,1)S(1)}, u32[]{:S(2)}, u32[]{:S(2)}) collective-permute-start(bf16[256,1536]{1,0:T(8,128)(2,1)} %get-tuple-element.23.far_ref), channel_id=1, source_target_pairs={{0,1},{1,0},{2,3},{3,2},{4,5},{5,4},{6,7},{7,6},{8,9},{9,8},{10,11... | collective-permute-start | bytes 2359304 | tf_op jit(solution)/shard_map/ppermute | solution.py:338
  36.5 0.9 copy-start.4
  36.6 1.2 copy-start.5
  44.2 117.9 %reduce-scatter.5.cloned.1.call-start = ((), (), s32[]{:S(2)}) async-start(), calls=%async_computation.6 | async-start | bytes 1474560 | tf_op jit(solution)/shard_map/reduce_scatter | solution.py:344
  110.5 12.4 %copy-start.2 = (f32[1,1536]{1,0:T(1,128)S(1)}, f32[1,1536]{1,0:T(1,128)}, u32[]{:S(2)}) copy-start(f32[1,1536]{1,0:T(1,128)} %get-tuple-element.34) | copy-start | bytes 18436
  110.5 12.4 %copy-start.3 = (f32[1,1536]{1,0:T(1,128)S(1)}, f32[1,1536]{1,0:T(1,128)}, u32[]{:S(2)}) copy-start(f32[1,1536]{1,0:T(1,128)} %get-tuple-element.33) | copy-start | bytes 18436
  110.5 12.4 %copy-start = (f32[1,1536]{1,0:T(1,128)S(1)}, f32[1,1536]{1,0:T(1,128)}, u32[]{:S(2)}) copy-start(f32[1,1536]{1,0:T(1,128)} %get-tuple-element.30) | copy-start | bytes 18436
  110.5 12.4 %copy-start.1 = (f32[1,1536]{1,0:T(1,128)S(1)}, f32[1,1536]{1,0:T(1,128)}, u32[]{:S(2)}) copy-start(f32[1,1536]{1,0:T(1,128)} %get-tuple-element.31) | copy-start | bytes 18436
  155.3 24.3 %all-to-all-start.2 = ((f32[256,1,384]{2,1,0:T(1,128)}), f32[256,1,384]{2,1,0:T(1,128)S(1)}, u32[]{:S(2)}, u32[]{:S(2)}) async-start(f32[256,1,384]{2,1,0:T(1,128)} %broadcast_in_dim.22), calls=%async_computation.4 | async-start | bytes 786432 | tf_op jit(solution)/shard_map/all_to_all | solution.py:370
  179.6 17.6 %all-to-all-start = ((bf16[16,72,128]{2,1,0:T(8,128)(2,1)}), bf16[16,72,128]{2,1,0:T(8,128)(2,1)S(1)}, u32[]{:S(2)}, u32[]{:S(2)}) async-start(bf16[16,72,128]{2,1,0:T(8,128)(2,1)} %reshape.88), calls=%async_computation.2 | async-start | bytes 589824 | tf_op jit(solution)/shard_map/all_to_all | solution.py:346
Sparse Core Ops, SparseCore 0:
  44.3 54.7 reduce-scatter.2
  101.7 25.1 reduce-scatter.4

commit v2 on v1

--- a/solution.py
+++ b/solution.py
@@ -1,3 +1,5 @@
+import functools
+
 import jax
 import jax.numpy as jnp
 import numpy as np
@@ -10,6 +12,7 @@
 LANES = 128
 EDGE = 8
 VMEM_LIMIT = 60 * 1024 * 1024
+SMALL = pl.CostEstimate(flops=1000, bytes_accessed=1000, transcendentals=0)
 
 
 def conv_norm_kernel(
@@ -94,11 +97,11 @@
             pltpu.VMEM((cells, feat), jnp.float32),
         ],
         compiler_params=pltpu.CompilerParams(vmem_limit_bytes=VMEM_LIMIT),
-        cost_estimate=pl.CostEstimate(flops=2 * 49 * cells * feat, bytes_accessed=cells * feat * 8, transcendentals=0),
-    )(image, taps, bias.reshape(1, -1), gain.reshape(1, -1), shift.reshape(1, -1), order)
-
-
-def slope_kernel(half_ref, normed_ref, w_ref, b_ref, cot_ref, grad_ref, sums_ref):
+        cost_estimate=SMALL,
+    )(image, taps, bias.reshape(1, -1), gain, shift.reshape(1, -1), order)
+
+
+def slope_kernel(start_ref, normed_ref, w_ref, b_ref, cot_ref, grad_ref, sums_ref):
     pre_act = jnp.dot(normed_ref[...], w_ref[...], preferred_element_type=jnp.float32) + b_ref[...]
     slope = 0.5 * (1.0 + lax.erf(pre_act * 0.7071067811865476)) + pre_act * jnp.exp(
         -0.5 * pre_act * pre_act
@@ -108,14 +111,9 @@
     sums_ref[...] = jnp.sum(pre_grad.astype(jnp.float32), axis=0, keepdims=True)
 
 
-def gelu_grad(half, normed, w_up, b_up, cot, width=512):
+def gelu_grad(start, steps, normed, w_up, b_up, cot, width):
     cells, feat = normed.shape
-    hid = w_up.shape[1] // 2
-    steps = hid // width
-
-    def block(i, half_ref):
-        return half_ref[0] * steps + i
-
+    hid = steps * width
     return pl.pallas_call(
         slope_kernel,
         name="gelu_grad",
@@ -123,14 +121,14 @@
             num_scalar_prefetch=1,
             grid=(steps,),
             in_specs=[
-                pl.BlockSpec((cells, feat), lambda i, h: (0, 0)),
-                pl.BlockSpec((feat, width), lambda i, h: (0, block(i, h))),
-                pl.BlockSpec((1, width), lambda i, h: (0, block(i, h))),
-                pl.BlockSpec((1, cells, width), lambda i, h: (0, 0, block(i, h))),
+                pl.BlockSpec((cells, feat), lambda i, s: (0, 0)),
+                pl.BlockSpec((feat, width), lambda i, s: (0, s[0] + i)),
+                pl.BlockSpec((1, width), lambda i, s: (0, s[0] + i)),
+                pl.BlockSpec((1, cells, width), lambda i, s: (0, 0, s[0] + i)),
             ],
             out_specs=[
-                pl.BlockSpec((cells, width), lambda i, h: (0, i)),
-                pl.BlockSpec((1, width), lambda i, h: (0, i)),
+                pl.BlockSpec((cells, width), lambda i, s: (0, i)),
+                pl.BlockSpec((1, width), lambda i, s: (0, i)),
             ],
         ),
         out_shape=(
@@ -138,32 +136,37 @@
             jax.ShapeDtypeStruct((1, hid), jnp.float32),
         ),
         compiler_params=pltpu.CompilerParams(vmem_limit_bytes=VMEM_LIMIT),
-        cost_estimate=pl.CostEstimate(
-            flops=2 * cells * feat * hid, bytes_accessed=2 * feat * hid, transcendentals=2 * cells * hid
-        ),
-    )(half, normed, w_up, b_up.reshape(1, -1), cot)
+        cost_estimate=SMALL,
+    )(start, normed, w_up, b_up, cot)
 
 
 def norm_grad_kernel(
-    half_ref, near_ref, far_ref, w_ref, unit_ref, sigma_ref, gain_ref,
+    start_ref, first_ref, second_ref, away_ref, w_ref, unit_ref, sigma_ref, gain_ref,
     conv_ref, gain_sum_ref, shift_sum_ref, total,
 ):
     step = pl.program_id(0)
-    half_steps = pl.num_programs(0) // 2
+    quarter = pl.num_programs(0) // 4
 
     @pl.when(step == 0)
     def _():
         total[...] = jnp.zeros_like(total)
 
-    dims = (((1,), (1,)), ((), ()))
-
-    @pl.when(step < half_steps)
+    def add(grad_ref):
+        total[...] += lax.dot_general(
+            grad_ref[...], w_ref[...], (((1,), (1,)), ((), ())), preferred_element_type=jnp.float32
+        )
+
+    @pl.when(step < quarter)
     def _():
-        total[...] += lax.dot_general(near_ref[...], w_ref[...], dims, preferred_element_type=jnp.float32)
-
-    @pl.when(step >= half_steps)
+        add(first_ref)
+
+    @pl.when((step >= quarter) & (step < 2 * quarter))
     def _():
-        total[...] += lax.dot_general(far_ref[...], w_ref[...], dims, preferred_element_type=jnp.float32)
+        add(second_ref)
+
+    @pl.when(step >= 2 * quarter)
+    def _():
+        add(away_ref)
 
     @pl.when(step == pl.num_programs(0) - 1)
     def _():
@@ -184,15 +187,11 @@
             conv_ref[cells, :] = sigma_ref[cells, 0:1] * (unit_grad - first - unit * second)
 
 
-def norm_grad(half, near, far, w_up, unit, sigma, gain, width=512):
+def norm_grad(start, first, second, away, w_up, unit, sigma, gain, width):
     cells, feat = unit.shape
     hid = w_up.shape[1]
     steps = hid // width
-    hs = steps // 2
-
-    def block(i, half_ref):
-        return lax.rem(half_ref[0] * hs + i, steps)
-
+    quarter = steps // 4
     return pl.pallas_call(
         norm_grad_kernel,
         name="norm_grad",
@@ -200,17 +199,18 @@
             num_scalar_prefetch=1,
             grid=(steps,),
             in_specs=[
-                pl.BlockSpec((cells, width), lambda i, h: (0, jnp.minimum(i, hs - 1))),
-                pl.BlockSpec((cells, width), lambda i, h: (0, jnp.maximum(i - hs, 0))),
-                pl.BlockSpec((feat, width), lambda i, h: (0, block(i, h))),
-                pl.BlockSpec((cells, feat), lambda i, h: (0, 0)),
-                pl.BlockSpec((cells, LANES), lambda i, h: (0, 0)),
-                pl.BlockSpec((1, feat), lambda i, h: (0, 0)),
+                pl.BlockSpec((cells, width), lambda i, s: (0, jnp.minimum(i, quarter - 1))),
+                pl.BlockSpec((cells, width), lambda i, s: (0, jnp.clip(i - quarter, 0, quarter - 1))),
+                pl.BlockSpec((cells, width), lambda i, s: (0, jnp.maximum(i - 2 * quarter, 0))),
+                pl.BlockSpec((feat, width), lambda i, s: (0, lax.rem(s[0] + i, steps))),
+                pl.BlockSpec((cells, feat), lambda i, s: (0, 0)),
+                pl.BlockSpec((cells, LANES), lambda i, s: (0, 0)),
+                pl.BlockSpec((1, feat), lambda i, s: (0, 0)),
             ],
             out_specs=[
-                pl.BlockSpec((cells, feat), lambda i, h: (0, 0)),
-                pl.BlockSpec((1, feat), lambda i, h: (0, 0)),
-                pl.BlockSpec((1, feat), lambda i, h: (0, 0)),
+                pl.BlockSpec((cells, feat), lambda i, s: (0, 0)),
+                pl.BlockSpec((1, feat), lambda i, s: (0, 0)),
+                pl.BlockSpec((1, feat), lambda i, s: (0, 0)),
             ],
             scratch_shapes=[pltpu.VMEM((cells, feat), jnp.float32)],
         ),
@@ -220,10 +220,8 @@
             jax.ShapeDtypeStruct((1, feat), jnp.float32),
         ),
         compiler_params=pltpu.CompilerParams(vmem_limit_bytes=VMEM_LIMIT),
-        cost_estimate=pl.CostEstimate(
-            flops=2 * cells * feat * hid, bytes_accessed=2 * feat * hid + 8 * cells * feat, transcendentals=0
-        ),
-    )(half, near, far, w_up, unit, sigma, gain.reshape(1, -1))
+        cost_estimate=SMALL,
+    )(start, first, second, away, w_up, unit, sigma, gain)
 
 
 def conv_grad_kernel(grad_ref, image_ref, res_ref, taps_ref, out_ref, tap_sum_ref, bias_sum_ref, padded, image):
@@ -291,85 +289,155 @@
             pltpu.VMEM((side, side, LANES), jnp.float32),
         ],
         compiler_params=pltpu.CompilerParams(vmem_limit_bytes=VMEM_LIMIT),
-        cost_estimate=pl.CostEstimate(flops=4 * 49 * cells * feat, bytes_accessed=cells * feat * 10, transcendentals=0),
+        cost_estimate=SMALL,
     )(grad, image, residual, taps)
 
 
-def product_kernel(near_t_ref, far_t_ref, near_ref, far_ref, out_ref):
-    out_ref[0] = (
-        jnp.dot(near_t_ref[0], near_ref[...], preferred_element_type=jnp.float32)
-        + jnp.dot(far_t_ref[0], far_ref[...], preferred_element_type=jnp.float32)
+def product_kernel(x_first, place_ref, near_t_ref, far_t_ref, near_ref, far_ref, *out_refs):
+    rows = near_t_ref.shape[2]
+    cells = near_t_ref.shape[3]
+    block = (
+        jnp.dot(near_t_ref[...].reshape(4 * rows, cells), near_ref[...], preferred_element_type=jnp.float32)
+        + jnp.dot(far_t_ref[...].reshape(4 * rows, cells), far_ref[...], preferred_element_type=jnp.float32)
     ).astype(jnp.bfloat16)
-
-
-def product(near_t, far_t, near, far):
-    blocks, rows, cells = near_t.shape
-    columns = near.shape[1]
-    left = pl.BlockSpec((1, rows, cells), lambda i: (i, 0, 0))
-    right = pl.BlockSpec((cells, columns), lambda i: (0, 0))
-    return pl.pallas_call(
-        product_kernel,
+    inner = place_ref[1] if x_first else place_ref[0]
+    for away in range(4):
+
+        @pl.when(pl.program_id(0) == away)
+        def _():
+            for index in range(4):
+                out_refs[away][lax.rem(index - inner + 4, 4)] = block[index * rows : (index + 1) * rows]
+
+
+def product(place, near_t, far_t, near, far, part, columns, x_first):
+    _, _, rows, cells = near_t.shape
+    if x_first:
+        left = pl.BlockSpec((1, 4, rows, cells), lambda i, p: (lax.rem(p[0] + i, 4), 0, 0, 0))
+    else:
+        left = pl.BlockSpec((4, 1, rows, cells), lambda i, p: (0, lax.rem(p[1] + i, 4), 0, 0))
+    return pl.pallas_call(
+        functools.partial(product_kernel, x_first),
         name="product",
-        grid=(blocks,),
-        in_specs=[left, left, right, right],
-        out_specs=pl.BlockSpec((1, rows, columns), lambda i: (i, 0, 0)),
-        out_shape=jax.ShapeDtypeStruct((blocks, rows, columns), jnp.bfloat16),
-        compiler_params=pltpu.CompilerParams(vmem_limit_bytes=VMEM_LIMIT),
-        cost_estimate=pl.CostEstimate(
-            flops=4 * blocks * rows * cells * columns, bytes_accessed=2 * blocks * rows * columns, transcendentals=0
-        ),
-    )(near_t, far_t, near, far)
+        grid_spec=pltpu.PrefetchScalarGridSpec(
+            num_scalar_prefetch=1,
+            grid=(4,),
+            in_specs=[
+                left,
+                left,
+                pl.BlockSpec((cells, columns), lambda i, p: (0, 0)),
+                pl.BlockSpec((cells, columns), lambda i, p: (0, part)),
+            ],
+            out_specs=[pl.BlockSpec((4, rows, columns), lambda i, p: (0, 0, 0))] * 4,
+        ),
+        out_shape=[jax.ShapeDtypeStruct((4, rows, columns), jnp.bfloat16)] * 4,
+        compiler_params=pltpu.CompilerParams(vmem_limit_bytes=VMEM_LIMIT),
+        cost_estimate=SMALL,
+    )(place, near_t, far_t, near, far)
+
+
+def sum_kernel(*refs):
+    for index in range(4):
+        total = refs[0][index].astype(jnp.float32)
+        for ref in refs[1:4]:
+            total = total + ref[index].astype(jnp.float32)
+        refs[4 + index][...] = total.astype(jnp.bfloat16)
+
+
+def sum_pieces(pieces):
+    _, rows, columns = pieces[0].shape
+    return pl.pallas_call(
+        sum_kernel,
+        name="sum_pieces",
+        out_shape=[jax.ShapeDtypeStruct((rows, columns), jnp.bfloat16)] * 4,
+        compiler_params=pltpu.CompilerParams(vmem_limit_bytes=VMEM_LIMIT),
+        cost_estimate=SMALL,
+    )(*pieces)
+
+
+def to_owners(pieces, axes):
+    named = range(4) if axes == "x" else [0, 2, 1, 3]
+    moved = [
+        lax.ppermute(piece, axes, [(named[i], named[(i + d) % 4]) for i in range(4)])
+        for d, piece in enumerate(pieces)
+        if d
+    ]
+    return [pieces[0]] + moved
+
+
+def swap_pieces(values, axes):
+    return lax.all_to_all(values, axes, 0, 0, tiled=True)
+
+
+def total_of(received):
+    return jnp.sum(received.astype(jnp.float32), axis=0)
 
 
 def per_device(images, hidden_cot, residual_cot, w_up, b_up, ln_gain, ln_bias, dw_weight, dw_bias):
     feat, hid = w_up.shape
-    everyone = ("y_lo", "x", "z", "y_hi", "core")
+    y_axes = ("y_lo", "y_hi")
+    plane = ("x", "y_hi", "y_lo")
     along_z = lax.axis_size("z")
-    devices = 1
-    for name in everyone:
-        devices *= lax.axis_size(name)
+    devices = 32 * along_z
     inverse_count = 1.0 / (images.shape[0] * devices)
-    mine = lax.axis_index("core").astype(jnp.int32).reshape(1)
+    core = lax.axis_index("core")
+    mine = core.astype(jnp.int32).reshape(1)
     swap = [(0, 1), (1, 0)]
-
-    unit, sigma, normed, turned = conv_norm(images, dw_weight, dw_bias, ln_gain, ln_bias, along_z)
+    width = hid // 8
+
+    b_row, gain_row = b_up.reshape(1, -1), ln_gain.reshape(1, -1)
+    unit, sigma, normed, turned = conv_norm(images, dw_weight, dw_bias, gain_row, ln_bias, along_z)
+    cells = normed.shape[0]
     far_turned = lax.ppermute(turned, "core", swap)
-    away, away_sums = gelu_grad(1 - mine, normed, w_up, b_up, hidden_cot)
+    away, away_sums = gelu_grad(4 - 4 * mine, 4, normed, w_up, b_row, hidden_cot, width)
     far = lax.ppermute(away, "core", swap)
-    near, near_sums = gelu_grad(mine, normed, w_up, b_up, hidden_cot)
-    cells = normed.shape[0]
-    partial = product(turned.reshape(4, -1, cells), far_turned.reshape(4, -1, cells), near, far)
-
-    by_x = lax.psum_scatter(partial.reshape(feat, -1), "x", scatter_dimension=0, tiled=True)
-    by_y = lax.psum_scatter(by_x, ("y_hi", "y_lo"), scatter_dimension=0, tiled=True)
-    pieces = 2 * along_z
-    last = lax.all_to_all(by_y.reshape(pieces, -1, LANES), ("z", "core"), 0, 0, tiled=True)
-    last = last.astype(jnp.float32).reshape(along_z, 2, feat // devices, hid // 2)
-    owned = jnp.sum(last, axis=0).transpose(1, 0, 2).reshape(feat // devices, hid) * inverse_count
-
-    conv_grad, gain_sum, shift_sum = norm_grad(mine, near, away, w_up, unit, sigma, ln_gain)
+    y_index = 2 * lax.axis_index("y_hi") + lax.axis_index("y_lo")
+    place = jnp.stack([lax.axis_index("x"), y_index]).astype(jnp.int32)
+    near_t, far_t = turned.reshape(4, 4, -1, cells), far_turned.reshape(4, 4, -1, cells)
+    near_a, sums_a = gelu_grad(4 * mine, 2, normed, w_up, b_row, hidden_cot, width)
+    part_a = to_owners(product(place, near_t, far_t, near_a, far, 0, 2 * width, True), "x")
+    near_b, sums_b = gelu_grad(4 * mine + 2, 2, normed, w_up, b_row, hidden_cot, width)
+    part_b = product(place, near_t, far_t, near_b, far, 1, 2 * width, False)
+    part_b, unit = lax.optimization_barrier((part_b, unit))
+    part_b = to_owners(part_b, y_axes)
+
+    conv_grad, gain_sum, shift_sum = norm_grad(
+        4 * mine, near_a, near_b, away, w_up, unit, sigma, gain_row, width
+    )
     grad_input, tap_sums, bias_sum = conv_backward(conv_grad, images, residual_cot, dw_weight)
-    first = jnp.where(mine == 0, near_sums, away_sums)
-    second = jnp.where(mine == 0, away_sums, near_sums)
+    near_sums = jnp.concatenate([sums_a, sums_b], axis=1)
     used = 49 + 3 + hid // feat
-    rows = -(-used // 64) * 64
+    rows = 2 * (-(-used // 4) * 2)
     small = jnp.concatenate(
         [
             tap_sums,
             gain_sum,
             shift_sum,
             bias_sum,
-            first.reshape(-1, feat),
-            second.reshape(-1, feat),
+            jnp.where(core == 0, near_sums, away_sums).reshape(-1, feat),
+            jnp.where(core == 0, away_sums, near_sums).reshape(-1, feat),
             jnp.zeros((rows - used, feat), jnp.float32),
         ],
         axis=0,
-    )
-    small = lax.all_to_all(small.reshape(devices, 1, -1), everyone, 0, 0, tiled=True)
-    small = jnp.sum(small, axis=0, keepdims=True) * inverse_count
-    small = lax.all_to_all(
-        jnp.broadcast_to(small, (devices, 1, small.shape[2])), everyone, 0, 0, tiled=True
-    ).reshape(rows, feat)
+    ).reshape(2, 16, 1, -1)
+    part_a, part_b, small = lax.optimization_barrier((part_a, part_b, small))
+
+    part_a = to_owners(sum_pieces(part_a), y_axes)
+    part_b = to_owners(sum_pieces(part_b), "x")
+
+    kept = jnp.where(core == 0, small[0], small[1])
+    small = kept + lax.ppermute(jnp.where(core == 0, small[1], small[0]), "core", swap)
+    small = jnp.sum(swap_pieces(small, plane), axis=0, keepdims=True)
+    small = jnp.broadcast_to(small, (along_z,) + small.shape[1:])
+    small = jnp.sum(swap_pieces(small, "z"), axis=0, keepdims=True) * inverse_count
+    small = swap_pieces(jnp.broadcast_to(small, (16,) + small.shape[1:]), plane)
+    other = lax.ppermute(small, "core", swap)
+    small = jnp.stack([jnp.where(core == 0, small, other), jnp.where(core == 0, other, small)])
+    small = small.reshape(rows, feat)
+
+    last = jnp.concatenate([total_of(jnp.stack(part_a)), total_of(jnp.stack(part_b))], axis=1).astype(jnp.bfloat16)
+    last = swap_pieces(last.reshape(2 * along_z, -1, LANES), ("z", "core"))
+    last = total_of(last.reshape(along_z, 2, feat // devices, hid // 2))
+    owned = last.transpose(1, 0, 2).reshape(feat // devices, hid) * inverse_count
     return (
         grad_input,
         owned,

time: 206 us -> 171 us (0.83)
  waiting for transfers between devices: 78.7 us -> 29.6 us
  starting transfers between devices: 15.3 us -> 56.4 us
  blocking collectives: 28.6 us -> 0 us
  Pallas kernels: 52.3 us -> 67.6 us
  between operations: 14.2 us -> 0.97 us
  local copies, waits for them, and re-layouts: 14.8 us -> 11.6 us
  other arithmetic: 1.04 us -> 3.95 us
    reduce_scatter x2 -> x0, waiting for transfers between devices: 54.9 us -> none  [the longest x1 54.8 us: per_device(): lax.psum_scatter(partial.reshape(feat, -1), 'x', scatter_dimension=0, til...]
    ppermute x0 -> x14, starting transfers between devices: none -> 28.8 us  [the longest x12 16.6 us: to_owners(): lax.ppermute(piece, axes, [(named[i], named[(i + d) % 4]) for i in range(...]
    all_to_all x1 -> x0, blocking collectives: 28.6 us -> none  [per_device(): lax.all_to_all(small.reshape(devices, 1, -1), everyone, 0, 0, tiled=True)]
    all_to_all x2 -> x4, starting transfers between devices: 12 us -> 24.2 us  [swap_pieces(): return lax.all_to_all(values, axes, 0, 0, tiled=True)]
    pallas_call x1 -> x4, Pallas kernels: 6.44 us -> 17.5 us  [the longest x2 12.4 us: product(): pl.pallas_call(functools.partial(product_kernel, x_first), name='product'...]
    all_to_all x2 -> x4, waiting for transfers between devices: 23.8 us -> 29.6 us  [swap_pieces(): return lax.all_to_all(values, axes, 0, 0, tiled=True)]
    ppermute x1, starting transfers between devices: 0.02 us -> 3.24 us  [per_device(): far = lax.ppermute(away, 'core', swap)]
    ppermute x1, starting transfers between devices: 3.24 us -> 0.1 us  [per_device(): far_turned = lax.ppermute(turned, 'core', swap)]
  transfers between devices with their start and end apart: 6 -> 20, of which waited for: 3 -> 4; matrix products, arithmetic and copies ran while one was open for 5% -> 4% of each run, Pallas kernels for 17% -> 26%
where the time goes in v2:
time: 171 us; the launch traced here: 170 us
  Pallas kernels  67.6 us (40%)
  starting transfers between devices  56.4 us (33%)
  waiting for transfers between devices  29.6 us (17%)
  local copies, waits for them, and re-layouts  11.6 us (7%)
  other arithmetic  3.95 us (2%)
    all_to_all x4, waiting for transfers between devices, swap_pieces(): return lax.all_to_all(values, axes, 0, 0, tiled=True)  29.6 us
    all_to_all x4, starting transfers between devices, swap_pieces(): return lax.all_to_all(values, axes, 0, 0, tiled=True)  24.2 us
    ppermute x12, starting transfers between devices, to_owners(): lax.ppermute(piece, axes, [(named[i], named[(i + d) % 4]) for i in range(...  16.6 us
    pallas_call x3, Pallas kernels, gelu_grad(): pl.pallas_call(slope_kernel, name='gelu_grad', grid_spec=pltpu.PrefetchSc...  13.8 us
    pallas_call x1, Pallas kernels, norm_grad(): pl.pallas_call(norm_grad_kernel, name='norm_grad', grid_spec=pltpu.Prefet...  13.2 us
    pallas_call x2, Pallas kernels, product(): pl.pallas_call(functools.partial(product_kernel, x_first), name='product'...  12.4 us
    pallas_call x1, Pallas kernels, conv_backward(): pl.pallas_call(conv_grad_kernel, name='conv_backward', grid=(feat // LANE...  12.3 us
    ppermute x1, starting transfers between devices, per_device(): lax.ppermute(jnp.where(core == 0, small[1], small[0]), 'core', swap)  11.9 us
  transfers between devices with their start and end apart: 20, of which 4 were waited for; matrix products, arithmetic and copies ran while one was open for 4% of the time, Pallas kernels for 26%

profile of v2, /device:TPU:1, one launch (start us, length us, event | category | flops | bytes accessed | tf_op | source)
XLA Modules:
  0.0 170.2 jit_solution(16697500971745423078)
XLA Ops:
  0.6 1.3 reshape.112.gain_ref
  1.9 1.3 reshape.111.bias_ref
  3.2 1.3 reshape.113.shift_ref
  4.5 10.9 %conv_norm.1 = (f32[256,1536]{1,0:T(8,128)}, f32[256,128]{1,0:T(8,128)}, bf16[256,1536]{1,0:T(8,128)(2,1)}, bf16[4,2,2,96,256]{4,3,2,1,0:T(8,128)(2,1)}) custom-call(bf16[1,16,16,1536]{3,2,1,0:T(8,128)(2,1)} %image_ref.3, f32[49,1536]{1,0:T(8,128)} %taps_ref.3, f32[1,1536]{1,0:T(1,128)} %reshape.111.bias_ref, f32[1,1536]{1,0:T(1,128)} %reshape.112.gain_ref, ...), custom_call_target="tpu_custom_call" | custom-call | flops 1000 | bytes 1000 | tf_op jit(solution)/shard_map/conv_norm/pallas_call | solution.py:86
  15.4 6.1 %gelu_grad.5 = (bf16[256,1536]{1,0:T(8,128)(2,1)}, f32[1,1536]{1,0:T(1,128)}) custom-call(s32[1]{0:T(128)S(6)} %sub.3.start_ref, bf16[256,1536]{1,0:T(8,128)(2,1)} %get-tuple-element.53.normed_ref, bf16[1536,3072]{1,0:T(8,128)(2,1)} %w_ref.7, f32[1,3072]{1,0:T(1,128)} %bitcast.25, bf16[1,256,3072]{2,1,0:T(8,128)(2,1)} %cot_ref.5), custom_call_target="tpu_custom_call" | custom-call | flops 1000 | bytes 1000 | tf_op jit(solution)/shard_map/gelu_grad/pallas_call | solution.py:117
  21.5 3.2 %collective-permute-start.1 = (bf16[256,1536]{1,0:T(8,128)(2,1)}, bf16[256,1536]{1,0:T(8,128)(2,1)S(1)}, u32[]{:S(2)}, u32[]{:S(2)}) collective-permute-start(bf16[256,1536]{1,0:T(8,128)(2,1)} %get-tuple-element.56.away_ref), channel_id=1, source_target_pairs={{0,1},{1,0},{2,3},{3,2},{4,5},{5,4},{6,7},{7,6},{8,9},{9,8},{10,11... | collective-permute-start | bytes 2359304 | tf_op jit(solution)/shard_map/ppermute | solution.py:392
  24.8 0.1 collective-permute-start
  24.9 3.8 %gelu_grad.4 = (bf16[256,768]{1,0:T(8,128)(2,1)}, f32[1,768]{1,0:T(1,128)}) custom-call(s32[1]{0:T(128)S(6)} %add.9.start_ref, bf16[256,1536]{1,0:T(8,128)(2,1)} %get-tuple-element.53.normed_ref, bf16[1536,3072]{1,0:T(8,128)(2,1)} %w_ref.7, f32[1,3072]{1,0:T(1,128)} %bitcast.26, bf16[1,256,3072]{2,1,0:T(8,128)(2,1)} %cot_ref.5), custom_call_target="tpu_custom_call" | custom-call | flops 1000 | bytes 1000 | tf_op jit(solution)/shard_map/gelu_grad/pallas_call | solution.py:117
  28.7 0.6 pad_add_fusion.place_ref
  29.3 0.9 copy-done.1
  30.2 0.3 copy-done.2
  30.5 6.3 %product.2 = (bf16[4,96,768]{2,1,0:T(8,128)(2,1)}, bf16[4,96,768]{2,1,0:T(8,128)(2,1)}, bf16[4,96,768]{2,1,0:T(8,128)(2,1)}, bf16[4,96,768]{2,1,0:T(8,128)(2,1)}) custom-call(s32[2]{0:T(128)} %pad_add_fusion.place_ref, bf16[4,4,96,256]{3,2,1,0:T(8,128)(2,1)} %bitcast.20, bf16[4,4,96,256]{3,2,1,0:T(8,128)(2,1)} %bitcast.22, ...), custom_call_target="tpu_custom_call" | custom-call | flops 1000 | bytes 1000 | tf_op jit(solution)/shard_map/product/pallas_call | solution.py:318
  36.8 3.8 %gelu_grad.3 = (bf16[256,768]{1,0:T(8,128)(2,1)}, f32[1,768]{1,0:T(1,128)}) custom-call(s32[1]{0:T(128)} %bitcast.start_ref, bf16[256,1536]{1,0:T(8,128)(2,1)} %get-tuple-element.53.normed_ref, bf16[1536,3072]{1,0:T(8,128)(2,1)} %w_ref.7, f32[1,3072]{1,0:T(1,128)} %bitcast.27, bf16[1,256,3072]{2,1,0:T(8,128)(2,1)} %cot_ref.5), custom_call_target="tpu_custom_call" | custom-call | flops 1000 | bytes 1000 | tf_op jit(solution)/shard_map/gelu_grad/pallas_call | solution.py:117
  40.6 0.0 copy-start.12
  40.6 2.2 %collective-permute-start.6 = (bf16[4,96,768]{2,1,0:T(8,128)(2,1)}, bf16[4,96,768]{2,1,0:T(8,128)(2,1)S(1)}, u32[]{:S(2)}, u32[]{:S(2)}) collective-permute-start(bf16[4,96,768]{2,1,0:T(8,128)(2,1)} %get-tuple-element.73), channel_id=1, source_target_pairs={{0,2},{128,130},{2,0},{130,128},{1,3},{129,131},{3,1},{131,129},{4... | collective-permute-start | bytes 1769480 | tf_op jit(solution)/shard_map/ppermute | solution.py:360
  42.8 1.1 collective-permute-start.7
  43.9 6.2 %product.3 = (bf16[4,96,768]{2,1,0:T(8,128)(2,1)}, bf16[4,96,768]{2,1,0:T(8,128)(2,1)}, bf16[4,96,768]{2,1,0:T(8,128)(2,1)}, bf16[4,96,768]{2,1,0:T(8,128)(2,1)}) custom-call(s32[2]{0:T(128)} %pad_add_fusion.place_ref, bf16[4,4,96,256]{3,2,1,0:T(8,128)(2,1)} %bitcast.21, bf16[4,4,96,256]{3,2,1,0:T(8,128)(2,1)} %bitcast.23, ...), custom_call_target="tpu_custom_call" | custom-call | flops 1000 | bytes 1000 | tf_op jit(solution)/shard_map/product/pallas_call | solution.py:318
  50.1 1.2 collective-permute-start.2
  51.3 2.5 %collective-permute-start.3 = (bf16[4,96,768]{2,1,0:T(8,128)(2,1)}, bf16[4,96,768]{2,1,0:T(8,128)(2,1)}, u32[]{:S(2)}, u32[]{:S(2)}) collective-permute-start(bf16[4,96,768]{2,1,0:T(8,128)(2,1)} %get-tuple-element.69), channel_id=1, source_target_pairs={{0,64},{32,96},{64,0},{96,32},{1,65},{33,97},{65,1},{97,33},{2,66}... | collective-permute-start | bytes 1769480 | tf_op jit(solution)/shard_map/ppermute | solution.py:360
  53.7 0.0 collective-permute-done.5.refs_1_
  53.7 1.2 collective-permute-start.4
  54.9 13.2 %norm_grad.1 = (f32[256,1536]{1,0:T(8,128)}, f32[1,1536]{1,0:T(1,128)}, f32[1,1536]{1,0:T(1,128)}) custom-call(s32[1]{0:T(128)} %bitcast.start_ref, bf16[256,768]{1,0:T(8,128)(2,1)} %get-tuple-element.54.first_ref.near_ref, bf16[256,768]{1,0:T(8,128)(2,1)} %get-tuple-element.55.near_ref.second_ref, bf16[256,1536]{1,0:T(8,128)(2,1)} %get-tuple-element.56.away_ref, ...), custom_call_target="tpu_custom_call" | custom-call | flops 1000 | bytes 1000 | tf_op jit(solution)/shard_map/norm_grad/pallas_call | solution.py:195
  68.1 0.0 copy-start.10
  68.1 0.0 copy-start.11
  68.1 12.3 %conv_backward.1 = (bf16[1,16,16,1536]{3,2,1,0:T(8,128)(2,1)}, f32[49,1536]{1,0:T(8,128)}, f32[1,1536]{1,0:T(1,128)}) custom-call(f32[256,1536]{1,0:T(8,128)} %get-tuple-element.65.grad_ref, bf16[1,16,16,1536]{3,2,1,0:T(8,128)(2,1)} %image_ref.3, bf16[1,16,16,1536]{3,2,1,0:T(8,128)(2,1)} %res_ref.1, f32[49,1536]{1,0:T(8,128)} %taps_ref.3), custom_call_target="tpu_custom_call" | custom-call | flops 1000 | bytes 1000 | tf_op jit(solution)/shard_map/conv_backward/pallas_call | solution.py:267
  80.5 1.8 %concatenate.11 = f32[56,1536]{1,0:T(8,128)S(1)} concatenate(f32[49,1536]{1,0:T(8,128)} %get-tuple-element.75, f32[1,1536]{1,0:T(1,128)S(1)} %copy-done.10, f32[1,1536]{1,0:T(1,128)S(1)} %copy-done.11, f32[1,1536]{1,0:T(1,128)} %get-tuple-element.78, f32[1,1536]{1,0:T(1,128)S(1)} %get-tuple-element.105, f32[1,1536]{1,0:T(1,128)S(1)} %get-tuple-element.104, ...), dimensions={0} | concatenate | bytes 688128 | tf_op jit(solution)/shard_map/concatenate | solution.py:410
  82.3 0.1 reshape.117
  82.4 0.0 collective-permute-done.7.refs_3_
  82.4 0.0 collective-permute-done.2.refs_1_
  82.4 0.0 collective-permute-done.4.refs_3_
  82.4 0.4 copy.31
  82.8 0.2 fusion.4
  83.0 11.9 %collective-permute-start.14 = (f32[16,1,2688]{2,1,0:T(1,128)S(1)}, f32[16,1,2688]{2,1,0:T(1,128)S(1)}, u32[]{:S(2)}, u32[]{:S(2)}) collective-permute-start(f32[16,1,2688]{2,1,0:T(1,128)S(1)} %fusion.4), channel_id=1, source_target_pairs={{0,1},{1,0},{2,3},{3,2},{4,5},{5,4},{6,7},{7,6},{8,9},{9,8},{10,11... | collective-permute-start | bytes 516104 | tf_op jit(solution)/shard_map/ppermute | solution.py:428
  94.9 2.5 %sum_pieces.2 = (bf16[96,768]{1,0:T(8,128)(2,1)}, bf16[96,768]{1,0:T(8,128)(2,1)}, bf16[96,768]{1,0:T(8,128)(2,1)}, bf16[96,768]{1,0:T(8,128)(2,1)}) custom-call(bf16[4,96,768]{2,1,0:T(8,128)(2,1)} %get-tuple-element.82.refs_0_, bf16[4,96,768]{2,1,0:T(8,128)(2,1)} %copy-done.6, bf16[4,96,768]{2,1,0:T(8,128)(2,1)} %collective-permute-done.3.refs_2_, ...), custom_call_target="tpu_custom_call" | custom-call | flops 1000 | bytes 1000 | tf_op jit(solution)/shard_map/sum_pieces/pallas_call | solution.py:348
  97.4 0.1 collective-permute-start.10
  97.5 1.5 collective-permute-start.8
  99.0 2.6 %collective-permute-start.9 = (bf16[96,768]{1,0:T(8,128)(2,1)}, bf16[96,768]{1,0:T(8,128)(2,1)S(1)}, u32[]{:S(2)}, u32[]{:S(2)}) collective-permute-start(bf16[96,768]{1,0:T(8,128)(2,1)} %get-tuple-element.88), channel_id=1, source_target_pairs={{0,2},{128,130},{2,0},{130,128},{1,3},{129,131},{3,1},{131,129},{4... | collective-permute-start | bytes 442376 | tf_op jit(solution)/shard_map/ppermute | solution.py:360
  101.6 2.5 %sum_pieces.3 = (bf16[96,768]{1,0:T(8,128)(2,1)}, bf16[96,768]{1,0:T(8,128)(2,1)}, bf16[96,768]{1,0:T(8,128)(2,1)}, bf16[96,768]{1,0:T(8,128)(2,1)}) custom-call(bf16[4,96,768]{2,1,0:T(8,128)(2,1)} %get-tuple-element.90.refs_0_, bf16[4,96,768]{2,1,0:T(8,128)(2,1)} %copy-done.3, bf16[4,96,768]{2,1,0:T(8,128)(2,1)} %copy-done.4, bf16[4,96,768]{2,1,0:T(8,128)(2,1)} %copy-done.5), custom_call_target="tpu_custom_call" | custom-call | flops 1000 | bytes 1000 | tf_op jit(solution)/shard_map/sum_pieces/pallas_call | solution.py:348
  104.1 1.7 %collective-permute-start.12 = (bf16[96,768]{1,0:T(8,128)(2,1)}, bf16[96,768]{1,0:T(8,128)(2,1)S(1)}, u32[]{:S(2)}, u32[]{:S(2)}) collective-permute-start(bf16[96,768]{1,0:T(8,128)(2,1)} %get-tuple-element.96), channel_id=1, source_target_pairs={{0,64},{32,96},{64,0},{96,32},{1,65},{33,97},{65,1},{97,33},{2,66}... | collective-permute-start | bytes 442376 | tf_op jit(solution)/shard_map/ppermute | solution.py:360
  105.8 1.0 fusion.3
  106.9 4.3 %all-to-all-start.1 = ((f32[16,1,2688]{2,1,0:T(1,128)}), f32[16,1,2688]{2,1,0:T(1,128)S(1)}, u32[]{:S(2)}, u32[]{:S(2)}) async-start(f32[16,1,2688]{2,1,0:T(1,128)} %fusion.3), calls=%async_computation.1 | async-start | bytes 344064 | tf_op jit(solution)/shard_map/all_to_all | solution.py:368
  111.2 2.7 %collective-permute-start.13 = (bf16[96,768]{1,0:T(8,128)(2,1)}, bf16[96,768]{1,0:T(8,128)(2,1)S(1)}, u32[]{:S(2)}, u32[]{:S(2)}) collective-permute-start(bf16[96,768]{1,0:T(8,128)(2,1)} %get-tuple-element.97), channel_id=1, source_target_pairs={{0,96},{32,0},{64,32},{96,64},{1,97},{33,1},{65,33},{97,65},{2,98}... | collective-permute-start | bytes 442376 | tf_op jit(solution)/shard_map/ppermute | solution.py:360
  113.9 4.2 %all-to-all-done.1 = f32[16,1,2688]{2,1,0:T(1,128)S(1)} async-done(((f32[16,1,2688]{2,1,0:T(1,128)}), f32[16,1,2688]{2,1,0:T(1,128)S(1)}, u32[]{:S(2)}, u32[]{:S(2)}) %all-to-all-start.1) | async-done | bytes 172064 | tf_op jit(solution)/shard_map/all_to_all | solution.py:368
  118.1 0.1 reduce_sum.48
  118.2 0.7 broadcast_in_dim.7
  118.9 7.2 %all-to-all-start.2 = ((f32[8,1,2688]{2,1,0:T(1,128)}), f32[8,1,2688]{2,1,0:T(1,128)S(1)}, u32[]{:S(2)}, u32[]{:S(2)}) async-start(f32[8,1,2688]{2,1,0:T(1,128)} %broadcast_in_dim.7), calls=%async_computation.2 | async-start | bytes 172032 | tf_op jit(solution)/shard_map/all_to_all | solution.py:368
  126.2 7.5 %all-to-all-done.2 = f32[8,1,2688]{2,1,0:T(1,128)S(1)} async-done(((f32[8,1,2688]{2,1,0:T(1,128)}), f32[8,1,2688]{2,1,0:T(1,128)S(1)}, u32[]{:S(2)}, u32[]{:S(2)}) %all-to-all-start.2) | async-done | bytes 86048 | tf_op jit(solution)/shard_map/all_to_all | solution.py:368
  133.7 0.1 reduce_sum.49
  133.8 0.8 broadcast_in_dim.8
  134.6 3.6 %all-to-all-start.3 = ((f32[16,1,2688]{2,1,0:T(1,128)}), f32[16,1,2688]{2,1,0:T(1,128)S(1)}, u32[]{:S(2)}, u32[]{:S(2)}) async-start(f32[16,1,2688]{2,1,0:T(1,128)} %broadcast_in_dim.8), calls=%async_computation.3 | async-start | bytes 344064 | tf_op jit(solution)/shard_map/all_to_all | solution.py:368
  138.2 1.1 convert_element_type.19
  139.3 5.7 %all-to-all-done.3 = f32[16,1,2688]{2,1,0:T(1,128)S(1)} async-done(((f32[16,1,2688]{2,1,0:T(1,128)}), f32[16,1,2688]{2,1,0:T(1,128)S(1)}, u32[]{:S(2)}, u32[]{:S(2)}) %all-to-all-start.3) | async-done | bytes 172064 | tf_op jit(solution)/shard_map/all_to_all | solution.py:368
  145.0 9.1 %all-to-all-start = ((bf16[16,72,128]{2,1,0:T(8,128)(2,1)}), bf16[16,72,128]{2,1,0:T(8,128)(2,1)S(1)}, u32[]{:S(2)}, u32[]{:S(2)}) async-start(bf16[16,72,128]{2,1,0:T(8,128)(2,1)} %convert_element_type.19), calls=%async_computation | async-start | bytes 589824 | tf_op jit(solution)/shard_map/all_to_all | solution.py:368
  154.1 0.3 collective-permute-start.15
  154.4 12.2 %all-to-all-done = bf16[16,72,128]{2,1,0:T(8,128)(2,1)S(1)} async-done(((bf16[16,72,128]{2,1,0:T(8,128)(2,1)}), bf16[16,72,128]{2,1,0:T(8,128)(2,1)S(1)}, u32[]{:S(2)}, u32[]{:S(2)}) %all-to-all-start) | async-done | bytes 294944 | tf_op jit(solution)/shard_map/all_to_all | solution.py:368
  166.5 0.3 reshape.120
  166.9 0.1 reduce_sum.47
  166.9 0.7 broadcast_multiply_fusion
  167.6 0.2 fusion
  167.8 0.9 maximum_reduce_fusion
  168.7 0.1 reshape.118
  168.8 0.0 copy-start.7
  168.9 0.7 slice_reduce_fusion
  169.6 0.6 reshape.119
  (47 shorter events, 0.2 us)
Async XLA Ops:
  15.4 9.4 %copy-start = (bf16[4,2,2,96,256]{4,3,2,1,0:T(8,128)(2,1)S(1)}, bf16[4,2,2,96,256]{4,3,2,1,0:T(8,128)(2,1)}, u32[]{:S(2)}) copy-start(bf16[4,2,2,96,256]{4,3,2,1,0:T(8,128)(2,1)} %get-tuple-element.57) | copy-start | bytes 2359300
  21.5 7.8 %collective-permute-start.1 = (bf16[256,1536]{1,0:T(8,128)(2,1)}, bf16[256,1536]{1,0:T(8,128)(2,1)S(1)}, u32[]{:S(2)}, u32[]{:S(2)}) collective-permute-start(bf16[256,1536]{1,0:T(8,128)(2,1)} %get-tuple-element.56.away_ref), channel_id=1, source_target_pairs={{0,1},{1,0},{2,3},{3,2},{4,5},{5,4},{6,7},{7,6},{8,9},{9,8},{10,11... | collective-permute-start | bytes 2359304 | tf_op jit(solution)/shard_map/ppermute | solution.py:392
  24.8 4.5 %collective-permute-start = (bf16[4,2,2,96,256]{4,3,2,1,0:T(8,128)(2,1)S(1)}, bf16[4,2,2,96,256]{4,3,2,1,0:T(8,128)(2,1)S(1)}, u32[]{:S(2)}, u32[]{:S(2)}) collective-permute-start(bf16[4,2,2,96,256]{4,3,2,1,0:T(8,128)(2,1)S(1)} %copy-done), channel_id=1, source_target_pairs={{0,1},{1,0},{2,3},{3,2},{4,5},{5,4},{6,7},{7,6},{8,9},{9,8},{10,11... | collective-permute-start | bytes 2359304 | tf_op jit(solution)/shard_map/ppermute | solution.py:390
  29.3 0.9 copy-start.1
  29.3 1.2 copy-start.2
  36.7 17.0 %collective-permute-start.5 = (bf16[4,96,768]{2,1,0:T(8,128)(2,1)}, bf16[4,96,768]{2,1,0:T(8,128)(2,1)S(1)}, u32[]{:S(2)}, u32[]{:S(2)}) collective-permute-start(bf16[4,96,768]{2,1,0:T(8,128)(2,1)} %get-tuple-element.72), channel_id=1, source_target_pairs={{0,128},{128,2},{2,130},{130,0},{1,129},{129,3},{3,131},{131,1},{4... | collective-permute-start | bytes 1769480 | tf_op jit(solution)/shard_map/ppermute | solution.py:360
  40.6 14.3 %copy-start.14 = (f32[1,768]{1,0:T(1,128)S(1)}, f32[1,768]{1,0:T(1,128)}, u32[]{:S(2)}) copy-start(f32[1,768]{1,0:T(1,128)} %get-tuple-element.79) | copy-start | bytes 9220
  40.6 14.3 %copy-start.13 = (f32[1,768]{1,0:T(1,128)S(1)}, f32[1,768]{1,0:T(1,128)}, u32[]{:S(2)}) copy-start(f32[1,768]{1,0:T(1,128)} %get-tuple-element.80) | copy-start | bytes 9220
  40.6 14.3 %copy-start.12 = (f32[1,1536]{1,0:T(1,128)S(1)}, f32[1,1536]{1,0:T(1,128)}, u32[]{:S(2)}) copy-start(f32[1,1536]{1,0:T(1,128)} %get-tuple-element.81) | copy-start | bytes 18436
  40.6 41.8 %collective-permute-start.6 = (bf16[4,96,768]{2,1,0:T(8,128)(2,1)}, bf16[4,96,768]{2,1,0:T(8,128)(2,1)S(1)}, u32[]{:S(2)}, u32[]{:S(2)}) collective-permute-start(bf16[4,96,768]{2,1,0:T(8,128)(2,1)} %get-tuple-element.73), channel_id=1, source_target_pairs={{0,2},{128,130},{2,0},{130,128},{1,3},{129,131},{3,1},{131,129},{4... | collective-permute-start | bytes 1769480 | tf_op jit(solution)/shard_map/ppermute | solution.py:360
  42.8 39.5 %collective-permute-start.7 = (bf16[4,96,768]{2,1,0:T(8,128)(2,1)}, bf16[4,96,768]{2,1,0:T(8,128)(2,1)S(1)}, u32[]{:S(2)}, u32[]{:S(2)}) collective-permute-start(bf16[4,96,768]{2,1,0:T(8,128)(2,1)} %get-tuple-element.74), channel_id=1, source_target_pairs={{0,130},{128,0},{2,128},{130,2},{1,131},{129,1},{3,129},{131,3},{4... | collective-permute-start | bytes 1769480 | tf_op jit(solution)/shard_map/ppermute | solution.py:360
  50.1 32.3 %collective-permute-start.2 = (bf16[4,96,768]{2,1,0:T(8,128)(2,1)}, bf16[4,96,768]{2,1,0:T(8,128)(2,1)S(1)}, u32[]{:S(2)}, u32[]{:S(2)}) collective-permute-start(bf16[4,96,768]{2,1,0:T(8,128)(2,1)} %get-tuple-element.68), channel_id=1, source_target_pairs={{0,32},{32,64},{64,96},{96,0},{1,33},{33,65},{65,97},{97,1},{2,34}... | collective-permute-start | bytes 1769480 | tf_op jit(solution)/shard_map/ppermute | solution.py:360
  51.3 31.1 %collective-permute-start.3 = (bf16[4,96,768]{2,1,0:T(8,128)(2,1)}, bf16[4,96,768]{2,1,0:T(8,128)(2,1)}, u32[]{:S(2)}, u32[]{:S(2)}) collective-permute-start(bf16[4,96,768]{2,1,0:T(8,128)(2,1)} %get-tuple-element.69), channel_id=1, source_target_pairs={{0,64},{32,96},{64,0},{96,32},{1,65},{33,97},{65,1},{97,33},{2,66}... | collective-permute-start | bytes 1769480 | tf_op jit(solution)/shard_map/ppermute | solution.py:360
  53.7 14.4 %copy-start.3 = (bf16[4,96,768]{2,1,0:T(8,128)(2,1)}, bf16[4,96,768]{2,1,0:T(8,128)(2,1)S(1)}, u32[]{:S(2)}) copy-start(bf16[4,96,768]{2,1,0:T(8,128)(2,1)S(1)} %collective-permute-done.5.refs_1_) | copy-start | bytes 1769476
  53.7 28.7 %collective-permute-start.4 = (bf16[4,96,768]{2,1,0:T(8,128)(2,1)}, bf16[4,96,768]{2,1,0:T(8,128)(2,1)}, u32[]{:S(2)}, u32[]{:S(2)}) collective-permute-start(bf16[4,96,768]{2,1,0:T(8,128)(2,1)} %get-tuple-element.70), channel_id=1, source_target_pairs={{0,96},{32,0},{64,32},{96,64},{1,97},{33,1},{65,33},{97,65},{2,98}... | collective-permute-start | bytes 1769480 | tf_op jit(solution)/shard_map/ppermute | solution.py:360
  68.1 12.3 %copy-start.10 = (f32[1,1536]{1,0:T(1,128)S(1)}, f32[1,1536]{1,0:T(1,128)}, u32[]{:S(2)}) copy-start(f32[1,1536]{1,0:T(1,128)} %get-tuple-element.76) | copy-start | bytes 18436
  68.1 12.3 %copy-start.11 = (f32[1,1536]{1,0:T(1,128)S(1)}, f32[1,1536]{1,0:T(1,128)}, u32[]{:S(2)}) copy-start(f32[1,1536]{1,0:T(1,128)} %get-tuple-element.77) | copy-start | bytes 18436
  82.4 15.0 %copy-start.4 = (bf16[4,96,768]{2,1,0:T(8,128)(2,1)}, bf16[4,96,768]{2,1,0:T(8,128)(2,1)S(1)}, u32[]{:S(2)}) copy-start(bf16[4,96,768]{2,1,0:T(8,128)(2,1)S(1)} %collective-permute-done.6.refs_2_) | copy-start | bytes 1769476
  82.4 15.0 %copy-start.5 = (bf16[4,96,768]{2,1,0:T(8,128)(2,1)}, bf16[4,96,768]{2,1,0:T(8,128)(2,1)S(1)}, u32[]{:S(2)}) copy-start(bf16[4,96,768]{2,1,0:T(8,128)(2,1)S(1)} %collective-permute-done.7.refs_3_) | copy-start | bytes 1769476
  82.4 12.5 %copy-start.6 = (bf16[4,96,768]{2,1,0:T(8,128)(2,1)}, bf16[4,96,768]{2,1,0:T(8,128)(2,1)S(1)}, u32[]{:S(2)}) copy-start(bf16[4,96,768]{2,1,0:T(8,128)(2,1)S(1)} %collective-permute-done.2.refs_1_) | copy-start | bytes 1769476
  83.0 21.1 %collective-permute-start.14 = (f32[16,1,2688]{2,1,0:T(1,128)S(1)}, f32[16,1,2688]{2,1,0:T(1,128)S(1)}, u32[]{:S(2)}, u32[]{:S(2)}) collective-permute-start(f32[16,1,2688]{2,1,0:T(1,128)S(1)} %fusion.4), channel_id=1, source_target_pairs={{0,1},{1,0},{2,3},{3,2},{4,5},{5,4},{6,7},{7,6},{8,9},{9,8},{10,11... | collective-permute-start | bytes 516104 | tf_op jit(solution)/shard_map/ppermute | solution.py:428
  97.4 13.8 %collective-permute-start.10 = (bf16[96,768]{1,0:T(8,128)(2,1)}, bf16[96,768]{1,0:T(8,128)(2,1)S(1)}, u32[]{:S(2)}, u32[]{:S(2)}) collective-permute-start(bf16[96,768]{1,0:T(8,128)(2,1)} %get-tuple-element.89), channel_id=1, source_target_pairs={{0,130},{128,0},{2,128},{130,2},{1,131},{129,1},{3,129},{131,3},{4... | collective-permute-start | bytes 442376 | tf_op jit(solution)/shard_map/ppermute | solution.py:360
  97.5 16.4 %collective-permute-start.8 = (bf16[96,768]{1,0:T(8,128)(2,1)}, bf16[96,768]{1,0:T(8,128)(2,1)S(1)}, u32[]{:S(2)}, u32[]{:S(2)}) collective-permute-start(bf16[96,768]{1,0:T(8,128)(2,1)} %get-tuple-element.87), channel_id=1, source_target_pairs={{0,128},{128,2},{2,130},{130,0},{1,129},{129,3},{3,131},{131,1},{4... | collective-permute-start | bytes 442376 | tf_op jit(solution)/shard_map/ppermute | solution.py:360
  99.0 14.9 %copy-start.9 = (bf16[96,768]{1,0:T(8,128)(2,1)S(1)}, bf16[96,768]{1,0:T(8,128)(2,1)}, u32[]{:S(2)}) copy-start(bf16[96,768]{1,0:T(8,128)(2,1)} %get-tuple-element.86) | copy-start | bytes 442372
  99.0 14.9 %collective-permute-start.9 = (bf16[96,768]{1,0:T(8,128)(2,1)}, bf16[96,768]{1,0:T(8,128)(2,1)S(1)}, u32[]{:S(2)}, u32[]{:S(2)}) collective-permute-start(bf16[96,768]{1,0:T(8,128)(2,1)} %get-tuple-element.88), channel_id=1, source_target_pairs={{0,2},{128,130},{2,0},{130,128},{1,3},{129,131},{3,1},{131,129},{4... | collective-permute-start | bytes 442376 | tf_op jit(solution)/shard_map/ppermute | solution.py:360
  104.1 22.1 %copy-start.8 = (bf16[96,768]{1,0:T(8,128)(2,1)S(1)}, bf16[96,768]{1,0:T(8,128)(2,1)}, u32[]{:S(2)}) copy-start(bf16[96,768]{1,0:T(8,128)(2,1)} %get-tuple-element.94) | copy-start | bytes 442372
  104.1 22.1 %collective-permute-start.11 = (bf16[96,768]{1,0:T(8,128)(2,1)}, bf16[96,768]{1,0:T(8,128)(2,1)S(1)}, u32[]{:S(2)}, u32[]{:S(2)}) collective-permute-start(bf16[96,768]{1,0:T(8,128)(2,1)} %get-tuple-element.95), channel_id=1, source_target_pairs={{0,32},{32,64},{64,96},{96,0},{1,33},{33,65},{65,97},{97,1},{2,34}... | collective-permute-start | bytes 442376 | tf_op jit(solution)/shard_map/ppermute | solution.py:360
  104.1 22.1 %collective-permute-start.12 = (bf16[96,768]{1,0:T(8,128)(2,1)}, bf16[96,768]{1,0:T(8,128)(2,1)S(1)}, u32[]{:S(2)}, u32[]{:S(2)}) collective-permute-start(bf16[96,768]{1,0:T(8,128)(2,1)} %get-tuple-element.96), channel_id=1, source_target_pairs={{0,64},{32,96},{64,0},{96,32},{1,65},{33,97},{65,1},{97,33},{2,66}... | collective-permute-start | bytes 442376 | tf_op jit(solution)/shard_map/ppermute | solution.py:360
  106.9 11.3 %all-to-all-start.1 = ((f32[16,1,2688]{2,1,0:T(1,128)}), f32[16,1,2688]{2,1,0:T(1,128)S(1)}, u32[]{:S(2)}, u32[]{:S(2)}) async-start(f32[16,1,2688]{2,1,0:T(1,128)} %fusion.3), calls=%async_computation.1 | async-start | bytes 344064 | tf_op jit(solution)/shard_map/all_to_all | solution.py:368
  111.2 15.0 %collective-permute-start.13 = (bf16[96,768]{1,0:T(8,128)(2,1)}, bf16[96,768]{1,0:T(8,128)(2,1)S(1)}, u32[]{:S(2)}, u32[]{:S(2)}) collective-permute-start(bf16[96,768]{1,0:T(8,128)(2,1)} %get-tuple-element.97), channel_id=1, source_target_pairs={{0,96},{32,0},{64,32},{96,64},{1,97},{33,1},{65,33},{97,65},{2,98}... | collective-permute-start | bytes 442376 | tf_op jit(solution)/shard_map/ppermute | solution.py:360
  118.9 14.8 %all-to-all-start.2 = ((f32[8,1,2688]{2,1,0:T(1,128)}), f32[8,1,2688]{2,1,0:T(1,128)S(1)}, u32[]{:S(2)}, u32[]{:S(2)}) async-start(f32[8,1,2688]{2,1,0:T(1,128)} %broadcast_in_dim.7), calls=%async_computation.2 | async-start | bytes 172032 | tf_op jit(solution)/shard_map/all_to_all | solution.py:368
  134.6 10.4 %all-to-all-start.3 = ((f32[16,1,2688]{2,1,0:T(1,128)}), f32[16,1,2688]{2,1,0:T(1,128)S(1)}, u32[]{:S(2)}, u32[]{:S(2)}) async-start(f32[16,1,2688]{2,1,0:T(1,128)} %broadcast_in_dim.8), calls=%async_computation.3 | async-start | bytes 344064 | tf_op jit(solution)/shard_map/all_to_all | solution.py:368
  145.0 21.5 %all-to-all-start = ((bf16[16,72,128]{2,1,0:T(8,128)(2,1)}), bf16[16,72,128]{2,1,0:T(8,128)(2,1)S(1)}, u32[]{:S(2)}, u32[]{:S(2)}) async-start(bf16[16,72,128]{2,1,0:T(8,128)(2,1)} %convert_element_type.19), calls=%async_computation | async-start | bytes 589824 | tf_op jit(solution)/shard_map/all_to_all | solution.py:368
  154.1 13.5 %collective-permute-start.15 = (f32[16,1,2688]{2,1,0:T(1,128)S(1)}, f32[16,1,2688]{2,1,0:T(1,128)S(1)}, u32[]{:S(2)}, u32[]{:S(2)}) collective-permute-start(f32[16,1,2688]{2,1,0:T(1,128)S(1)} %all-to-all-done.3), channel_id=1, source_target_pairs={{0,1},{1,0},{2,3},{3,2},{4,5},{5,4},{6,7},{7,6},{8,9},{9,8},{10,11... | collective-permute-start | bytes 516104 | tf_op jit(solution)/shard_map/ppermute | solution.py:433
  168.8 1.3 copy-start.7

commit v3 on v1

v3 whole, which is shorter than its diff:
```python
import jax
import jax.numpy as jnp
import numpy as np
from jax import lax
from jax.experimental import pallas as pl
from jax.experimental.pallas import tpu as pltpu
from jax.sharding import Mesh
from jax.sharding import PartitionSpec as P

LANES = 128
EDGE = 8
VMEM_LIMIT = 60 * 1024 * 1024
SMALL = pl.CostEstimate(flops=1000, bytes_accessed=1000, transcendentals=0)
SMALL_ROWS = 64


def front_kernel(
    core_ref, image_ref, taps_ref, bias_ref, gain_ref, shift_ref, order_ref, b_ref, w_hbm, cot_hbm,
    unit_out, sigma_ref, turned_ref, away_out, near_out, sums_ref,
    padded, conv, unit, normed, weights, cots, grads, in_sems, out_sems,
):
    side, feat = image_ref.shape[1], image_ref.shape[3]
    parts, _, width = weights.shape
    half = parts // 2
    core = core_ref[0]

    def column(part):
        owner = 1 - core if part < half else core
        return pl.multiple_of((owner * half + part % half) * width, width)

    loads = []
    for part in range(parts):
        columns = pl.ds(column(part), width)
        loads.append(
            (
                pltpu.make_async_copy(w_hbm.at[:, columns], weights.at[part], in_sems.at[2 * part]),
                pltpu.make_async_copy(cot_hbm.at[0, :, columns], cots.at[part], in_sems.at[2 * part + 1]),
            )
        )
    for pair in loads:
        pair[0].start()
        pair[1].start()

    blank = jnp.zeros((side, EDGE, LANES), jnp.float32)
    padded[:, 0:EDGE, :] = blank
    padded[:, EDGE + side : EDGE + side + EDGE, :] = blank

    @pl.loop(0, feat // LANES)
    def _(block):
        lanes = pl.ds(pl.multiple_of(block * LANES, LANES), LANES)
        padded[:, EDGE : EDGE + side, :] = image_ref[0, :, :, lanes].astype(jnp.float32)
        start = jnp.broadcast_to(bias_ref[lanes].reshape(1, LANES), (side, LANES))
        sums = [start] * side
        for tap_col in range(7):
            taps = [
                jnp.broadcast_to(taps_ref[pl.ds(7 * tap_row + tap_col, 1), lanes], (side, LANES))
                for tap_row in range(7)
            ]
            for source in range(side):
                cells = padded[source, EDGE - 3 + tap_col : EDGE - 3 + tap_col + side, :]
                for tap_row in range(7):
                    target = source + 3 - tap_row
                    if 0 <= target < side:
                        sums[target] = sums[target] + cells * taps[tap_row]
        for row in range(side):
            conv[row * side : (row + 1) * side, lanes] = sums[row]

    gain = gain_ref[...].reshape(1, feat)
    shift = shift_ref[...].reshape(1, feat)

    @pl.loop(0, side)
    def _(row):
        cells = pl.ds(pl.multiple_of(row * side, side), side)
        values = conv[cells, :]
        centred = values - jnp.mean(values, axis=-1, keepdims=True)
        inv_sigma = lax.rsqrt(jnp.mean(centred * centred, axis=-1, keepdims=True) + 1e-06)
        scaled = centred * inv_sigma
        unit[cells, :] = scaled
        sigma_ref[cells, :] = jnp.broadcast_to(inv_sigma, (side, LANES))
        normed[cells, :] = (scaled * gain + shift).astype(jnp.bfloat16)

    unit_copy = pltpu.make_async_copy(unit, unit_out, out_sems.at[0])
    unit_copy.start()

    group = order_ref.shape[0]
    rows = turned_ref.shape[3]
    for index in range(feat // group):
        y_lo, pair = divmod(index, 2)
        turned = lax.dot_general(
            order_ref[...],
            normed[:, index * group : (index + 1) * group],
            (((1,), (1,)), ((), ())),
            preferred_element_type=jnp.float32,
        ).astype(jnp.bfloat16)
        for within in range(2):
            for y_hi in range(2):
                first = (within * 2 + y_hi) * rows
                turned_ref[2 * pair + within, y_hi, y_lo] = turned[first : first + rows]

    stores = [unit_copy]
    for part in range(parts):
        loads[part][0].wait()
        loads[part][1].wait()
        columns = pl.ds(column(part), width)
        pre_act = jnp.dot(normed[...], weights[part], preferred_element_type=jnp.float32)
        pre_act = pre_act + b_ref[:, columns]
        slope = 0.5 * (1.0 + lax.erf(pre_act * 0.7071067811865476)) + pre_act * jnp.exp(
            -0.5 * pre_act * pre_act
        ) * 0.3989422804014327
        grad = (cots[part].astype(jnp.float32) * slope).astype(jnp.bfloat16)
        grads[part] = grad
        sums_ref[:, columns] = jnp.sum(grad.astype(jnp.float32), axis=0, keepdims=True)
        target = away_out if part < half else near_out
        copy = pltpu.make_async_copy(
            grads.at[part], target.at[:, (part % half) * width : (part % half + 1) * width], out_sems.at[1 + part]
        )
        copy.start()
        stores.append(copy)
    for copy in stores:
        copy.wait()


def channel_order(rows, along_z):
    width = 4 * rows
    owned = rows // along_z
    target = np.arange(width).reshape(2, along_z, 2, owned).transpose(0, 2, 1, 3).reshape(-1)
    return jnp.asarray(np.eye(width, dtype=np.float32)[target], jnp.bfloat16)


def front(core, image, taps, bias, gain, shift, w_up, b_row, cot, along_z, parts=4):
    side, feat = image.shape[1], image.shape[3]
    cells = side * side
    hid = w_up.shape[1]
    rows = feat // 16
    width = hid // parts
    whole = pl.BlockSpec(memory_space=pltpu.VMEM)
    remain = pl.BlockSpec(memory_space=pl.ANY)
    return pl.pallas_call(
        front_kernel,
        name="front",
        in_specs=[pl.BlockSpec(memory_space=pltpu.SMEM)] + [whole] * 7 + [remain] * 2,
        out_specs=[remain, whole, whole, remain, remain, whole],
        out_shape=(
            jax.ShapeDtypeStruct((cells, feat), jnp.float32),
            jax.ShapeDtypeStruct((cells, LANES), jnp.float32),
            jax.ShapeDtypeStruct((4, 2, 2, rows, cells), jnp.bfloat16),
            jax.ShapeDtypeStruct((cells, hid // 2), jnp.bfloat16),
            jax.ShapeDtypeStruct((cells, hid // 2), jnp.bfloat16),
            jax.ShapeDtypeStruct((1, hid), jnp.float32),
        ),
        scratch_shapes=[
            pltpu.VMEM((side, side + 2 * EDGE, LANES), jnp.float32),
            pltpu.VMEM((cells, feat), jnp.float32),
            pltpu.VMEM((cells, feat), jnp.float32),
            pltpu.VMEM((cells, feat), jnp.bfloat16),
            pltpu.VMEM((parts, feat, width), jnp.bfloat16),
            pltpu.VMEM((parts, cells, width), jnp.bfloat16),
            pltpu.VMEM((parts, cells, width), jnp.bfloat16),
            pltpu.SemaphoreType.DMA((2 * parts,)),
            pltpu.SemaphoreType.DMA((1 + parts,)),
        ],
        compiler_params=pltpu.CompilerParams(vmem_limit_bytes=VMEM_LIMIT),
        cost_estimate=SMALL,
    )(core, image, taps, bias, gain, shift, channel_order(rows, along_z), b_row, w_up, cot)


def finish_rows(total, unit_ref, sigma_ref, gain_ref, conv_ref, gain_sum_ref, shift_sum_ref):
    feat = total.shape[1]
    gain = gain_ref[...].reshape(1, feat)

    def body(row, carry):
        gain_sum, shift_sum = carry
        cells = pl.ds(pl.multiple_of(row * 8, 8), 8)
        grad = total[cells, :]
        unit = unit_ref[cells, :]
        gain_sum = gain_sum + grad * unit
        shift_sum = shift_sum + grad
        unit_grad = grad * gain
        first = jnp.sum(unit_grad, axis=-1, keepdims=True) * (1.0 / feat)
        second = jnp.sum(unit_grad * unit, axis=-1, keepdims=True) * (1.0 / feat)
        conv_ref[cells, :] = sigma_ref[cells, 0:1] * (unit_grad - first - unit * second)
        return gain_sum, shift_sum

    zero = jnp.zeros((8, feat), jnp.float32)
    gain_sum, shift_sum = lax.fori_loop(0, total.shape[0] // 8, body, (zero, zero))
    gain_sum_ref[...] = jnp.sum(gain_sum, axis=0, keepdims=True)
    shift_sum_ref[...] = jnp.sum(shift_sum, axis=0, keepdims=True)


def norm_grad_kernel(
    core_ref, away_ref, near_ref, unit_ref, sigma_ref, gain_ref, w_hbm,
    conv_ref, gain_sum_ref, shift_sum_ref, weights, total, sems,
):
    parts, feat, width = weights.shape
    half = parts // 2
    core = core_ref[0]
    loads = []
    for part in range(parts):
        owner = 1 - core if part < half else core
        columns = pl.ds(pl.multiple_of((owner * half + part % half) * width, width), width)
        loads.append(pltpu.make_async_copy(w_hbm.at[:, columns], weights.at[part], sems.at[part]))
        loads[-1].start()
    for part in range(parts):
        loads[part].wait()
        grad_ref = away_ref if part < half else near_ref
        grad = grad_ref[:, (part % half) * width : (part % half + 1) * width]
        value = lax.dot_general(grad, weights[part], (((1,), (1,)), ((), ())), preferred_element_type=jnp.float32)
        if part:
            total[...] += value
        else:
            total[...] = value
    finish_rows(total, unit_ref, sigma_ref, gain_ref, conv_ref, gain_sum_ref, shift_sum_ref)


def norm_grad(core, away, near, w_up, unit, sigma, gain, parts=4):
    cells, feat = unit.shape
    width = w_up.shape[1] // parts
    whole = pl.BlockSpec(memory_space=pltpu.VMEM)
    return pl.pallas_call(
        norm_grad_kernel,
        name="norm_grad",
        in_specs=[pl.BlockSpec(memory_space=pltpu.SMEM)] + [whole] * 5 + [pl.BlockSpec(memory_space=pl.ANY)],
        out_specs=[whole] * 3,
        out_shape=(
            jax.ShapeDtypeStruct((cells, feat), jnp.float32),
            jax.ShapeDtypeStruct((1, feat), jnp.float32),
            jax.ShapeDtypeStruct((1, feat), jnp.float32),
        ),
        scratch_shapes=[
            pltpu.VMEM((parts, feat, width), jnp.bfloat16),
            pltpu.VMEM((cells, feat), jnp.float32),
            pltpu.SemaphoreType.DMA((parts,)),
        ],
        compiler_params=pltpu.CompilerParams(vmem_limit_bytes=VMEM_LIMIT),
        cost_estimate=SMALL,
    )(core, away, near, unit, sigma, gain, w_up)


def product_kernel(near_t_ref, far_t_ref, near_ref, far_ref, *out_refs):
    block = (
        jnp.dot(near_t_ref[0], near_ref[...], preferred_element_type=jnp.float32)
        + jnp.dot(far_t_ref[0], far_ref[...], preferred_element_type=jnp.float32)
    ).astype(jnp.bfloat16)
    first = 0
    for out_ref in out_refs:
        columns = out_ref.shape[-1]
        out_ref[...] = block[:, first : first + columns].reshape(out_ref.shape)
        first += columns


def product(near_t, far_t, near, far, splits):
    blocks, rows, cells = near_t.shape
    left = pl.BlockSpec((1, rows, cells), lambda i: (i, 0, 0))
    right = pl.BlockSpec((cells, near.shape[1]), lambda i: (0, 0))
    return pl.pallas_call(
        product_kernel,
        name="product",
        grid=(blocks,),
        in_specs=[left, left, right, right],
        out_specs=[pl.BlockSpec((1, rows, n), lambda i: (i, 0, 0)) for n in splits],
        out_shape=[jax.ShapeDtypeStruct((blocks, rows, n), jnp.bfloat16) for n in splits],
        compiler_params=pltpu.CompilerParams(vmem_limit_bytes=VMEM_LIMIT),
        cost_estimate=SMALL,
    )(near_t, far_t, near, far)


def conv_grad_kernel(
    grad_ref, image_ref, res_ref, taps_ref, gain_sum_ref, shift_sum_ref, up_first_ref, up_second_ref,
    out_ref, sums_ref, padded, image,
):
    side = image_ref.shape[1]
    blank = jnp.zeros((side, EDGE, LANES), jnp.float32)
    padded[:, 0:EDGE, :] = blank
    padded[:, EDGE + side : EDGE + side + EDGE, :] = blank
    image[...] = image_ref[0].astype(jnp.float32)
    bias_sum = jnp.zeros((side, LANES), jnp.float32)
    for row in range(side):
        cells = grad_ref[row * side : (row + 1) * side, :]
        padded[row, EDGE : EDGE + side, :] = cells
        bias_sum = bias_sum + cells
    sums_ref[49:50, :] = gain_sum_ref[...]
    sums_ref[50:51, :] = shift_sum_ref[...]
    sums_ref[51:52, :] = jnp.sum(bias_sum, axis=0, keepdims=True)
    sums_ref[52:53, :] = up_first_ref[...]
    sums_ref[53:54, :] = up_second_ref[...]
    sums_ref[54:, :] = jnp.zeros((SMALL_ROWS - 54, LANES), jnp.float32)
    sums = [res_ref[0, row].astype(jnp.float32) for row in range(side)]
    for turn_col in range(7):
        weights = [
            jnp.broadcast_to(
                taps_ref[pl.ds(7 * (6 - turn_row) + 6 - turn_col, 1), :], (side, LANES)
            )
            for turn_row in range(7)
        ]
        parts = [jnp.zeros((8, LANES), jnp.float32) for _ in range(7)]
        for source in range(side):
            cells = padded[source, EDGE - 3 + turn_col : EDGE - 3 + turn_col + side, :]
            for turn_row in range(7):
                target = source + 3 - turn_row
                if 0 <= target < side:
                    sums[target] = sums[target] + cells * weights[turn_row]
                    product = cells * image[target]
                    parts[turn_row] = parts[turn_row] + (product[:8] + product[8:])
        for turn_row in range(7):
            tap = 7 * (6 - turn_row) + 6 - turn_col
            sums_ref[tap : tap + 1, :] = jnp.sum(parts[turn_row], axis=0, keepdims=True)
    for row in range(side):
        out_ref[0, row] = sums[row].astype(jnp.bfloat16)


def conv_backward(grad, image, residual, taps, gain_sum, shift_sum, up_sums):
    side, feat = image.shape[1], image.shape[3]
    cells = side * side
    picture = pl.BlockSpec((1, side, side, LANES), lambda i: (0, 0, 0, i))
    return pl.pallas_call(
        conv_grad_kernel,
        name="conv_backward",
        grid=(feat // LANES,),
        in_specs=[
            pl.BlockSpec((cells, LANES), lambda i: (0, i)),
            picture,
            picture,
            pl.BlockSpec((49, LANES), lambda i: (0, i)),
            pl.BlockSpec((1, LANES), lambda i: (0, i)),
            pl.BlockSpec((1, LANES), lambda i: (0, i)),
            pl.BlockSpec((1, LANES), lambda i: (0, i)),
            pl.BlockSpec((1, LANES), lambda i: (0, i + feat // LANES)),
        ],
        out_specs=[
            picture,
            pl.BlockSpec((SMALL_ROWS, LANES), lambda i: (0, i)),
        ],
        out_shape=(
            jax.ShapeDtypeStruct(image.shape, jnp.bfloat16),
            jax.ShapeDtypeStruct((SMALL_ROWS, feat), jnp.float32),
        ),
        scratch_shapes=[
            pltpu.VMEM((side, side + 2 * EDGE, LANES), jnp.float32),
            pltpu.VMEM((side, side, LANES), jnp.float32),
        ],
        compiler_params=pltpu.CompilerParams(vmem_limit_bytes=VMEM_LIMIT),
        cost_estimate=SMALL,
    )(grad, image, residual, taps, gain_sum, shift_sum, up_sums, up_sums)


def swap_pieces(values, axes):
    return lax.all_to_all(values, axes, 0, 0, tiled=True)


def total_of(received):
    return jnp.sum(received.astype(jnp.float32), axis=0)


def per_device(images, hidden_cot, residual_cot, w_up, b_up, ln_gain, ln_bias, dw_weight, dw_bias):
    feat, hid = w_up.shape
    plane = ("x", "y_hi", "y_lo")
    others = ("y_lo", "x", "z", "y_hi")
    along_z = lax.axis_size("z")
    chips = 16 * along_z
    owned_rows = feat // (2 * chips)
    inverse_count = 1.0 / (images.shape[0] * 2 * chips)
    core = lax.axis_index("core")
    mine = core.astype(jnp.int32).reshape(1)
    swap = [(0, 1), (1, 0)]

    unit, sigma, turned, away, near, up_sums = front(
        mine, images, dw_weight, dw_bias, ln_gain, ln_bias, w_up, b_up.reshape(1, -1), hidden_cot, along_z
    )
    far = lax.ppermute(away, "core", swap)
    far_turned = lax.ppermute(turned, "core", swap)
    cells = unit.shape[0]
    ringed = hid // 4
    part_a, part_b = product(
        turned.reshape(4, -1, cells), far_turned.reshape(4, -1, cells), near, far, (ringed, hid // 2 - ringed)
    )
    part_b, unit = lax.optimization_barrier((part_b, unit))
    part_a = lax.psum_scatter(part_a.reshape(feat, -1), "x", scatter_dimension=0, tiled=True)
    part_b = swap_pieces(part_b.reshape(16, feat // 16, -1), plane)

    conv_grad, gain_sum, shift_sum = norm_grad(mine, away, near, w_up, unit, sigma, ln_gain)
    grad_input, small = conv_backward(
        conv_grad, images, residual_cot, dw_weight, gain_sum, shift_sum, up_sums
    )
    part_a, part_b, small = lax.optimization_barrier((part_a, part_b, small))
    part_a = lax.psum_scatter(part_a, ("y_hi", "y_lo"), scatter_dimension=0, tiled=True)
    part_b = total_of(part_b).astype(jnp.bfloat16)

    small = small.reshape(2, chips, 1, -1)
    kept = jnp.where(core == 0, small[0], small[1])
    small = kept + lax.ppermute(jnp.where(core == 0, small[1], small[0]), "core", swap)
    small = jnp.sum(swap_pieces(small, others), axis=0, keepdims=True) * inverse_count
    small = swap_pieces(jnp.broadcast_to(small, (chips,) + small.shape[1:]), others)
    other = lax.ppermute(small, "core", swap)
    part_a, small, other = lax.optimization_barrier((part_a, small, other))

    last = jnp.concatenate([part_a, part_b], axis=1)
    last = swap_pieces(last.reshape(2 * along_z, -1, LANES), ("z", "core"))
    last = total_of(last.reshape(along_z, 2, owned_rows, hid // 2))
    owned = last.transpose(1, 0, 2).reshape(owned_rows, hid) * inverse_count
    small = jnp.stack([jnp.where(core == 0, small, other), jnp.where(core == 0, other, small)])
    small = small.reshape(SMALL_ROWS, feat)
    return (
        grad_input,
        owned,
        small[52:54].reshape(hid),
        small[49],
        small[50],
        small[:49],
        small[51],
    )


def solution(mesh):
    x, z = 4, mesh.devices.size // 32
    split = Mesh(mesh.devices.reshape(2, x, z, 2, 2), ("y_lo", "x", "z", "y_hi", "core"))
    images = P(("y_lo", "x", "z", "y_hi", "core"))
    return jax.shard_map(
        per_device,
        mesh=split,
        in_specs=(images, images, images, P(), P(), P(), P(), P(), P()),
        out_specs=(images, images, P(), P(), P(), P(), P()),
        check_vma=False,
    )
```

time: 206 us -> 170 us (0.83)
  waiting for transfers between devices: 78.7 us -> 48.9 us
  starting transfers between devices: 15.3 us -> 29.5 us
  blocking collectives: 28.6 us -> 18.6 us
  local copies, waits for them, and re-layouts: 14.8 us -> 4.91 us
  Pallas kernels: 52.3 us -> 47.5 us
  other arithmetic: 1.04 us -> 5.4 us
    reduce_scatter x2, waiting for transfers between devices: 54.9 us -> 5.95 us  [the longest x1 5.95 us: per_device(): lax.psum_scatter(part_a.reshape(feat, -1), 'x', scatter_dimension=0, tile...]
    all_to_all x2 -> x3, waiting for transfers between devices: 23.8 us -> 37.5 us  [swap_pieces(): return lax.all_to_all(values, axes, 0, 0, tiled=True)]
    all_to_all x2 -> x3, starting transfers between devices: 12 us -> 22.7 us  [swap_pieces(): return lax.all_to_all(values, axes, 0, 0, tiled=True)]
    all_to_all x1, blocking collectives: 28.6 us -> 18.6 us  [swap_pieces(): return lax.all_to_all(values, axes, 0, 0, tiled=True)]
    pallas_call x4 -> x2, Pallas kernels: 33.5 us -> 28.4 us  [the longest x1 16.5 us: front(): pl.pallas_call(front_kernel, name='front', in_specs=[pl.BlockSpec(memory_...]
    reshape x6 -> x3, local copies, waits for them, and re-layouts: 6.69 us -> 1.74 us  [the longest x1 1.07 us: per_device(): last = swap_pieces(last.reshape(2 * along_z, -1, LANES), ('z', 'core'))]
    ppermute x0 -> x2, starting transfers between devices: none -> 3.31 us  [the longest x1 2.82 us: per_device(): other = lax.ppermute(small, 'core', swap)]
  transfers between devices with their start and end apart: 6 -> 9, of which waited for: 3 -> 8; matrix products, arithmetic and copies ran while one was open for 5% -> 3% of each run, Pallas kernels for 17% -> 15%
where the time goes in v3:
time: 170 us; the launch traced here: 169 us
  waiting for transfers between devices  48.9 us (29%)
  Pallas kernels  47.5 us (28%)
  starting transfers between devices  29.5 us (17%)
  blocking collectives  18.6 us (11%)
  between operations  14.1 us (8%)
  other arithmetic  5.4 us (3%)
  local copies, waits for them, and re-layouts  4.91 us (3%)
    all_to_all x3, waiting for transfers between devices, swap_pieces(): return lax.all_to_all(values, axes, 0, 0, tiled=True)  37.5 us
    all_to_all x3, starting transfers between devices, swap_pieces(): return lax.all_to_all(values, axes, 0, 0, tiled=True)  22.7 us
    all_to_all x1, blocking collectives, swap_pieces(): return lax.all_to_all(values, axes, 0, 0, tiled=True)  18.6 us
    pallas_call x1, Pallas kernels, front(): pl.pallas_call(front_kernel, name='front', in_specs=[pl.BlockSpec(memory_...  16.5 us
    pallas_call x1, Pallas kernels, conv_backward(): pl.pallas_call(conv_grad_kernel, name='conv_backward', grid=(feat // LANE...  12.9 us
    pallas_call x1, Pallas kernels, norm_grad(): pl.pallas_call(norm_grad_kernel, name='norm_grad', in_specs=[pl.BlockSpec...  11.9 us
    pallas_call x1, Pallas kernels, product(): pl.pallas_call(product_kernel, name='product', grid=(blocks,), in_specs=[...  6.24 us
    reduce_scatter x1, waiting for transfers between devices, per_device(): lax.psum_scatter(part_a.reshape(feat, -1), 'x', scatter_dimension=0, tile...  5.95 us
  transfers between devices with their start and end apart: 9, of which 8 were waited for; matrix products, arithmetic and copies ran while one was open for 3% of the time, Pallas kernels for 15%

profile of v3, /device:TPU:1, one launch (start us, length us, event | category | flops | bytes accessed | tf_op | source)
XLA Modules:
  0.0 168.9 jit_solution(12928493353505097462)
XLA Ops:
  7.2 0.0 reduce-scatter.3.cloned.1.call-start
  7.2 16.5 %front.1 = (f32[256,1536]{1,0:T(8,128)}, f32[256,128]{1,0:T(8,128)}, bf16[4,2,2,96,256]{4,3,2,1,0:T(8,128)(2,1)}, bf16[256,1536]{1,0:T(8,128)(2,1)}, bf16[256,1536]{1,0:T(8,128)(2,1)}, /*index=5*/f32[1,3072]{1,0:T(1,128)}) custom-call(s32[1]{0:T(128)} %bitcast.core_ref, bf16[1,16,16,1536]{3,2,1,0:T(8,128)(2,1)} %image_ref.3, f32[49,1536]{1,0:T(8,128)} %taps_ref.3, ...), custom_call_target="tpu_custom_call" | custom-call | flops 1000 | bytes 1000 | tf_op jit(solution)/shard_map/front/pallas_call | solution.py:138
  23.7 3.3 %collective-permute-start = (bf16[4,2,2,96,256]{4,3,2,1,0:T(8,128)(2,1)}, bf16[4,2,2,96,256]{4,3,2,1,0:T(8,128)(2,1)S(1)}, u32[]{:S(2)}, u32[]{:S(2)}) collective-permute-start(bf16[4,2,2,96,256]{4,3,2,1,0:T(8,128)(2,1)} %get-tuple-element.30), channel_id=1, source_target_pairs={{0,1},{1,0},{2,3},{3,2},{4,5},{5,4},{6,7},{7,6},{8,9},{9,8},{10,11... | collective-permute-start | bytes 2359304 | tf_op jit(solution)/shard_map/ppermute | solution.py:370
  27.0 0.1 collective-permute-start.1
  27.1 2.0 %collective-permute-done = bf16[4,2,2,96,256]{4,3,2,1,0:T(8,128)(2,1)S(1)} collective-permute-done((bf16[4,2,2,96,256]{4,3,2,1,0:T(8,128)(2,1)}, bf16[4,2,2,96,256]{4,3,2,1,0:T(8,128)(2,1)S(1)}, u32[]{:S(2)}, u32[]{:S(2)}) %collective-permute-start) | collective-permute-done | bytes 786464 | tf_op jit(solution)/shard_map/ppermute | solution.py:370
  29.2 0.0 copy-start
  29.2 1.1 collective-permute-done.1.far_ref
  30.3 0.0 copy-start.1
  30.3 0.0 copy-done
  30.3 0.9 copy-done.1
  31.2 6.2 %product.1 = (bf16[4,384,768]{2,1,0:T(8,128)(2,1)}, bf16[4,384,768]{2,1,0:T(8,128)(2,1)}) custom-call(bf16[4,384,256]{2,1,0:T(8,128)(2,1)} %bitcast.15, bf16[4,384,256]{2,1,0:T(8,128)(2,1)} %bitcast.16, bf16[256,1536]{1,0:T(8,128)(2,1)} %get-tuple-element.29.near_ref, bf16[256,1536]{1,0:T(8,128)(2,1)} %copy-done.1), custom_call_target="tpu_custom_call" | custom-call | flops 1000 | bytes 1000 | tf_op jit(solution)/shard_map/product/pallas_call | solution.py:255
  37.4 0.0 reduce-scatter.3.cloned.1.call-update
  37.4 5.0 %all-to-all-start = ((bf16[16,96,768]{2,1,0:T(8,128)(2,1)}), bf16[16,96,768]{2,1,0:T(8,128)(2,1)S(1)}, u32[]{:S(2)}, u32[]{:S(2)}) async-start(bf16[16,96,768]{2,1,0:T(8,128)(2,1)} %bitcast.14), calls=%async_computation.1 | async-start | bytes 4718592 | tf_op jit(solution)/shard_map/all_to_all | solution.py:347
  42.5 11.9 %norm_grad.1 = (f32[256,1536]{1,0:T(8,128)}, f32[1,1536]{1,0:T(1,128)}, f32[1,1536]{1,0:T(1,128)}) custom-call(s32[1]{0:T(128)} %bitcast.core_ref, bf16[256,1536]{1,0:T(8,128)(2,1)} %get-tuple-element.28.away_ref, bf16[256,1536]{1,0:T(8,128)(2,1)} %get-tuple-element.29.near_ref, f32[256,1536]{1,0:T(8,128)} %get-tuple-element.33.unit_ref, ...), custom_call_target="tpu_custom_call" | custom-call | flops 1000 | bytes 1000 | tf_op jit(solution)/shard_map/norm_grad/pallas_call | solution.py:219
  54.4 12.9 %conv_backward.1 = (bf16[1,16,16,1536]{3,2,1,0:T(8,128)(2,1)}, f32[64,1536]{1,0:T(8,128)}) custom-call(f32[256,1536]{1,0:T(8,128)} %get-tuple-element.35.grad_ref, bf16[1,16,16,1536]{3,2,1,0:T(8,128)(2,1)} %image_ref.3, bf16[1,16,16,1536]{3,2,1,0:T(8,128)(2,1)} %res_ref.1, f32[49,1536]{1,0:T(8,128)} %taps_ref.3, f32[1,1536]{1,0:T(1,128)} %get-tuple-element.36.gain_sum_ref, ...), custom_call_target="tpu_custom_call" | custom-call | flops 1000 | bytes 1000 | tf_op jit(solution)/shard_map/conv_backward/pallas_call | solution.py:315
  67.2 18.1 %all-to-all-done = bf16[16,96,768]{2,1,0:T(8,128)(2,1)S(1)} async-done(((bf16[16,96,768]{2,1,0:T(8,128)(2,1)}), bf16[16,96,768]{2,1,0:T(8,128)(2,1)S(1)}, u32[]{:S(2)}, u32[]{:S(2)}) %all-to-all-start) | async-done | bytes 2359328 | tf_op jit(solution)/shard_map/all_to_all | solution.py:347
  85.4 5.9 %reduce-scatter.3.cloned.1.call-done = bf16[384,768]{1,0:T(8,128)(2,1)} async-done(((bf16[1536,768]{1,0:T(8,128)(2,1)}), bf16[384,768]{1,0:T(8,128)(2,1)}) %reduce-scatter.3.cloned.1.call-update) | async-done | bytes 589840 | tf_op jit(solution)/shard_map/reduce_scatter | solution.py:377
  91.3 1.0 slice_select_fusion
  92.4 0.2 select_n.53
  92.6 0.5 collective-permute-start.2
  93.1 0.2 select_n.52
  93.4 0.8 collective-permute-done.2
  94.2 0.9 add.7
  95.1 14.0 %all-to-all-start.1 = ((f32[128,1,384]{2,1,0:T(1,128)}), f32[128,1,384]{2,1,0:T(1,128)S(1)}, u32[]{:S(2)}, u32[]{:S(2)}) async-start(f32[128,1,384]{2,1,0:T(1,128)} %add.7), calls=%async_computation.3 | async-start | bytes 393216 | tf_op jit(solution)/shard_map/all_to_all | solution.py:347
  109.1 0.0 reduce-scatter.5.cloned.1.call-start
  109.1 0.7 reduce-scatter.5.cloned.1.call-update
  109.8 10.3 %all-to-all-done.1 = f32[128,1,384]{2,1,0:T(1,128)S(1)} async-done(((f32[128,1,384]{2,1,0:T(1,128)}), f32[128,1,384]{2,1,0:T(1,128)S(1)}, u32[]{:S(2)}, u32[]{:S(2)}) %all-to-all-start.1) | async-done | bytes 196640 | tf_op jit(solution)/shard_map/all_to_all | solution.py:347
  120.1 0.2 reduce_sum.30
  120.3 0.1 broadcast_in_dim.2
  120.4 18.6 %all_to_all.20 = f32[128,1,384]{2,1,0:T(1,128)S(1)} all-to-all(f32[128,1,384]{2,1,0:T(1,128)S(1)} %broadcast_in_dim.2), channel_id=1, replica_groups=mesh['y_lo'=2,'x'=4,'z'=8,'y_hi'=2,'core'=2] {'y_lo','x','z','y_hi'}, dimensions={0} | all-to-all | bytes 393216 | tf_op jit(solution)/shard_map/all_to_all | solution.py:347
  139.0 2.8 %collective-permute-start.3 = (f32[128,1,384]{2,1,0:T(1,128)S(1)}, f32[128,1,384]{2,1,0:T(1,128)S(1)}, u32[]{:S(2)}, u32[]{:S(2)}) collective-permute-start(f32[128,1,384]{2,1,0:T(1,128)S(1)} %all_to_all.20), channel_id=1, source_target_pairs={{0,1},{1,0},{2,3},{3,2},{4,5},{5,4},{6,7},{7,6},{8,9},{9,8},{10,11... | collective-permute-start | bytes 589832 | tf_op jit(solution)/shard_map/ppermute | solution.py:393
  141.8 0.3 reduce_sum.31
  142.1 0.7 collective-permute-done.3
  142.9 0.0 reduce-scatter.5.cloned.1.call-done
  142.9 0.9 pad_maximum_fusion
  143.8 1.1 reshape.111
  144.9 3.7 %all-to-all-start.3 = ((bf16[16,72,128]{2,1,0:T(8,128)(2,1)}), bf16[16,72,128]{2,1,0:T(8,128)(2,1)S(1)}, u32[]{:S(2)}, u32[]{:S(2)}) async-start(bf16[16,72,128]{2,1,0:T(8,128)(2,1)} %reshape.111), calls=%async_computation.5 | async-start | bytes 589824 | tf_op jit(solution)/shard_map/all_to_all | solution.py:347
  148.6 0.3 fusion
  148.8 1.0 maximum_reduce_fusion
  149.9 0.1 reshape.112
  150.0 0.8 slice.35
  150.7 0.6 reshape.113
  151.3 0.7 slice_reduce_fusion
  152.0 9.0 %all-to-all-done.3 = bf16[16,72,128]{2,1,0:T(8,128)(2,1)S(1)} async-done(((bf16[16,72,128]{2,1,0:T(8,128)(2,1)}), bf16[16,72,128]{2,1,0:T(8,128)(2,1)S(1)}, u32[]{:S(2)}, u32[]{:S(2)}) %all-to-all-start.3) | async-done | bytes 294944 | tf_op jit(solution)/shard_map/all_to_all | solution.py:347
  161.0 0.3 reshape.114
  161.3 0.1 reduce_sum.32
  161.4 0.7 broadcast_multiply_fusion
  (2 shorter events, 0.0 us)
Async XLA Ops:
  7.2 84.2 %reduce-scatter.3.cloned.1.call-start = ((), (), s32[]{:S(2)}) async-start(), calls=%async_computation.6 | async-start | bytes 2949120 | tf_op jit(solution)/shard_map/reduce_scatter | solution.py:377
  23.7 5.4 %collective-permute-start = (bf16[4,2,2,96,256]{4,3,2,1,0:T(8,128)(2,1)}, bf16[4,2,2,96,256]{4,3,2,1,0:T(8,128)(2,1)S(1)}, u32[]{:S(2)}, u32[]{:S(2)}) collective-permute-start(bf16[4,2,2,96,256]{4,3,2,1,0:T(8,128)(2,1)} %get-tuple-element.30), channel_id=1, source_target_pairs={{0,1},{1,0},{2,3},{3,2},{4,5},{5,4},{6,7},{7,6},{8,9},{9,8},{10,11... | collective-permute-start | bytes 2359304 | tf_op jit(solution)/shard_map/ppermute | solution.py:370
  27.0 3.2 %collective-permute-start.1 = (bf16[256,1536]{1,0:T(8,128)(2,1)}, bf16[256,1536]{1,0:T(8,128)(2,1)S(1)}, u32[]{:S(2)}, u32[]{:S(2)}) collective-permute-start(bf16[256,1536]{1,0:T(8,128)(2,1)} %get-tuple-element.28.away_ref), channel_id=1, source_target_pairs={{0,1},{1,0},{2,3},{3,2},{4,5},{5,4},{6,7},{7,6},{8,9},{9,8},{10,11... | collective-permute-start | bytes 2359304 | tf_op jit(solution)/shard_map/ppermute | solution.py:369
  29.2 1.1 copy-start
  30.3 0.9 copy-start.1
  37.4 48.0 %all-to-all-start = ((bf16[16,96,768]{2,1,0:T(8,128)(2,1)}), bf16[16,96,768]{2,1,0:T(8,128)(2,1)S(1)}, u32[]{:S(2)}, u32[]{:S(2)}) async-start(bf16[16,96,768]{2,1,0:T(8,128)(2,1)} %bitcast.14), calls=%async_computation.1 | async-start | bytes 4718592 | tf_op jit(solution)/shard_map/all_to_all | solution.py:347
  92.6 1.6 collective-permute-start.2
  95.1 25.0 %all-to-all-start.1 = ((f32[128,1,384]{2,1,0:T(1,128)}), f32[128,1,384]{2,1,0:T(1,128)S(1)}, u32[]{:S(2)}, u32[]{:S(2)}) async-start(f32[128,1,384]{2,1,0:T(1,128)} %add.7), calls=%async_computation.3 | async-start | bytes 393216 | tf_op jit(solution)/shard_map/all_to_all | solution.py:347
  109.1 33.8 %reduce-scatter.5.cloned.1.call-start = ((), (), s32[]{:S(2)}) async-start(), calls=%async_computation.7 | async-start | bytes 737280 | tf_op jit(solution)/shard_map/reduce_scatter | solution.py:385
  139.0 3.9 %collective-permute-start.3 = (f32[128,1,384]{2,1,0:T(1,128)S(1)}, f32[128,1,384]{2,1,0:T(1,128)S(1)}, u32[]{:S(2)}, u32[]{:S(2)}) collective-permute-start(f32[128,1,384]{2,1,0:T(1,128)S(1)} %all_to_all.20), channel_id=1, source_target_pairs={{0,1},{1,0},{2,3},{3,2},{4,5},{5,4},{6,7},{7,6},{8,9},{9,8},{10,11... | collective-permute-start | bytes 589832 | tf_op jit(solution)/shard_map/ppermute | solution.py:393
  144.9 16.2 %all-to-all-start.3 = ((bf16[16,72,128]{2,1,0:T(8,128)(2,1)}), bf16[16,72,128]{2,1,0:T(8,128)(2,1)S(1)}, u32[]{:S(2)}, u32[]{:S(2)}) async-start(bf16[16,72,128]{2,1,0:T(8,128)(2,1)} %reshape.111), calls=%async_computation.5 | async-start | bytes 589824 | tf_op jit(solution)/shard_map/all_to_all | solution.py:347
Sparse Core Ops, SparseCore 0:
  37.6 53.7 reduce-scatter.2
  112.4 23.5 reduce-scatter.4

commit v4 on v3

--- a/solution.py
+++ b/solution.py
@@ -11,7 +11,7 @@
 EDGE = 8
 VMEM_LIMIT = 60 * 1024 * 1024
 SMALL = pl.CostEstimate(flops=1000, bytes_accessed=1000, transcendentals=0)
-SMALL_ROWS = 64
+SMALL_ROWS = 56
 
 
 def front_kernel(
@@ -236,32 +236,71 @@
     )(core, away, near, unit, sigma, gain, w_up)
 
 
-def product_kernel(near_t_ref, far_t_ref, near_ref, far_ref, *out_refs):
+def product_kernel(place_ref, near_t_ref, far_t_ref, near_ref, far_ref, *out_refs):
+    _, along_y, rows, cells = near_t_ref.shape
     block = (
-        jnp.dot(near_t_ref[0], near_ref[...], preferred_element_type=jnp.float32)
-        + jnp.dot(far_t_ref[0], far_ref[...], preferred_element_type=jnp.float32)
+        jnp.dot(near_t_ref[...].reshape(along_y * rows, cells), near_ref[...], preferred_element_type=jnp.float32)
+        + jnp.dot(far_t_ref[...].reshape(along_y * rows, cells), far_ref[...], preferred_element_type=jnp.float32)
     ).astype(jnp.bfloat16)
-    first = 0
-    for out_ref in out_refs:
-        columns = out_ref.shape[-1]
-        out_ref[...] = block[:, first : first + columns].reshape(out_ref.shape)
-        first += columns
-
-
-def product(near_t, far_t, near, far, splits):
-    blocks, rows, cells = near_t.shape
-    left = pl.BlockSpec((1, rows, cells), lambda i: (i, 0, 0))
-    right = pl.BlockSpec((cells, near.shape[1]), lambda i: (0, 0))
+    columns = out_refs[0].shape[2]
+    out_refs[4][...] = block[:, columns:].reshape(out_refs[4].shape)
+    for steps in range(4):
+
+        @pl.when(pl.program_id(0) == steps)
+        def _():
+            for y in range(along_y):
+                out_refs[steps][lax.rem(y - place_ref[1] + 4, 4)] = block[y * rows : (y + 1) * rows, :columns]
+
+
+def product(place, near_t, far_t, near, far, columns):
+    _, _, rows, cells = near_t.shape
+    others = near.shape[1] - columns
+    left = pl.BlockSpec((1, 4, rows, cells), lambda i, p: (lax.rem(p[0] + i, 4), 0, 0, 0))
+    right = pl.BlockSpec((cells, near.shape[1]), lambda i, p: (0, 0))
     return pl.pallas_call(
         product_kernel,
         name="product",
-        grid=(blocks,),
-        in_specs=[left, left, right, right],
-        out_specs=[pl.BlockSpec((1, rows, n), lambda i: (i, 0, 0)) for n in splits],
-        out_shape=[jax.ShapeDtypeStruct((blocks, rows, n), jnp.bfloat16) for n in splits],
+        grid_spec=pltpu.PrefetchScalarGridSpec(
+            num_scalar_prefetch=1,
+            grid=(4,),
+            in_specs=[left, left, right, right],
+            out_specs=[pl.BlockSpec((4, rows, columns), lambda i, p: (0, 0, 0))] * 4
+            + [pl.BlockSpec((4, 1, rows, others), lambda i, p: (0, lax.rem(p[0] + i, 4), 0, 0))],
+        ),
+        out_shape=[jax.ShapeDtypeStruct((4, rows, columns), jnp.bfloat16)] * 4
+        + [jax.ShapeDtypeStruct((4, 4, rows, others), jnp.bfloat16)],
         compiler_params=pltpu.CompilerParams(vmem_limit_bytes=VMEM_LIMIT),
         cost_estimate=SMALL,
-    )(near_t, far_t, near, far)
+    )(place, near_t, far_t, near, far)
+
+
+def sum_kernel(*refs):
+    for index in range(4):
+        total = refs[0][index].astype(jnp.float32)
+        for ref in refs[1:4]:
+            total = total + ref[index].astype(jnp.float32)
+        refs[4 + index][...] = total.astype(jnp.bfloat16)
+
+
+def sum_pieces(pieces):
+    _, rows, columns = pieces[0].shape
+    return pl.pallas_call(
+        sum_kernel,
+        name="sum_pieces",
+        out_shape=[jax.ShapeDtypeStruct((rows, columns), jnp.bfloat16)] * 4,
+        compiler_params=pltpu.CompilerParams(vmem_limit_bytes=VMEM_LIMIT),
+        cost_estimate=SMALL,
+    )(*pieces)
+
+
+def to_owners(pieces, axes):
+    named = range(4) if axes == "x" else [0, 2, 1, 3]
+    moved = [
+        lax.ppermute(piece, axes, [(named[i], named[(i + d) % 4]) for i in range(4)])
+        for d, piece in enumerate(pieces)
+        if d
+    ]
+    return [pieces[0]] + moved
 
 
 def conv_grad_kernel(
@@ -354,13 +393,12 @@
 def per_device(images, hidden_cot, residual_cot, w_up, b_up, ln_gain, ln_bias, dw_weight, dw_bias):
     feat, hid = w_up.shape
     plane = ("x", "y_hi", "y_lo")
-    others = ("y_lo", "x", "z", "y_hi")
     along_z = lax.axis_size("z")
-    chips = 16 * along_z
-    owned_rows = feat // (2 * chips)
-    inverse_count = 1.0 / (images.shape[0] * 2 * chips)
-    core = lax.axis_index("core")
-    mine = core.astype(jnp.int32).reshape(1)
+    owned_rows = feat // (32 * along_z)
+    inverse_count = 1.0 / (images.shape[0] * 32 * along_z)
+    mine = lax.axis_index("core").astype(jnp.int32).reshape(1)
+    y_index = 2 * lax.axis_index("y_hi") + lax.axis_index("y_lo")
+    place = jnp.stack([lax.axis_index("x"), y_index]).astype(jnp.int32)
     swap = [(0, 1), (1, 0)]
 
     unit, sigma, turned, away, near, up_sums = front(
@@ -369,36 +407,31 @@
     far = lax.ppermute(away, "core", swap)
     far_turned = lax.ppermute(turned, "core", swap)
     cells = unit.shape[0]
-    ringed = hid // 4
-    part_a, part_b = product(
-        turned.reshape(4, -1, cells), far_turned.reshape(4, -1, cells), near, far, (ringed, hid // 2 - ringed)
+    *part_a, part_b = product(
+        place, turned.reshape(4, 4, -1, cells), far_turned.reshape(4, 4, -1, cells), near, far, hid // 4
     )
     part_b, unit = lax.optimization_barrier((part_b, unit))
-    part_a = lax.psum_scatter(part_a.reshape(feat, -1), "x", scatter_dimension=0, tiled=True)
-    part_b = swap_pieces(part_b.reshape(16, feat // 16, -1), plane)
+    part_a = to_owners(part_a, "x")
+    part_b = swap_pieces(part_b, ("y_hi", "y_lo"))
 
     conv_grad, gain_sum, shift_sum = norm_grad(mine, away, near, w_up, unit, sigma, ln_gain)
     grad_input, small = conv_backward(
         conv_grad, images, residual_cot, dw_weight, gain_sum, shift_sum, up_sums
     )
     part_a, part_b, small = lax.optimization_barrier((part_a, part_b, small))
-    part_a = lax.psum_scatter(part_a, ("y_hi", "y_lo"), scatter_dimension=0, tiled=True)
-    part_b = total_of(part_b).astype(jnp.bfloat16)
-
-    small = small.reshape(2, chips, 1, -1)
-    kept = jnp.where(core == 0, small[0], small[1])
-    small = kept + lax.ppermute(jnp.where(core == 0, small[1], small[0]), "core", swap)
-    small = jnp.sum(swap_pieces(small, others), axis=0, keepdims=True) * inverse_count
-    small = swap_pieces(jnp.broadcast_to(small, (chips,) + small.shape[1:]), others)
-    other = lax.ppermute(small, "core", swap)
-    part_a, small, other = lax.optimization_barrier((part_a, small, other))
-
-    last = jnp.concatenate([part_a, part_b], axis=1)
-    last = swap_pieces(last.reshape(2 * along_z, -1, LANES), ("z", "core"))
-    last = total_of(last.reshape(along_z, 2, owned_rows, hid // 2))
+    part_a = to_owners(sum_pieces(part_a), ("y_lo", "y_hi"))
+    part_b = swap_pieces(total_of(part_b).astype(jnp.bfloat16), "x")
+    small = total_of(swap_pieces(small.reshape(16, -1, LANES), plane)).astype(jnp.bfloat16)
+
+    last = jnp.concatenate([total_of(jnp.stack(part_a)), total_of(part_b)], axis=1).astype(jnp.bfloat16)
+    last = last.reshape(2 * along_z, -1, LANES)
+    height = last.shape[1]
+    small = jnp.broadcast_to(small, (2 * along_z,) + small.shape)
+    last = swap_pieces(jnp.concatenate([last, small], axis=1), ("z", "core"))
+    small = total_of(last[:, height:]) * inverse_count
+    small = swap_pieces(jnp.broadcast_to(small, (16,) + small.shape), plane).reshape(SMALL_ROWS, feat)
+    last = total_of(last[:, :height].reshape(along_z, 2, owned_rows, hid // 2))
     owned = last.transpose(1, 0, 2).reshape(owned_rows, hid) * inverse_count
-    small = jnp.stack([jnp.where(core == 0, small, other), jnp.where(core == 0, other, small)])
-    small = small.reshape(SMALL_ROWS, feat)
     return (
         grad_input,
         owned,

time: 170 us -> 146 us (0.86)
  waiting for transfers between devices: 48.9 us -> 25.7 us
  between operations: 14.1 us -> 0.82 us
  blocking collectives: 18.6 us -> 26 us
  Pallas kernels: 47.5 us -> 51.6 us
  starting transfers between devices: 29.5 us -> 31.3 us
    all_to_all x3 -> x4, waiting for transfers between devices: 37.5 us -> 16.9 us  [swap_pieces(): return lax.all_to_all(values, axes, 0, 0, tiled=True)]
    all_to_all x1, blocking collectives: 18.6 us -> 26 us  [swap_pieces(): return lax.all_to_all(values, axes, 0, 0, tiled=True)]
    reduce_scatter x2 -> x0, waiting for transfers between devices: 5.95 us -> none  [the longest x1 5.95 us: per_device(): lax.psum_scatter(part_a.reshape(feat, -1), 'x', scatter_dimension=0, tile...]
    ppermute x2 -> x6, waiting for transfers between devices: 1.57 us -> 6.15 us  [to_owners(): lax.ppermute(piece, axes, [(named[i], named[(i + d) % 4]) for i in range(...]
    pallas_call x1 -> x2, Pallas kernels: 6.24 us -> 10.4 us  [the longest x1 7.86 us: product(): pl.pallas_call(product_kernel, name='product', grid_spec=pltpu.PrefetchSc...]
    ppermute x2 -> x6, starting transfers between devices: 3.31 us -> 6.63 us  [to_owners(): lax.ppermute(piece, axes, [(named[i], named[(i + d) % 4]) for i in range(...]
    ppermute x1, starting transfers between devices: 0.1 us -> 3.33 us  [per_device(): far = lax.ppermute(away, 'core', swap)]
    ppermute x1, starting transfers between devices: 3.32 us -> 0.1 us  [per_device(): far_turned = lax.ppermute(turned, 'core', swap)]
  transfers between devices with their start and end apart: 9 -> 12, of which waited for: 8 -> 7; matrix products, arithmetic and copies ran while one was open for 3% -> 2% of each run, Pallas kernels for 15% -> 19%
where the time goes in v4:
time: 146 us; the launch traced here: 145 us
  Pallas kernels  51.6 us (35%)
  starting transfers between devices  31.3 us (21%)
  blocking collectives  26 us (18%)
  waiting for transfers between devices  25.7 us (18%)
  local copies, waits for them, and re-layouts  6.13 us (4%)
  other arithmetic  3.84 us (3%)
    all_to_all x1, blocking collectives, swap_pieces(): return lax.all_to_all(values, axes, 0, 0, tiled=True)  26 us
    all_to_all x4, starting transfers between devices, swap_pieces(): return lax.all_to_all(values, axes, 0, 0, tiled=True)  21.3 us
    all_to_all x4, waiting for transfers between devices, swap_pieces(): return lax.all_to_all(values, axes, 0, 0, tiled=True)  16.9 us
    pallas_call x1, Pallas kernels, front(): pl.pallas_call(front_kernel, name='front', in_specs=[pl.BlockSpec(memory_...  16.4 us
    pallas_call x1, Pallas kernels, conv_backward(): pl.pallas_call(conv_grad_kernel, name='conv_backward', grid=(feat // LANE...  12.9 us
    pallas_call x1, Pallas kernels, norm_grad(): pl.pallas_call(norm_grad_kernel, name='norm_grad', in_specs=[pl.BlockSpec...  11.9 us
    pallas_call x1, Pallas kernels, product(): pl.pallas_call(product_kernel, name='product', grid_spec=pltpu.PrefetchSc...  7.86 us
    ppermute x6, starting transfers between devices, to_owners(): lax.ppermute(piece, axes, [(named[i], named[(i + d) % 4]) for i in range(...  6.63 us
  transfers between devices with their start and end apart: 12, of which 7 were waited for; matrix products, arithmetic and copies ran while one was open for 2% of the time, Pallas kernels for 19%

profile of v4, /device:TPU:1, one launch (start us, length us, event | category | flops | bytes accessed | tf_op | source)
XLA Modules:
  0.0 145.4 jit_solution(9216194451549176352)
XLA Ops:
  0.6 16.4 %front.1 = (f32[256,1536]{1,0:T(8,128)}, f32[256,128]{1,0:T(8,128)}, bf16[4,2,2,96,256]{4,3,2,1,0:T(8,128)(2,1)}, bf16[256,1536]{1,0:T(8,128)(2,1)}, bf16[256,1536]{1,0:T(8,128)(2,1)}, /*index=5*/f32[1,3072]{1,0:T(1,128)}) custom-call(s32[1]{0:T(128)} %bitcast.core_ref, bf16[1,16,16,1536]{3,2,1,0:T(8,128)(2,1)} %image_ref.3, f32[49,1536]{1,0:T(8,128)} %taps_ref.3, ...), custom_call_target="tpu_custom_call" | custom-call | flops 1000 | bytes 1000 | tf_op jit(solution)/shard_map/front/pallas_call | solution.py:138
  17.1 3.3 %collective-permute-start.1 = (bf16[256,1536]{1,0:T(8,128)(2,1)}, bf16[256,1536]{1,0:T(8,128)(2,1)S(1)}, u32[]{:S(2)}, u32[]{:S(2)}) collective-permute-start(bf16[256,1536]{1,0:T(8,128)(2,1)} %get-tuple-element.35.away_ref), channel_id=1, source_target_pairs={{0,1},{1,0},{2,3},{3,2},{4,5},{5,4},{6,7},{7,6},{8,9},{9,8},{10,11... | collective-permute-start | bytes 2359304 | tf_op jit(solution)/shard_map/ppermute | solution.py:407
  20.4 0.1 collective-permute-start
  20.5 0.6 pad_add_fusion.place_ref
  21.1 1.4 collective-permute-done.1.far_ref
  22.5 0.0 copy-start
  22.5 1.1 collective-permute-done
  23.7 0.0 copy-start.1
  23.7 0.0 copy-done
  23.7 0.9 copy-done.1
  24.6 7.9 %product.1 = (bf16[4,96,768]{2,1,0:T(8,128)(2,1)}, bf16[4,96,768]{2,1,0:T(8,128)(2,1)}, bf16[4,96,768]{2,1,0:T(8,128)(2,1)}, bf16[4,96,768]{2,1,0:T(8,128)(2,1)}, bf16[4,4,96,768]{3,2,1,0:T(8,128)(2,1)}) custom-call(s32[2]{0:T(128)} %pad_add_fusion.place_ref, bf16[4,4,96,256]{3,2,1,0:T(8,128)(2,1)} %bitcast.9, bf16[4,4,96,256]{3,2,1,0:T(8,128)(2,1)} %bitcast.10, ...), custom_call_target="tpu_custom_call" | custom-call | flops 1000 | bytes 1000 | tf_op jit(solution)/shard_map/product/pallas_call | solution.py:260
  32.4 0.0 copy-start.3
  32.4 3.8 %all-to-all-start = ((bf16[4,4,96,768]{3,2,1,0:T(8,128)(2,1)}), bf16[4,4,96,768]{3,2,1,0:T(8,128)(2,1)S(1)}, u32[]{:S(2)}, u32[]{:S(2)}) async-start(bf16[4,4,96,768]{3,2,1,0:T(8,128)(2,1)} %get-tuple-element.51), calls=%async_computation | async-start | bytes 4718592 | tf_op jit(solution)/shard_map/all_to_all | solution.py:386
  36.2 0.1 collective-permute-start.2
  36.3 2.3 %collective-permute-start.3 = (bf16[4,96,768]{2,1,0:T(8,128)(2,1)}, bf16[4,96,768]{2,1,0:T(8,128)(2,1)}, u32[]{:S(2)}, u32[]{:S(2)}) collective-permute-start(bf16[4,96,768]{2,1,0:T(8,128)(2,1)} %get-tuple-element.49), channel_id=1, source_target_pairs={{0,64},{32,96},{64,0},{96,32},{1,65},{33,97},{65,1},{97,33},{2,66}... | collective-permute-start | bytes 1769480 | tf_op jit(solution)/shard_map/ppermute | solution.py:299
  38.6 0.0 copy-done.3
  38.6 1.1 collective-permute-start.4
  39.8 11.9 %norm_grad.1 = (f32[256,1536]{1,0:T(8,128)}, f32[1,1536]{1,0:T(1,128)}, f32[1,1536]{1,0:T(1,128)}) custom-call(s32[1]{0:T(128)} %bitcast.core_ref, bf16[256,1536]{1,0:T(8,128)(2,1)} %get-tuple-element.35.away_ref, bf16[256,1536]{1,0:T(8,128)(2,1)} %get-tuple-element.36.near_ref, f32[256,1536]{1,0:T(8,128)} %get-tuple-element.40.unit_ref, ...), custom_call_target="tpu_custom_call" | custom-call | flops 1000 | bytes 1000 | tf_op jit(solution)/shard_map/norm_grad/pallas_call | solution.py:219
  51.7 12.9 %conv_backward.1 = (bf16[1,16,16,1536]{3,2,1,0:T(8,128)(2,1)}, f32[56,1536]{1,0:T(8,128)}) custom-call(f32[256,1536]{1,0:T(8,128)} %get-tuple-element.42.grad_ref, bf16[1,16,16,1536]{3,2,1,0:T(8,128)(2,1)} %image_ref.3, bf16[1,16,16,1536]{3,2,1,0:T(8,128)(2,1)} %res_ref.1, f32[49,1536]{1,0:T(8,128)} %taps_ref.3, f32[1,1536]{1,0:T(1,128)} %get-tuple-element.43.gain_sum_ref, ...), custom_call_target="tpu_custom_call" | custom-call | flops 1000 | bytes 1000 | tf_op jit(solution)/shard_map/conv_backward/pallas_call | solution.py:354
  64.5 0.0 collective-permute-done.2.refs_1_
  64.5 0.0 copy-start.2
  64.5 0.0 collective-permute-done.3.refs_2_
  64.5 0.7 collective-permute-done.4.refs_3_
  65.3 0.0 all-to-all-done
  65.3 1.8 %reshape.49 = f32[16,42,128]{2,1,0:T(8,128)} reshape(f32[56,1536]{1,0:T(8,128)} %get-tuple-element.62) | data formatting | bytes 688128 | tf_op jit(solution)/shard_map/reshape | solution.py:424
  67.1 7.3 %all-to-all-start.2 = ((f32[16,42,128]{2,1,0:T(8,128)}), f32[16,42,128]{2,1,0:T(8,128)S(1)}, u32[]{:S(2)}, u32[]{:S(2)}) async-start(f32[16,42,128]{2,1,0:T(8,128)} %reshape.49), calls=%async_computation.2 | async-start | bytes 786432 | tf_op jit(solution)/shard_map/all_to_all | solution.py:386
  74.4 1.3 reduce_sum.58
  75.8 7.7 %all-to-all-done.2 = f32[16,42,128]{2,1,0:T(8,128)S(1)} async-done(((f32[16,42,128]{2,1,0:T(8,128)}), f32[16,42,128]{2,1,0:T(8,128)S(1)}, u32[]{:S(2)}, u32[]{:S(2)}) %all-to-all-start.2) | async-done | bytes 344096 | tf_op jit(solution)/shard_map/all_to_all | solution.py:386
  83.5 0.0 copy-done.2
  83.5 3.5 %all-to-all-start.1 = ((bf16[4,96,768]{2,1,0:T(8,128)(2,1)}), bf16[4,96,768]{2,1,0:T(8,128)(2,1)S(1)}, u32[]{:S(2)}, u32[]{:S(2)}) async-start(bf16[4,96,768]{2,1,0:T(8,128)(2,1)} %reduce_sum.58), calls=%async_computation.1 | async-start | bytes 1179648 | tf_op jit(solution)/shard_map/all_to_all | solution.py:386
  86.9 2.5 %sum_pieces.1 = (bf16[96,768]{1,0:T(8,128)(2,1)}, bf16[96,768]{1,0:T(8,128)(2,1)}, bf16[96,768]{1,0:T(8,128)(2,1)}, bf16[96,768]{1,0:T(8,128)(2,1)}) custom-call(bf16[4,96,768]{2,1,0:T(8,128)(2,1)} %get-tuple-element.53.refs_0_, bf16[4,96,768]{2,1,0:T(8,128)(2,1)} %copy-done.2, bf16[4,96,768]{2,1,0:T(8,128)(2,1)} %collective-permute-done.3.refs_2_, ...), custom_call_target="tpu_custom_call" | custom-call | flops 1000 | bytes 1000 | tf_op jit(solution)/shard_map/sum_pieces/pallas_call | solution.py:287
  89.5 0.4 collective-permute-start.5
  89.9 1.5 %collective-permute-start.6 = (bf16[96,768]{1,0:T(8,128)(2,1)}, bf16[96,768]{1,0:T(8,128)(2,1)S(1)}, u32[]{:S(2)}, u32[]{:S(2)}) collective-permute-start(bf16[96,768]{1,0:T(8,128)(2,1)} %get-tuple-element.59), channel_id=1, source_target_pairs={{0,2},{128,130},{2,0},{130,128},{1,3},{129,131},{3,1},{131,129},{4... | collective-permute-start | bytes 442376 | tf_op jit(solution)/shard_map/ppermute | solution.py:299
  91.4 1.2 collective-permute-start.7
  92.6 4.5 %collective-permute-done.5 = bf16[96,768]{1,0:T(8,128)(2,1)S(1)} collective-permute-done((bf16[96,768]{1,0:T(8,128)(2,1)}, bf16[96,768]{1,0:T(8,128)(2,1)S(1)}, u32[]{:S(2)}, u32[]{:S(2)}) %collective-permute-start.5) | collective-permute-done | bytes 147488 | tf_op jit(solution)/shard_map/ppermute | solution.py:299
  97.1 0.0 collective-permute-done.6
  97.1 0.9 collective-permute-done.7
  98.0 0.9 add_add_fusion
  99.0 0.0 all-to-all-done.1
  99.0 0.1 reduce.2
  99.1 0.4 convert_element_type.27
  99.6 26.0 %all_to_all.25 = bf16[16,114,128]{2,1,0:T(8,128)(2,1)S(1)} all-to-all(bf16[16,114,128]{2,1,0:T(8,128)(2,1)S(1)} %pad_maximum_fusion), channel_id=1, replica_groups=mesh['y_lo'=2,'x'=4,'z'=8,'y_hi'=2,'core'=2] {'z','core'}, dimensions={0} | all-to-all | bytes 933888 | tf_op jit(solution)/shard_map/all_to_all | solution.py:386
  125.7 0.1 reshape.52
  125.8 0.1 reduce_sum.61
  125.8 0.8 broadcast_in_dim.7
  126.6 6.7 %all-to-all-start.4 = ((f32[16,42,128]{2,1,0:T(8,128)}), f32[16,42,128]{2,1,0:T(8,128)S(1)}, u32[]{:S(2)}, u32[]{:S(2)}) async-start(f32[16,42,128]{2,1,0:T(8,128)} %broadcast_in_dim.7), calls=%async_computation.4 | async-start | bytes 786432 | tf_op jit(solution)/shard_map/all_to_all | solution.py:386
  133.3 0.7 broadcast_multiply_fusion
  134.0 9.2 %all-to-all-done.4 = f32[16,42,128]{2,1,0:T(8,128)S(1)} async-done(((f32[16,42,128]{2,1,0:T(8,128)}), f32[16,42,128]{2,1,0:T(8,128)S(1)}, u32[]{:S(2)}, u32[]{:S(2)}) %all-to-all-start.4) | async-done | bytes 344096 | tf_op jit(solution)/shard_map/all_to_all | solution.py:386
  143.2 0.1 reshape.50
  143.3 0.7 slice_reduce_fusion
  144.0 0.8 slice.30
  144.8 0.6 reshape.51
  (9 shorter events, 0.2 us)
Async XLA Ops:
  17.1 5.5 %collective-permute-start.1 = (bf16[256,1536]{1,0:T(8,128)(2,1)}, bf16[256,1536]{1,0:T(8,128)(2,1)S(1)}, u32[]{:S(2)}, u32[]{:S(2)}) collective-permute-start(bf16[256,1536]{1,0:T(8,128)(2,1)} %get-tuple-element.35.away_ref), channel_id=1, source_target_pairs={{0,1},{1,0},{2,3},{3,2},{4,5},{5,4},{6,7},{7,6},{8,9},{9,8},{10,11... | collective-permute-start | bytes 2359304 | tf_op jit(solution)/shard_map/ppermute | solution.py:407
  20.4 3.2 %collective-permute-start = (bf16[4,2,2,96,256]{4,3,2,1,0:T(8,128)(2,1)}, bf16[4,2,2,96,256]{4,3,2,1,0:T(8,128)(2,1)S(1)}, u32[]{:S(2)}, u32[]{:S(2)}) collective-permute-start(bf16[4,2,2,96,256]{4,3,2,1,0:T(8,128)(2,1)} %get-tuple-element.37), channel_id=1, source_target_pairs={{0,1},{1,0},{2,3},{3,2},{4,5},{5,4},{6,7},{7,6},{8,9},{9,8},{10,11... | collective-permute-start | bytes 2359304 | tf_op jit(solution)/shard_map/ppermute | solution.py:408
  22.5 1.1 copy-start
  23.7 0.9 copy-start.1
  32.4 6.2 %copy-start.3 = (bf16[4,96,768]{2,1,0:T(8,128)(2,1)S(1)}, bf16[4,96,768]{2,1,0:T(8,128)(2,1)}, u32[]{:S(2)}) copy-start(bf16[4,96,768]{2,1,0:T(8,128)(2,1)} %get-tuple-element.50) | copy-start | bytes 1769476
  32.4 32.9 %all-to-all-start = ((bf16[4,4,96,768]{3,2,1,0:T(8,128)(2,1)}), bf16[4,4,96,768]{3,2,1,0:T(8,128)(2,1)S(1)}, u32[]{:S(2)}, u32[]{:S(2)}) async-start(bf16[4,4,96,768]{3,2,1,0:T(8,128)(2,1)} %get-tuple-element.51), calls=%async_computation | async-start | bytes 4718592 | tf_op jit(solution)/shard_map/all_to_all | solution.py:386
  36.2 28.3 %collective-permute-start.2 = (bf16[4,96,768]{2,1,0:T(8,128)(2,1)}, bf16[4,96,768]{2,1,0:T(8,128)(2,1)S(1)}, u32[]{:S(2)}, u32[]{:S(2)}) collective-permute-start(bf16[4,96,768]{2,1,0:T(8,128)(2,1)} %get-tuple-element.48), channel_id=1, source_target_pairs={{0,32},{32,64},{64,96},{96,0},{1,33},{33,65},{65,97},{97,1},{2,34}... | collective-permute-start | bytes 1769480 | tf_op jit(solution)/shard_map/ppermute | solution.py:299
  36.3 28.3 %collective-permute-start.3 = (bf16[4,96,768]{2,1,0:T(8,128)(2,1)}, bf16[4,96,768]{2,1,0:T(8,128)(2,1)}, u32[]{:S(2)}, u32[]{:S(2)}) collective-permute-start(bf16[4,96,768]{2,1,0:T(8,128)(2,1)} %get-tuple-element.49), channel_id=1, source_target_pairs={{0,64},{32,96},{64,0},{96,32},{1,65},{33,97},{65,1},{97,33},{2,66}... | collective-permute-start | bytes 1769480 | tf_op jit(solution)/shard_map/ppermute | solution.py:299
  38.6 26.7 %collective-permute-start.4 = (bf16[4,96,768]{2,1,0:T(8,128)(2,1)S(1)}, bf16[4,96,768]{2,1,0:T(8,128)(2,1)}, u32[]{:S(2)}, u32[]{:S(2)}) collective-permute-start(bf16[4,96,768]{2,1,0:T(8,128)(2,1)S(1)} %copy-done.3), channel_id=1, source_target_pairs={{0,96},{32,0},{64,32},{96,64},{1,97},{33,1},{65,33},{97,65},{2,98}... | collective-permute-start | bytes 1769480 | tf_op jit(solution)/shard_map/ppermute | solution.py:299
  64.5 18.9 %copy-start.2 = (bf16[4,96,768]{2,1,0:T(8,128)(2,1)}, bf16[4,96,768]{2,1,0:T(8,128)(2,1)S(1)}, u32[]{:S(2)}) copy-start(bf16[4,96,768]{2,1,0:T(8,128)(2,1)S(1)} %collective-permute-done.2.refs_1_) | copy-start | bytes 1769476
  67.1 16.4 %all-to-all-start.2 = ((f32[16,42,128]{2,1,0:T(8,128)}), f32[16,42,128]{2,1,0:T(8,128)S(1)}, u32[]{:S(2)}, u32[]{:S(2)}) async-start(f32[16,42,128]{2,1,0:T(8,128)} %reshape.49), calls=%async_computation.2 | async-start | bytes 786432 | tf_op jit(solution)/shard_map/all_to_all | solution.py:386
  83.5 15.5 %all-to-all-start.1 = ((bf16[4,96,768]{2,1,0:T(8,128)(2,1)}), bf16[4,96,768]{2,1,0:T(8,128)(2,1)S(1)}, u32[]{:S(2)}, u32[]{:S(2)}) async-start(bf16[4,96,768]{2,1,0:T(8,128)(2,1)} %reduce_sum.58), calls=%async_computation.1 | async-start | bytes 1179648 | tf_op jit(solution)/shard_map/all_to_all | solution.py:386
  89.5 7.6 %collective-permute-start.5 = (bf16[96,768]{1,0:T(8,128)(2,1)}, bf16[96,768]{1,0:T(8,128)(2,1)S(1)}, u32[]{:S(2)}, u32[]{:S(2)}) collective-permute-start(bf16[96,768]{1,0:T(8,128)(2,1)} %get-tuple-element.58), channel_id=1, source_target_pairs={{0,128},{128,2},{2,130},{130,0},{1,129},{129,3},{3,131},{131,1},{4... | collective-permute-start | bytes 442376 | tf_op jit(solution)/shard_map/ppermute | solution.py:299
  89.9 7.2 %collective-permute-start.6 = (bf16[96,768]{1,0:T(8,128)(2,1)}, bf16[96,768]{1,0:T(8,128)(2,1)S(1)}, u32[]{:S(2)}, u32[]{:S(2)}) collective-permute-start(bf16[96,768]{1,0:T(8,128)(2,1)} %get-tuple-element.59), channel_id=1, source_target_pairs={{0,2},{128,130},{2,0},{130,128},{1,3},{129,131},{3,1},{131,129},{4... | collective-permute-start | bytes 442376 | tf_op jit(solution)/shard_map/ppermute | solution.py:299
  91.4 6.6 %collective-permute-start.7 = (bf16[96,768]{1,0:T(8,128)(2,1)}, bf16[96,768]{1,0:T(8,128)(2,1)S(1)}, u32[]{:S(2)}, u32[]{:S(2)}) collective-permute-start(bf16[96,768]{1,0:T(8,128)(2,1)} %get-tuple-element.60), channel_id=1, source_target_pairs={{0,130},{128,0},{2,128},{130,2},{1,131},{129,1},{3,129},{131,3},{4... | collective-permute-start | bytes 442376 | tf_op jit(solution)/shard_map/ppermute | solution.py:299
  126.6 16.6 %all-to-all-start.4 = ((f32[16,42,128]{2,1,0:T(8,128)}), f32[16,42,128]{2,1,0:T(8,128)S(1)}, u32[]{:S(2)}, u32[]{:S(2)}) async-start(f32[16,42,128]{2,1,0:T(8,128)} %broadcast_in_dim.7), calls=%async_computation.4 | async-start | bytes 786432 | tf_op jit(solution)/shard_map/all_to_all | solution.py:386

commit v5 on v4

--- a/solution.py
+++ b/solution.py
@@ -11,7 +11,7 @@
 EDGE = 8
 VMEM_LIMIT = 60 * 1024 * 1024
 SMALL = pl.CostEstimate(flops=1000, bytes_accessed=1000, transcendentals=0)
-SMALL_ROWS = 56
+SMALL_ROWS = 64
 
 
 def front_kernel(
@@ -68,7 +68,7 @@
     gain = gain_ref[...].reshape(1, feat)
     shift = shift_ref[...].reshape(1, feat)
 
-    @pl.loop(0, side)
+    @pl.loop(0, side, unroll=4)
     def _(row):
         cells = pl.ds(pl.multiple_of(row * side, side), side)
         values = conv[cells, :]
@@ -164,78 +164,6 @@
     )(core, image, taps, bias, gain, shift, channel_order(rows, along_z), b_row, w_up, cot)
 
 
-def finish_rows(total, unit_ref, sigma_ref, gain_ref, conv_ref, gain_sum_ref, shift_sum_ref):
-    feat = total.shape[1]
-    gain = gain_ref[...].reshape(1, feat)
-
-    def body(row, carry):
-        gain_sum, shift_sum = carry
-        cells = pl.ds(pl.multiple_of(row * 8, 8), 8)
-        grad = total[cells, :]
-        unit = unit_ref[cells, :]
-        gain_sum = gain_sum + grad * unit
-        shift_sum = shift_sum + grad
-        unit_grad = grad * gain
-        first = jnp.sum(unit_grad, axis=-1, keepdims=True) * (1.0 / feat)
-        second = jnp.sum(unit_grad * unit, axis=-1, keepdims=True) * (1.0 / feat)
-        conv_ref[cells, :] = sigma_ref[cells, 0:1] * (unit_grad - first - unit * second)
-        return gain_sum, shift_sum
-
-    zero = jnp.zeros((8, feat), jnp.float32)
-    gain_sum, shift_sum = lax.fori_loop(0, total.shape[0] // 8, body, (zero, zero))
-    gain_sum_ref[...] = jnp.sum(gain_sum, axis=0, keepdims=True)
-    shift_sum_ref[...] = jnp.sum(shift_sum, axis=0, keepdims=True)
-
-
-def norm_grad_kernel(
-    core_ref, away_ref, near_ref, unit_ref, sigma_ref, gain_ref, w_hbm,
-    conv_ref, gain_sum_ref, shift_sum_ref, weights, total, sems,
-):
-    parts, feat, width = weights.shape
-    half = parts // 2
-    core = core_ref[0]
-    loads = []
-    for part in range(parts):
-        owner = 1 - core if part < half else core
-        columns = pl.ds(pl.multiple_of((owner * half + part % half) * width, width), width)
-        loads.append(pltpu.make_async_copy(w_hbm.at[:, columns], weights.at[part], sems.at[part]))
-        loads[-1].start()
-    for part in range(parts):
-        loads[part].wait()
-        grad_ref = away_ref if part < half else near_ref
-        grad = grad_ref[:, (part % half) * width : (part % half + 1) * width]
-        value = lax.dot_general(grad, weights[part], (((1,), (1,)), ((), ())), preferred_element_type=jnp.float32)
-        if part:
-            total[...] += value
-        else:
-            total[...] = value
-    finish_rows(total, unit_ref, sigma_ref, gain_ref, conv_ref, gain_sum_ref, shift_sum_ref)
-
-
-def norm_grad(core, away, near, w_up, unit, sigma, gain, parts=4):
-    cells, feat = unit.shape
-    width = w_up.shape[1] // parts
-    whole = pl.BlockSpec(memory_space=pltpu.VMEM)
-    return pl.pallas_call(
-        norm_grad_kernel,
-        name="norm_grad",
-        in_specs=[pl.BlockSpec(memory_space=pltpu.SMEM)] + [whole] * 5 + [pl.BlockSpec(memory_space=pl.ANY)],
-        out_specs=[whole] * 3,
-        out_shape=(
-            jax.ShapeDtypeStruct((cells, feat), jnp.float32),
-            jax.ShapeDtypeStruct((1, feat), jnp.float32),
-            jax.ShapeDtypeStruct((1, feat), jnp.float32),
-        ),
-        scratch_shapes=[
-            pltpu.VMEM((parts, feat, width), jnp.bfloat16),
-            pltpu.VMEM((cells, feat), jnp.float32),
-            pltpu.SemaphoreType.DMA((parts,)),
-        ],
-        compiler_params=pltpu.CompilerParams(vmem_limit_bytes=VMEM_LIMIT),
-        cost_estimate=SMALL,
-    )(core, away, near, unit, sigma, gain, w_up)
-
-
 def product_kernel(place_ref, near_t_ref, far_t_ref, near_ref, far_ref, *out_refs):
     _, along_y, rows, cells = near_t_ref.shape
     block = (
@@ -265,7 +193,7 @@
             grid=(4,),
             in_specs=[left, left, right, right],
             out_specs=[pl.BlockSpec((4, rows, columns), lambda i, p: (0, 0, 0))] * 4
-            + [pl.BlockSpec((4, 1, rows, others), lambda i, p: (0, lax.rem(p[0] + i, 4), 0, 0))],
+            + [pl.BlockSpec((4, 1, rows, others), lambda i, p: (0, i, 0, 0))],
         ),
         out_shape=[jax.ShapeDtypeStruct((4, rows, columns), jnp.bfloat16)] * 4
         + [jax.ShapeDtypeStruct((4, 4, rows, others), jnp.bfloat16)],
@@ -275,15 +203,20 @@
 
 
 def sum_kernel(*refs):
+    ins, outs = refs[:-4], refs[-4:]
     for index in range(4):
-        total = refs[0][index].astype(jnp.float32)
-        for ref in refs[1:4]:
-            total = total + ref[index].astype(jnp.float32)
-        refs[4 + index][...] = total.astype(jnp.bfloat16)
+        if len(ins) == 1:
+            parts = [ins[0][source, index] for source in range(4)]
+        else:
+            parts = [ref[index] for ref in ins]
+        total = parts[0].astype(jnp.float32)
+        for part in parts[1:]:
+            total = total + part.astype(jnp.float32)
+        outs[index][...] = total.astype(jnp.bfloat16)
 
 
 def sum_pieces(pieces):
-    _, rows, columns = pieces[0].shape
+    rows, columns = pieces[0].shape[-2:]
     return pl.pallas_call(
         sum_kernel,
         name="sum_pieces",
@@ -303,83 +236,168 @@
     return [pieces[0]] + moved
 
 
-def conv_grad_kernel(
-    grad_ref, image_ref, res_ref, taps_ref, gain_sum_ref, shift_sum_ref, up_first_ref, up_second_ref,
-    out_ref, sums_ref, padded, image,
+def back_kernel(
+    core_ref, away_ref, near_ref, sigma_ref, gain_ref, up_first_ref, up_second_ref, image_ref, res_ref, taps_ref,
+    unit_hbm, w_hbm, out_ref, sums_ref, weights, unit, total, norm_sums, padded, image, small, sems,
 ):
     side = image_ref.shape[1]
-    blank = jnp.zeros((side, EDGE, LANES), jnp.float32)
-    padded[:, 0:EDGE, :] = blank
-    padded[:, EDGE + side : EDGE + side + EDGE, :] = blank
+    feat = total.shape[1]
+
+    @pl.when(pl.program_id(0) == 0)
+    def _():
+        parts, _, width = weights.shape
+        half = parts // 2
+        core = core_ref[0]
+        loads = []
+        for part in range(parts):
+            owner = 1 - core if part < half else core
+            columns = pl.ds(pl.multiple_of((owner * half + part % half) * width, width), width)
+            loads.append(pltpu.make_async_copy(w_hbm.at[:, columns], weights.at[part], sems.at[part]))
+        loads.append(pltpu.make_async_copy(unit_hbm, unit, sems.at[parts]))
+        for load in loads:
+            load.start()
+        blank = jnp.zeros((side, EDGE, LANES), jnp.float32)
+        padded[:, 0:EDGE, :] = blank
+        padded[:, EDGE + side : EDGE + side + EDGE, :] = blank
+        for part in range(parts):
+            loads[part].wait()
+            grad_ref = away_ref if part < half else near_ref
+            grad = grad_ref[:, (part % half) * width : (part % half + 1) * width]
+            value = lax.dot_general(
+                grad, weights[part], (((1,), (1,)), ((), ())), preferred_element_type=jnp.float32
+            )
+            if part:
+                total[...] += value
+            else:
+                total[...] = value
+        loads[parts].wait()
+        gain = gain_ref[...].reshape(1, feat)
+
+        def finish(row, carry):
+            gain_sum, shift_sum = carry
+            cells = pl.ds(pl.multiple_of(row * 32, 32), 32)
+            grad = total[cells, :]
+            scaled = unit[cells, :]
+            gain_sum = gain_sum + jnp.sum((grad * scaled).reshape(4, 8, feat), axis=0)
+            shift_sum = shift_sum + jnp.sum(grad.reshape(4, 8, feat), axis=0)
+            unit_grad = grad * gain
+            first = jnp.sum(unit_grad, axis=-1, keepdims=True) * (1.0 / feat)
+            second = jnp.sum(unit_grad * scaled, axis=-1, keepdims=True) * (1.0 / feat)
+            total[cells, :] = sigma_ref[cells, 0:1] * (unit_grad - first - scaled * second)
+            return gain_sum, shift_sum
+
+        zero = jnp.zeros((8, feat), jnp.float32)
+        gain_sum, shift_sum = lax.fori_loop(0, total.shape[0] // 32, finish, (zero, zero))
+        norm_sums[0:1, :] = jnp.sum(gain_sum, axis=0, keepdims=True)
+        norm_sums[1:2, :] = jnp.sum(shift_sum, axis=0, keepdims=True)
+
+    lanes = pl.ds(pl.multiple_of(pl.program_id(0) * LANES, LANES), LANES)
     image[...] = image_ref[0].astype(jnp.float32)
     bias_sum = jnp.zeros((side, LANES), jnp.float32)
     for row in range(side):
-        cells = grad_ref[row * side : (row + 1) * side, :]
+        cells = total[row * side : (row + 1) * side, lanes]
         padded[row, EDGE : EDGE + side, :] = cells
         bias_sum = bias_sum + cells
-    sums_ref[49:50, :] = gain_sum_ref[...]
-    sums_ref[50:51, :] = shift_sum_ref[...]
-    sums_ref[51:52, :] = jnp.sum(bias_sum, axis=0, keepdims=True)
-    sums_ref[52:53, :] = up_first_ref[...]
-    sums_ref[53:54, :] = up_second_ref[...]
-    sums_ref[54:, :] = jnp.zeros((SMALL_ROWS - 54, LANES), jnp.float32)
+    tap_sums = [None] * 49
     sums = [res_ref[0, row].astype(jnp.float32) for row in range(side)]
     for turn_col in range(7):
-        weights = [
-            jnp.broadcast_to(
-                taps_ref[pl.ds(7 * (6 - turn_row) + 6 - turn_col, 1), :], (side, LANES)
-            )
+        weights_here = [
+            jnp.broadcast_to(taps_ref[pl.ds(7 * (6 - turn_row) + 6 - turn_col, 1), :], (side, LANES))
             for turn_row in range(7)
         ]
-        parts = [jnp.zeros((8, LANES), jnp.float32) for _ in range(7)]
+        parts_here = [jnp.zeros((8, LANES), jnp.float32) for _ in range(7)]
         for source in range(side):
             cells = padded[source, EDGE - 3 + turn_col : EDGE - 3 + turn_col + side, :]
             for turn_row in range(7):
                 target = source + 3 - turn_row
                 if 0 <= target < side:
-                    sums[target] = sums[target] + cells * weights[turn_row]
+                    sums[target] = sums[target] + cells * weights_here[turn_row]
                     product = cells * image[target]
-                    parts[turn_row] = parts[turn_row] + (product[:8] + product[8:])
+                    parts_here[turn_row] = parts_here[turn_row] + (product[:8] + product[8:])
         for turn_row in range(7):
             tap = 7 * (6 - turn_row) + 6 - turn_col
-            sums_ref[tap : tap + 1, :] = jnp.sum(parts[turn_row], axis=0, keepdims=True)
+            small[tap : tap + 1, :] = jnp.sum(parts_here[turn_row], axis=0, keepdims=True)
+    small[49:51, :] = norm_sums[0:2, lanes]
+    small[51:52, :] = jnp.sum(bias_sum, axis=0, keepdims=True)
+    small[52:53, :] = up_first_ref[...]
+    small[53:54, :] = up_second_ref[...]
+    small[54:, :] = jnp.zeros((SMALL_ROWS - 54, LANES), jnp.float32)
+    sums_ref[0] = small[...].astype(jnp.bfloat16)
     for row in range(side):
         out_ref[0, row] = sums[row].astype(jnp.bfloat16)
 
 
-def conv_backward(grad, image, residual, taps, gain_sum, shift_sum, up_sums):
-    side, feat = image.shape[1], image.shape[3]
-    cells = side * side
+def back(core, away, near, w_up, unit, sigma, gain, up_sums, image, residual, taps, parts=4):
+    cells, feat = unit.shape
+    side = image.shape[1]
+    width = w_up.shape[1] // parts
+    whole = pl.BlockSpec(memory_space=pltpu.VMEM)
+    remain = pl.BlockSpec(memory_space=pl.ANY)
     picture = pl.BlockSpec((1, side, side, LANES), lambda i: (0, 0, 0, i))
     return pl.pallas_call(
-        conv_grad_kernel,
-        name="conv_backward",
+        back_kernel,
+        name="back",
         grid=(feat // LANES,),
-        in_specs=[
-            pl.BlockSpec((cells, LANES), lambda i: (0, i)),
+        in_specs=[pl.BlockSpec(memory_space=pltpu.SMEM)]
+        + [whole] * 4
+        + [
+            pl.BlockSpec((1, LANES), lambda i: (0, i)),
+            pl.BlockSpec((1, LANES), lambda i: (0, i + feat // LANES)),
             picture,
             picture,
             pl.BlockSpec((49, LANES), lambda i: (0, i)),
-            pl.BlockSpec((1, LANES), lambda i: (0, i)),
-            pl.BlockSpec((1, LANES), lambda i: (0, i)),
-            pl.BlockSpec((1, LANES), lambda i: (0, i)),
-            pl.BlockSpec((1, LANES), lambda i: (0, i + feat // LANES)),
+            remain,
+            remain,
         ],
-        out_specs=[
-            picture,
-            pl.BlockSpec((SMALL_ROWS, LANES), lambda i: (0, i)),
-        ],
+        out_specs=[picture, pl.BlockSpec((1, SMALL_ROWS, LANES), lambda i: (i, 0, 0))],
         out_shape=(
             jax.ShapeDtypeStruct(image.shape, jnp.bfloat16),
-            jax.ShapeDtypeStruct((SMALL_ROWS, feat), jnp.float32),
+            jax.ShapeDtypeStruct((feat // LANES, SMALL_ROWS, LANES), jnp.bfloat16),
         ),
         scratch_shapes=[
+            pltpu.VMEM((parts, feat, width), jnp.bfloat16),
+            pltpu.VMEM((cells, feat), jnp.float32),
+            pltpu.VMEM((cells, feat), jnp.float32),
+            pltpu.VMEM((8, feat), jnp.float32),
             pltpu.VMEM((side, side + 2 * EDGE, LANES), jnp.float32),
             pltpu.VMEM((side, side, LANES), jnp.float32),
+            pltpu.VMEM((SMALL_ROWS, LANES), jnp.float32),
+            pltpu.SemaphoreType.DMA((1 + parts,)),
         ],
         compiler_params=pltpu.CompilerParams(vmem_limit_bytes=VMEM_LIMIT),
         cost_estimate=SMALL,
-    )(grad, image, residual, taps, gain_sum, shift_sum, up_sums, up_sums)
+    )(core, away, near, sigma, gain, up_sums, up_sums, image, residual, taps, unit, w_up)
+
+
+def unpack_kernel(small_ref, up_ref, gain_ref, shift_ref, taps_ref, bias_ref):
+    blocks = small_ref.shape[0]
+    for block in range(blocks):
+        values = small_ref[block].astype(jnp.float32)
+        lanes = slice(block * LANES, (block + 1) * LANES)
+        taps_ref[:, lanes] = values[:49]
+        gain_ref[lanes] = values[49]
+        shift_ref[lanes] = values[50]
+        bias_ref[lanes] = values[51]
+        up_ref[lanes] = values[52]
+        up_ref[blocks * LANES + block * LANES : blocks * LANES + (block + 1) * LANES] = values[53]
+
+
+def unpack(small):
+    feat = small.shape[0] * LANES
+    row = jax.ShapeDtypeStruct((feat,), jnp.float32)
+    return pl.pallas_call(
+        unpack_kernel,
+        name="unpack",
+        out_shape=(
+            jax.ShapeDtypeStruct((2 * feat,), jnp.float32),
+            row,
+            row,
+            jax.ShapeDtypeStruct((49, feat), jnp.float32),
+            row,
+        ),
+        compiler_params=pltpu.CompilerParams(vmem_limit_bytes=VMEM_LIMIT),
+        cost_estimate=SMALL,
+    )(small)
 
 
 def swap_pieces(values, axes):
@@ -414,33 +432,25 @@
     part_a = to_owners(part_a, "x")
     part_b = swap_pieces(part_b, ("y_hi", "y_lo"))
 
-    conv_grad, gain_sum, shift_sum = norm_grad(mine, away, near, w_up, unit, sigma, ln_gain)
-    grad_input, small = conv_backward(
-        conv_grad, images, residual_cot, dw_weight, gain_sum, shift_sum, up_sums
+    grad_input, small = back(
+        mine, away, near, w_up, unit, sigma, ln_gain, up_sums, images, residual_cot, dw_weight
     )
     part_a, part_b, small = lax.optimization_barrier((part_a, part_b, small))
+    small = total_of(swap_pieces(small.reshape(16, -1, LANES), plane)).astype(jnp.bfloat16)
     part_a = to_owners(sum_pieces(part_a), ("y_lo", "y_hi"))
-    part_b = swap_pieces(total_of(part_b).astype(jnp.bfloat16), "x")
-    small = total_of(swap_pieces(small.reshape(16, -1, LANES), plane)).astype(jnp.bfloat16)
-
-    last = jnp.concatenate([total_of(jnp.stack(part_a)), total_of(part_b)], axis=1).astype(jnp.bfloat16)
-    last = last.reshape(2 * along_z, -1, LANES)
+    part_b = to_owners(sum_pieces([part_b]), "x")
+
+    last = jnp.concatenate([total_of(jnp.stack(part_a)), total_of(jnp.stack(part_b))], axis=1)
+    last = last.astype(jnp.bfloat16).reshape(2 * along_z, -1, LANES)
     height = last.shape[1]
     small = jnp.broadcast_to(small, (2 * along_z,) + small.shape)
     last = swap_pieces(jnp.concatenate([last, small], axis=1), ("z", "core"))
-    small = total_of(last[:, height:]) * inverse_count
-    small = swap_pieces(jnp.broadcast_to(small, (16,) + small.shape), plane).reshape(SMALL_ROWS, feat)
+    small = (total_of(last[:, height:]) * inverse_count).astype(jnp.bfloat16)
+    small = swap_pieces(jnp.broadcast_to(small, (16,) + small.shape), plane)
+    small = small.reshape(-1, SMALL_ROWS, LANES)
     last = total_of(last[:, :height].reshape(along_z, 2, owned_rows, hid // 2))
     owned = last.transpose(1, 0, 2).reshape(owned_rows, hid) * inverse_count
-    return (
-        grad_input,
-        owned,
-        small[52:54].reshape(hid),
-        small[49],
-        small[50],
-        small[:49],
-        small[51],
-    )
+    return (grad_input, owned, *unpack(small))
 
 
 def solution(mesh):

time: 146 us -> 134 us (0.918)
  waiting for transfers between devices: 25.7 us -> 20 us
  local copies, waits for them, and re-layouts: 6.13 us -> 2.75 us
  Pallas kernels: 51.6 us -> 49.1 us
    all_to_all x4 -> x3, waiting for transfers between devices: 16.9 us -> 6.84 us  [swap_pieces(): return lax.all_to_all(values, axes, 0, 0, tiled=True)]
    ppermute x6 -> x9, starting transfers between devices: 6.63 us -> 13.4 us  [to_owners(): lax.ppermute(piece, axes, [(named[i], named[(i + d) % 4]) for i in range(...]
    all_to_all x4 -> x3, starting transfers between devices: 21.3 us -> 14.6 us  [swap_pieces(): return lax.all_to_all(values, axes, 0, 0, tiled=True)]
    ppermute x6 -> x9, waiting for transfers between devices: 6.15 us -> 10.6 us  [to_owners(): lax.ppermute(piece, axes, [(named[i], named[(i + d) % 4]) for i in range(...]
    pallas_call x2, Pallas kernels: 24.7 us -> 20.9 us  [the longest x1 19.2 us: back(): pl.pallas_call(back_kernel, name='back', grid=(feat // LANES,), in_specs=...]
    pallas_call x1 -> x2, Pallas kernels: 2.55 us -> 6.04 us  [sum_pieces(): pl.pallas_call(sum_kernel, name='sum_pieces', out_shape=[jax.ShapeDtypeSt...]
    reshape x3 -> x0, local copies, waits for them, and re-layouts: 2.49 us -> none  [the longest x1 1.81 us: per_device(): small.reshape(16, -1, LANES)]
    pallas_call x1, Pallas kernels: 16.4 us -> 14.3 us  [front(): pl.pallas_call(front_kernel, name='front', in_specs=[pl.BlockSpec(memory_...]
  transfers between devices with their start and end apart: 12 -> 14, of which waited for: 7 -> 8; matrix products, arithmetic and copies ran while one was open for 2% -> 2% of each run, Pallas kernels for 19% -> 16%
where the time goes in v5:
time: 134 us; the launch traced here: 133 us
  Pallas kernels  49.1 us (37%)
  starting transfers between devices  31.5 us (24%)
  blocking collectives  26.4 us (20%)
  waiting for transfers between devices  20 us (15%)
  local copies, waits for them, and re-layouts  2.75 us (2%)
  other arithmetic  2.45 us (2%)
    all_to_all x1, blocking collectives, swap_pieces(): return lax.all_to_all(values, axes, 0, 0, tiled=True)  26.4 us
    pallas_call x1, Pallas kernels, back(): pl.pallas_call(back_kernel, name='back', grid=(feat // LANES,), in_specs=...  19.2 us
    all_to_all x3, starting transfers between devices, swap_pieces(): return lax.all_to_all(values, axes, 0, 0, tiled=True)  14.6 us
    pallas_call x1, Pallas kernels, front(): pl.pallas_call(front_kernel, name='front', in_specs=[pl.BlockSpec(memory_...  14.3 us
    ppermute x9, starting transfers between devices, to_owners(): lax.ppermute(piece, axes, [(named[i], named[(i + d) % 4]) for i in range(...  13.4 us
    ppermute x9, waiting for transfers between devices, to_owners(): lax.ppermute(piece, axes, [(named[i], named[(i + d) % 4]) for i in range(...  10.6 us
    pallas_call x1, Pallas kernels, product(): pl.pallas_call(product_kernel, name='product', grid_spec=pltpu.PrefetchSc...  7.87 us
    all_to_all x3, waiting for transfers between devices, swap_pieces(): return lax.all_to_all(values, axes, 0, 0, tiled=True)  6.84 us
  transfers between devices with their start and end apart: 14, of which 8 were waited for; matrix products, arithmetic and copies ran while one was open for 2% of the time, Pallas kernels for 16%

profile of v5, /device:TPU:1, one launch (start us, length us, event | category | flops | bytes accessed | tf_op | source)
XLA Modules:
  0.0 132.9 jit_solution(14868108486774106300)
XLA Ops:
  0.6 14.3 %front.1 = (f32[256,1536]{1,0:T(8,128)}, f32[256,128]{1,0:T(8,128)}, bf16[4,2,2,96,256]{4,3,2,1,0:T(8,128)(2,1)}, bf16[256,1536]{1,0:T(8,128)(2,1)}, bf16[256,1536]{1,0:T(8,128)(2,1)}, /*index=5*/f32[1,3072]{1,0:T(1,128)}) custom-call(s32[1]{0:T(128)} %bitcast.core_ref, bf16[1,16,16,1536]{3,2,1,0:T(8,128)(2,1)} %image_ref.3, f32[49,1536]{1,0:T(8,128)} %taps_ref.3, ...), custom_call_target="tpu_custom_call" | custom-call | flops 1000 | bytes 1000 | tf_op jit(solution)/shard_map/front/pallas_call | solution.py:138
  14.9 3.3 %collective-permute-start.1 = (bf16[256,1536]{1,0:T(8,128)(2,1)}, bf16[256,1536]{1,0:T(8,128)(2,1)S(1)}, u32[]{:S(2)}, u32[]{:S(2)}) collective-permute-start(bf16[256,1536]{1,0:T(8,128)(2,1)} %get-tuple-element.41.away_ref), channel_id=1, source_target_pairs={{0,1},{1,0},{2,3},{3,2},{4,5},{5,4},{6,7},{7,6},{8,9},{9,8},{10,11... | collective-permute-start | bytes 2359304 | tf_op jit(solution)/shard_map/ppermute | solution.py:425
  18.2 0.1 collective-permute-start
  18.3 0.6 pad_add_fusion.place_ref
  18.9 1.4 %collective-permute-done.1.far_ref = bf16[256,1536]{1,0:T(8,128)(2,1)S(1)} collective-permute-done((bf16[256,1536]{1,0:T(8,128)(2,1)}, bf16[256,1536]{1,0:T(8,128)(2,1)S(1)}, u32[]{:S(2)}, u32[]{:S(2)}) %collective-permute-start.1) | collective-permute-done | bytes 786464 | tf_op jit(solution)/shard_map/ppermute | solution.py:425
  20.4 0.0 copy-start.2
  20.4 1.1 collective-permute-done
  21.5 0.0 copy-start.3
  21.5 0.0 copy-done.2
  21.5 0.9 copy-done.3
  22.4 7.9 %product.1 = (bf16[4,96,768]{2,1,0:T(8,128)(2,1)}, bf16[4,96,768]{2,1,0:T(8,128)(2,1)}, bf16[4,96,768]{2,1,0:T(8,128)(2,1)}, bf16[4,96,768]{2,1,0:T(8,128)(2,1)}, bf16[4,4,96,768]{3,2,1,0:T(8,128)(2,1)}) custom-call(s32[2]{0:T(128)} %pad_add_fusion.place_ref, bf16[4,4,96,256]{3,2,1,0:T(8,128)(2,1)} %bitcast.12, bf16[4,4,96,256]{3,2,1,0:T(8,128)(2,1)} %bitcast.13, ...), custom_call_target="tpu_custom_call" | custom-call | flops 1000 | bytes 1000 | tf_op jit(solution)/shard_map/product/pallas_call | solution.py:188
  30.2 3.6 %all-to-all-start = ((bf16[4,4,96,768]{3,2,1,0:T(8,128)(2,1)}), bf16[4,4,96,768]{3,2,1,0:T(8,128)(2,1)S(1)}, u32[]{:S(2)}, u32[]{:S(2)}) async-start(bf16[4,4,96,768]{3,2,1,0:T(8,128)(2,1)} %get-tuple-element.54), calls=%async_computation | async-start | bytes 4718592 | tf_op jit(solution)/shard_map/all_to_all | solution.py:404
  33.9 0.1 collective-permute-start.2
  34.0 2.4 %collective-permute-start.3 = (bf16[4,96,768]{2,1,0:T(8,128)(2,1)}, bf16[4,96,768]{2,1,0:T(8,128)(2,1)S(1)}, u32[]{:S(2)}, u32[]{:S(2)}) collective-permute-start(bf16[4,96,768]{2,1,0:T(8,128)(2,1)} %get-tuple-element.52), channel_id=1, source_target_pairs={{0,64},{32,96},{64,0},{96,32},{1,65},{33,97},{65,1},{97,33},{2,66}... | collective-permute-start | bytes 1769480 | tf_op jit(solution)/shard_map/ppermute | solution.py:232
  36.4 1.1 collective-permute-start.4
  37.5 19.2 %back.1 = (bf16[1,16,16,1536]{3,2,1,0:T(8,128)(2,1)}, bf16[12,64,128]{2,1,0:T(8,128)(2,1)}) custom-call(s32[1]{0:T(128)} %bitcast.core_ref, bf16[256,1536]{1,0:T(8,128)(2,1)} %get-tuple-element.41.away_ref, bf16[256,1536]{1,0:T(8,128)(2,1)} %get-tuple-element.42.near_ref, f32[256,128]{1,0:T(8,128)} %get-tuple-element.43.sigma_ref, f32[1536]{0:T(1024)} %gain_ref.3, ...), custom_call_target="tpu_custom_call" | custom-call | flops 1000 | bytes 1000 | tf_op jit(solution)/shard_map/back/pallas_call | solution.py:337
  56.7 0.0 collective-permute-done.2.refs_1_
  56.7 0.0 copy-start.4
  56.8 5.3 %collective-permute-done.3.refs_2_ = bf16[4,96,768]{2,1,0:T(8,128)(2,1)S(1)} collective-permute-done((bf16[4,96,768]{2,1,0:T(8,128)(2,1)}, bf16[4,96,768]{2,1,0:T(8,128)(2,1)S(1)}, u32[]{:S(2)}, u32[]{:S(2)}) %collective-permute-start.3) | collective-permute-done | bytes 589856 | tf_op jit(solution)/shard_map/ppermute | solution.py:232
  62.0 0.0 copy-start.5
  62.0 0.9 collective-permute-done.4.refs_3_
  63.0 0.0 all-to-all-done.refs_0_
  63.0 0.0 copy-start
  63.0 0.0 copy-done.4
  63.0 0.0 copy-done.5
  63.0 3.4 %sum_pieces.2 = (bf16[96,768]{1,0:T(8,128)(2,1)}, bf16[96,768]{1,0:T(8,128)(2,1)}, bf16[96,768]{1,0:T(8,128)(2,1)}, bf16[96,768]{1,0:T(8,128)(2,1)}) custom-call(bf16[4,96,768]{2,1,0:T(8,128)(2,1)} %get-tuple-element.56.refs_0_, bf16[4,96,768]{2,1,0:T(8,128)(2,1)} %copy-done.4, bf16[4,96,768]{2,1,0:T(8,128)(2,1)} %copy-done.5, ...), custom_call_target="tpu_custom_call" | custom-call | flops 1000 | bytes 1000 | tf_op jit(solution)/shard_map/sum_pieces/pallas_call | solution.py:220
  66.4 0.0 copy-start.6
  66.4 1.3 collective-permute-start.5
  67.7 2.4 %collective-permute-start.6 = (bf16[96,768]{1,0:T(8,128)(2,1)}, bf16[96,768]{1,0:T(8,128)(2,1)S(1)}, u32[]{:S(2)}, u32[]{:S(2)}) collective-permute-start(bf16[96,768]{1,0:T(8,128)(2,1)} %get-tuple-element.62), channel_id=1, source_target_pairs={{0,2},{128,130},{2,0},{130,128},{1,3},{129,131},{3,1},{131,129},{4... | collective-permute-start | bytes 442376 | tf_op jit(solution)/shard_map/ppermute | solution.py:232
  70.1 1.2 collective-permute-start.7
  71.3 4.8 %all-to-all-start.1 = ((bf16[16,48,128]{2,1,0:T(8,128)(2,1)}), bf16[16,48,128]{2,1,0:T(8,128)(2,1)S(1)}, u32[]{:S(2)}, u32[]{:S(2)}) async-start(bf16[16,48,128]{2,1,0:T(8,128)(2,1)} %bitcast.14), calls=%async_computation.1 | async-start | bytes 393216 | tf_op jit(solution)/shard_map/all_to_all | solution.py:404
  76.1 0.0 copy-done
  76.1 2.6 %sum_pieces.3 = (bf16[96,768]{1,0:T(8,128)(2,1)}, bf16[96,768]{1,0:T(8,128)(2,1)}, bf16[96,768]{1,0:T(8,128)(2,1)}, bf16[96,768]{1,0:T(8,128)(2,1)}) custom-call(bf16[4,4,96,768]{3,2,1,0:T(8,128)(2,1)} %copy-done), custom_call_target="tpu_custom_call" | custom-call | flops 1000 | bytes 1000 | tf_op jit(solution)/shard_map/sum_pieces/pallas_call | solution.py:220
  78.7 1.4 %collective-permute-start.8 = (bf16[96,768]{1,0:T(8,128)(2,1)}, bf16[96,768]{1,0:T(8,128)(2,1)S(1)}, u32[]{:S(2)}, u32[]{:S(2)}) collective-permute-start(bf16[96,768]{1,0:T(8,128)(2,1)} %get-tuple-element.66), channel_id=1, source_target_pairs={{0,32},{32,64},{64,96},{96,0},{1,33},{33,65},{65,97},{97,1},{2,34}... | collective-permute-start | bytes 442376 | tf_op jit(solution)/shard_map/ppermute | solution.py:232
  80.1 2.4 %collective-permute-start.9 = (bf16[96,768]{1,0:T(8,128)(2,1)}, bf16[96,768]{1,0:T(8,128)(2,1)S(1)}, u32[]{:S(2)}, u32[]{:S(2)}) collective-permute-start(bf16[96,768]{1,0:T(8,128)(2,1)} %get-tuple-element.67), channel_id=1, source_target_pairs={{0,64},{32,96},{64,0},{96,32},{1,65},{33,97},{65,1},{97,33},{2,66}... | collective-permute-start | bytes 442376 | tf_op jit(solution)/shard_map/ppermute | solution.py:232
  82.5 0.0 collective-permute-done.5
  82.5 1.2 collective-permute-start.10
  83.7 0.0 collective-permute-done.6
  83.7 0.0 collective-permute-done.7
  83.7 0.0 copy-done.6
  83.7 1.1 collective-permute-done.8
  84.9 2.7 %collective-permute-done.9 = bf16[96,768]{1,0:T(8,128)(2,1)S(1)} collective-permute-done((bf16[96,768]{1,0:T(8,128)(2,1)}, bf16[96,768]{1,0:T(8,128)(2,1)S(1)}, u32[]{:S(2)}, u32[]{:S(2)}) %collective-permute-start.9) | collective-permute-done | bytes 147488 | tf_op jit(solution)/shard_map/ppermute | solution.py:232
  87.6 0.5 collective-permute-done.10
  88.1 0.9 add_add_fusion
  89.1 0.4 convert_element_type.27
  89.4 0.0 all-to-all-done.1
  89.6 26.4 %all_to_all.20 = bf16[16,120,128]{2,1,0:T(8,128)(2,1)S(1)} all-to-all(bf16[16,120,128]{2,1,0:T(8,128)(2,1)S(1)} %pad_maximum_fusion), channel_id=1, replica_groups=mesh['y_lo'=2,'x'=4,'z'=8,'y_hi'=2,'core'=2] {'z','core'}, dimensions={0} | all-to-all | bytes 983040 | tf_op jit(solution)/shard_map/all_to_all | solution.py:404
  116.0 0.7 broadcast_in_dim.7
  116.7 6.2 %all-to-all-start.3 = ((bf16[16,48,128]{2,1,0:T(8,128)(2,1)}), bf16[16,48,128]{2,1,0:T(8,128)(2,1)S(1)}, u32[]{:S(2)}, u32[]{:S(2)}) async-start(bf16[16,48,128]{2,1,0:T(8,128)(2,1)} %broadcast_in_dim.7), calls=%async_computation.3 | async-start | bytes 393216 | tf_op jit(solution)/shard_map/all_to_all | solution.py:404
  122.9 0.1 reshape.47
  123.0 0.1 reduce_sum.51
  123.1 0.7 broadcast_multiply_fusion
  123.8 6.8 %all-to-all-done.3 = bf16[16,48,128]{2,1,0:T(8,128)(2,1)S(1)} async-done(((bf16[16,48,128]{2,1,0:T(8,128)(2,1)}), bf16[16,48,128]{2,1,0:T(8,128)(2,1)S(1)}, u32[]{:S(2)}, u32[]{:S(2)}) %all-to-all-start.3) | async-done | bytes 196640 | tf_op jit(solution)/shard_map/all_to_all | solution.py:404
  130.6 0.0 copy-start.1
  130.6 0.7 copy-done.1
  131.3 1.7 %unpack.1 = (f32[3072]{0:T(1024)}, f32[1536]{0:T(1024)}, f32[1536]{0:T(1024)}, f32[49,1536]{1,0:T(8,128)}, f32[1536]{0:T(1024)}) custom-call(bf16[12,64,128]{2,1,0:T(8,128)(2,1)} %bitcast.11), custom_call_target="tpu_custom_call" | custom-call | flops 1000 | bytes 1000 | tf_op jit(solution)/shard_map/unpack/pallas_call | solution.py:388
  (8 shorter events, 0.2 us)
Async XLA Ops:
  14.9 5.4 %collective-permute-start.1 = (bf16[256,1536]{1,0:T(8,128)(2,1)}, bf16[256,1536]{1,0:T(8,128)(2,1)S(1)}, u32[]{:S(2)}, u32[]{:S(2)}) collective-permute-start(bf16[256,1536]{1,0:T(8,128)(2,1)} %get-tuple-element.41.away_ref), channel_id=1, source_target_pairs={{0,1},{1,0},{2,3},{3,2},{4,5},{5,4},{6,7},{7,6},{8,9},{9,8},{10,11... | collective-permute-start | bytes 2359304 | tf_op jit(solution)/shard_map/ppermute | solution.py:425
  18.2 3.2 %collective-permute-start = (bf16[4,2,2,96,256]{4,3,2,1,0:T(8,128)(2,1)}, bf16[4,2,2,96,256]{4,3,2,1,0:T(8,128)(2,1)S(1)}, u32[]{:S(2)}, u32[]{:S(2)}) collective-permute-start(bf16[4,2,2,96,256]{4,3,2,1,0:T(8,128)(2,1)} %get-tuple-element.45), channel_id=1, source_target_pairs={{0,1},{1,0},{2,3},{3,2},{4,5},{5,4},{6,7},{7,6},{8,9},{9,8},{10,11... | collective-permute-start | bytes 2359304 | tf_op jit(solution)/shard_map/ppermute | solution.py:426
  20.4 1.1 copy-start.2
  21.5 0.9 copy-start.3
  30.2 32.7 %all-to-all-start = ((bf16[4,4,96,768]{3,2,1,0:T(8,128)(2,1)}), bf16[4,4,96,768]{3,2,1,0:T(8,128)(2,1)S(1)}, u32[]{:S(2)}, u32[]{:S(2)}) async-start(bf16[4,4,96,768]{3,2,1,0:T(8,128)(2,1)} %get-tuple-element.54), calls=%async_computation | async-start | bytes 4718592 | tf_op jit(solution)/shard_map/all_to_all | solution.py:404
  33.9 22.9 %collective-permute-start.2 = (bf16[4,96,768]{2,1,0:T(8,128)(2,1)}, bf16[4,96,768]{2,1,0:T(8,128)(2,1)S(1)}, u32[]{:S(2)}, u32[]{:S(2)}) collective-permute-start(bf16[4,96,768]{2,1,0:T(8,128)(2,1)} %get-tuple-element.51), channel_id=1, source_target_pairs={{0,32},{32,64},{64,96},{96,0},{1,33},{33,65},{65,97},{97,1},{2,34}... | collective-permute-start | bytes 1769480 | tf_op jit(solution)/shard_map/ppermute | solution.py:232
  34.0 28.0 %collective-permute-start.3 = (bf16[4,96,768]{2,1,0:T(8,128)(2,1)}, bf16[4,96,768]{2,1,0:T(8,128)(2,1)S(1)}, u32[]{:S(2)}, u32[]{:S(2)}) collective-permute-start(bf16[4,96,768]{2,1,0:T(8,128)(2,1)} %get-tuple-element.52), channel_id=1, source_target_pairs={{0,64},{32,96},{64,0},{96,32},{1,65},{33,97},{65,1},{97,33},{2,66}... | collective-permute-start | bytes 1769480 | tf_op jit(solution)/shard_map/ppermute | solution.py:232
  36.4 26.6 %collective-permute-start.4 = (bf16[4,96,768]{2,1,0:T(8,128)(2,1)}, bf16[4,96,768]{2,1,0:T(8,128)(2,1)}, u32[]{:S(2)}, u32[]{:S(2)}) collective-permute-start(bf16[4,96,768]{2,1,0:T(8,128)(2,1)} %get-tuple-element.53), channel_id=1, source_target_pairs={{0,96},{32,0},{64,32},{96,64},{1,97},{33,1},{65,33},{97,65},{2,98}... | collective-permute-start | bytes 1769480 | tf_op jit(solution)/shard_map/ppermute | solution.py:232
  56.7 6.2 %copy-start.4 = (bf16[4,96,768]{2,1,0:T(8,128)(2,1)}, bf16[4,96,768]{2,1,0:T(8,128)(2,1)S(1)}, u32[]{:S(2)}) copy-start(bf16[4,96,768]{2,1,0:T(8,128)(2,1)S(1)} %collective-permute-done.2.refs_1_) | copy-start | bytes 1769476
  62.0 1.0 copy-start.5
  63.0 13.1 %copy-start = (bf16[4,4,96,768]{3,2,1,0:T(8,128)(2,1)}, bf16[4,4,96,768]{3,2,1,0:T(8,128)(2,1)S(1)}, u32[]{:S(2)}) copy-start(bf16[4,4,96,768]{3,2,1,0:T(8,128)(2,1)S(1)} %all-to-all-done.refs_0_) | copy-start | bytes 7077892
  66.4 17.3 %copy-start.6 = (bf16[96,768]{1,0:T(8,128)(2,1)S(1)}, bf16[96,768]{1,0:T(8,128)(2,1)}, u32[]{:S(2)}) copy-start(bf16[96,768]{1,0:T(8,128)(2,1)} %get-tuple-element.60) | copy-start | bytes 442372
  66.4 16.1 %collective-permute-start.5 = (bf16[96,768]{1,0:T(8,128)(2,1)}, bf16[96,768]{1,0:T(8,128)(2,1)S(1)}, u32[]{:S(2)}, u32[]{:S(2)}) collective-permute-start(bf16[96,768]{1,0:T(8,128)(2,1)} %get-tuple-element.61), channel_id=1, source_target_pairs={{0,128},{128,2},{2,130},{130,0},{1,129},{129,3},{3,131},{131,1},{4... | collective-permute-start | bytes 442376 | tf_op jit(solution)/shard_map/ppermute | solution.py:232
  67.7 16.0 %collective-permute-start.6 = (bf16[96,768]{1,0:T(8,128)(2,1)}, bf16[96,768]{1,0:T(8,128)(2,1)S(1)}, u32[]{:S(2)}, u32[]{:S(2)}) collective-permute-start(bf16[96,768]{1,0:T(8,128)(2,1)} %get-tuple-element.62), channel_id=1, source_target_pairs={{0,2},{128,130},{2,0},{130,128},{1,3},{129,131},{3,1},{131,129},{4... | collective-permute-start | bytes 442376 | tf_op jit(solution)/shard_map/ppermute | solution.py:232
  70.1 13.6 %collective-permute-start.7 = (bf16[96,768]{1,0:T(8,128)(2,1)}, bf16[96,768]{1,0:T(8,128)(2,1)S(1)}, u32[]{:S(2)}, u32[]{:S(2)}) collective-permute-start(bf16[96,768]{1,0:T(8,128)(2,1)} %get-tuple-element.63), channel_id=1, source_target_pairs={{0,130},{128,0},{2,128},{130,2},{1,131},{129,1},{3,129},{131,3},{4... | collective-permute-start | bytes 442376 | tf_op jit(solution)/shard_map/ppermute | solution.py:232
  71.3 18.1 %all-to-all-start.1 = ((bf16[16,48,128]{2,1,0:T(8,128)(2,1)}), bf16[16,48,128]{2,1,0:T(8,128)(2,1)S(1)}, u32[]{:S(2)}, u32[]{:S(2)}) async-start(bf16[16,48,128]{2,1,0:T(8,128)(2,1)} %bitcast.14), calls=%async_computation.1 | async-start | bytes 393216 | tf_op jit(solution)/shard_map/all_to_all | solution.py:404
  78.7 6.1 %collective-permute-start.8 = (bf16[96,768]{1,0:T(8,128)(2,1)}, bf16[96,768]{1,0:T(8,128)(2,1)S(1)}, u32[]{:S(2)}, u32[]{:S(2)}) collective-permute-start(bf16[96,768]{1,0:T(8,128)(2,1)} %get-tuple-element.66), channel_id=1, source_target_pairs={{0,32},{32,64},{64,96},{96,0},{1,33},{33,65},{65,97},{97,1},{2,34}... | collective-permute-start | bytes 442376 | tf_op jit(solution)/shard_map/ppermute | solution.py:232
  80.1 7.5 %collective-permute-start.9 = (bf16[96,768]{1,0:T(8,128)(2,1)}, bf16[96,768]{1,0:T(8,128)(2,1)S(1)}, u32[]{:S(2)}, u32[]{:S(2)}) collective-permute-start(bf16[96,768]{1,0:T(8,128)(2,1)} %get-tuple-element.67), channel_id=1, source_target_pairs={{0,64},{32,96},{64,0},{96,32},{1,65},{33,97},{65,1},{97,33},{2,66}... | collective-permute-start | bytes 442376 | tf_op jit(solution)/shard_map/ppermute | solution.py:232
  82.5 5.6 %collective-permute-start.10 = (bf16[96,768]{1,0:T(8,128)(2,1)}, bf16[96,768]{1,0:T(8,128)(2,1)S(1)}, u32[]{:S(2)}, u32[]{:S(2)}) collective-permute-start(bf16[96,768]{1,0:T(8,128)(2,1)} %get-tuple-element.68), channel_id=1, source_target_pairs={{0,96},{32,0},{64,32},{96,64},{1,97},{33,1},{65,33},{97,65},{2,98}... | collective-permute-start | bytes 442376 | tf_op jit(solution)/shard_map/ppermute | solution.py:232
  116.7 13.9 %all-to-all-start.3 = ((bf16[16,48,128]{2,1,0:T(8,128)(2,1)}), bf16[16,48,128]{2,1,0:T(8,128)(2,1)S(1)}, u32[]{:S(2)}, u32[]{:S(2)}) async-start(bf16[16,48,128]{2,1,0:T(8,128)(2,1)} %broadcast_in_dim.7), calls=%async_computation.3 | async-start | bytes 393216 | tf_op jit(solution)/shard_map/all_to_all | solution.py:404
  130.6 0.7 copy-start.1

commit v6 on v5

--- a/solution.py
+++ b/solution.py
@@ -426,7 +426,7 @@
     far_turned = lax.ppermute(turned, "core", swap)
     cells = unit.shape[0]
     *part_a, part_b = product(
-        place, turned.reshape(4, 4, -1, cells), far_turned.reshape(4, 4, -1, cells), near, far, hid // 4
+        place, turned.reshape(4, 4, -1, cells), far_turned.reshape(4, 4, -1, cells), near, far, 7 * hid // 24
     )
     part_b, unit = lax.optimization_barrier((part_b, unit))
     part_a = to_owners(part_a, "x")
@@ -435,20 +435,22 @@
     grad_input, small = back(
         mine, away, near, w_up, unit, sigma, ln_gain, up_sums, images, residual_cot, dw_weight
     )
-    part_a, part_b, small = lax.optimization_barrier((part_a, part_b, small))
+    part_b, small = lax.optimization_barrier((part_b, small))
+
+    around = ("z", "core")
     small = total_of(swap_pieces(small.reshape(16, -1, LANES), plane)).astype(jnp.bfloat16)
+    part_a, small = lax.optimization_barrier((part_a, small))
+    small = swap_pieces(jnp.broadcast_to(small, (2 * along_z,) + small.shape), around)
+    small = (total_of(small) * inverse_count).astype(jnp.bfloat16)
+    small = swap_pieces(jnp.broadcast_to(small, (16,) + small.shape), plane)
+    small = small.reshape(-1, SMALL_ROWS, LANES)
+
     part_a = to_owners(sum_pieces(part_a), ("y_lo", "y_hi"))
     part_b = to_owners(sum_pieces([part_b]), "x")
-
     last = jnp.concatenate([total_of(jnp.stack(part_a)), total_of(jnp.stack(part_b))], axis=1)
     last = last.astype(jnp.bfloat16).reshape(2 * along_z, -1, LANES)
-    height = last.shape[1]
-    small = jnp.broadcast_to(small, (2 * along_z,) + small.shape)
-    last = swap_pieces(jnp.concatenate([last, small], axis=1), ("z", "core"))
-    small = (total_of(last[:, height:]) * inverse_count).astype(jnp.bfloat16)
-    small = swap_pieces(jnp.broadcast_to(small, (16,) + small.shape), plane)
-    small = small.reshape(-1, SMALL_ROWS, LANES)
-    last = total_of(last[:, :height].reshape(along_z, 2, owned_rows, hid // 2))
+    last, small = lax.optimization_barrier((last, small))
+    last = total_of(swap_pieces(last, around).reshape(along_z, 2, owned_rows, hid // 2))
     owned = last.transpose(1, 0, 2).reshape(owned_rows, hid) * inverse_count
     return (grad_input, owned, *unpack(small))
 

time: 134 us -> 133 us (level)
  blocking collectives: 26.4 us -> 0 us
  starting transfers between devices: 31.5 us -> 43.8 us
  waiting for transfers between devices: 20 us -> 31.5 us
  local copies, waits for them, and re-layouts: 2.75 us -> 4.56 us
    all_to_all x1 -> x0, blocking collectives: 26.4 us -> none  [swap_pieces(): return lax.all_to_all(values, axes, 0, 0, tiled=True)]
    all_to_all x3 -> x5, waiting for transfers between devices: 6.84 us -> 24 us  [swap_pieces(): return lax.all_to_all(values, axes, 0, 0, tiled=True)]
    all_to_all x3 -> x5, starting transfers between devices: 14.6 us -> 28.9 us  [swap_pieces(): return lax.all_to_all(values, axes, 0, 0, tiled=True)]
    ppermute x9, waiting for transfers between devices: 10.6 us -> 4.89 us  [to_owners(): lax.ppermute(piece, axes, [(named[i], named[(i + d) % 4]) for i in range(...]
    ppermute x9, starting transfers between devices: 13.4 us -> 11.4 us  [to_owners(): lax.ppermute(piece, axes, [(named[i], named[(i + d) % 4]) for i in range(...]
  transfers between devices with their start and end apart: 14 -> 16, of which waited for: 8 -> 8; matrix products, arithmetic and copies ran while one was open for 2% -> 3% of each run, Pallas kernels for 16% -> 20%
where the time goes in v6:
time: 133 us; the launch traced here: 131 us
  Pallas kernels  48.3 us (36%)
  starting transfers between devices  43.8 us (33%)
  waiting for transfers between devices  31.5 us (24%)
  local copies, waits for them, and re-layouts  4.56 us (3%)
  other arithmetic  2.4 us (2%)
    all_to_all x5, starting transfers between devices, swap_pieces(): return lax.all_to_all(values, axes, 0, 0, tiled=True)  28.9 us
    all_to_all x5, waiting for transfers between devices, swap_pieces(): return lax.all_to_all(values, axes, 0, 0, tiled=True)  24 us
    pallas_call x1, Pallas kernels, back(): pl.pallas_call(back_kernel, name='back', grid=(feat // LANES,), in_specs=...  19.2 us
    pallas_call x1, Pallas kernels, front(): pl.pallas_call(front_kernel, name='front', in_specs=[pl.BlockSpec(memory_...  14.3 us
    ppermute x9, starting transfers between devices, to_owners(): lax.ppermute(piece, axes, [(named[i], named[(i + d) % 4]) for i in range(...  11.4 us
    pallas_call x1, Pallas kernels, product(): pl.pallas_call(product_kernel, name='product', grid_spec=pltpu.PrefetchSc...  7.92 us
    pallas_call x2, Pallas kernels, sum_pieces(): pl.pallas_call(sum_kernel, name='sum_pieces', out_shape=[jax.ShapeDtypeSt...  5.18 us
    ppermute x9, waiting for transfers between devices, to_owners(): lax.ppermute(piece, axes, [(named[i], named[(i + d) % 4]) for i in range(...  4.89 us
  transfers between devices with their start and end apart: 16, of which 8 were waited for; matrix products, arithmetic and copies ran while one was open for 3% of the time, Pallas kernels for 20%

profile of v6, /device:TPU:1, one launch (start us, length us, event | category | flops | bytes accessed | tf_op | source)
XLA Modules:
  0.0 131.3 jit_solution(17215407224784655515)
XLA Ops:
  0.6 14.3 %front.1 = (f32[256,1536]{1,0:T(8,128)}, f32[256,128]{1,0:T(8,128)}, bf16[4,2,2,96,256]{4,3,2,1,0:T(8,128)(2,1)}, bf16[256,1536]{1,0:T(8,128)(2,1)}, bf16[256,1536]{1,0:T(8,128)(2,1)}, /*index=5*/f32[1,3072]{1,0:T(1,128)}) custom-call(s32[1]{0:T(128)} %bitcast.core_ref, bf16[1,16,16,1536]{3,2,1,0:T(8,128)(2,1)} %image_ref.3, f32[49,1536]{1,0:T(8,128)} %taps_ref.3, ...), custom_call_target="tpu_custom_call" | custom-call | flops 1000 | bytes 1000 | tf_op jit(solution)/shard_map/front/pallas_call | solution.py:138
  14.9 3.3 %collective-permute-start.1 = (bf16[256,1536]{1,0:T(8,128)(2,1)}, bf16[256,1536]{1,0:T(8,128)(2,1)S(1)}, u32[]{:S(2)}, u32[]{:S(2)}) collective-permute-start(bf16[256,1536]{1,0:T(8,128)(2,1)} %get-tuple-element.44.away_ref), channel_id=1, source_target_pairs={{0,1},{1,0},{2,3},{3,2},{4,5},{5,4},{6,7},{7,6},{8,9},{9,8},{10,11... | collective-permute-start | bytes 2359304 | tf_op jit(solution)/shard_map/ppermute | solution.py:425
  18.3 0.1 collective-permute-start
  18.4 0.6 pad_add_fusion.place_ref
  18.9 1.4 %collective-permute-done.1.far_ref = bf16[256,1536]{1,0:T(8,128)(2,1)S(1)} collective-permute-done((bf16[256,1536]{1,0:T(8,128)(2,1)}, bf16[256,1536]{1,0:T(8,128)(2,1)S(1)}, u32[]{:S(2)}, u32[]{:S(2)}) %collective-permute-start.1) | collective-permute-done | bytes 786464 | tf_op jit(solution)/shard_map/ppermute | solution.py:425
  20.4 0.0 copy-start.2
  20.4 1.1 collective-permute-done
  21.5 0.0 copy-start.3
  21.5 0.0 copy-done.2
  21.5 0.9 copy-done.3
  22.4 7.9 %product.1 = (bf16[4,96,896]{2,1,0:T(8,128)(2,1)}, bf16[4,96,896]{2,1,0:T(8,128)(2,1)}, bf16[4,96,896]{2,1,0:T(8,128)(2,1)}, bf16[4,96,896]{2,1,0:T(8,128)(2,1)}, bf16[4,4,96,640]{3,2,1,0:T(8,128)(2,1)}) custom-call(s32[2]{0:T(128)} %pad_add_fusion.place_ref, bf16[4,4,96,256]{3,2,1,0:T(8,128)(2,1)} %bitcast.12, bf16[4,4,96,256]{3,2,1,0:T(8,128)(2,1)} %bitcast.13, ...), custom_call_target="tpu_custom_call" | custom-call | flops 1000 | bytes 1000 | tf_op jit(solution)/shard_map/product/pallas_call | solution.py:188
  30.4 3.6 %all-to-all-start = ((bf16[4,4,96,640]{3,2,1,0:T(8,128)(2,1)}), bf16[4,4,96,640]{3,2,1,0:T(8,128)(2,1)S(1)}, u32[]{:S(2)}, u32[]{:S(2)}) async-start(bf16[4,4,96,640]{3,2,1,0:T(8,128)(2,1)} %get-tuple-element.57), calls=%async_computation | async-start | bytes 3932160 | tf_op jit(solution)/shard_map/all_to_all | solution.py:404
  34.0 0.1 collective-permute-start.2
  34.0 2.4 %collective-permute-start.3 = (bf16[4,96,896]{2,1,0:T(8,128)(2,1)}, bf16[4,96,896]{2,1,0:T(8,128)(2,1)S(1)}, u32[]{:S(2)}, u32[]{:S(2)}) collective-permute-start(bf16[4,96,896]{2,1,0:T(8,128)(2,1)} %get-tuple-element.55), channel_id=1, source_target_pairs={{0,64},{32,96},{64,0},{96,32},{1,65},{33,97},{65,1},{97,33},{2,66}... | collective-permute-start | bytes 2064392 | tf_op jit(solution)/shard_map/ppermute | solution.py:232
  36.5 1.1 collective-permute-start.4
  37.6 19.2 %back.1 = (bf16[1,16,16,1536]{3,2,1,0:T(8,128)(2,1)}, bf16[12,64,128]{2,1,0:T(8,128)(2,1)}) custom-call(s32[1]{0:T(128)} %bitcast.core_ref, bf16[256,1536]{1,0:T(8,128)(2,1)} %get-tuple-element.44.away_ref, bf16[256,1536]{1,0:T(8,128)(2,1)} %get-tuple-element.45.near_ref, f32[256,128]{1,0:T(8,128)} %get-tuple-element.46.sigma_ref, f32[1536]{0:T(1024)} %gain_ref.3, ...), custom_call_target="tpu_custom_call" | custom-call | flops 1000 | bytes 1000 | tf_op jit(solution)/shard_map/back/pallas_call | solution.py:337
  56.8 1.8 %all-to-all-done.refs_0_ = bf16[4,4,96,640]{3,2,1,0:T(8,128)(2,1)S(1)} async-done(((bf16[4,4,96,640]{3,2,1,0:T(8,128)(2,1)}), bf16[4,4,96,640]{3,2,1,0:T(8,128)(2,1)S(1)}, u32[]{:S(2)}, u32[]{:S(2)}) %all-to-all-start) | async-done | bytes 1966112 | tf_op jit(solution)/shard_map/all_to_all | solution.py:404
  58.6 0.0 copy-start
  58.6 3.7 %all-to-all-start.1 = ((bf16[16,48,128]{2,1,0:T(8,128)(2,1)}), bf16[16,48,128]{2,1,0:T(8,128)(2,1)S(1)}, u32[]{:S(2)}, u32[]{:S(2)}) async-start(bf16[16,48,128]{2,1,0:T(8,128)(2,1)} %bitcast.14), calls=%async_computation.1 | async-start | bytes 393216 | tf_op jit(solution)/shard_map/all_to_all | solution.py:404
  62.3 0.0 copy-done
  62.3 2.5 %sum_pieces.3 = (bf16[96,640]{1,0:T(8,128)(2,1)}, bf16[96,640]{1,0:T(8,128)(2,1)}, bf16[96,640]{1,0:T(8,128)(2,1)}, bf16[96,640]{1,0:T(8,128)(2,1)}) custom-call(bf16[4,4,96,640]{3,2,1,0:T(8,128)(2,1)} %copy-done), custom_call_target="tpu_custom_call" | custom-call | flops 1000 | bytes 1000 | tf_op jit(solution)/shard_map/sum_pieces/pallas_call | solution.py:220
  64.8 0.0 copy-start.6
  64.8 1.3 %collective-permute-start.8 = (bf16[96,640]{1,0:T(8,128)(2,1)}, bf16[96,640]{1,0:T(8,128)(2,1)S(1)}, u32[]{:S(2)}, u32[]{:S(2)}) collective-permute-start(bf16[96,640]{1,0:T(8,128)(2,1)} %get-tuple-element.70), channel_id=1, source_target_pairs={{0,32},{32,64},{64,96},{96,0},{1,33},{33,65},{65,97},{97,1},{2,34}... | collective-permute-start | bytes 368648 | tf_op jit(solution)/shard_map/ppermute | solution.py:232
  66.1 2.4 %collective-permute-start.9 = (bf16[96,640]{1,0:T(8,128)(2,1)}, bf16[96,640]{1,0:T(8,128)(2,1)S(1)}, u32[]{:S(2)}, u32[]{:S(2)}) collective-permute-start(bf16[96,640]{1,0:T(8,128)(2,1)} %get-tuple-element.71), channel_id=1, source_target_pairs={{0,64},{32,96},{64,0},{96,32},{1,65},{33,97},{65,1},{97,33},{2,66}... | collective-permute-start | bytes 368648 | tf_op jit(solution)/shard_map/ppermute | solution.py:232
  68.5 0.0 collective-permute-done.2.refs_1_
  68.5 0.0 copy-start.4
  68.5 1.2 collective-permute-start.10
  69.7 2.0 %all-to-all-done.1 = bf16[16,48,128]{2,1,0:T(8,128)(2,1)S(1)} async-done(((bf16[16,48,128]{2,1,0:T(8,128)(2,1)}), bf16[16,48,128]{2,1,0:T(8,128)(2,1)S(1)}, u32[]{:S(2)}, u32[]{:S(2)}) %all-to-all-start.1) | async-done | bytes 196640 | tf_op jit(solution)/shard_map/all_to_all | solution.py:404
  71.8 0.0 collective-permute-done.3.refs_2_
  71.8 0.0 copy-start.5
  71.8 0.0 collective-permute-done.4.refs_3_
  71.8 0.0 copy-done.4
  71.8 0.8 copy-done.5
  72.6 2.7 %sum_pieces.2 = (bf16[96,896]{1,0:T(8,128)(2,1)}, bf16[96,896]{1,0:T(8,128)(2,1)}, bf16[96,896]{1,0:T(8,128)(2,1)}, bf16[96,896]{1,0:T(8,128)(2,1)}) custom-call(bf16[4,96,896]{2,1,0:T(8,128)(2,1)} %get-tuple-element.60.refs_0_, bf16[4,96,896]{2,1,0:T(8,128)(2,1)} %copy-done.4, bf16[4,96,896]{2,1,0:T(8,128)(2,1)} %copy-done.5, ...), custom_call_target="tpu_custom_call" | custom-call | flops 1000 | bytes 1000 | tf_op jit(solution)/shard_map/sum_pieces/pallas_call | solution.py:220
  75.4 0.1 collective-permute-start.5
  75.4 1.5 %collective-permute-start.6 = (bf16[96,896]{1,0:T(8,128)(2,1)}, bf16[96,896]{1,0:T(8,128)(2,1)S(1)}, u32[]{:S(2)}, u32[]{:S(2)}) collective-permute-start(bf16[96,896]{1,0:T(8,128)(2,1)} %get-tuple-element.66), channel_id=1, source_target_pairs={{0,2},{128,130},{2,0},{130,128},{1,3},{129,131},{3,1},{131,129},{4... | collective-permute-start | bytes 516104 | tf_op jit(solution)/shard_map/ppermute | solution.py:232
  76.9 0.7 broadcast_in_dim.6
  77.6 11.6 %all-to-all-start.2 = ((bf16[16,48,128]{2,1,0:T(8,128)(2,1)}), bf16[16,48,128]{2,1,0:T(8,128)(2,1)S(1)}, u32[]{:S(2)}, u32[]{:S(2)}) async-start(bf16[16,48,128]{2,1,0:T(8,128)(2,1)} %broadcast_in_dim.6), calls=%async_computation.2 | async-start | bytes 393216 | tf_op jit(solution)/shard_map/all_to_all | solution.py:404
  89.2 0.0 collective-permute-done.8
  89.2 1.3 collective-permute-start.7
  90.5 0.0 collective-permute-done.9
  90.5 0.0 collective-permute-done.10
  90.5 0.0 copy-done.6
  90.5 0.0 collective-permute-done.5
  90.6 0.0 collective-permute-done.6
  90.6 4.9 %collective-permute-done.7 = bf16[96,896]{1,0:T(8,128)(2,1)S(1)} collective-permute-done((bf16[96,896]{1,0:T(8,128)(2,1)}, bf16[96,896]{1,0:T(8,128)(2,1)S(1)}, u32[]{:S(2)}, u32[]{:S(2)}) %collective-permute-start.7) | collective-permute-done | bytes 172064 | tf_op jit(solution)/shard_map/ppermute | solution.py:232
  95.4 1.0 add_add_fusion
  96.4 3.1 %all-to-all-done.2 = bf16[16,48,128]{2,1,0:T(8,128)(2,1)S(1)} async-done(((bf16[16,48,128]{2,1,0:T(8,128)(2,1)}), bf16[16,48,128]{2,1,0:T(8,128)(2,1)S(1)}, u32[]{:S(2)}, u32[]{:S(2)}) %all-to-all-start.2) | async-done | bytes 196640 | tf_op jit(solution)/shard_map/all_to_all | solution.py:404
  99.6 0.7 broadcast_in_dim.7
  100.3 3.5 %all-to-all-start.3 = ((bf16[16,48,128]{2,1,0:T(8,128)(2,1)}), bf16[16,48,128]{2,1,0:T(8,128)(2,1)S(1)}, u32[]{:S(2)}, u32[]{:S(2)}) async-start(bf16[16,48,128]{2,1,0:T(8,128)(2,1)} %broadcast_in_dim.7), calls=%async_computation.3 | async-start | bytes 393216 | tf_op jit(solution)/shard_map/all_to_all | solution.py:404
  103.8 1.1 convert_element_type.27
  104.9 6.4 %all-to-all-done.3 = bf16[16,48,128]{2,1,0:T(8,128)(2,1)S(1)} async-done(((bf16[16,48,128]{2,1,0:T(8,128)(2,1)}), bf16[16,48,128]{2,1,0:T(8,128)(2,1)S(1)}, u32[]{:S(2)}, u32[]{:S(2)}) %all-to-all-start.3) | async-done | bytes 196640 | tf_op jit(solution)/shard_map/all_to_all | solution.py:404
  111.3 0.0 copy-start.1
  111.3 6.5 %all-to-all-start.4 = ((bf16[16,72,128]{2,1,0:T(8,128)(2,1)}), bf16[16,72,128]{2,1,0:T(8,128)(2,1)S(1)}, u32[]{:S(2)}, u32[]{:S(2)}) async-start(bf16[16,72,128]{2,1,0:T(8,128)(2,1)} %convert_element_type.27), calls=%async_computation.4 | async-start | bytes 589824 | tf_op jit(solution)/shard_map/all_to_all | solution.py:404
  117.9 0.0 copy-done.1
  117.9 1.7 %unpack.1 = (f32[3072]{0:T(1024)}, f32[1536]{0:T(1024)}, f32[1536]{0:T(1024)}, f32[49,1536]{1,0:T(8,128)}, f32[1536]{0:T(1024)}) custom-call(bf16[12,64,128]{2,1,0:T(8,128)(2,1)} %bitcast.11), custom_call_target="tpu_custom_call" | custom-call | flops 1000 | bytes 1000 | tf_op jit(solution)/shard_map/unpack/pallas_call | solution.py:388
  119.6 10.7 %all-to-all-done.4 = bf16[16,72,128]{2,1,0:T(8,128)(2,1)S(1)} async-done(((bf16[16,72,128]{2,1,0:T(8,128)(2,1)}), bf16[16,72,128]{2,1,0:T(8,128)(2,1)S(1)}, u32[]{:S(2)}, u32[]{:S(2)}) %all-to-all-start.4) | async-done | bytes 294944 | tf_op jit(solution)/shard_map/all_to_all | solution.py:404
  130.2 0.3 reshape.47
  130.6 0.1 reduce_sum.52
  130.6 0.7 broadcast_multiply_fusion
  (5 shorter events, 0.1 us)
Async XLA Ops:
  14.9 5.4 %collective-permute-start.1 = (bf16[256,1536]{1,0:T(8,128)(2,1)}, bf16[256,1536]{1,0:T(8,128)(2,1)S(1)}, u32[]{:S(2)}, u32[]{:S(2)}) collective-permute-start(bf16[256,1536]{1,0:T(8,128)(2,1)} %get-tuple-element.44.away_ref), channel_id=1, source_target_pairs={{0,1},{1,0},{2,3},{3,2},{4,5},{5,4},{6,7},{7,6},{8,9},{9,8},{10,11... | collective-permute-start | bytes 2359304 | tf_op jit(solution)/shard_map/ppermute | solution.py:425
  18.3 3.2 %collective-permute-start = (bf16[4,2,2,96,256]{4,3,2,1,0:T(8,128)(2,1)}, bf16[4,2,2,96,256]{4,3,2,1,0:T(8,128)(2,1)S(1)}, u32[]{:S(2)}, u32[]{:S(2)}) collective-permute-start(bf16[4,2,2,96,256]{4,3,2,1,0:T(8,128)(2,1)} %get-tuple-element.48), channel_id=1, source_target_pairs={{0,1},{1,0},{2,3},{3,2},{4,5},{5,4},{6,7},{7,6},{8,9},{9,8},{10,11... | collective-permute-start | bytes 2359304 | tf_op jit(solution)/shard_map/ppermute | solution.py:426
  20.4 1.1 copy-start.2
  21.5 0.9 copy-start.3
  30.4 28.2 %all-to-all-start = ((bf16[4,4,96,640]{3,2,1,0:T(8,128)(2,1)}), bf16[4,4,96,640]{3,2,1,0:T(8,128)(2,1)S(1)}, u32[]{:S(2)}, u32[]{:S(2)}) async-start(bf16[4,4,96,640]{3,2,1,0:T(8,128)(2,1)} %get-tuple-element.57), calls=%async_computation | async-start | bytes 3932160 | tf_op jit(solution)/shard_map/all_to_all | solution.py:404
  34.0 34.6 %collective-permute-start.2 = (bf16[4,96,896]{2,1,0:T(8,128)(2,1)}, bf16[4,96,896]{2,1,0:T(8,128)(2,1)S(1)}, u32[]{:S(2)}, u32[]{:S(2)}) collective-permute-start(bf16[4,96,896]{2,1,0:T(8,128)(2,1)} %get-tuple-element.54), channel_id=1, source_target_pairs={{0,32},{32,64},{64,96},{96,0},{1,33},{33,65},{65,97},{97,1},{2,34}... | collective-permute-start | bytes 2064392 | tf_op jit(solution)/shard_map/ppermute | solution.py:232
  34.0 37.7 %collective-permute-start.3 = (bf16[4,96,896]{2,1,0:T(8,128)(2,1)}, bf16[4,96,896]{2,1,0:T(8,128)(2,1)S(1)}, u32[]{:S(2)}, u32[]{:S(2)}) collective-permute-start(bf16[4,96,896]{2,1,0:T(8,128)(2,1)} %get-tuple-element.55), channel_id=1, source_target_pairs={{0,64},{32,96},{64,0},{96,32},{1,65},{33,97},{65,1},{97,33},{2,66}... | collective-permute-start | bytes 2064392 | tf_op jit(solution)/shard_map/ppermute | solution.py:232
  36.5 35.3 %collective-permute-start.4 = (bf16[4,96,896]{2,1,0:T(8,128)(2,1)}, bf16[4,96,896]{2,1,0:T(8,128)(2,1)}, u32[]{:S(2)}, u32[]{:S(2)}) collective-permute-start(bf16[4,96,896]{2,1,0:T(8,128)(2,1)} %get-tuple-element.56), channel_id=1, source_target_pairs={{0,96},{32,0},{64,32},{96,64},{1,97},{33,1},{65,33},{97,65},{2,98}... | collective-permute-start | bytes 2064392 | tf_op jit(solution)/shard_map/ppermute | solution.py:232
  58.6 3.7 %copy-start = (bf16[4,4,96,640]{3,2,1,0:T(8,128)(2,1)}, bf16[4,4,96,640]{3,2,1,0:T(8,128)(2,1)S(1)}, u32[]{:S(2)}) copy-start(bf16[4,4,96,640]{3,2,1,0:T(8,128)(2,1)S(1)} %all-to-all-done.refs_0_) | copy-start | bytes 5898244
  58.6 13.1 %all-to-all-start.1 = ((bf16[16,48,128]{2,1,0:T(8,128)(2,1)}), bf16[16,48,128]{2,1,0:T(8,128)(2,1)S(1)}, u32[]{:S(2)}, u32[]{:S(2)}) async-start(bf16[16,48,128]{2,1,0:T(8,128)(2,1)} %bitcast.14), calls=%async_computation.1 | async-start | bytes 393216 | tf_op jit(solution)/shard_map/all_to_all | solution.py:404
  64.8 25.7 %copy-start.6 = (bf16[96,640]{1,0:T(8,128)(2,1)S(1)}, bf16[96,640]{1,0:T(8,128)(2,1)}, u32[]{:S(2)}) copy-start(bf16[96,640]{1,0:T(8,128)(2,1)} %get-tuple-element.69) | copy-start | bytes 368644
  64.8 24.4 %collective-permute-start.8 = (bf16[96,640]{1,0:T(8,128)(2,1)}, bf16[96,640]{1,0:T(8,128)(2,1)S(1)}, u32[]{:S(2)}, u32[]{:S(2)}) collective-permute-start(bf16[96,640]{1,0:T(8,128)(2,1)} %get-tuple-element.70), channel_id=1, source_target_pairs={{0,32},{32,64},{64,96},{96,0},{1,33},{33,65},{65,97},{97,1},{2,34}... | collective-permute-start | bytes 368648 | tf_op jit(solution)/shard_map/ppermute | solution.py:232
  66.1 24.4 %collective-permute-start.9 = (bf16[96,640]{1,0:T(8,128)(2,1)}, bf16[96,640]{1,0:T(8,128)(2,1)S(1)}, u32[]{:S(2)}, u32[]{:S(2)}) collective-permute-start(bf16[96,640]{1,0:T(8,128)(2,1)} %get-tuple-element.71), channel_id=1, source_target_pairs={{0,64},{32,96},{64,0},{96,32},{1,65},{33,97},{65,1},{97,33},{2,66}... | collective-permute-start | bytes 368648 | tf_op jit(solution)/shard_map/ppermute | solution.py:232
  68.5 3.3 %copy-start.4 = (bf16[4,96,896]{2,1,0:T(8,128)(2,1)}, bf16[4,96,896]{2,1,0:T(8,128)(2,1)S(1)}, u32[]{:S(2)}) copy-start(bf16[4,96,896]{2,1,0:T(8,128)(2,1)S(1)} %collective-permute-done.2.refs_1_) | copy-start | bytes 2064388
  68.5 22.0 %collective-permute-start.10 = (bf16[96,640]{1,0:T(8,128)(2,1)}, bf16[96,640]{1,0:T(8,128)(2,1)S(1)}, u32[]{:S(2)}, u32[]{:S(2)}) collective-permute-start(bf16[96,640]{1,0:T(8,128)(2,1)} %get-tuple-element.72), channel_id=1, source_target_pairs={{0,96},{32,0},{64,32},{96,64},{1,97},{33,1},{65,33},{97,65},{2,98}... | collective-permute-start | bytes 368648 | tf_op jit(solution)/shard_map/ppermute | solution.py:232
  71.8 0.9 copy-start.5
  75.4 15.2 %collective-permute-start.5 = (bf16[96,896]{1,0:T(8,128)(2,1)}, bf16[96,896]{1,0:T(8,128)(2,1)S(1)}, u32[]{:S(2)}, u32[]{:S(2)}) collective-permute-start(bf16[96,896]{1,0:T(8,128)(2,1)} %get-tuple-element.65), channel_id=1, source_target_pairs={{0,128},{128,2},{2,130},{130,0},{1,129},{129,3},{3,131},{131,1},{4... | collective-permute-start | bytes 516104 | tf_op jit(solution)/shard_map/ppermute | solution.py:232
  75.4 15.1 %collective-permute-start.6 = (bf16[96,896]{1,0:T(8,128)(2,1)}, bf16[96,896]{1,0:T(8,128)(2,1)S(1)}, u32[]{:S(2)}, u32[]{:S(2)}) collective-permute-start(bf16[96,896]{1,0:T(8,128)(2,1)} %get-tuple-element.66), channel_id=1, source_target_pairs={{0,2},{128,130},{2,0},{130,128},{1,3},{129,131},{3,1},{131,129},{4... | collective-permute-start | bytes 516104 | tf_op jit(solution)/shard_map/ppermute | solution.py:232
  77.6 21.9 %all-to-all-start.2 = ((bf16[16,48,128]{2,1,0:T(8,128)(2,1)}), bf16[16,48,128]{2,1,0:T(8,128)(2,1)S(1)}, u32[]{:S(2)}, u32[]{:S(2)}) async-start(bf16[16,48,128]{2,1,0:T(8,128)(2,1)} %broadcast_in_dim.6), calls=%async_computation.2 | async-start | bytes 393216 | tf_op jit(solution)/shard_map/all_to_all | solution.py:404
  89.2 6.2 %collective-permute-start.7 = (bf16[96,896]{1,0:T(8,128)(2,1)}, bf16[96,896]{1,0:T(8,128)(2,1)S(1)}, u32[]{:S(2)}, u32[]{:S(2)}) collective-permute-start(bf16[96,896]{1,0:T(8,128)(2,1)} %get-tuple-element.67), channel_id=1, source_target_pairs={{0,130},{128,0},{2,128},{130,2},{1,131},{129,1},{3,129},{131,3},{4... | collective-permute-start | bytes 516104 | tf_op jit(solution)/shard_map/ppermute | solution.py:232
  100.3 11.0 %all-to-all-start.3 = ((bf16[16,48,128]{2,1,0:T(8,128)(2,1)}), bf16[16,48,128]{2,1,0:T(8,128)(2,1)S(1)}, u32[]{:S(2)}, u32[]{:S(2)}) async-start(bf16[16,48,128]{2,1,0:T(8,128)(2,1)} %broadcast_in_dim.7), calls=%async_computation.3 | async-start | bytes 393216 | tf_op jit(solution)/shard_map/all_to_all | solution.py:404
  111.3 6.5 %copy-start.1 = (bf16[16,48,128]{2,1,0:T(8,128)(2,1)}, bf16[16,48,128]{2,1,0:T(8,128)(2,1)S(1)}, u32[]{:S(2)}) copy-start(bf16[16,48,128]{2,1,0:T(8,128)(2,1)S(1)} %all-to-all-done.3) | copy-start | bytes 589828
  111.3 18.9 %all-to-all-start.4 = ((bf16[16,72,128]{2,1,0:T(8,128)(2,1)}), bf16[16,72,128]{2,1,0:T(8,128)(2,1)S(1)}, u32[]{:S(2)}, u32[]{:S(2)}) async-start(bf16[16,72,128]{2,1,0:T(8,128)(2,1)} %convert_element_type.27), calls=%async_computation.4 | async-start | bytes 589824 | tf_op jit(solution)/shard_map/all_to_all | solution.py:404

commit v7 on v6

--- a/solution.py
+++ b/solution.py
@@ -1,3 +1,5 @@
+import functools
+
 import jax
 import jax.numpy as jnp
 import numpy as np
@@ -369,27 +371,48 @@
     )(core, away, near, sigma, gain, up_sums, up_sums, image, residual, taps, unit, w_up)
 
 
-def unpack_kernel(small_ref, up_ref, gain_ref, shift_ref, taps_ref, bias_ref):
-    blocks = small_ref.shape[0]
-    for block in range(blocks):
-        values = small_ref[block].astype(jnp.float32)
+def finish_kernel(inverse_count, received_ref, owned_ref, up_ref, gain_ref, shift_ref, taps_ref, bias_ref):
+    pieces, height, _ = received_ref.shape
+    owned_rows, hid = owned_ref.shape
+    blocks = hid // 2 // LANES
+    share = height - owned_rows * blocks
+    for core in range(2):
+        total = received_ref[core, share:, :].astype(jnp.float32)
+        for z in range(1, pieces // 2):
+            total = total + received_ref[2 * z + core, share:, :].astype(jnp.float32)
+        total = total * inverse_count
+        for row in range(owned_rows):
+            for block in range(blocks):
+                first = (core * blocks + block) * LANES
+                index = row * blocks + block
+                owned_ref[row : row + 1, first : first + LANES] = total[index : index + 1]
+    feat = gain_ref.shape[0]
+    for block in range(feat // LANES):
+        parts = []
+        row, end = block * SMALL_ROWS, (block + 1) * SMALL_ROWS
+        while row < end:
+            stop = min(end, (row // share + 1) * share)
+            first = row % share
+            parts.append(received_ref[row // share, first : first + stop - row, :].astype(jnp.float32))
+            row = stop
+        values = jnp.concatenate(parts, axis=0)
         lanes = slice(block * LANES, (block + 1) * LANES)
         taps_ref[:, lanes] = values[:49]
         gain_ref[lanes] = values[49]
         shift_ref[lanes] = values[50]
         bias_ref[lanes] = values[51]
         up_ref[lanes] = values[52]
-        up_ref[blocks * LANES + block * LANES : blocks * LANES + (block + 1) * LANES] = values[53]
-
-
-def unpack(small):
-    feat = small.shape[0] * LANES
+        up_ref[feat + block * LANES : feat + (block + 1) * LANES] = values[53]
+
+
+def finish(received, owned_rows, feat, hid, inverse_count):
     row = jax.ShapeDtypeStruct((feat,), jnp.float32)
     return pl.pallas_call(
-        unpack_kernel,
-        name="unpack",
+        functools.partial(finish_kernel, inverse_count),
+        name="finish",
         out_shape=(
-            jax.ShapeDtypeStruct((2 * feat,), jnp.float32),
+            jax.ShapeDtypeStruct((owned_rows, hid), jnp.float32),
+            jax.ShapeDtypeStruct((hid,), jnp.float32),
             row,
             row,
             jax.ShapeDtypeStruct((49, feat), jnp.float32),
@@ -397,7 +420,7 @@
         ),
         compiler_params=pltpu.CompilerParams(vmem_limit_bytes=VMEM_LIMIT),
         cost_estimate=SMALL,
-    )(small)
+    )(received)
 
 
 def swap_pieces(values, axes):
@@ -438,21 +461,20 @@
     part_b, small = lax.optimization_barrier((part_b, small))
 
     around = ("z", "core")
-    small = total_of(swap_pieces(small.reshape(16, -1, LANES), plane)).astype(jnp.bfloat16)
+    small = swap_pieces(small.reshape(2 * along_z, -1, LANES), around)
+    small = total_of(small).astype(jnp.bfloat16)
     part_a, small = lax.optimization_barrier((part_a, small))
-    small = swap_pieces(jnp.broadcast_to(small, (2 * along_z,) + small.shape), around)
-    small = (total_of(small) * inverse_count).astype(jnp.bfloat16)
     small = swap_pieces(jnp.broadcast_to(small, (16,) + small.shape), plane)
-    small = small.reshape(-1, SMALL_ROWS, LANES)
-
+
+    part_b = to_owners(sum_pieces([part_b]), "x")
+    part_a, part_b = lax.optimization_barrier((part_a, part_b))
     part_a = to_owners(sum_pieces(part_a), ("y_lo", "y_hi"))
-    part_b = to_owners(sum_pieces([part_b]), "x")
     last = jnp.concatenate([total_of(jnp.stack(part_a)), total_of(jnp.stack(part_b))], axis=1)
     last = last.astype(jnp.bfloat16).reshape(2 * along_z, -1, LANES)
-    last, small = lax.optimization_barrier((last, small))
-    last = total_of(swap_pieces(last, around).reshape(along_z, 2, owned_rows, hid // 2))
-    owned = last.transpose(1, 0, 2).reshape(owned_rows, hid) * inverse_count
-    return (grad_input, owned, *unpack(small))
+    small = (total_of(small) * inverse_count).astype(jnp.bfloat16)
+    small = jnp.broadcast_to(small, (2 * along_z,) + small.shape)
+    last = swap_pieces(jnp.concatenate([small, last], axis=1), around)
+    return (grad_input, *finish(last, owned_rows, feat, hid, inverse_count))
 
 
 def solution(mesh):

time: 133 us -> 128 us (0.962)
  blocking collectives: 0 us -> 26.2 us
  waiting for transfers between devices: 31.5 us -> 14.9 us
  starting transfers between devices: 43.8 us -> 32.8 us
  local copies, waits for them, and re-layouts: 4.56 us -> 2.04 us
    all_to_all x0 -> x1, blocking collectives: none -> 26.2 us  [swap_pieces(): return lax.all_to_all(values, axes, 0, 0, tiled=True)]
    all_to_all x5 -> x3, waiting for transfers between devices: 24 us -> 9.5 us  [swap_pieces(): return lax.all_to_all(values, axes, 0, 0, tiled=True)]
    all_to_all x5 -> x3, starting transfers between devices: 28.9 us -> 16.6 us  [swap_pieces(): return lax.all_to_all(values, axes, 0, 0, tiled=True)]
    ppermute x9, waiting for transfers between devices: 4.89 us -> 2.88 us  [to_owners(): lax.ppermute(piece, axes, [(named[i], named[(i + d) % 4]) for i in range(...]
    ppermute x9, starting transfers between devices: 11.4 us -> 12.8 us  [to_owners(): lax.ppermute(piece, axes, [(named[i], named[(i + d) % 4]) for i in range(...]
  transfers between devices with their start and end apart: 16 -> 14, of which waited for: 8 -> 8; matrix products, arithmetic and copies ran while one was open for 3% -> 2% of each run, Pallas kernels for 20% -> 17%
where the time goes in v7:
time: 128 us; the launch traced here: 127 us
  Pallas kernels  48.5 us (38%)
  starting transfers between devices  32.8 us (26%)
  blocking collectives  26.2 us (20%)
  waiting for transfers between devices  14.9 us (12%)
  local copies, waits for them, and re-layouts  2.04 us (2%)
  other arithmetic  1.73 us (1%)
    all_to_all x1, blocking collectives, swap_pieces(): return lax.all_to_all(values, axes, 0, 0, tiled=True)  26.2 us
    pallas_call x1, Pallas kernels, back(): pl.pallas_call(back_kernel, name='back', grid=(feat // LANES,), in_specs=...  19.2 us
    all_to_all x3, starting transfers between devices, swap_pieces(): return lax.all_to_all(values, axes, 0, 0, tiled=True)  16.6 us
    pallas_call x1, Pallas kernels, front(): pl.pallas_call(front_kernel, name='front', in_specs=[pl.BlockSpec(memory_...  14.3 us
    ppermute x9, starting transfers between devices, to_owners(): lax.ppermute(piece, axes, [(named[i], named[(i + d) % 4]) for i in range(...  12.8 us
    all_to_all x3, waiting for transfers between devices, swap_pieces(): return lax.all_to_all(values, axes, 0, 0, tiled=True)  9.5 us
    pallas_call x1, Pallas kernels, product(): pl.pallas_call(product_kernel, name='product', grid_spec=pltpu.PrefetchSc...  7.9 us
    pallas_call x2, Pallas kernels, sum_pieces(): pl.pallas_call(sum_kernel, name='sum_pieces', out_shape=[jax.ShapeDtypeSt...  5.17 us
  transfers between devices with their start and end apart: 14, of which 8 were waited for; matrix products, arithmetic and copies ran while one was open for 2% of the time, Pallas kernels for 17%

profile of v7, /device:TPU:1, one launch (start us, length us, event | category | flops | bytes accessed | tf_op | source)
XLA Modules:
  0.0 127.0 jit_solution(6809344774642600559)
XLA Ops:
  0.6 14.3 %front.1 = (f32[256,1536]{1,0:T(8,128)}, f32[256,128]{1,0:T(8,128)}, bf16[4,2,2,96,256]{4,3,2,1,0:T(8,128)(2,1)}, bf16[256,1536]{1,0:T(8,128)(2,1)}, bf16[256,1536]{1,0:T(8,128)(2,1)}, /*index=5*/f32[1,3072]{1,0:T(1,128)}) custom-call(s32[1]{0:T(128)} %bitcast.core_ref, bf16[1,16,16,1536]{3,2,1,0:T(8,128)(2,1)} %image_ref.3, f32[49,1536]{1,0:T(8,128)} %taps_ref.3, ...), custom_call_target="tpu_custom_call" | custom-call | flops 1000 | bytes 1000 | tf_op jit(solution)/shard_map/front/pallas_call | solution.py:140
  15.0 3.3 %collective-permute-start.1 = (bf16[256,1536]{1,0:T(8,128)(2,1)}, bf16[256,1536]{1,0:T(8,128)(2,1)S(1)}, u32[]{:S(2)}, u32[]{:S(2)}) collective-permute-start(bf16[256,1536]{1,0:T(8,128)(2,1)} %get-tuple-element.51.away_ref), channel_id=1, source_target_pairs={{0,1},{1,0},{2,3},{3,2},{4,5},{5,4},{6,7},{7,6},{8,9},{9,8},{10,11... | collective-permute-start | bytes 2359304 | tf_op jit(solution)/shard_map/ppermute | solution.py:448
  18.3 0.1 collective-permute-start
  18.4 0.6 pad_add_fusion.place_ref
  19.0 1.4 %collective-permute-done.1.far_ref = bf16[256,1536]{1,0:T(8,128)(2,1)S(1)} collective-permute-done((bf16[256,1536]{1,0:T(8,128)(2,1)}, bf16[256,1536]{1,0:T(8,128)(2,1)S(1)}, u32[]{:S(2)}, u32[]{:S(2)}) %collective-permute-start.1) | collective-permute-done | bytes 786464 | tf_op jit(solution)/shard_map/ppermute | solution.py:448
  20.4 0.0 copy-start.1
  20.4 1.1 collective-permute-done
  21.5 0.0 copy-start.2
  21.5 0.0 copy-done.1
  21.5 0.9 copy-done.2
  22.5 7.9 %product.1 = (bf16[4,96,896]{2,1,0:T(8,128)(2,1)}, bf16[4,96,896]{2,1,0:T(8,128)(2,1)}, bf16[4,96,896]{2,1,0:T(8,128)(2,1)}, bf16[4,96,896]{2,1,0:T(8,128)(2,1)}, bf16[4,4,96,640]{3,2,1,0:T(8,128)(2,1)}) custom-call(s32[2]{0:T(128)} %pad_add_fusion.place_ref, bf16[4,4,96,256]{3,2,1,0:T(8,128)(2,1)} %bitcast.7, bf16[4,4,96,256]{3,2,1,0:T(8,128)(2,1)} %bitcast.8, ...), custom_call_target="tpu_custom_call" | custom-call | flops 1000 | bytes 1000 | tf_op jit(solution)/shard_map/product/pallas_call | solution.py:190
  30.4 3.6 %all-to-all-start = ((bf16[4,4,96,640]{3,2,1,0:T(8,128)(2,1)}), bf16[4,4,96,640]{3,2,1,0:T(8,128)(2,1)S(1)}, u32[]{:S(2)}, u32[]{:S(2)}) async-start(bf16[4,4,96,640]{3,2,1,0:T(8,128)(2,1)} %get-tuple-element.64), calls=%async_computation | async-start | bytes 3932160 | tf_op jit(solution)/shard_map/all_to_all | solution.py:427
  34.0 0.1 collective-permute-start.2
  34.1 2.4 %collective-permute-start.3 = (bf16[4,96,896]{2,1,0:T(8,128)(2,1)}, bf16[4,96,896]{2,1,0:T(8,128)(2,1)S(1)}, u32[]{:S(2)}, u32[]{:S(2)}) collective-permute-start(bf16[4,96,896]{2,1,0:T(8,128)(2,1)} %get-tuple-element.62), channel_id=1, source_target_pairs={{0,64},{32,96},{64,0},{96,32},{1,65},{33,97},{65,1},{97,33},{2,66}... | collective-permute-start | bytes 2064392 | tf_op jit(solution)/shard_map/ppermute | solution.py:234
  36.5 1.1 collective-permute-start.4
  37.6 19.2 %back.1 = (bf16[1,16,16,1536]{3,2,1,0:T(8,128)(2,1)}, bf16[12,64,128]{2,1,0:T(8,128)(2,1)}) custom-call(s32[1]{0:T(128)} %bitcast.core_ref, bf16[256,1536]{1,0:T(8,128)(2,1)} %get-tuple-element.51.away_ref, bf16[256,1536]{1,0:T(8,128)(2,1)} %get-tuple-element.52.near_ref, f32[256,128]{1,0:T(8,128)} %get-tuple-element.53.sigma_ref, f32[1536]{0:T(1024)} %gain_ref.3, ...), custom_call_target="tpu_custom_call" | custom-call | flops 1000 | bytes 1000 | tf_op jit(solution)/shard_map/back/pallas_call | solution.py:339
  56.9 1.8 %all-to-all-done.refs_0_ = bf16[4,4,96,640]{3,2,1,0:T(8,128)(2,1)S(1)} async-done(((bf16[4,4,96,640]{3,2,1,0:T(8,128)(2,1)}), bf16[4,4,96,640]{3,2,1,0:T(8,128)(2,1)S(1)}, u32[]{:S(2)}, u32[]{:S(2)}) %all-to-all-start) | async-done | bytes 1966112 | tf_op jit(solution)/shard_map/all_to_all | solution.py:427
  58.6 0.0 copy-start
  58.6 8.6 %all-to-all-start.1 = ((bf16[16,48,128]{2,1,0:T(8,128)(2,1)}), bf16[16,48,128]{2,1,0:T(8,128)(2,1)S(1)}, u32[]{:S(2)}, u32[]{:S(2)}) async-start(bf16[16,48,128]{2,1,0:T(8,128)(2,1)} %bitcast.9), calls=%async_computation.1 | async-start | bytes 393216 | tf_op jit(solution)/shard_map/all_to_all | solution.py:427
  67.2 0.0 copy-done
  67.2 2.4 %sum_pieces.2 = (bf16[96,640]{1,0:T(8,128)(2,1)}, bf16[96,640]{1,0:T(8,128)(2,1)}, bf16[96,640]{1,0:T(8,128)(2,1)}, bf16[96,640]{1,0:T(8,128)(2,1)}) custom-call(bf16[4,4,96,640]{3,2,1,0:T(8,128)(2,1)} %copy-done), custom_call_target="tpu_custom_call" | custom-call | flops 1000 | bytes 1000 | tf_op jit(solution)/shard_map/sum_pieces/pallas_call | solution.py:222
  69.6 0.0 copy-start.5
  69.6 1.2 collective-permute-start.5
  70.9 2.5 %collective-permute-start.6 = (bf16[96,640]{1,0:T(8,128)(2,1)}, bf16[96,640]{1,0:T(8,128)(2,1)S(1)}, u32[]{:S(2)}, u32[]{:S(2)}) collective-permute-start(bf16[96,640]{1,0:T(8,128)(2,1)} %get-tuple-element.75), channel_id=1, source_target_pairs={{0,64},{32,96},{64,0},{96,32},{1,65},{33,97},{65,1},{97,33},{2,66}... | collective-permute-start | bytes 368648 | tf_op jit(solution)/shard_map/ppermute | solution.py:234
  73.3 0.0 collective-permute-done.2.refs_1_
  73.3 0.0 copy-start.3
  73.3 1.2 collective-permute-start.7
  74.5 3.0 %all-to-all-done.1 = bf16[16,48,128]{2,1,0:T(8,128)(2,1)S(1)} async-done(((bf16[16,48,128]{2,1,0:T(8,128)(2,1)}), bf16[16,48,128]{2,1,0:T(8,128)(2,1)S(1)}, u32[]{:S(2)}, u32[]{:S(2)}) %all-to-all-start.1) | async-done | bytes 196640 | tf_op jit(solution)/shard_map/all_to_all | solution.py:427
  77.5 0.0 collective-permute-done.3.refs_2_
  77.5 0.0 copy-start.4
  77.6 0.0 collective-permute-done.4.refs_3_
  77.6 0.0 collective-permute-done.5
  77.6 2.0 %collective-permute-done.6 = bf16[96,640]{1,0:T(8,128)(2,1)S(1)} collective-permute-done((bf16[96,640]{1,0:T(8,128)(2,1)}, bf16[96,640]{1,0:T(8,128)(2,1)S(1)}, u32[]{:S(2)}, u32[]{:S(2)}) %collective-permute-start.6) | collective-permute-done | bytes 122912 | tf_op jit(solution)/shard_map/ppermute | solution.py:234
  79.6 0.0 collective-permute-done.7
  79.6 0.0 copy-done.3
  79.6 0.0 copy-done.4
  79.6 2.7 %sum_pieces.3 = (bf16[96,896]{1,0:T(8,128)(2,1)}, bf16[96,896]{1,0:T(8,128)(2,1)}, bf16[96,896]{1,0:T(8,128)(2,1)}, bf16[96,896]{1,0:T(8,128)(2,1)}) custom-call(bf16[4,96,896]{2,1,0:T(8,128)(2,1)} %get-tuple-element.77.refs_0_, bf16[4,96,896]{2,1,0:T(8,128)(2,1)} %copy-done.3, bf16[4,96,896]{2,1,0:T(8,128)(2,1)} %copy-done.4, ...), custom_call_target="tpu_custom_call" | custom-call | flops 1000 | bytes 1000 | tf_op jit(solution)/shard_map/sum_pieces/pallas_call | solution.py:222
  82.3 0.7 collective-permute-start.8
  83.0 2.4 %collective-permute-start.9 = (bf16[96,896]{1,0:T(8,128)(2,1)}, bf16[96,896]{1,0:T(8,128)(2,1)S(1)}, u32[]{:S(2)}, u32[]{:S(2)}) collective-permute-start(bf16[96,896]{1,0:T(8,128)(2,1)} %get-tuple-element.83), channel_id=1, source_target_pairs={{0,2},{128,130},{2,0},{130,128},{1,3},{129,131},{3,1},{131,129},{4... | collective-permute-start | bytes 516104 | tf_op jit(solution)/shard_map/ppermute | solution.py:234
  85.4 1.2 collective-permute-start.10
  86.6 0.7 broadcast_in_dim.6
  87.3 4.4 %all-to-all-start.2 = ((bf16[16,48,128]{2,1,0:T(8,128)(2,1)}), bf16[16,48,128]{2,1,0:T(8,128)(2,1)S(1)}, u32[]{:S(2)}, u32[]{:S(2)}) async-start(bf16[16,48,128]{2,1,0:T(8,128)(2,1)} %broadcast_in_dim.6), calls=%async_computation.2 | async-start | bytes 393216 | tf_op jit(solution)/shard_map/all_to_all | solution.py:427
  91.8 0.0 copy-done.5
  91.8 0.0 collective-permute-done.8
  91.8 0.7 collective-permute-done.9
  92.5 0.2 collective-permute-done.10
  92.7 1.0 add_add_fusion
  93.7 0.4 convert_element_type.23
  94.1 4.7 %all-to-all-done.2 = bf16[16,48,128]{2,1,0:T(8,128)(2,1)S(1)} async-done(((bf16[16,48,128]{2,1,0:T(8,128)(2,1)}), bf16[16,48,128]{2,1,0:T(8,128)(2,1)S(1)}, u32[]{:S(2)}, u32[]{:S(2)}) %all-to-all-start.2) | async-done | bytes 196640 | tf_op jit(solution)/shard_map/all_to_all | solution.py:427
  98.9 26.2 %all_to_all.20.received_ref = bf16[16,120,128]{2,1,0:T(8,128)(2,1)} all-to-all(bf16[16,120,128]{2,1,0:T(8,128)(2,1)S(1)} %pad_maximum_fusion), channel_id=1, replica_groups=mesh['y_lo'=2,'x'=4,'z'=8,'y_hi'=2,'core'=2] {'z','core'}, dimensions={0} | all-to-all | bytes 983040 | tf_op jit(solution)/shard_map/all_to_all | solution.py:427
  125.1 1.9 %finish.1 = (f32[6,3072]{1,0:T(8,128)}, f32[3072]{0:T(1024)}, f32[1536]{0:T(1024)}, f32[1536]{0:T(1024)}, f32[49,1536]{1,0:T(8,128)}, /*index=5*/f32[1536]{0:T(1024)}) custom-call(bf16[16,120,128]{2,1,0:T(8,128)(2,1)} %all_to_all.20.received_ref), custom_call_target="tpu_custom_call" | custom-call | flops 1000 | bytes 1000 | tf_op jit(solution)/shard_map/finish/pallas_call | solution.py:410
  (7 shorter events, 0.2 us)
Async XLA Ops:
  15.0 5.4 %collective-permute-start.1 = (bf16[256,1536]{1,0:T(8,128)(2,1)}, bf16[256,1536]{1,0:T(8,128)(2,1)S(1)}, u32[]{:S(2)}, u32[]{:S(2)}) collective-permute-start(bf16[256,1536]{1,0:T(8,128)(2,1)} %get-tuple-element.51.away_ref), channel_id=1, source_target_pairs={{0,1},{1,0},{2,3},{3,2},{4,5},{5,4},{6,7},{7,6},{8,9},{9,8},{10,11... | collective-permute-start | bytes 2359304 | tf_op jit(solution)/shard_map/ppermute | solution.py:448
  18.3 3.2 %collective-permute-start = (bf16[4,2,2,96,256]{4,3,2,1,0:T(8,128)(2,1)}, bf16[4,2,2,96,256]{4,3,2,1,0:T(8,128)(2,1)S(1)}, u32[]{:S(2)}, u32[]{:S(2)}) collective-permute-start(bf16[4,2,2,96,256]{4,3,2,1,0:T(8,128)(2,1)} %get-tuple-element.55), channel_id=1, source_target_pairs={{0,1},{1,0},{2,3},{3,2},{4,5},{5,4},{6,7},{7,6},{8,9},{9,8},{10,11... | collective-permute-start | bytes 2359304 | tf_op jit(solution)/shard_map/ppermute | solution.py:449
  20.4 1.1 copy-start.1
  21.5 0.9 copy-start.2
  30.4 28.2 %all-to-all-start = ((bf16[4,4,96,640]{3,2,1,0:T(8,128)(2,1)}), bf16[4,4,96,640]{3,2,1,0:T(8,128)(2,1)S(1)}, u32[]{:S(2)}, u32[]{:S(2)}) async-start(bf16[4,4,96,640]{3,2,1,0:T(8,128)(2,1)} %get-tuple-element.64), calls=%async_computation | async-start | bytes 3932160 | tf_op jit(solution)/shard_map/all_to_all | solution.py:427
  34.0 39.3 %collective-permute-start.2 = (bf16[4,96,896]{2,1,0:T(8,128)(2,1)}, bf16[4,96,896]{2,1,0:T(8,128)(2,1)S(1)}, u32[]{:S(2)}, u32[]{:S(2)}) collective-permute-start(bf16[4,96,896]{2,1,0:T(8,128)(2,1)} %get-tuple-element.61), channel_id=1, source_target_pairs={{0,32},{32,64},{64,96},{96,0},{1,33},{33,65},{65,97},{97,1},{2,34}... | collective-permute-start | bytes 2064392 | tf_op jit(solution)/shard_map/ppermute | solution.py:234
  34.1 43.5 %collective-permute-start.3 = (bf16[4,96,896]{2,1,0:T(8,128)(2,1)}, bf16[4,96,896]{2,1,0:T(8,128)(2,1)S(1)}, u32[]{:S(2)}, u32[]{:S(2)}) collective-permute-start(bf16[4,96,896]{2,1,0:T(8,128)(2,1)} %get-tuple-element.62), channel_id=1, source_target_pairs={{0,64},{32,96},{64,0},{96,32},{1,65},{33,97},{65,1},{97,33},{2,66}... | collective-permute-start | bytes 2064392 | tf_op jit(solution)/shard_map/ppermute | solution.py:234
  36.5 41.1 %collective-permute-start.4 = (bf16[4,96,896]{2,1,0:T(8,128)(2,1)}, bf16[4,96,896]{2,1,0:T(8,128)(2,1)}, u32[]{:S(2)}, u32[]{:S(2)}) collective-permute-start(bf16[4,96,896]{2,1,0:T(8,128)(2,1)} %get-tuple-element.63), channel_id=1, source_target_pairs={{0,96},{32,0},{64,32},{96,64},{1,97},{33,1},{65,33},{97,65},{2,98}... | collective-permute-start | bytes 2064392 | tf_op jit(solution)/shard_map/ppermute | solution.py:234
  58.6 8.6 %copy-start = (bf16[4,4,96,640]{3,2,1,0:T(8,128)(2,1)}, bf16[4,4,96,640]{3,2,1,0:T(8,128)(2,1)S(1)}, u32[]{:S(2)}) copy-start(bf16[4,4,96,640]{3,2,1,0:T(8,128)(2,1)S(1)} %all-to-all-done.refs_0_) | copy-start | bytes 5898244
  58.6 18.9 %all-to-all-start.1 = ((bf16[16,48,128]{2,1,0:T(8,128)(2,1)}), bf16[16,48,128]{2,1,0:T(8,128)(2,1)S(1)}, u32[]{:S(2)}, u32[]{:S(2)}) async-start(bf16[16,48,128]{2,1,0:T(8,128)(2,1)} %bitcast.9), calls=%async_computation.1 | async-start | bytes 393216 | tf_op jit(solution)/shard_map/all_to_all | solution.py:427
  69.6 22.1 %copy-start.5 = (bf16[96,640]{1,0:T(8,128)(2,1)S(1)}, bf16[96,640]{1,0:T(8,128)(2,1)}, u32[]{:S(2)}) copy-start(bf16[96,640]{1,0:T(8,128)(2,1)} %get-tuple-element.85) | copy-start | bytes 368644
  69.6 7.9 %collective-permute-start.5 = (bf16[96,640]{1,0:T(8,128)(2,1)}, bf16[96,640]{1,0:T(8,128)(2,1)S(1)}, u32[]{:S(2)}, u32[]{:S(2)}) collective-permute-start(bf16[96,640]{1,0:T(8,128)(2,1)} %get-tuple-element.74), channel_id=1, source_target_pairs={{0,32},{32,64},{64,96},{96,0},{1,33},{33,65},{65,97},{97,1},{2,34}... | collective-permute-start | bytes 368648 | tf_op jit(solution)/shard_map/ppermute | solution.py:234
  70.9 8.7 %collective-permute-start.6 = (bf16[96,640]{1,0:T(8,128)(2,1)}, bf16[96,640]{1,0:T(8,128)(2,1)S(1)}, u32[]{:S(2)}, u32[]{:S(2)}) collective-permute-start(bf16[96,640]{1,0:T(8,128)(2,1)} %get-tuple-element.75), channel_id=1, source_target_pairs={{0,64},{32,96},{64,0},{96,32},{1,65},{33,97},{65,1},{97,33},{2,66}... | collective-permute-start | bytes 368648 | tf_op jit(solution)/shard_map/ppermute | solution.py:234
  73.3 6.2 %copy-start.3 = (bf16[4,96,896]{2,1,0:T(8,128)(2,1)}, bf16[4,96,896]{2,1,0:T(8,128)(2,1)S(1)}, u32[]{:S(2)}) copy-start(bf16[4,96,896]{2,1,0:T(8,128)(2,1)S(1)} %collective-permute-done.2.refs_1_) | copy-start | bytes 2064388
  73.3 6.2 %collective-permute-start.7 = (bf16[96,640]{1,0:T(8,128)(2,1)}, bf16[96,640]{1,0:T(8,128)(2,1)S(1)}, u32[]{:S(2)}, u32[]{:S(2)}) collective-permute-start(bf16[96,640]{1,0:T(8,128)(2,1)} %get-tuple-element.76), channel_id=1, source_target_pairs={{0,96},{32,0},{64,32},{96,64},{1,97},{33,1},{65,33},{97,65},{2,98}... | collective-permute-start | bytes 368648 | tf_op jit(solution)/shard_map/ppermute | solution.py:234
  77.5 2.0 %copy-start.4 = (bf16[4,96,896]{2,1,0:T(8,128)(2,1)}, bf16[4,96,896]{2,1,0:T(8,128)(2,1)S(1)}, u32[]{:S(2)}) copy-start(bf16[4,96,896]{2,1,0:T(8,128)(2,1)S(1)} %collective-permute-done.3.refs_2_) | copy-start | bytes 2064388
  82.3 9.5 %collective-permute-start.8 = (bf16[96,896]{1,0:T(8,128)(2,1)}, bf16[96,896]{1,0:T(8,128)(2,1)S(1)}, u32[]{:S(2)}, u32[]{:S(2)}) collective-permute-start(bf16[96,896]{1,0:T(8,128)(2,1)} %get-tuple-element.82), channel_id=1, source_target_pairs={{0,128},{128,2},{2,130},{130,0},{1,129},{129,3},{3,131},{131,1},{4... | collective-permute-start | bytes 516104 | tf_op jit(solution)/shard_map/ppermute | solution.py:234
  83.0 9.5 %collective-permute-start.9 = (bf16[96,896]{1,0:T(8,128)(2,1)}, bf16[96,896]{1,0:T(8,128)(2,1)S(1)}, u32[]{:S(2)}, u32[]{:S(2)}) collective-permute-start(bf16[96,896]{1,0:T(8,128)(2,1)} %get-tuple-element.83), channel_id=1, source_target_pairs={{0,2},{128,130},{2,0},{130,128},{1,3},{129,131},{3,1},{131,129},{4... | collective-permute-start | bytes 516104 | tf_op jit(solution)/shard_map/ppermute | solution.py:234
  85.4 7.3 %collective-permute-start.10 = (bf16[96,896]{1,0:T(8,128)(2,1)}, bf16[96,896]{1,0:T(8,128)(2,1)S(1)}, u32[]{:S(2)}, u32[]{:S(2)}) collective-permute-start(bf16[96,896]{1,0:T(8,128)(2,1)} %get-tuple-element.84), channel_id=1, source_target_pairs={{0,130},{128,0},{2,128},{130,2},{1,131},{129,1},{3,129},{131,3},{4... | collective-permute-start | bytes 516104 | tf_op jit(solution)/shard_map/ppermute | solution.py:234
  87.3 11.5 %all-to-all-start.2 = ((bf16[16,48,128]{2,1,0:T(8,128)(2,1)}), bf16[16,48,128]{2,1,0:T(8,128)(2,1)S(1)}, u32[]{:S(2)}, u32[]{:S(2)}) async-start(bf16[16,48,128]{2,1,0:T(8,128)(2,1)} %broadcast_in_dim.6), calls=%async_computation.2 | async-start | bytes 393216 | tf_op jit(solution)/shard_map/all_to_all | solution.py:427

commit v8 on v7

--- a/solution.py
+++ b/solution.py
@@ -16,32 +16,89 @@
 SMALL_ROWS = 64
 
 
-def front_kernel(
-    core_ref, image_ref, taps_ref, bias_ref, gain_ref, shift_ref, order_ref, b_ref, w_hbm, cot_hbm,
-    unit_out, sigma_ref, turned_ref, away_out, near_out, sums_ref,
-    padded, conv, unit, normed, weights, cots, grads, in_sems, out_sems,
-):
-    side, feat = image_ref.shape[1], image_ref.shape[3]
+def hidden_grads(first, normed, b_ref, sums_ref, loads, weights, cots, grads, target, sems):
     parts, _, width = weights.shape
-    half = parts // 2
-    core = core_ref[0]
-
-    def column(part):
-        owner = 1 - core if part < half else core
-        return pl.multiple_of((owner * half + part % half) * width, width)
-
+    stores = []
+    for part in range(parts):
+        for load in loads[part]:
+            load.wait()
+        pre_act = jnp.dot(normed[...], weights[part], preferred_element_type=jnp.float32)
+        pre_act = pre_act + b_ref[:, pl.ds(pl.multiple_of(first + part * width, width), width)]
+        slope = 0.5 * (1.0 + lax.erf(pre_act * 0.7071067811865476)) + pre_act * jnp.exp(
+            -0.5 * pre_act * pre_act
+        ) * 0.3989422804014327
+        grad = (cots[part].astype(jnp.float32) * slope).astype(jnp.bfloat16)
+        grads[part] = grad
+        here = slice(part * width, (part + 1) * width)
+        sums_ref[:, here] = jnp.sum(grad.astype(jnp.float32), axis=0, keepdims=True)
+        stores.append(pltpu.make_async_copy(grads.at[part], target.at[:, here], sems.at[part]))
+        stores[-1].start()
+    return stores
+
+
+def start_loads(first, w_hbm, cot_hbm, weights, cots, sems):
+    parts, _, width = weights.shape
     loads = []
     for part in range(parts):
-        columns = pl.ds(column(part), width)
+        columns = pl.ds(pl.multiple_of(first + part * width, width), width)
         loads.append(
             (
-                pltpu.make_async_copy(w_hbm.at[:, columns], weights.at[part], in_sems.at[2 * part]),
-                pltpu.make_async_copy(cot_hbm.at[0, :, columns], cots.at[part], in_sems.at[2 * part + 1]),
+                pltpu.make_async_copy(w_hbm.at[:, columns], weights.at[part], sems.at[2 * part]),
+                pltpu.make_async_copy(cot_hbm.at[0, :, columns], cots.at[part], sems.at[2 * part + 1]),
             )
         )
     for pair in loads:
         pair[0].start()
         pair[1].start()
+    return loads
+
+
+def near_kernel(
+    core_ref, normed_ref, b_ref, w_hbm, cot_hbm, near_out, sums_ref, weights, cots, grads, in_sems, out_sems
+):
+    parts, _, width = weights.shape
+    first = core_ref[0] * (parts * width)
+    loads = start_loads(first, w_hbm, cot_hbm, weights, cots, in_sems)
+    for copy in hidden_grads(first, normed_ref, b_ref, sums_ref, loads, weights, cots, grads, near_out, out_sems):
+        copy.wait()
+
+
+def near_half(core, normed, b_row, w_up, cot, parts=4):
+    cells, feat = normed.shape
+    hid = w_up.shape[1]
+    width = hid // 2 // parts
+    whole = pl.BlockSpec(memory_space=pltpu.VMEM)
+    remain = pl.BlockSpec(memory_space=pl.ANY)
+    return pl.pallas_call(
+        near_kernel,
+        name="near_half",
+        in_specs=[pl.BlockSpec(memory_space=pltpu.SMEM), whole, whole, remain, remain],
+        out_specs=[remain, whole],
+        out_shape=(
+            jax.ShapeDtypeStruct((cells, hid // 2), jnp.bfloat16),
+            jax.ShapeDtypeStruct((1, hid // 2), jnp.float32),
+        ),
+        scratch_shapes=[
+            pltpu.VMEM((parts, feat, width), jnp.bfloat16),
+            pltpu.VMEM((parts, cells, width), jnp.bfloat16),
+            pltpu.VMEM((parts, cells, width), jnp.bfloat16),
+            pltpu.SemaphoreType.DMA((2 * parts,)),
+            pltpu.SemaphoreType.DMA((parts,)),
+        ],
+        compiler_params=pltpu.CompilerParams(vmem_limit_bytes=VMEM_LIMIT),
+        cost_estimate=SMALL,
+    )(core, normed, b_row, w_up, cot)
+
+
+def front_kernel(
+    core_ref, image_ref, taps_ref, bias_ref, gain_ref, shift_ref, order_ref, b_ref, w_hbm, cot_hbm,
+    unit_out, sigma_ref, turned_ref, normed_out, away_out, sums_ref,
+    padded, conv, unit, normed, weights, cots, grads, in_sems, out_sems, grad_sems,
+):
+    side, feat = image_ref.shape[1], image_ref.shape[3]
+    parts, _, width = weights.shape
+    first_unit = (1 - core_ref[0]) * (parts * width)
+    loads = start_loads(first_unit, w_hbm, cot_hbm, weights, cots, in_sems)
 
     blank = jnp.zeros((side, EDGE, LANES), jnp.float32)
     padded[:, 0:EDGE, :] = blank
@@ -81,8 +138,12 @@
         sigma_ref[cells, :] = jnp.broadcast_to(inv_sigma, (side, LANES))
         normed[cells, :] = (scaled * gain + shift).astype(jnp.bfloat16)
 
-    unit_copy = pltpu.make_async_copy(unit, unit_out, out_sems.at[0])
-    unit_copy.start()
+    stores = [
+        pltpu.make_async_copy(normed, normed_out, out_sems.at[0]),
+        pltpu.make_async_copy(unit, unit_out, out_sems.at[1]),
+    ]
+    for copy in stores:
+        copy.start()
 
     group = order_ref.shape[0]
     rows = turned_ref.shape[3]
@@ -99,25 +160,9 @@
                 first = (within * 2 + y_hi) * rows
                 turned_ref[2 * pair + within, y_hi, y_lo] = turned[first : first + rows]
 
-    stores = [unit_copy]
-    for part in range(parts):
-        loads[part][0].wait()
-        loads[part][1].wait()
-        columns = pl.ds(column(part), width)
-        pre_act = jnp.dot(normed[...], weights[part], preferred_element_type=jnp.float32)
-        pre_act = pre_act + b_ref[:, columns]
-        slope = 0.5 * (1.0 + lax.erf(pre_act * 0.7071067811865476)) + pre_act * jnp.exp(
-            -0.5 * pre_act * pre_act
-        ) * 0.3989422804014327
-        grad = (cots[part].astype(jnp.float32) * slope).astype(jnp.bfloat16)
-        grads[part] = grad
-        sums_ref[:, columns] = jnp.sum(grad.astype(jnp.float32), axis=0, keepdims=True)
-        target = away_out if part < half else near_out
-        copy = pltpu.make_async_copy(
-            grads.at[part], target.at[:, (part % half) * width : (part % half + 1) * width], out_sems.at[1 + part]
-        )
-        copy.start()
-        stores.append(copy)
+    stores += hidden_grads(
+        first_unit, normed, b_ref, sums_ref, loads, weights, cots, grads, away_out, grad_sems
+    )
     for copy in stores:
         copy.wait()
 
@@ -129,12 +174,12 @@
     return jnp.asarray(np.eye(width, dtype=np.float32)[target], jnp.bfloat16)
 
 
-def front(core, image, taps, bias, gain, shift, w_up, b_row, cot, along_z, parts=4):
+def front(core, image, taps, bias, gain, shift, w_up, b_row, cot, along_z, parts=2):
     side, feat = image.shape[1], image.shape[3]
     cells = side * side
     hid = w_up.shape[1]
     rows = feat // 16
-    width = hid // parts
+    width = hid // 2 // parts
     whole = pl.BlockSpec(memory_space=pltpu.VMEM)
     remain = pl.BlockSpec(memory_space=pl.ANY)
     return pl.pallas_call(
@@ -146,9 +191,9 @@
             jax.ShapeDtypeStruct((cells, feat), jnp.float32),
             jax.ShapeDtypeStruct((cells, LANES), jnp.float32),
             jax.ShapeDtypeStruct((4, 2, 2, rows, cells), jnp.bfloat16),
+            jax.ShapeDtypeStruct((cells, feat), jnp.bfloat16),
             jax.ShapeDtypeStruct((cells, hid // 2), jnp.bfloat16),
-            jax.ShapeDtypeStruct((cells, hid // 2), jnp.bfloat16),
-            jax.ShapeDtypeStruct((1, hid), jnp.float32),
+            jax.ShapeDtypeStruct((1, hid // 2), jnp.float32),
         ),
         scratch_shapes=[
             pltpu.VMEM((side, side + 2 * EDGE, LANES), jnp.float32),
@@ -159,14 +204,16 @@
             pltpu.VMEM((parts, cells, width), jnp.bfloat16),
             pltpu.VMEM((parts, cells, width), jnp.bfloat16),
             pltpu.SemaphoreType.DMA((2 * parts,)),
-            pltpu.SemaphoreType.DMA((1 + parts,)),
+            pltpu.SemaphoreType.DMA((2,)),
+            pltpu.SemaphoreType.DMA((parts,)),
         ],
         compiler_params=pltpu.CompilerParams(vmem_limit_bytes=VMEM_LIMIT),
         cost_estimate=SMALL,
     )(core, image, taps, bias, gain, shift, channel_order(rows, along_z), b_row, w_up, cot)
 
 
-def product_kernel(place_ref, near_t_ref, far_t_ref, near_ref, far_ref, *out_refs):
+def product_kernel(place_ref, near_t_ref, far_t_ref, near_ref, far_ref, *refs):
+    out_refs, pieces, sems = refs[:5], refs[5], refs[6]
     _, along_y, rows, cells = near_t_ref.shape
     block = (
         jnp.dot(near_t_ref[...].reshape(along_y * rows, cells), near_ref[...], preferred_element_type=jnp.float32)
@@ -174,12 +221,20 @@
     ).astype(jnp.bfloat16)
     columns = out_refs[0].shape[2]
     out_refs[4][...] = block[:, columns:].reshape(out_refs[4].shape)
-    for steps in range(4):
-
-        @pl.when(pl.program_id(0) == steps)
+    step = pl.program_id(0)
+    for y in range(along_y):
+        pieces[step, lax.rem(y - place_ref[1] + 4, 4)] = block[y * rows : (y + 1) * rows, :columns]
+    copies = [pltpu.make_async_copy(pieces.at[i], out_refs[i], sems.at[i]) for i in range(4)]
+    for i in range(4):
+
+        @pl.when(step == i)
         def _():
-            for y in range(along_y):
-                out_refs[steps][lax.rem(y - place_ref[1] + 4, 4)] = block[y * rows : (y + 1) * rows, :columns]
+            copies[i].start()
+
+    @pl.when(step == 3)
+    def _():
+        for copy in copies:
+            copy.wait()
 
 
 def product(place, near_t, far_t, near, far, columns):
@@ -194,8 +249,9 @@
             num_scalar_prefetch=1,
             grid=(4,),
             in_specs=[left, left, right, right],
-            out_specs=[pl.BlockSpec((4, rows, columns), lambda i, p: (0, 0, 0))] * 4
+            out_specs=[pl.BlockSpec(memory_space=pl.ANY)] * 4
             + [pl.BlockSpec((4, 1, rows, others), lambda i, p: (0, i, 0, 0))],
+            scratch_shapes=[pltpu.VMEM((4, 4, rows, columns), jnp.bfloat16), pltpu.SemaphoreType.DMA((4,))],
         ),
         out_shape=[jax.ShapeDtypeStruct((4, rows, columns), jnp.bfloat16)] * 4
         + [jax.ShapeDtypeStruct((4, 4, rows, others), jnp.bfloat16)],
@@ -239,7 +295,7 @@
 
 
 def back_kernel(
-    core_ref, away_ref, near_ref, sigma_ref, gain_ref, up_first_ref, up_second_ref, image_ref, res_ref, taps_ref,
+    core_ref, away_ref, near_ref, sigma_ref, gain_ref, near_sum_ref, away_sum_ref, image_ref, res_ref, taps_ref,
     unit_hbm, w_hbm, out_ref, sums_ref, weights, unit, total, norm_sums, padded, image, small, sems,
 ):
     side = image_ref.shape[1]
@@ -321,15 +377,15 @@
             small[tap : tap + 1, :] = jnp.sum(parts_here[turn_row], axis=0, keepdims=True)
     small[49:51, :] = norm_sums[0:2, lanes]
     small[51:52, :] = jnp.sum(bias_sum, axis=0, keepdims=True)
-    small[52:53, :] = up_first_ref[...]
-    small[53:54, :] = up_second_ref[...]
+    small[52:53, :] = jnp.where(core_ref[0] == 0, near_sum_ref[...], away_sum_ref[...])
+    small[53:54, :] = jnp.where(core_ref[0] == 0, away_sum_ref[...], near_sum_ref[...])
     small[54:, :] = jnp.zeros((SMALL_ROWS - 54, LANES), jnp.float32)
     sums_ref[0] = small[...].astype(jnp.bfloat16)
     for row in range(side):
         out_ref[0, row] = sums[row].astype(jnp.bfloat16)
 
 
-def back(core, away, near, w_up, unit, sigma, gain, up_sums, image, residual, taps, parts=4):
+def back(core, away, near, w_up, unit, sigma, gain, near_sums, away_sums, image, residual, taps, parts=4):
     cells, feat = unit.shape
     side = image.shape[1]
     width = w_up.shape[1] // parts
@@ -344,7 +400,7 @@
         + [whole] * 4
         + [
             pl.BlockSpec((1, LANES), lambda i: (0, i)),
-            pl.BlockSpec((1, LANES), lambda i: (0, i + feat // LANES)),
+            pl.BlockSpec((1, LANES), lambda i: (0, i)),
             picture,
             picture,
             pl.BlockSpec((49, LANES), lambda i: (0, i)),
@@ -368,7 +424,7 @@
         ],
         compiler_params=pltpu.CompilerParams(vmem_limit_bytes=VMEM_LIMIT),
         cost_estimate=SMALL,
-    )(core, away, near, sigma, gain, up_sums, up_sums, image, residual, taps, unit, w_up)
+    )(core, away, near, sigma, gain, near_sums, away_sums, image, residual, taps, unit, w_up)
 
 
 def finish_kernel(inverse_count, received_ref, owned_ref, up_ref, gain_ref, shift_ref, taps_ref, bias_ref):
@@ -442,11 +498,13 @@
     place = jnp.stack([lax.axis_index("x"), y_index]).astype(jnp.int32)
     swap = [(0, 1), (1, 0)]
 
-    unit, sigma, turned, away, near, up_sums = front(
-        mine, images, dw_weight, dw_bias, ln_gain, ln_bias, w_up, b_up.reshape(1, -1), hidden_cot, along_z
+    b_row = b_up.reshape(1, -1)
+    unit, sigma, turned, normed, away, away_sums = front(
+        mine, images, dw_weight, dw_bias, ln_gain, ln_bias, w_up, b_row, hidden_cot, along_z
     )
+    far_turned = lax.ppermute(turned, "core", swap)
     far = lax.ppermute(away, "core", swap)
-    far_turned = lax.ppermute(turned, "core", swap)
+    near, near_sums = near_half(mine, normed, b_row, w_up, hidden_cot)
     cells = unit.shape[0]
     *part_a, part_b = product(
         place, turned.reshape(4, 4, -1, cells), far_turned.reshape(4, 4, -1, cells), near, far, 7 * hid // 24
@@ -456,18 +514,17 @@
     part_b = swap_pieces(part_b, ("y_hi", "y_lo"))
 
     grad_input, small = back(
-        mine, away, near, w_up, unit, sigma, ln_gain, up_sums, images, residual_cot, dw_weight
+        mine, away, near, w_up, unit, sigma, ln_gain, near_sums, away_sums, images, residual_cot, dw_weight
     )
     part_b, small = lax.optimization_barrier((part_b, small))
 
     around = ("z", "core")
     small = swap_pieces(small.reshape(2 * along_z, -1, LANES), around)
     small = total_of(small).astype(jnp.bfloat16)
+    part_b = to_owners(sum_pieces([part_b]), "x")
     part_a, small = lax.optimization_barrier((part_a, small))
+    part_b, small = lax.optimization_barrier((part_b, small))
     small = swap_pieces(jnp.broadcast_to(small, (16,) + small.shape), plane)
-
-    part_b = to_owners(sum_pieces([part_b]), "x")
-    part_a, part_b = lax.optimization_barrier((part_a, part_b))
     part_a = to_owners(sum_pieces(part_a), ("y_lo", "y_hi"))
     last = jnp.concatenate([total_of(jnp.stack(part_a)), total_of(jnp.stack(part_b))], axis=1)
     last = last.astype(jnp.bfloat16).reshape(2 * along_z, -1, LANES)

time: 128 us -> 132 us (1.031)
  Pallas kernels: 48.5 us -> 52.4 us
  starting transfers between devices: 32.8 us -> 35.1 us
    pallas_call x0 -> x1, Pallas kernels: none -> 6.77 us  [near_half(): pl.pallas_call(near_kernel, name='near_half', in_specs=[pl.BlockSpec(memo...]
    ppermute x9, waiting for transfers between devices: 2.88 us -> 8.95 us  [to_owners(): lax.ppermute(piece, axes, [(named[i], named[(i + d) % 4]) for i in range(...]
    all_to_all x3, waiting for transfers between devices: 9.5 us -> 4.85 us  [swap_pieces(): return lax.all_to_all(values, axes, 0, 0, tiled=True)]
    pallas_call x1, Pallas kernels: 14.3 us -> 11.8 us  [front(): pl.pallas_call(front_kernel, name='front', in_specs=[pl.BlockSpec(memory_...]
    all_to_all x3, starting transfers between devices: 16.6 us -> 18.2 us  [swap_pieces(): return lax.all_to_all(values, axes, 0, 0, tiled=True)]
    ppermute x1, waiting for transfers between devices: 1.44 us -> 0.01 us  [per_device(): far = lax.ppermute(away, 'core', swap)]
  transfers between devices with their start and end apart: 14 -> 14, of which waited for: 8 -> 5; matrix products, arithmetic and copies ran while one was open for 2% -> 2% of each run, Pallas kernels for 17% -> 24%
where the time goes in v8:
time: 132 us; the launch traced here: 131 us
  Pallas kernels  52.4 us (40%)
  starting transfers between devices  35.1 us (27%)
  blocking collectives  24.9 us (19%)
  waiting for transfers between devices  13.8 us (10%)
  local copies, waits for them, and re-layouts  2.28 us (2%)
  other arithmetic  1.74 us (1%)
    all_to_all x1, blocking collectives, swap_pieces(): return lax.all_to_all(values, axes, 0, 0, tiled=True)  24.9 us
    pallas_call x1, Pallas kernels, back(): pl.pallas_call(back_kernel, name='back', grid=(feat // LANES,), in_specs=...  19.1 us
    all_to_all x3, starting transfers between devices, swap_pieces(): return lax.all_to_all(values, axes, 0, 0, tiled=True)  18.2 us
    ppermute x9, starting transfers between devices, to_owners(): lax.ppermute(piece, axes, [(named[i], named[(i + d) % 4]) for i in range(...  13.4 us
    pallas_call x1, Pallas kernels, front(): pl.pallas_call(front_kernel, name='front', in_specs=[pl.BlockSpec(memory_...  11.8 us
    ppermute x9, waiting for transfers between devices, to_owners(): lax.ppermute(piece, axes, [(named[i], named[(i + d) % 4]) for i in range(...  8.95 us
    pallas_call x1, Pallas kernels, product(): pl.pallas_call(product_kernel, name='product', grid_spec=pltpu.PrefetchSc...  7.67 us
    pallas_call x1, Pallas kernels, near_half(): pl.pallas_call(near_kernel, name='near_half', in_specs=[pl.BlockSpec(memo...  6.77 us
  transfers between devices with their start and end apart: 14, of which 5 were waited for; matrix products, arithmetic and copies ran while one was open for 2% of the time, Pallas kernels for 24%

profile of v8, /device:TPU:1, one launch (start us, length us, event | category | flops | bytes accessed | tf_op | source)
XLA Modules:
  0.0 131.1 jit_solution(10254638502382901979)
XLA Ops:
  0.6 11.8 %front.1 = (f32[256,1536]{1,0:T(8,128)}, f32[256,128]{1,0:T(8,128)}, bf16[4,2,2,96,256]{4,3,2,1,0:T(8,128)(2,1)}, bf16[256,1536]{1,0:T(8,128)(2,1)}, bf16[256,1536]{1,0:T(8,128)(2,1)}, /*index=5*/f32[1,1536]{1,0:T(1,128)}) custom-call(s32[1]{0:T(128)} %bitcast.core_ref, bf16[1,16,16,1536]{3,2,1,0:T(8,128)(2,1)} %image_ref.3, f32[49,1536]{1,0:T(8,128)} %taps_ref.3, ...), custom_call_target="tpu_custom_call" | custom-call | flops 1000 | bytes 1000 | tf_op jit(solution)/shard_map/front/pallas_call | solution.py:185
  12.5 3.3 %collective-permute-start.1 = (bf16[256,1536]{1,0:T(8,128)(2,1)}, bf16[256,1536]{1,0:T(8,128)(2,1)S(1)}, u32[]{:S(2)}, u32[]{:S(2)}) collective-permute-start(bf16[256,1536]{1,0:T(8,128)(2,1)} %get-tuple-element.50.away_ref), channel_id=1, source_target_pairs={{0,1},{1,0},{2,3},{3,2},{4,5},{5,4},{6,7},{7,6},{8,9},{9,8},{10,11... | collective-permute-start | bytes 2359304 | tf_op jit(solution)/shard_map/ppermute | solution.py:506
  15.8 0.1 collective-permute-start
  15.9 6.8 %near_half.1 = (bf16[256,1536]{1,0:T(8,128)(2,1)}, f32[1,1536]{1,0:T(1,128)}) custom-call(s32[1]{0:T(128)} %bitcast.core_ref, bf16[256,1536]{1,0:T(8,128)(2,1)} %get-tuple-element.51.normed_ref, f32[1,3072]{1,0:T(1,128)} %bitcast.11, bf16[1536,3072]{1,0:T(8,128)(2,1)} %w_hbm.5, bf16[1,256,3072]{2,1,0:T(8,128)(2,1)} %cot_hbm.3), custom_call_target="tpu_custom_call" | custom-call | flops 1000 | bytes 1000 | tf_op jit(solution)/shard_map/near_half/pallas_call | solution.py:72
  22.7 0.6 pad_add_fusion.place_ref
  23.3 0.0 collective-permute-done.1.far_ref
  23.3 0.0 copy-start.1
  23.3 0.0 collective-permute-done
  23.3 0.0 copy-start.2
  23.3 0.9 copy-done.1
  24.1 0.3 copy-done.2
  24.4 7.7 %product.1 = (bf16[4,96,896]{2,1,0:T(8,128)(2,1)}, bf16[4,96,896]{2,1,0:T(8,128)(2,1)}, bf16[4,96,896]{2,1,0:T(8,128)(2,1)}, bf16[4,96,896]{2,1,0:T(8,128)(2,1)}, bf16[4,4,96,640]{3,2,1,0:T(8,128)(2,1)}) custom-call(s32[2]{0:T(128)} %pad_add_fusion.place_ref, bf16[4,4,96,256]{3,2,1,0:T(8,128)(2,1)} %bitcast.7, bf16[4,4,96,256]{3,2,1,0:T(8,128)(2,1)} %bitcast.8, ...), custom_call_target="tpu_custom_call" | custom-call | flops 1000 | bytes 1000 | tf_op jit(solution)/shard_map/product/pallas_call | solution.py:245
  32.1 3.6 %all-to-all-start = ((bf16[4,4,96,640]{3,2,1,0:T(8,128)(2,1)}), bf16[4,4,96,640]{3,2,1,0:T(8,128)(2,1)S(1)}, u32[]{:S(2)}, u32[]{:S(2)}) async-start(bf16[4,4,96,640]{3,2,1,0:T(8,128)(2,1)} %get-tuple-element.61), calls=%async_computation | async-start | bytes 3932160 | tf_op jit(solution)/shard_map/all_to_all | solution.py:483
  35.7 0.1 collective-permute-start.5
  35.8 2.4 %collective-permute-start.6 = (bf16[4,96,896]{2,1,0:T(8,128)(2,1)}, bf16[4,96,896]{2,1,0:T(8,128)(2,1)S(1)}, u32[]{:S(2)}, u32[]{:S(2)}) collective-permute-start(bf16[4,96,896]{2,1,0:T(8,128)(2,1)} %get-tuple-element.70), channel_id=1, source_target_pairs={{0,64},{32,96},{64,0},{96,32},{1,65},{33,97},{65,1},{97,33},{2,66}... | collective-permute-start | bytes 2064392 | tf_op jit(solution)/shard_map/ppermute | solution.py:290
  38.2 1.2 collective-permute-start.7
  39.4 19.1 %back.1 = (bf16[1,16,16,1536]{3,2,1,0:T(8,128)(2,1)}, bf16[12,64,128]{2,1,0:T(8,128)(2,1)}) custom-call(s32[1]{0:T(128)} %bitcast.core_ref, bf16[256,1536]{1,0:T(8,128)(2,1)} %get-tuple-element.50.away_ref, bf16[256,1536]{1,0:T(8,128)(2,1)} %get-tuple-element.52.near_ref, f32[256,128]{1,0:T(8,128)} %get-tuple-element.53.sigma_ref, f32[1536]{0:T(1024)} %gain_ref.3, ...), custom_call_target="tpu_custom_call" | custom-call | flops 1000 | bytes 1000 | tf_op jit(solution)/shard_map/back/pallas_call | solution.py:395
  58.5 1.8 %all-to-all-done.refs_0_ = bf16[4,4,96,640]{3,2,1,0:T(8,128)(2,1)S(1)} async-done(((bf16[4,4,96,640]{3,2,1,0:T(8,128)(2,1)}), bf16[4,4,96,640]{3,2,1,0:T(8,128)(2,1)S(1)}, u32[]{:S(2)}, u32[]{:S(2)}) %all-to-all-start) | async-done | bytes 1966112 | tf_op jit(solution)/shard_map/all_to_all | solution.py:483
  60.3 0.0 copy-start
  60.3 8.6 %all-to-all-start.1 = ((bf16[16,48,128]{2,1,0:T(8,128)(2,1)}), bf16[16,48,128]{2,1,0:T(8,128)(2,1)S(1)}, u32[]{:S(2)}, u32[]{:S(2)}) async-start(bf16[16,48,128]{2,1,0:T(8,128)(2,1)} %bitcast.9), calls=%async_computation.1 | async-start | bytes 393216 | tf_op jit(solution)/shard_map/all_to_all | solution.py:483
  69.0 0.0 copy-done
  69.0 2.4 %sum_pieces.2 = (bf16[96,640]{1,0:T(8,128)(2,1)}, bf16[96,640]{1,0:T(8,128)(2,1)}, bf16[96,640]{1,0:T(8,128)(2,1)}, bf16[96,640]{1,0:T(8,128)(2,1)}) custom-call(bf16[4,4,96,640]{3,2,1,0:T(8,128)(2,1)} %copy-done), custom_call_target="tpu_custom_call" | custom-call | flops 1000 | bytes 1000 | tf_op jit(solution)/shard_map/sum_pieces/pallas_call | solution.py:278
  71.4 0.0 copy-start.5
  71.4 1.2 collective-permute-start.2
  72.6 2.4 %collective-permute-start.3 = (bf16[96,640]{1,0:T(8,128)(2,1)}, bf16[96,640]{1,0:T(8,128)(2,1)S(1)}, u32[]{:S(2)}, u32[]{:S(2)}) collective-permute-start(bf16[96,640]{1,0:T(8,128)(2,1)} %get-tuple-element.66), channel_id=1, source_target_pairs={{0,64},{32,96},{64,0},{96,32},{1,65},{33,97},{65,1},{97,33},{2,66}... | collective-permute-start | bytes 368648 | tf_op jit(solution)/shard_map/ppermute | solution.py:290
  75.1 0.0 collective-permute-done.5.refs_1_
  75.1 0.0 copy-start.3
  75.1 1.2 collective-permute-start.4
  76.2 3.0 %all-to-all-done.1 = bf16[16,48,128]{2,1,0:T(8,128)(2,1)S(1)} async-done(((bf16[16,48,128]{2,1,0:T(8,128)(2,1)}), bf16[16,48,128]{2,1,0:T(8,128)(2,1)S(1)}, u32[]{:S(2)}, u32[]{:S(2)}) %all-to-all-start.1) | async-done | bytes 196640 | tf_op jit(solution)/shard_map/all_to_all | solution.py:483
  79.3 0.0 collective-permute-done.6.refs_2_
  79.3 0.0 copy-start.4
  79.3 0.0 collective-permute-done.7.refs_3_
  79.3 0.0 collective-permute-done.2
  79.4 2.0 %collective-permute-done.3 = bf16[96,640]{1,0:T(8,128)(2,1)S(1)} collective-permute-done((bf16[96,640]{1,0:T(8,128)(2,1)}, bf16[96,640]{1,0:T(8,128)(2,1)S(1)}, u32[]{:S(2)}, u32[]{:S(2)}) %collective-permute-start.3) | collective-permute-done | bytes 122912 | tf_op jit(solution)/shard_map/ppermute | solution.py:290
  81.3 0.0 collective-permute-done.4
  81.3 0.7 broadcast_in_dim.6
  82.0 6.0 %all-to-all-start.2 = ((bf16[16,48,128]{2,1,0:T(8,128)(2,1)}), bf16[16,48,128]{2,1,0:T(8,128)(2,1)S(1)}, u32[]{:S(2)}, u32[]{:S(2)}) async-start(bf16[16,48,128]{2,1,0:T(8,128)(2,1)} %broadcast_in_dim.6), calls=%async_computation.2 | async-start | bytes 393216 | tf_op jit(solution)/shard_map/all_to_all | solution.py:483
  88.1 0.0 copy-done.3
  88.1 0.0 copy-done.4
  88.1 2.7 %sum_pieces.3 = (bf16[96,896]{1,0:T(8,128)(2,1)}, bf16[96,896]{1,0:T(8,128)(2,1)}, bf16[96,896]{1,0:T(8,128)(2,1)}, bf16[96,896]{1,0:T(8,128)(2,1)}) custom-call(bf16[4,96,896]{2,1,0:T(8,128)(2,1)} %get-tuple-element.75.refs_0_, bf16[4,96,896]{2,1,0:T(8,128)(2,1)} %copy-done.3, bf16[4,96,896]{2,1,0:T(8,128)(2,1)} %copy-done.4, ...), custom_call_target="tpu_custom_call" | custom-call | flops 1000 | bytes 1000 | tf_op jit(solution)/shard_map/sum_pieces/pallas_call | solution.py:278
  90.8 1.4 %collective-permute-start.8 = (bf16[96,896]{1,0:T(8,128)(2,1)}, bf16[96,896]{1,0:T(8,128)(2,1)S(1)}, u32[]{:S(2)}, u32[]{:S(2)}) collective-permute-start(bf16[96,896]{1,0:T(8,128)(2,1)} %get-tuple-element.80), channel_id=1, source_target_pairs={{0,128},{128,2},{2,130},{130,0},{1,129},{129,3},{3,131},{131,1},{4... | collective-permute-start | bytes 516104 | tf_op jit(solution)/shard_map/ppermute | solution.py:290
  92.2 2.4 %collective-permute-start.9 = (bf16[96,896]{1,0:T(8,128)(2,1)}, bf16[96,896]{1,0:T(8,128)(2,1)S(1)}, u32[]{:S(2)}, u32[]{:S(2)}) collective-permute-start(bf16[96,896]{1,0:T(8,128)(2,1)} %get-tuple-element.81), channel_id=1, source_target_pairs={{0,2},{128,130},{2,0},{130,128},{1,3},{129,131},{3,1},{131,129},{4... | collective-permute-start | bytes 516104 | tf_op jit(solution)/shard_map/ppermute | solution.py:290
  94.6 1.2 collective-permute-start.10
  95.7 0.0 copy-done.5
  95.8 3.4 %collective-permute-done.8 = bf16[96,896]{1,0:T(8,128)(2,1)S(1)} collective-permute-done((bf16[96,896]{1,0:T(8,128)(2,1)}, bf16[96,896]{1,0:T(8,128)(2,1)S(1)}, u32[]{:S(2)}, u32[]{:S(2)}) %collective-permute-start.8) | collective-permute-done | bytes 172064 | tf_op jit(solution)/shard_map/ppermute | solution.py:290
  99.1 3.6 %collective-permute-done.9 = bf16[96,896]{1,0:T(8,128)(2,1)S(1)} collective-permute-done((bf16[96,896]{1,0:T(8,128)(2,1)}, bf16[96,896]{1,0:T(8,128)(2,1)S(1)}, u32[]{:S(2)}, u32[]{:S(2)}) %collective-permute-start.9) | collective-permute-done | bytes 172064 | tf_op jit(solution)/shard_map/ppermute | solution.py:290
  102.8 0.0 collective-permute-done.10
  102.8 1.0 add_add_fusion
  103.8 0.4 convert_element_type.23
  104.1 0.0 all-to-all-done.2
  104.3 24.9 %all_to_all.20.received_ref = bf16[16,120,128]{2,1,0:T(8,128)(2,1)} all-to-all(bf16[16,120,128]{2,1,0:T(8,128)(2,1)S(1)} %pad_maximum_fusion), channel_id=1, replica_groups=mesh['y_lo'=2,'x'=4,'z'=8,'y_hi'=2,'core'=2] {'z','core'}, dimensions={0} | all-to-all | bytes 983040 | tf_op jit(solution)/shard_map/all_to_all | solution.py:483
  129.2 1.9 %finish.1 = (f32[6,3072]{1,0:T(8,128)}, f32[3072]{0:T(1024)}, f32[1536]{0:T(1024)}, f32[1536]{0:T(1024)}, f32[49,1536]{1,0:T(8,128)}, /*index=5*/f32[1536]{0:T(1024)}) custom-call(bf16[16,120,128]{2,1,0:T(8,128)(2,1)} %all_to_all.20.received_ref), custom_call_target="tpu_custom_call" | custom-call | flops 1000 | bytes 1000 | tf_op jit(solution)/shard_map/finish/pallas_call | solution.py:466
  (7 shorter events, 0.2 us)
Async XLA Ops:
  12.5 10.8 %collective-permute-start.1 = (bf16[256,1536]{1,0:T(8,128)(2,1)}, bf16[256,1536]{1,0:T(8,128)(2,1)S(1)}, u32[]{:S(2)}, u32[]{:S(2)}) collective-permute-start(bf16[256,1536]{1,0:T(8,128)(2,1)} %get-tuple-element.50.away_ref), channel_id=1, source_target_pairs={{0,1},{1,0},{2,3},{3,2},{4,5},{5,4},{6,7},{7,6},{8,9},{9,8},{10,11... | collective-permute-start | bytes 2359304 | tf_op jit(solution)/shard_map/ppermute | solution.py:506
  15.8 7.5 %collective-permute-start = (bf16[4,2,2,96,256]{4,3,2,1,0:T(8,128)(2,1)}, bf16[4,2,2,96,256]{4,3,2,1,0:T(8,128)(2,1)S(1)}, u32[]{:S(2)}, u32[]{:S(2)}) collective-permute-start(bf16[4,2,2,96,256]{4,3,2,1,0:T(8,128)(2,1)} %get-tuple-element.56), channel_id=1, source_target_pairs={{0,1},{1,0},{2,3},{3,2},{4,5},{5,4},{6,7},{7,6},{8,9},{9,8},{10,11... | collective-permute-start | bytes 2359304 | tf_op jit(solution)/shard_map/ppermute | solution.py:505
  23.3 0.9 copy-start.1
  23.3 1.2 copy-start.2
  32.1 28.2 %all-to-all-start = ((bf16[4,4,96,640]{3,2,1,0:T(8,128)(2,1)}), bf16[4,4,96,640]{3,2,1,0:T(8,128)(2,1)S(1)}, u32[]{:S(2)}, u32[]{:S(2)}) async-start(bf16[4,4,96,640]{3,2,1,0:T(8,128)(2,1)} %get-tuple-element.61), calls=%async_computation | async-start | bytes 3932160 | tf_op jit(solution)/shard_map/all_to_all | solution.py:483
  35.7 39.3 %collective-permute-start.5 = (bf16[4,96,896]{2,1,0:T(8,128)(2,1)}, bf16[4,96,896]{2,1,0:T(8,128)(2,1)S(1)}, u32[]{:S(2)}, u32[]{:S(2)}) collective-permute-start(bf16[4,96,896]{2,1,0:T(8,128)(2,1)} %get-tuple-element.69), channel_id=1, source_target_pairs={{0,32},{32,64},{64,96},{96,0},{1,33},{33,65},{65,97},{97,1},{2,34}... | collective-permute-start | bytes 2064392 | tf_op jit(solution)/shard_map/ppermute | solution.py:290
  35.8 43.5 %collective-permute-start.6 = (bf16[4,96,896]{2,1,0:T(8,128)(2,1)}, bf16[4,96,896]{2,1,0:T(8,128)(2,1)S(1)}, u32[]{:S(2)}, u32[]{:S(2)}) collective-permute-start(bf16[4,96,896]{2,1,0:T(8,128)(2,1)} %get-tuple-element.70), channel_id=1, source_target_pairs={{0,64},{32,96},{64,0},{96,32},{1,65},{33,97},{65,1},{97,33},{2,66}... | collective-permute-start | bytes 2064392 | tf_op jit(solution)/shard_map/ppermute | solution.py:290
  38.2 41.1 %collective-permute-start.7 = (bf16[4,96,896]{2,1,0:T(8,128)(2,1)}, bf16[4,96,896]{2,1,0:T(8,128)(2,1)}, u32[]{:S(2)}, u32[]{:S(2)}) collective-permute-start(bf16[4,96,896]{2,1,0:T(8,128)(2,1)} %get-tuple-element.71), channel_id=1, source_target_pairs={{0,96},{32,0},{64,32},{96,64},{1,97},{33,1},{65,33},{97,65},{2,98}... | collective-permute-start | bytes 2064392 | tf_op jit(solution)/shard_map/ppermute | solution.py:290
  60.3 8.6 %copy-start = (bf16[4,4,96,640]{3,2,1,0:T(8,128)(2,1)}, bf16[4,4,96,640]{3,2,1,0:T(8,128)(2,1)S(1)}, u32[]{:S(2)}) copy-start(bf16[4,4,96,640]{3,2,1,0:T(8,128)(2,1)S(1)} %all-to-all-done.refs_0_) | copy-start | bytes 5898244
  60.3 18.9 %all-to-all-start.1 = ((bf16[16,48,128]{2,1,0:T(8,128)(2,1)}), bf16[16,48,128]{2,1,0:T(8,128)(2,1)S(1)}, u32[]{:S(2)}, u32[]{:S(2)}) async-start(bf16[16,48,128]{2,1,0:T(8,128)(2,1)} %bitcast.9), calls=%async_computation.1 | async-start | bytes 393216 | tf_op jit(solution)/shard_map/all_to_all | solution.py:483
  71.4 24.4 %copy-start.5 = (bf16[96,640]{1,0:T(8,128)(2,1)S(1)}, bf16[96,640]{1,0:T(8,128)(2,1)}, u32[]{:S(2)}) copy-start(bf16[96,640]{1,0:T(8,128)(2,1)} %get-tuple-element.83) | copy-start | bytes 368644
  71.4 8.0 %collective-permute-start.2 = (bf16[96,640]{1,0:T(8,128)(2,1)}, bf16[96,640]{1,0:T(8,128)(2,1)S(1)}, u32[]{:S(2)}, u32[]{:S(2)}) collective-permute-start(bf16[96,640]{1,0:T(8,128)(2,1)} %get-tuple-element.65), channel_id=1, source_target_pairs={{0,32},{32,64},{64,96},{96,0},{1,33},{33,65},{65,97},{97,1},{2,34}... | collective-permute-start | bytes 368648 | tf_op jit(solution)/shard_map/ppermute | solution.py:290
  72.6 8.7 %collective-permute-start.3 = (bf16[96,640]{1,0:T(8,128)(2,1)}, bf16[96,640]{1,0:T(8,128)(2,1)S(1)}, u32[]{:S(2)}, u32[]{:S(2)}) collective-permute-start(bf16[96,640]{1,0:T(8,128)(2,1)} %get-tuple-element.66), channel_id=1, source_target_pairs={{0,64},{32,96},{64,0},{96,32},{1,65},{33,97},{65,1},{97,33},{2,66}... | collective-permute-start | bytes 368648 | tf_op jit(solution)/shard_map/ppermute | solution.py:290
  75.1 13.0 %copy-start.3 = (bf16[4,96,896]{2,1,0:T(8,128)(2,1)}, bf16[4,96,896]{2,1,0:T(8,128)(2,1)S(1)}, u32[]{:S(2)}) copy-start(bf16[4,96,896]{2,1,0:T(8,128)(2,1)S(1)} %collective-permute-done.5.refs_1_) | copy-start | bytes 2064388
  75.1 6.2 %collective-permute-start.4 = (bf16[96,640]{1,0:T(8,128)(2,1)}, bf16[96,640]{1,0:T(8,128)(2,1)S(1)}, u32[]{:S(2)}, u32[]{:S(2)}) collective-permute-start(bf16[96,640]{1,0:T(8,128)(2,1)} %get-tuple-element.67), channel_id=1, source_target_pairs={{0,96},{32,0},{64,32},{96,64},{1,97},{33,1},{65,33},{97,65},{2,98}... | collective-permute-start | bytes 368648 | tf_op jit(solution)/shard_map/ppermute | solution.py:290
  79.3 8.7 %copy-start.4 = (bf16[4,96,896]{2,1,0:T(8,128)(2,1)}, bf16[4,96,896]{2,1,0:T(8,128)(2,1)S(1)}, u32[]{:S(2)}) copy-start(bf16[4,96,896]{2,1,0:T(8,128)(2,1)S(1)} %collective-permute-done.6.refs_2_) | copy-start | bytes 2064388
  82.0 22.1 %all-to-all-start.2 = ((bf16[16,48,128]{2,1,0:T(8,128)(2,1)}), bf16[16,48,128]{2,1,0:T(8,128)(2,1)S(1)}, u32[]{:S(2)}, u32[]{:S(2)}) async-start(bf16[16,48,128]{2,1,0:T(8,128)(2,1)} %broadcast_in_dim.6), calls=%async_computation.2 | async-start | bytes 393216 | tf_op jit(solution)/shard_map/all_to_all | solution.py:483
  90.8 8.3 %collective-permute-start.8 = (bf16[96,896]{1,0:T(8,128)(2,1)}, bf16[96,896]{1,0:T(8,128)(2,1)S(1)}, u32[]{:S(2)}, u32[]{:S(2)}) collective-permute-start(bf16[96,896]{1,0:T(8,128)(2,1)} %get-tuple-element.80), channel_id=1, source_target_pairs={{0,128},{128,2},{2,130},{130,0},{1,129},{129,3},{3,131},{131,1},{4... | collective-permute-start | bytes 516104 | tf_op jit(solution)/shard_map/ppermute | solution.py:290
  92.2 10.6 %collective-permute-start.9 = (bf16[96,896]{1,0:T(8,128)(2,1)}, bf16[96,896]{1,0:T(8,128)(2,1)S(1)}, u32[]{:S(2)}, u32[]{:S(2)}) collective-permute-start(bf16[96,896]{1,0:T(8,128)(2,1)} %get-tuple-element.81), channel_id=1, source_target_pairs={{0,2},{128,130},{2,0},{130,128},{1,3},{129,131},{3,1},{131,129},{4... | collective-permute-start | bytes 516104 | tf_op jit(solution)/shard_map/ppermute | solution.py:290
  94.6 8.2 %collective-permute-start.10 = (bf16[96,896]{1,0:T(8,128)(2,1)}, bf16[96,896]{1,0:T(8,128)(2,1)S(1)}, u32[]{:S(2)}, u32[]{:S(2)}) collective-permute-start(bf16[96,896]{1,0:T(8,128)(2,1)} %get-tuple-element.82), channel_id=1, source_target_pairs={{0,130},{128,0},{2,128},{130,2},{1,131},{129,1},{3,129},{131,3},{4... | collective-permute-start | bytes 516104 | tf_op jit(solution)/shard_map/ppermute | solution.py:290

commit v9 on v7

--- a/solution.py
+++ b/solution.py
@@ -166,39 +166,47 @@
     )(core, image, taps, bias, gain, shift, channel_order(rows, along_z), b_row, w_up, cot)
 
 
-def product_kernel(place_ref, near_t_ref, far_t_ref, near_ref, far_ref, *out_refs):
+def product_kernel(place_ref, near_t_ref, far_t_ref, near_ref, far_ref, *refs):
+    out_refs, pieces, others, sems = refs[:5], refs[5], refs[6], refs[7]
     _, along_y, rows, cells = near_t_ref.shape
-    block = (
-        jnp.dot(near_t_ref[...].reshape(along_y * rows, cells), near_ref[...], preferred_element_type=jnp.float32)
-        + jnp.dot(far_t_ref[...].reshape(along_y * rows, cells), far_ref[...], preferred_element_type=jnp.float32)
-    ).astype(jnp.bfloat16)
-    columns = out_refs[0].shape[2]
-    out_refs[4][...] = block[:, columns:].reshape(out_refs[4].shape)
-    for steps in range(4):
-
-        @pl.when(pl.program_id(0) == steps)
-        def _():
-            for y in range(along_y):
-                out_refs[steps][lax.rem(y - place_ref[1] + 4, 4)] = block[y * rows : (y + 1) * rows, :columns]
+    columns = pieces.shape[3]
+    copies = []
+    for step in range(4):
+        x = lax.rem(place_ref[0] + step, 4)
+        near_t = near_t_ref[x].reshape(along_y * rows, cells)
+        far_t = far_t_ref[x].reshape(along_y * rows, cells)
+        block = (
+            jnp.dot(near_t, near_ref[...], preferred_element_type=jnp.float32)
+            + jnp.dot(far_t, far_ref[...], preferred_element_type=jnp.float32)
+        ).astype(jnp.bfloat16)
+        for y in range(along_y):
+            part = block[y * rows : (y + 1) * rows]
+            pieces[step, lax.rem(y - place_ref[1] + 4, 4)] = part[:, :columns]
+            others[y, step] = part[:, columns:]
+        copies.append(pltpu.make_async_copy(pieces.at[step], out_refs[step], sems.at[step]))
+        copies.append(pltpu.make_async_copy(others.at[:, step], out_refs[4].at[:, step], sems.at[4 + step]))
+        for copy in copies[-2:]:
+            copy.start()
+    for copy in copies:
+        copy.wait()
 
 
 def product(place, near_t, far_t, near, far, columns):
     _, _, rows, cells = near_t.shape
-    others = near.shape[1] - columns
-    left = pl.BlockSpec((1, 4, rows, cells), lambda i, p: (lax.rem(p[0] + i, 4), 0, 0, 0))
-    right = pl.BlockSpec((cells, near.shape[1]), lambda i, p: (0, 0))
+    rest = near.shape[1] - columns
+    whole = pl.BlockSpec(memory_space=pltpu.VMEM)
     return pl.pallas_call(
         product_kernel,
         name="product",
-        grid_spec=pltpu.PrefetchScalarGridSpec(
-            num_scalar_prefetch=1,
-            grid=(4,),
-            in_specs=[left, left, right, right],
-            out_specs=[pl.BlockSpec((4, rows, columns), lambda i, p: (0, 0, 0))] * 4
-            + [pl.BlockSpec((4, 1, rows, others), lambda i, p: (0, i, 0, 0))],
-        ),
+        in_specs=[pl.BlockSpec(memory_space=pltpu.SMEM)] + [whole] * 4,
+        out_specs=[pl.BlockSpec(memory_space=pl.ANY)] * 5,
         out_shape=[jax.ShapeDtypeStruct((4, rows, columns), jnp.bfloat16)] * 4
-        + [jax.ShapeDtypeStruct((4, 4, rows, others), jnp.bfloat16)],
+        + [jax.ShapeDtypeStruct((4, 4, rows, rest), jnp.bfloat16)],
+        scratch_shapes=[
+            pltpu.VMEM((4, 4, rows, columns), jnp.bfloat16),
+            pltpu.VMEM((4, 4, rows, rest), jnp.bfloat16),
+            pltpu.SemaphoreType.DMA((8,)),
+        ],
         compiler_params=pltpu.CompilerParams(vmem_limit_bytes=VMEM_LIMIT),
         cost_estimate=SMALL,
     )(place, near_t, far_t, near, far)
@@ -467,7 +475,7 @@
     small = swap_pieces(jnp.broadcast_to(small, (16,) + small.shape), plane)
 
     part_b = to_owners(sum_pieces([part_b]), "x")
-    part_a, part_b = lax.optimization_barrier((part_a, part_b))
+    part_b[1], part_a = lax.optimization_barrier((part_b[1], part_a))
     part_a = to_owners(sum_pieces(part_a), ("y_lo", "y_hi"))
     last = jnp.concatenate([total_of(jnp.stack(part_a)), total_of(jnp.stack(part_b))], axis=1)
     last = last.astype(jnp.bfloat16).reshape(2 * along_z, -1, LANES)

time: 128 us -> 124 us (0.969)
  Pallas kernels: 48.5 us -> 46.1 us
  waiting for transfers between devices: 14.9 us -> 12.8 us
    pallas_call x1, Pallas kernels: 7.9 us -> 5.49 us  [product(): pl.pallas_call(product_kernel, name='product', in_specs=[pl.BlockSpec(mem...]
  transfers between devices with their start and end apart: 14 -> 14, of which waited for: 8 -> 6; matrix products, arithmetic and copies ran while one was open for 2% -> 2% of each run, Pallas kernels for 17% -> 20%
where the time goes in v9:
time: 124 us; the launch traced here: 123 us
  Pallas kernels  46.1 us (37%)
  starting transfers between devices  33 us (27%)
  blocking collectives  26 us (21%)
  waiting for transfers between devices  12.8 us (10%)
  local copies, waits for them, and re-layouts  2.87 us (2%)
  other arithmetic  1.73 us (1%)
    all_to_all x1, blocking collectives, swap_pieces(): return lax.all_to_all(values, axes, 0, 0, tiled=True)  26 us
    pallas_call x1, Pallas kernels, back(): pl.pallas_call(back_kernel, name='back', grid=(feat // LANES,), in_specs=...  19.2 us
    all_to_all x3, starting transfers between devices, swap_pieces(): return lax.all_to_all(values, axes, 0, 0, tiled=True)  15.9 us
    pallas_call x1, Pallas kernels, front(): pl.pallas_call(front_kernel, name='front', in_specs=[pl.BlockSpec(memory_...  14.3 us
    ppermute x9, starting transfers between devices, to_owners(): lax.ppermute(piece, axes, [(named[i], named[(i + d) % 4]) for i in range(...  13.7 us
    all_to_all x3, waiting for transfers between devices, swap_pieces(): return lax.all_to_all(values, axes, 0, 0, tiled=True)  8.5 us
    pallas_call x1, Pallas kernels, product(): pl.pallas_call(product_kernel, name='product', in_specs=[pl.BlockSpec(mem...  5.49 us
    pallas_call x2, Pallas kernels, sum_pieces(): pl.pallas_call(sum_kernel, name='sum_pieces', out_shape=[jax.ShapeDtypeSt...  5.17 us
  transfers between devices with their start and end apart: 14, of which 6 were waited for; matrix products, arithmetic and copies ran while one was open for 2% of the time, Pallas kernels for 20%

profile of v9, /device:TPU:1, one launch (start us, length us, event | category | flops | bytes accessed | tf_op | source)
XLA Modules:
  0.0 123.3 jit_solution(1621099425335367744)
XLA Ops:
  0.6 14.3 %front.1 = (f32[256,1536]{1,0:T(8,128)}, f32[256,128]{1,0:T(8,128)}, bf16[4,2,2,96,256]{4,3,2,1,0:T(8,128)(2,1)}, bf16[256,1536]{1,0:T(8,128)(2,1)}, bf16[256,1536]{1,0:T(8,128)(2,1)}, /*index=5*/f32[1,3072]{1,0:T(1,128)}) custom-call(s32[1]{0:T(128)} %bitcast.core_ref, bf16[1,16,16,1536]{3,2,1,0:T(8,128)(2,1)} %image_ref.3, f32[49,1536]{1,0:T(8,128)} %taps_ref.3, ...), custom_call_target="tpu_custom_call" | custom-call | flops 1000 | bytes 1000 | tf_op jit(solution)/shard_map/front/pallas_call | solution.py:140
  15.0 3.3 %collective-permute-start.1 = (bf16[256,1536]{1,0:T(8,128)(2,1)}, bf16[256,1536]{1,0:T(8,128)(2,1)S(1)}, u32[]{:S(2)}, u32[]{:S(2)}) collective-permute-start(bf16[256,1536]{1,0:T(8,128)(2,1)} %get-tuple-element.48.away_ref), channel_id=1, source_target_pairs={{0,1},{1,0},{2,3},{3,2},{4,5},{5,4},{6,7},{7,6},{8,9},{9,8},{10,11... | collective-permute-start | bytes 2359304 | tf_op jit(solution)/shard_map/ppermute | solution.py:456
  18.3 0.1 collective-permute-start
  18.4 0.6 pad_add_fusion.place_ref
  19.0 1.4 %collective-permute-done.1.far_ref = bf16[256,1536]{1,0:T(8,128)(2,1)S(1)} collective-permute-done((bf16[256,1536]{1,0:T(8,128)(2,1)}, bf16[256,1536]{1,0:T(8,128)(2,1)S(1)}, u32[]{:S(2)}, u32[]{:S(2)}) %collective-permute-start.1) | collective-permute-done | bytes 786464 | tf_op jit(solution)/shard_map/ppermute | solution.py:456
  20.4 0.0 copy-start.1
  20.4 1.1 collective-permute-done
  21.5 0.0 copy-start.2
  21.5 0.0 copy-done.1
  21.5 0.9 copy-done.2
  22.5 5.5 %product.1 = (bf16[4,96,896]{2,1,0:T(8,128)(2,1)}, bf16[4,96,896]{2,1,0:T(8,128)(2,1)}, bf16[4,96,896]{2,1,0:T(8,128)(2,1)}, bf16[4,96,896]{2,1,0:T(8,128)(2,1)}, bf16[4,4,96,640]{3,2,1,0:T(8,128)(2,1)}) custom-call(s32[2]{0:T(128)} %pad_add_fusion.place_ref, bf16[4,4,96,256]{3,2,1,0:T(8,128)(2,1)} %bitcast.7, bf16[4,4,96,256]{3,2,1,0:T(8,128)(2,1)} %bitcast.8, ...), custom_call_target="tpu_custom_call" | custom-call | flops 1000 | bytes 1000 | tf_op jit(solution)/shard_map/product/pallas_call | solution.py:198
  28.0 3.6 %all-to-all-start = ((bf16[4,4,96,640]{3,2,1,0:T(8,128)(2,1)}), bf16[4,4,96,640]{3,2,1,0:T(8,128)(2,1)S(1)}, u32[]{:S(2)}, u32[]{:S(2)}) async-start(bf16[4,4,96,640]{3,2,1,0:T(8,128)(2,1)} %get-tuple-element.61), calls=%async_computation | async-start | bytes 3932160 | tf_op jit(solution)/shard_map/all_to_all | solution.py:435
  31.6 0.1 collective-permute-start.2
  31.7 2.4 %collective-permute-start.3 = (bf16[4,96,896]{2,1,0:T(8,128)(2,1)}, bf16[4,96,896]{2,1,0:T(8,128)(2,1)S(1)}, u32[]{:S(2)}, u32[]{:S(2)}) collective-permute-start(bf16[4,96,896]{2,1,0:T(8,128)(2,1)} %get-tuple-element.59), channel_id=1, source_target_pairs={{0,64},{32,96},{64,0},{96,32},{1,65},{33,97},{65,1},{97,33},{2,66}... | collective-permute-start | bytes 2064392 | tf_op jit(solution)/shard_map/ppermute | solution.py:242
  34.1 1.1 collective-permute-start.4
  35.2 19.2 %back.1 = (bf16[1,16,16,1536]{3,2,1,0:T(8,128)(2,1)}, bf16[12,64,128]{2,1,0:T(8,128)(2,1)}) custom-call(s32[1]{0:T(128)} %bitcast.core_ref, bf16[256,1536]{1,0:T(8,128)(2,1)} %get-tuple-element.48.away_ref, bf16[256,1536]{1,0:T(8,128)(2,1)} %get-tuple-element.49.near_ref, f32[256,128]{1,0:T(8,128)} %get-tuple-element.50.sigma_ref, f32[1536]{0:T(1024)} %gain_ref.3, ...), custom_call_target="tpu_custom_call" | custom-call | flops 1000 | bytes 1000 | tf_op jit(solution)/shard_map/back/pallas_call | solution.py:347
  54.5 1.8 %all-to-all-done.refs_0_ = bf16[4,4,96,640]{3,2,1,0:T(8,128)(2,1)S(1)} async-done(((bf16[4,4,96,640]{3,2,1,0:T(8,128)(2,1)}), bf16[4,4,96,640]{3,2,1,0:T(8,128)(2,1)S(1)}, u32[]{:S(2)}, u32[]{:S(2)}) %all-to-all-start) | async-done | bytes 1966112 | tf_op jit(solution)/shard_map/all_to_all | solution.py:435
  56.2 0.0 copy-start
  56.2 8.6 %all-to-all-start.1 = ((bf16[16,48,128]{2,1,0:T(8,128)(2,1)}), bf16[16,48,128]{2,1,0:T(8,128)(2,1)S(1)}, u32[]{:S(2)}, u32[]{:S(2)}) async-start(bf16[16,48,128]{2,1,0:T(8,128)(2,1)} %bitcast.9), calls=%async_computation.1 | async-start | bytes 393216 | tf_op jit(solution)/shard_map/all_to_all | solution.py:435
  64.8 0.0 copy-done
  64.8 2.4 %sum_pieces.2 = (bf16[96,640]{1,0:T(8,128)(2,1)}, bf16[96,640]{1,0:T(8,128)(2,1)}, bf16[96,640]{1,0:T(8,128)(2,1)}, bf16[96,640]{1,0:T(8,128)(2,1)}) custom-call(bf16[4,4,96,640]{3,2,1,0:T(8,128)(2,1)} %copy-done), custom_call_target="tpu_custom_call" | custom-call | flops 1000 | bytes 1000 | tf_op jit(solution)/shard_map/sum_pieces/pallas_call | solution.py:230
  67.2 0.0 copy-start.5
  67.2 1.2 %collective-permute-start.5 = (bf16[96,640]{1,0:T(8,128)(2,1)}, bf16[96,640]{1,0:T(8,128)(2,1)S(1)}, u32[]{:S(2)}, u32[]{:S(2)}) collective-permute-start(bf16[96,640]{1,0:T(8,128)(2,1)} %get-tuple-element.66), channel_id=1, source_target_pairs={{0,32},{32,64},{64,96},{96,0},{1,33},{33,65},{65,97},{97,1},{2,34}... | collective-permute-start | bytes 368648 | tf_op jit(solution)/shard_map/ppermute | solution.py:242
  68.5 2.5 %collective-permute-start.9 = (bf16[96,640]{1,0:T(8,128)(2,1)}, bf16[96,640]{1,0:T(8,128)(2,1)S(1)}, u32[]{:S(2)}, u32[]{:S(2)}) collective-permute-start(bf16[96,640]{1,0:T(8,128)(2,1)} %get-tuple-element.81), channel_id=1, source_target_pairs={{0,64},{32,96},{64,0},{96,32},{1,65},{33,97},{65,1},{97,33},{2,66}... | collective-permute-start | bytes 368648 | tf_op jit(solution)/shard_map/ppermute | solution.py:242
  70.9 0.0 collective-permute-done.2.refs_1_
  70.9 0.0 copy-start.3
  70.9 1.2 collective-permute-start.10
  72.1 3.0 %all-to-all-done.1 = bf16[16,48,128]{2,1,0:T(8,128)(2,1)S(1)} async-done(((bf16[16,48,128]{2,1,0:T(8,128)(2,1)}), bf16[16,48,128]{2,1,0:T(8,128)(2,1)S(1)}, u32[]{:S(2)}, u32[]{:S(2)}) %all-to-all-start.1) | async-done | bytes 196640 | tf_op jit(solution)/shard_map/all_to_all | solution.py:435
  75.2 0.0 collective-permute-done.3.refs_2_
  75.2 0.0 copy-start.4
  75.2 0.0 collective-permute-done.4.refs_3_
  75.2 0.0 collective-permute-done.5
  75.2 0.0 copy-done.3
  75.2 0.8 copy-done.4
  76.0 2.7 %sum_pieces.3 = (bf16[96,896]{1,0:T(8,128)(2,1)}, bf16[96,896]{1,0:T(8,128)(2,1)}, bf16[96,896]{1,0:T(8,128)(2,1)}, bf16[96,896]{1,0:T(8,128)(2,1)}) custom-call(bf16[4,96,896]{2,1,0:T(8,128)(2,1)} %get-tuple-element.71.refs_0_, bf16[4,96,896]{2,1,0:T(8,128)(2,1)} %copy-done.3, bf16[4,96,896]{2,1,0:T(8,128)(2,1)} %copy-done.4, ...), custom_call_target="tpu_custom_call" | custom-call | flops 1000 | bytes 1000 | tf_op jit(solution)/shard_map/sum_pieces/pallas_call | solution.py:230
  78.8 1.4 %collective-permute-start.6 = (bf16[96,896]{1,0:T(8,128)(2,1)}, bf16[96,896]{1,0:T(8,128)(2,1)S(1)}, u32[]{:S(2)}, u32[]{:S(2)}) collective-permute-start(bf16[96,896]{1,0:T(8,128)(2,1)} %get-tuple-element.76), channel_id=1, source_target_pairs={{0,128},{128,2},{2,130},{130,0},{1,129},{129,3},{3,131},{131,1},{4... | collective-permute-start | bytes 516104 | tf_op jit(solution)/shard_map/ppermute | solution.py:242
  80.2 2.5 %collective-permute-start.7 = (bf16[96,896]{1,0:T(8,128)(2,1)}, bf16[96,896]{1,0:T(8,128)(2,1)S(1)}, u32[]{:S(2)}, u32[]{:S(2)}) collective-permute-start(bf16[96,896]{1,0:T(8,128)(2,1)} %get-tuple-element.77), channel_id=1, source_target_pairs={{0,2},{128,130},{2,0},{130,128},{1,3},{129,131},{3,1},{131,129},{4... | collective-permute-start | bytes 516104 | tf_op jit(solution)/shard_map/ppermute | solution.py:242
  82.7 1.2 collective-permute-start.8
  83.9 0.7 broadcast_in_dim.6
  84.6 3.7 %all-to-all-start.2 = ((bf16[16,48,128]{2,1,0:T(8,128)(2,1)}), bf16[16,48,128]{2,1,0:T(8,128)(2,1)S(1)}, u32[]{:S(2)}, u32[]{:S(2)}) async-start(bf16[16,48,128]{2,1,0:T(8,128)(2,1)} %broadcast_in_dim.6), calls=%async_computation.2 | async-start | bytes 393216 | tf_op jit(solution)/shard_map/all_to_all | solution.py:435
  88.4 0.0 collective-permute-done.9
  88.4 0.0 collective-permute-done.10
  88.4 0.0 copy-done.5
  88.4 0.0 collective-permute-done.6
  88.5 1.7 %collective-permute-done.7 = bf16[96,896]{1,0:T(8,128)(2,1)S(1)} collective-permute-done((bf16[96,896]{1,0:T(8,128)(2,1)}, bf16[96,896]{1,0:T(8,128)(2,1)S(1)}, u32[]{:S(2)}, u32[]{:S(2)}) %collective-permute-start.7) | collective-permute-done | bytes 172064 | tf_op jit(solution)/shard_map/ppermute | solution.py:242
  90.2 0.0 collective-permute-done.8
  90.2 1.0 add_add_fusion
  91.2 0.4 convert_element_type.23
  91.6 3.7 %all-to-all-done.2 = bf16[16,48,128]{2,1,0:T(8,128)(2,1)S(1)} async-done(((bf16[16,48,128]{2,1,0:T(8,128)(2,1)}), bf16[16,48,128]{2,1,0:T(8,128)(2,1)S(1)}, u32[]{:S(2)}, u32[]{:S(2)}) %all-to-all-start.2) | async-done | bytes 196640 | tf_op jit(solution)/shard_map/all_to_all | solution.py:435
  95.4 26.0 %all_to_all.20.received_ref = bf16[16,120,128]{2,1,0:T(8,128)(2,1)} all-to-all(bf16[16,120,128]{2,1,0:T(8,128)(2,1)S(1)} %pad_maximum_fusion), channel_id=1, replica_groups=mesh['y_lo'=2,'x'=4,'z'=8,'y_hi'=2,'core'=2] {'z','core'}, dimensions={0} | all-to-all | bytes 983040 | tf_op jit(solution)/shard_map/all_to_all | solution.py:435
  121.4 1.9 %finish.1 = (f32[6,3072]{1,0:T(8,128)}, f32[3072]{0:T(1024)}, f32[1536]{0:T(1024)}, f32[1536]{0:T(1024)}, f32[49,1536]{1,0:T(8,128)}, /*index=5*/f32[1536]{0:T(1024)}) custom-call(bf16[16,120,128]{2,1,0:T(8,128)(2,1)} %all_to_all.20.received_ref), custom_call_target="tpu_custom_call" | custom-call | flops 1000 | bytes 1000 | tf_op jit(solution)/shard_map/finish/pallas_call | solution.py:418
  (7 shorter events, 0.2 us)
Async XLA Ops:
  15.0 5.4 %collective-permute-start.1 = (bf16[256,1536]{1,0:T(8,128)(2,1)}, bf16[256,1536]{1,0:T(8,128)(2,1)S(1)}, u32[]{:S(2)}, u32[]{:S(2)}) collective-permute-start(bf16[256,1536]{1,0:T(8,128)(2,1)} %get-tuple-element.48.away_ref), channel_id=1, source_target_pairs={{0,1},{1,0},{2,3},{3,2},{4,5},{5,4},{6,7},{7,6},{8,9},{9,8},{10,11... | collective-permute-start | bytes 2359304 | tf_op jit(solution)/shard_map/ppermute | solution.py:456
  18.3 3.2 %collective-permute-start = (bf16[4,2,2,96,256]{4,3,2,1,0:T(8,128)(2,1)}, bf16[4,2,2,96,256]{4,3,2,1,0:T(8,128)(2,1)S(1)}, u32[]{:S(2)}, u32[]{:S(2)}) collective-permute-start(bf16[4,2,2,96,256]{4,3,2,1,0:T(8,128)(2,1)} %get-tuple-element.52), channel_id=1, source_target_pairs={{0,1},{1,0},{2,3},{3,2},{4,5},{5,4},{6,7},{7,6},{8,9},{9,8},{10,11... | collective-permute-start | bytes 2359304 | tf_op jit(solution)/shard_map/ppermute | solution.py:457
  20.4 1.1 copy-start.1
  21.5 0.9 copy-start.2
  28.0 28.3 %all-to-all-start = ((bf16[4,4,96,640]{3,2,1,0:T(8,128)(2,1)}), bf16[4,4,96,640]{3,2,1,0:T(8,128)(2,1)S(1)}, u32[]{:S(2)}, u32[]{:S(2)}) async-start(bf16[4,4,96,640]{3,2,1,0:T(8,128)(2,1)} %get-tuple-element.61), calls=%async_computation | async-start | bytes 3932160 | tf_op jit(solution)/shard_map/all_to_all | solution.py:435
  31.6 39.3 %collective-permute-start.2 = (bf16[4,96,896]{2,1,0:T(8,128)(2,1)}, bf16[4,96,896]{2,1,0:T(8,128)(2,1)S(1)}, u32[]{:S(2)}, u32[]{:S(2)}) collective-permute-start(bf16[4,96,896]{2,1,0:T(8,128)(2,1)} %get-tuple-element.58), channel_id=1, source_target_pairs={{0,32},{32,64},{64,96},{96,0},{1,33},{33,65},{65,97},{97,1},{2,34}... | collective-permute-start | bytes 2064392 | tf_op jit(solution)/shard_map/ppermute | solution.py:242
  31.7 43.5 %collective-permute-start.3 = (bf16[4,96,896]{2,1,0:T(8,128)(2,1)}, bf16[4,96,896]{2,1,0:T(8,128)(2,1)S(1)}, u32[]{:S(2)}, u32[]{:S(2)}) collective-permute-start(bf16[4,96,896]{2,1,0:T(8,128)(2,1)} %get-tuple-element.59), channel_id=1, source_target_pairs={{0,64},{32,96},{64,0},{96,32},{1,65},{33,97},{65,1},{97,33},{2,66}... | collective-permute-start | bytes 2064392 | tf_op jit(solution)/shard_map/ppermute | solution.py:242
  34.1 41.1 %collective-permute-start.4 = (bf16[4,96,896]{2,1,0:T(8,128)(2,1)}, bf16[4,96,896]{2,1,0:T(8,128)(2,1)}, u32[]{:S(2)}, u32[]{:S(2)}) collective-permute-start(bf16[4,96,896]{2,1,0:T(8,128)(2,1)} %get-tuple-element.60), channel_id=1, source_target_pairs={{0,96},{32,0},{64,32},{96,64},{1,97},{33,1},{65,33},{97,65},{2,98}... | collective-permute-start | bytes 2064392 | tf_op jit(solution)/shard_map/ppermute | solution.py:242
  56.2 8.6 %copy-start = (bf16[4,4,96,640]{3,2,1,0:T(8,128)(2,1)}, bf16[4,4,96,640]{3,2,1,0:T(8,128)(2,1)S(1)}, u32[]{:S(2)}) copy-start(bf16[4,4,96,640]{3,2,1,0:T(8,128)(2,1)S(1)} %all-to-all-done.refs_0_) | copy-start | bytes 5898244
  56.2 18.9 %all-to-all-start.1 = ((bf16[16,48,128]{2,1,0:T(8,128)(2,1)}), bf16[16,48,128]{2,1,0:T(8,128)(2,1)S(1)}, u32[]{:S(2)}, u32[]{:S(2)}) async-start(bf16[16,48,128]{2,1,0:T(8,128)(2,1)} %bitcast.9), calls=%async_computation.1 | async-start | bytes 393216 | tf_op jit(solution)/shard_map/all_to_all | solution.py:435
  67.2 21.2 %copy-start.5 = (bf16[96,640]{1,0:T(8,128)(2,1)S(1)}, bf16[96,640]{1,0:T(8,128)(2,1)}, u32[]{:S(2)}) copy-start(bf16[96,640]{1,0:T(8,128)(2,1)} %get-tuple-element.79) | copy-start | bytes 368644
  67.2 7.9 %collective-permute-start.5 = (bf16[96,640]{1,0:T(8,128)(2,1)}, bf16[96,640]{1,0:T(8,128)(2,1)S(1)}, u32[]{:S(2)}, u32[]{:S(2)}) collective-permute-start(bf16[96,640]{1,0:T(8,128)(2,1)} %get-tuple-element.66), channel_id=1, source_target_pairs={{0,32},{32,64},{64,96},{96,0},{1,33},{33,65},{65,97},{97,1},{2,34}... | collective-permute-start | bytes 368648 | tf_op jit(solution)/shard_map/ppermute | solution.py:242
  68.5 19.9 %collective-permute-start.9 = (bf16[96,640]{1,0:T(8,128)(2,1)}, bf16[96,640]{1,0:T(8,128)(2,1)S(1)}, u32[]{:S(2)}, u32[]{:S(2)}) collective-permute-start(bf16[96,640]{1,0:T(8,128)(2,1)} %get-tuple-element.81), channel_id=1, source_target_pairs={{0,64},{32,96},{64,0},{96,32},{1,65},{33,97},{65,1},{97,33},{2,66}... | collective-permute-start | bytes 368648 | tf_op jit(solution)/shard_map/ppermute | solution.py:242
  70.9 4.3 %copy-start.3 = (bf16[4,96,896]{2,1,0:T(8,128)(2,1)}, bf16[4,96,896]{2,1,0:T(8,128)(2,1)S(1)}, u32[]{:S(2)}) copy-start(bf16[4,96,896]{2,1,0:T(8,128)(2,1)S(1)} %collective-permute-done.2.refs_1_) | copy-start | bytes 2064388
  70.9 17.4 %collective-permute-start.10 = (bf16[96,640]{1,0:T(8,128)(2,1)}, bf16[96,640]{1,0:T(8,128)(2,1)S(1)}, u32[]{:S(2)}, u32[]{:S(2)}) collective-permute-start(bf16[96,640]{1,0:T(8,128)(2,1)} %get-tuple-element.82), channel_id=1, source_target_pairs={{0,96},{32,0},{64,32},{96,64},{1,97},{33,1},{65,33},{97,65},{2,98}... | collective-permute-start | bytes 368648 | tf_op jit(solution)/shard_map/ppermute | solution.py:242
  75.2 0.9 copy-start.4
  78.8 9.7 %collective-permute-start.6 = (bf16[96,896]{1,0:T(8,128)(2,1)}, bf16[96,896]{1,0:T(8,128)(2,1)S(1)}, u32[]{:S(2)}, u32[]{:S(2)}) collective-permute-start(bf16[96,896]{1,0:T(8,128)(2,1)} %get-tuple-element.76), channel_id=1, source_target_pairs={{0,128},{128,2},{2,130},{130,0},{1,129},{129,3},{3,131},{131,1},{4... | collective-permute-start | bytes 516104 | tf_op jit(solution)/shard_map/ppermute | solution.py:242
  80.2 10.0 %collective-permute-start.7 = (bf16[96,896]{1,0:T(8,128)(2,1)}, bf16[96,896]{1,0:T(8,128)(2,1)S(1)}, u32[]{:S(2)}, u32[]{:S(2)}) collective-permute-start(bf16[96,896]{1,0:T(8,128)(2,1)} %get-tuple-element.77), channel_id=1, source_target_pairs={{0,2},{128,130},{2,0},{130,128},{1,3},{129,131},{3,1},{131,129},{4... | collective-permute-start | bytes 516104 | tf_op jit(solution)/shard_map/ppermute | solution.py:242
  82.7 7.5 %collective-permute-start.8 = (bf16[96,896]{1,0:T(8,128)(2,1)}, bf16[96,896]{1,0:T(8,128)(2,1)S(1)}, u32[]{:S(2)}, u32[]{:S(2)}) collective-permute-start(bf16[96,896]{1,0:T(8,128)(2,1)} %get-tuple-element.78), channel_id=1, source_target_pairs={{0,130},{128,0},{2,128},{130,2},{1,131},{129,1},{3,129},{131,3},{4... | collective-permute-start | bytes 516104 | tf_op jit(solution)/shard_map/ppermute | solution.py:242
  84.6 10.7 %all-to-all-start.2 = ((bf16[16,48,128]{2,1,0:T(8,128)(2,1)}), bf16[16,48,128]{2,1,0:T(8,128)(2,1)S(1)}, u32[]{:S(2)}, u32[]{:S(2)}) async-start(bf16[16,48,128]{2,1,0:T(8,128)(2,1)} %broadcast_in_dim.6), calls=%async_computation.2 | async-start | bytes 393216 | tf_op jit(solution)/shard_map/all_to_all | solution.py:435

commit v10 on v9

--- a/solution.py
+++ b/solution.py
@@ -166,15 +166,27 @@
     )(core, image, taps, bias, gain, shift, channel_order(rows, along_z), b_row, w_up, cot)
 
 
-def product_kernel(place_ref, near_t_ref, far_t_ref, near_ref, far_ref, *refs):
-    out_refs, pieces, others, sems = refs[:5], refs[5], refs[6], refs[7]
+def product_kernel(place_ref, near_t_hbm, far_t_hbm, near_hbm, far_hbm, *refs):
+    out_refs = refs[:5]
+    pieces, others, near_t_ref, far_t_ref, near_ref, far_ref, sems, in_sems = refs[5:]
     _, along_y, rows, cells = near_t_ref.shape
     columns = pieces.shape[3]
+    loads = [
+        pltpu.make_async_copy(near_hbm, near_ref, in_sems.at[0]),
+        pltpu.make_async_copy(far_hbm, far_ref, in_sems.at[1]),
+    ]
+    for step in range(4):
+        x = lax.rem(place_ref[0] + step, 4)
+        loads.append(pltpu.make_async_copy(near_t_hbm.at[x], near_t_ref.at[step], in_sems.at[2 + 2 * step]))
+        loads.append(pltpu.make_async_copy(far_t_hbm.at[x], far_t_ref.at[step], in_sems.at[3 + 2 * step]))
+    for load in loads:
+        load.start()
     copies = []
     for step in range(4):
-        x = lax.rem(place_ref[0] + step, 4)
-        near_t = near_t_ref[x].reshape(along_y * rows, cells)
-        far_t = far_t_ref[x].reshape(along_y * rows, cells)
+        for load in loads[:4] if step == 0 else loads[2 + 2 * step : 4 + 2 * step]:
+            load.wait()
+        near_t = near_t_ref[step].reshape(along_y * rows, cells)
+        far_t = far_t_ref[step].reshape(along_y * rows, cells)
         block = (
             jnp.dot(near_t, near_ref[...], preferred_element_type=jnp.float32)
             + jnp.dot(far_t, far_ref[...], preferred_element_type=jnp.float32)
@@ -194,18 +206,23 @@
 def product(place, near_t, far_t, near, far, columns):
     _, _, rows, cells = near_t.shape
     rest = near.shape[1] - columns
-    whole = pl.BlockSpec(memory_space=pltpu.VMEM)
+    remain = pl.BlockSpec(memory_space=pl.ANY)
     return pl.pallas_call(
         product_kernel,
         name="product",
-        in_specs=[pl.BlockSpec(memory_space=pltpu.SMEM)] + [whole] * 4,
-        out_specs=[pl.BlockSpec(memory_space=pl.ANY)] * 5,
+        in_specs=[pl.BlockSpec(memory_space=pltpu.SMEM)] + [remain] * 4,
+        out_specs=[remain] * 5,
         out_shape=[jax.ShapeDtypeStruct((4, rows, columns), jnp.bfloat16)] * 4
         + [jax.ShapeDtypeStruct((4, 4, rows, rest), jnp.bfloat16)],
         scratch_shapes=[
             pltpu.VMEM((4, 4, rows, columns), jnp.bfloat16),
             pltpu.VMEM((4, 4, rows, rest), jnp.bfloat16),
+            pltpu.VMEM(near_t.shape, jnp.bfloat16),
+            pltpu.VMEM(far_t.shape, jnp.bfloat16),
+            pltpu.VMEM(near.shape, jnp.bfloat16),
+            pltpu.VMEM(far.shape, jnp.bfloat16),
             pltpu.SemaphoreType.DMA((8,)),
+            pltpu.SemaphoreType.DMA((10,)),
         ],
         compiler_params=pltpu.CompilerParams(vmem_limit_bytes=VMEM_LIMIT),
         cost_estimate=SMALL,
@@ -213,24 +230,42 @@
 
 
 def sum_kernel(*refs):
-    ins, outs = refs[:-4], refs[-4:]
+    outs = refs[-8:-4]
+    ins, held, sums, in_sems, out_sems = refs[:-8], refs[-4], refs[-3], refs[-2], refs[-1]
+    loads, stores = [], []
     for index in range(4):
-        if len(ins) == 1:
-            parts = [ins[0][source, index] for source in range(4)]
-        else:
-            parts = [ref[index] for ref in ins]
-        total = parts[0].astype(jnp.float32)
-        for part in parts[1:]:
-            total = total + part.astype(jnp.float32)
-        outs[index][...] = total.astype(jnp.bfloat16)
+        for source in range(4):
+            piece = ins[0].at[source, index] if len(ins) == 1 else ins[source].at[index]
+            loads.append(pltpu.make_async_copy(piece, held.at[index, source], in_sems.at[4 * index + source]))
+            loads[-1].start()
+    for index in range(4):
+        for load in loads[4 * index : 4 * index + 4]:
+            load.wait()
+        total = held[index, 0].astype(jnp.float32)
+        for source in range(1, 4):
+            total = total + held[index, source].astype(jnp.float32)
+        sums[index] = total.astype(jnp.bfloat16)
+        stores.append(pltpu.make_async_copy(sums.at[index], outs[index], out_sems.at[index]))
+        stores[-1].start()
+    for store in stores:
+        store.wait()
 
 
 def sum_pieces(pieces):
     rows, columns = pieces[0].shape[-2:]
+    remain = pl.BlockSpec(memory_space=pl.ANY)
     return pl.pallas_call(
         sum_kernel,
         name="sum_pieces",
+        in_specs=[remain] * len(pieces),
+        out_specs=[remain] * 4,
         out_shape=[jax.ShapeDtypeStruct((rows, columns), jnp.bfloat16)] * 4,
+        scratch_shapes=[
+            pltpu.VMEM((4, 4, rows, columns), jnp.bfloat16),
+            pltpu.VMEM((4, rows, columns), jnp.bfloat16),
+            pltpu.SemaphoreType.DMA((16,)),
+            pltpu.SemaphoreType.DMA((4,)),
+        ],
         compiler_params=pltpu.CompilerParams(vmem_limit_bytes=VMEM_LIMIT),
         cost_estimate=SMALL,
     )(*pieces)

time: 124 us -> 126 us (1.016)
  no operation moved by 1% of the time
where the time goes in v10:
time: 126 us; the launch traced here: 124 us
  Pallas kernels  47 us (37%)
  starting transfers between devices  33.1 us (26%)
  blocking collectives  26.1 us (21%)
  waiting for transfers between devices  12.7 us (10%)
  local copies, waits for them, and re-layouts  2.87 us (2%)
  other arithmetic  1.73 us (1%)
    all_to_all x1, blocking collectives, swap_pieces(): return lax.all_to_all(values, axes, 0, 0, tiled=True)  26.1 us
    pallas_call x1, Pallas kernels, back(): pl.pallas_call(back_kernel, name='back', grid=(feat // LANES,), in_specs=...  19.2 us
    all_to_all x3, starting transfers between devices, swap_pieces(): return lax.all_to_all(values, axes, 0, 0, tiled=True)  15.8 us
    pallas_call x1, Pallas kernels, front(): pl.pallas_call(front_kernel, name='front', in_specs=[pl.BlockSpec(memory_...  14.3 us
    ppermute x9, starting transfers between devices, to_owners(): lax.ppermute(piece, axes, [(named[i], named[(i + d) % 4]) for i in range(...  13.9 us
    all_to_all x3, waiting for transfers between devices, swap_pieces(): return lax.all_to_all(values, axes, 0, 0, tiled=True)  8.29 us
    pallas_call x1, Pallas kernels, product(): pl.pallas_call(product_kernel, name='product', in_specs=[pl.BlockSpec(mem...  6.36 us
    pallas_call x2, Pallas kernels, sum_pieces(): pl.pallas_call(sum_kernel, name='sum_pieces', in_specs=[remain] * len(pie...  5.21 us
  transfers between devices with their start and end apart: 14, of which 6 were waited for; matrix products, arithmetic and copies ran while one was open for 2% of the time, Pallas kernels for 20%

profile of v10, /device:TPU:1, one launch (start us, length us, event | category | flops | bytes accessed | tf_op | source)
XLA Modules:
  0.0 124.4 jit_solution(9740720975812255428)
XLA Ops:
  0.6 14.3 %front.1 = (f32[256,1536]{1,0:T(8,128)}, f32[256,128]{1,0:T(8,128)}, bf16[4,2,2,96,256]{4,3,2,1,0:T(8,128)(2,1)}, bf16[256,1536]{1,0:T(8,128)(2,1)}, bf16[256,1536]{1,0:T(8,128)(2,1)}, /*index=5*/f32[1,3072]{1,0:T(1,128)}) custom-call(s32[1]{0:T(128)} %bitcast.core_ref, bf16[1,16,16,1536]{3,2,1,0:T(8,128)(2,1)} %image_ref.3, f32[49,1536]{1,0:T(8,128)} %taps_ref.3, ...), custom_call_target="tpu_custom_call" | custom-call | flops 1000 | bytes 1000 | tf_op jit(solution)/shard_map/front/pallas_call | solution.py:140
  15.0 3.3 %collective-permute-start.1 = (bf16[256,1536]{1,0:T(8,128)(2,1)}, bf16[256,1536]{1,0:T(8,128)(2,1)S(1)}, u32[]{:S(2)}, u32[]{:S(2)}) collective-permute-start(bf16[256,1536]{1,0:T(8,128)(2,1)} %get-tuple-element.48.away_ref), channel_id=1, source_target_pairs={{0,1},{1,0},{2,3},{3,2},{4,5},{5,4},{6,7},{7,6},{8,9},{9,8},{10,11... | collective-permute-start | bytes 2359304 | tf_op jit(solution)/shard_map/ppermute | solution.py:491
  18.3 0.1 collective-permute-start
  18.4 0.6 pad_add_fusion.place_ref
  19.0 1.4 %collective-permute-done.1.far_hbm = bf16[256,1536]{1,0:T(8,128)(2,1)S(1)} collective-permute-done((bf16[256,1536]{1,0:T(8,128)(2,1)}, bf16[256,1536]{1,0:T(8,128)(2,1)S(1)}, u32[]{:S(2)}, u32[]{:S(2)}) %collective-permute-start.1) | collective-permute-done | bytes 786464 | tf_op jit(solution)/shard_map/ppermute | solution.py:491
  20.4 0.0 copy-start.1
  20.4 1.1 collective-permute-done
  21.5 0.0 copy-start.2
  21.5 0.0 copy-done.1
  21.5 0.9 copy-done.2
  22.5 6.4 %product.1 = (bf16[4,96,896]{2,1,0:T(8,128)(2,1)}, bf16[4,96,896]{2,1,0:T(8,128)(2,1)}, bf16[4,96,896]{2,1,0:T(8,128)(2,1)}, bf16[4,96,896]{2,1,0:T(8,128)(2,1)}, bf16[4,4,96,640]{3,2,1,0:T(8,128)(2,1)}) custom-call(s32[2]{0:T(128)} %pad_add_fusion.place_ref, bf16[4,4,96,256]{3,2,1,0:T(8,128)(2,1)} %bitcast.7, bf16[4,4,96,256]{3,2,1,0:T(8,128)(2,1)} %bitcast.8, ...), custom_call_target="tpu_custom_call" | custom-call | flops 1000 | bytes 1000 | tf_op jit(solution)/shard_map/product/pallas_call | solution.py:210
  28.8 3.6 %all-to-all-start = ((bf16[4,4,96,640]{3,2,1,0:T(8,128)(2,1)}), bf16[4,4,96,640]{3,2,1,0:T(8,128)(2,1)S(1)}, u32[]{:S(2)}, u32[]{:S(2)}) async-start(bf16[4,4,96,640]{3,2,1,0:T(8,128)(2,1)} %get-tuple-element.61), calls=%async_computation | async-start | bytes 3932160 | tf_op jit(solution)/shard_map/all_to_all | solution.py:470
  32.5 0.1 collective-permute-start.2
  32.5 2.4 %collective-permute-start.3 = (bf16[4,96,896]{2,1,0:T(8,128)(2,1)}, bf16[4,96,896]{2,1,0:T(8,128)(2,1)S(1)}, u32[]{:S(2)}, u32[]{:S(2)}) collective-permute-start(bf16[4,96,896]{2,1,0:T(8,128)(2,1)} %get-tuple-element.59), channel_id=1, source_target_pairs={{0,64},{32,96},{64,0},{96,32},{1,65},{33,97},{65,1},{97,33},{2,66}... | collective-permute-start | bytes 2064392 | tf_op jit(solution)/shard_map/ppermute | solution.py:277
  35.0 1.1 collective-permute-start.4
  36.1 19.2 %back.1 = (bf16[1,16,16,1536]{3,2,1,0:T(8,128)(2,1)}, bf16[12,64,128]{2,1,0:T(8,128)(2,1)}) custom-call(s32[1]{0:T(128)} %bitcast.core_ref, bf16[256,1536]{1,0:T(8,128)(2,1)} %get-tuple-element.48.away_ref, bf16[256,1536]{1,0:T(8,128)(2,1)} %get-tuple-element.49.near_hbm.near_ref, f32[256,128]{1,0:T(8,128)} %get-tuple-element.50.sigma_ref, f32[1536]{0:T(1024)} %gain_ref.3, ...), custom_call_target="tpu_custom_call" | custom-call | flops 1000 | bytes 1000 | tf_op jit(solution)/shard_map/back/pallas_call | solution.py:382
  55.3 1.8 %all-to-all-done.refs_0_ = bf16[4,4,96,640]{3,2,1,0:T(8,128)(2,1)S(1)} async-done(((bf16[4,4,96,640]{3,2,1,0:T(8,128)(2,1)}), bf16[4,4,96,640]{3,2,1,0:T(8,128)(2,1)S(1)}, u32[]{:S(2)}, u32[]{:S(2)}) %all-to-all-start) | async-done | bytes 1966112 | tf_op jit(solution)/shard_map/all_to_all | solution.py:470
  57.1 0.0 copy-start
  57.1 8.6 %all-to-all-start.1 = ((bf16[16,48,128]{2,1,0:T(8,128)(2,1)}), bf16[16,48,128]{2,1,0:T(8,128)(2,1)S(1)}, u32[]{:S(2)}, u32[]{:S(2)}) async-start(bf16[16,48,128]{2,1,0:T(8,128)(2,1)} %bitcast.9), calls=%async_computation.1 | async-start | bytes 393216 | tf_op jit(solution)/shard_map/all_to_all | solution.py:470
  65.7 0.0 copy-done
  65.7 2.5 %sum_pieces.2 = (bf16[96,640]{1,0:T(8,128)(2,1)}, bf16[96,640]{1,0:T(8,128)(2,1)}, bf16[96,640]{1,0:T(8,128)(2,1)}, bf16[96,640]{1,0:T(8,128)(2,1)}) custom-call(bf16[4,4,96,640]{3,2,1,0:T(8,128)(2,1)} %copy-done), custom_call_target="tpu_custom_call" | custom-call | flops 1000 | bytes 1000 | tf_op jit(solution)/shard_map/sum_pieces/pallas_call | solution.py:257
  68.1 0.0 copy-start.5
  68.1 1.3 %collective-permute-start.5 = (bf16[96,640]{1,0:T(8,128)(2,1)}, bf16[96,640]{1,0:T(8,128)(2,1)S(1)}, u32[]{:S(2)}, u32[]{:S(2)}) collective-permute-start(bf16[96,640]{1,0:T(8,128)(2,1)} %get-tuple-element.66), channel_id=1, source_target_pairs={{0,32},{32,64},{64,96},{96,0},{1,33},{33,65},{65,97},{97,1},{2,34}... | collective-permute-start | bytes 368648 | tf_op jit(solution)/shard_map/ppermute | solution.py:277
  69.4 2.5 %collective-permute-start.9 = (bf16[96,640]{1,0:T(8,128)(2,1)}, bf16[96,640]{1,0:T(8,128)(2,1)S(1)}, u32[]{:S(2)}, u32[]{:S(2)}) collective-permute-start(bf16[96,640]{1,0:T(8,128)(2,1)} %get-tuple-element.81), channel_id=1, source_target_pairs={{0,64},{32,96},{64,0},{96,32},{1,65},{33,97},{65,1},{97,33},{2,66}... | collective-permute-start | bytes 368648 | tf_op jit(solution)/shard_map/ppermute | solution.py:277
  71.9 0.0 collective-permute-done.2.refs_1_
  71.9 0.0 copy-start.3
  71.9 1.2 collective-permute-start.10
  73.1 2.9 %all-to-all-done.1 = bf16[16,48,128]{2,1,0:T(8,128)(2,1)S(1)} async-done(((bf16[16,48,128]{2,1,0:T(8,128)(2,1)}), bf16[16,48,128]{2,1,0:T(8,128)(2,1)S(1)}, u32[]{:S(2)}, u32[]{:S(2)}) %all-to-all-start.1) | async-done | bytes 196640 | tf_op jit(solution)/shard_map/all_to_all | solution.py:470
  76.0 0.0 collective-permute-done.3.refs_2_
  76.0 0.0 copy-start.4
  76.0 0.0 collective-permute-done.4.refs_3_
  76.1 0.0 collective-permute-done.5
  76.1 0.0 copy-done.3
  76.1 0.8 copy-done.4
  76.9 2.8 %sum_pieces.3 = (bf16[96,896]{1,0:T(8,128)(2,1)}, bf16[96,896]{1,0:T(8,128)(2,1)}, bf16[96,896]{1,0:T(8,128)(2,1)}, bf16[96,896]{1,0:T(8,128)(2,1)}) custom-call(bf16[4,96,896]{2,1,0:T(8,128)(2,1)} %get-tuple-element.71.refs_0_, bf16[4,96,896]{2,1,0:T(8,128)(2,1)} %copy-done.3, bf16[4,96,896]{2,1,0:T(8,128)(2,1)} %copy-done.4, ...), custom_call_target="tpu_custom_call" | custom-call | flops 1000 | bytes 1000 | tf_op jit(solution)/shard_map/sum_pieces/pallas_call | solution.py:257
  79.7 1.5 %collective-permute-start.6 = (bf16[96,896]{1,0:T(8,128)(2,1)}, bf16[96,896]{1,0:T(8,128)(2,1)S(1)}, u32[]{:S(2)}, u32[]{:S(2)}) collective-permute-start(bf16[96,896]{1,0:T(8,128)(2,1)} %get-tuple-element.76), channel_id=1, source_target_pairs={{0,128},{128,2},{2,130},{130,0},{1,129},{129,3},{3,131},{131,1},{4... | collective-permute-start | bytes 516104 | tf_op jit(solution)/shard_map/ppermute | solution.py:277
  81.2 2.7 %collective-permute-start.7 = (bf16[96,896]{1,0:T(8,128)(2,1)}, bf16[96,896]{1,0:T(8,128)(2,1)S(1)}, u32[]{:S(2)}, u32[]{:S(2)}) collective-permute-start(bf16[96,896]{1,0:T(8,128)(2,1)} %get-tuple-element.77), channel_id=1, source_target_pairs={{0,2},{128,130},{2,0},{130,128},{1,3},{129,131},{3,1},{131,129},{4... | collective-permute-start | bytes 516104 | tf_op jit(solution)/shard_map/ppermute | solution.py:277
  83.8 1.2 collective-permute-start.8
  85.0 0.7 broadcast_in_dim.6
  85.7 3.6 %all-to-all-start.2 = ((bf16[16,48,128]{2,1,0:T(8,128)(2,1)}), bf16[16,48,128]{2,1,0:T(8,128)(2,1)S(1)}, u32[]{:S(2)}, u32[]{:S(2)}) async-start(bf16[16,48,128]{2,1,0:T(8,128)(2,1)} %broadcast_in_dim.6), calls=%async_computation.2 | async-start | bytes 393216 | tf_op jit(solution)/shard_map/all_to_all | solution.py:470
  89.3 0.0 collective-permute-done.9
  89.4 0.0 collective-permute-done.10
  89.4 0.0 copy-done.5
  89.4 0.0 collective-permute-done.6
  89.4 1.9 %collective-permute-done.7 = bf16[96,896]{1,0:T(8,128)(2,1)S(1)} collective-permute-done((bf16[96,896]{1,0:T(8,128)(2,1)}, bf16[96,896]{1,0:T(8,128)(2,1)S(1)}, u32[]{:S(2)}, u32[]{:S(2)}) %collective-permute-start.7) | collective-permute-done | bytes 172064 | tf_op jit(solution)/shard_map/ppermute | solution.py:277
  91.3 0.0 collective-permute-done.8
  91.3 1.0 add_add_fusion
  92.3 0.4 convert_element_type.23
  92.7 3.6 %all-to-all-done.2 = bf16[16,48,128]{2,1,0:T(8,128)(2,1)S(1)} async-done(((bf16[16,48,128]{2,1,0:T(8,128)(2,1)}), bf16[16,48,128]{2,1,0:T(8,128)(2,1)S(1)}, u32[]{:S(2)}, u32[]{:S(2)}) %all-to-all-start.2) | async-done | bytes 196640 | tf_op jit(solution)/shard_map/all_to_all | solution.py:470
  96.4 26.1 %all_to_all.20.received_ref = bf16[16,120,128]{2,1,0:T(8,128)(2,1)} all-to-all(bf16[16,120,128]{2,1,0:T(8,128)(2,1)S(1)} %pad_maximum_fusion), channel_id=1, replica_groups=mesh['y_lo'=2,'x'=4,'z'=8,'y_hi'=2,'core'=2] {'z','core'}, dimensions={0} | all-to-all | bytes 983040 | tf_op jit(solution)/shard_map/all_to_all | solution.py:470
  122.5 1.9 %finish.1 = (f32[6,3072]{1,0:T(8,128)}, f32[3072]{0:T(1024)}, f32[1536]{0:T(1024)}, f32[1536]{0:T(1024)}, f32[49,1536]{1,0:T(8,128)}, /*index=5*/f32[1536]{0:T(1024)}) custom-call(bf16[16,120,128]{2,1,0:T(8,128)(2,1)} %all_to_all.20.received_ref), custom_call_target="tpu_custom_call" | custom-call | flops 1000 | bytes 1000 | tf_op jit(solution)/shard_map/finish/pallas_call | solution.py:453
  (7 shorter events, 0.2 us)
Async XLA Ops:
  15.0 5.4 %collective-permute-start.1 = (bf16[256,1536]{1,0:T(8,128)(2,1)}, bf16[256,1536]{1,0:T(8,128)(2,1)S(1)}, u32[]{:S(2)}, u32[]{:S(2)}) collective-permute-start(bf16[256,1536]{1,0:T(8,128)(2,1)} %get-tuple-element.48.away_ref), channel_id=1, source_target_pairs={{0,1},{1,0},{2,3},{3,2},{4,5},{5,4},{6,7},{7,6},{8,9},{9,8},{10,11... | collective-permute-start | bytes 2359304 | tf_op jit(solution)/shard_map/ppermute | solution.py:491
  18.3 3.2 %collective-permute-start = (bf16[4,2,2,96,256]{4,3,2,1,0:T(8,128)(2,1)}, bf16[4,2,2,96,256]{4,3,2,1,0:T(8,128)(2,1)S(1)}, u32[]{:S(2)}, u32[]{:S(2)}) collective-permute-start(bf16[4,2,2,96,256]{4,3,2,1,0:T(8,128)(2,1)} %get-tuple-element.52), channel_id=1, source_target_pairs={{0,1},{1,0},{2,3},{3,2},{4,5},{5,4},{6,7},{7,6},{8,9},{9,8},{10,11... | collective-permute-start | bytes 2359304 | tf_op jit(solution)/shard_map/ppermute | solution.py:492
  20.4 1.1 copy-start.1
  21.5 0.9 copy-start.2
  28.8 28.3 %all-to-all-start = ((bf16[4,4,96,640]{3,2,1,0:T(8,128)(2,1)}), bf16[4,4,96,640]{3,2,1,0:T(8,128)(2,1)S(1)}, u32[]{:S(2)}, u32[]{:S(2)}) async-start(bf16[4,4,96,640]{3,2,1,0:T(8,128)(2,1)} %get-tuple-element.61), calls=%async_computation | async-start | bytes 3932160 | tf_op jit(solution)/shard_map/all_to_all | solution.py:470
  32.5 39.5 %collective-permute-start.2 = (bf16[4,96,896]{2,1,0:T(8,128)(2,1)}, bf16[4,96,896]{2,1,0:T(8,128)(2,1)S(1)}, u32[]{:S(2)}, u32[]{:S(2)}) collective-permute-start(bf16[4,96,896]{2,1,0:T(8,128)(2,1)} %get-tuple-element.58), channel_id=1, source_target_pairs={{0,32},{32,64},{64,96},{96,0},{1,33},{33,65},{65,97},{97,1},{2,34}... | collective-permute-start | bytes 2064392 | tf_op jit(solution)/shard_map/ppermute | solution.py:277
  32.5 43.5 %collective-permute-start.3 = (bf16[4,96,896]{2,1,0:T(8,128)(2,1)}, bf16[4,96,896]{2,1,0:T(8,128)(2,1)S(1)}, u32[]{:S(2)}, u32[]{:S(2)}) collective-permute-start(bf16[4,96,896]{2,1,0:T(8,128)(2,1)} %get-tuple-element.59), channel_id=1, source_target_pairs={{0,64},{32,96},{64,0},{96,32},{1,65},{33,97},{65,1},{97,33},{2,66}... | collective-permute-start | bytes 2064392 | tf_op jit(solution)/shard_map/ppermute | solution.py:277
  35.0 41.1 %collective-permute-start.4 = (bf16[4,96,896]{2,1,0:T(8,128)(2,1)}, bf16[4,96,896]{2,1,0:T(8,128)(2,1)}, u32[]{:S(2)}, u32[]{:S(2)}) collective-permute-start(bf16[4,96,896]{2,1,0:T(8,128)(2,1)} %get-tuple-element.60), channel_id=1, source_target_pairs={{0,96},{32,0},{64,32},{96,64},{1,97},{33,1},{65,33},{97,65},{2,98}... | collective-permute-start | bytes 2064392 | tf_op jit(solution)/shard_map/ppermute | solution.py:277
  57.1 8.6 %copy-start = (bf16[4,4,96,640]{3,2,1,0:T(8,128)(2,1)}, bf16[4,4,96,640]{3,2,1,0:T(8,128)(2,1)S(1)}, u32[]{:S(2)}) copy-start(bf16[4,4,96,640]{3,2,1,0:T(8,128)(2,1)S(1)} %all-to-all-done.refs_0_) | copy-start | bytes 5898244
  57.1 18.9 %all-to-all-start.1 = ((bf16[16,48,128]{2,1,0:T(8,128)(2,1)}), bf16[16,48,128]{2,1,0:T(8,128)(2,1)S(1)}, u32[]{:S(2)}, u32[]{:S(2)}) async-start(bf16[16,48,128]{2,1,0:T(8,128)(2,1)} %bitcast.9), calls=%async_computation.1 | async-start | bytes 393216 | tf_op jit(solution)/shard_map/all_to_all | solution.py:470
  68.1 21.2 %copy-start.5 = (bf16[96,640]{1,0:T(8,128)(2,1)S(1)}, bf16[96,640]{1,0:T(8,128)(2,1)}, u32[]{:S(2)}) copy-start(bf16[96,640]{1,0:T(8,128)(2,1)} %get-tuple-element.79) | copy-start | bytes 368644
  68.1 7.9 %collective-permute-start.5 = (bf16[96,640]{1,0:T(8,128)(2,1)}, bf16[96,640]{1,0:T(8,128)(2,1)S(1)}, u32[]{:S(2)}, u32[]{:S(2)}) collective-permute-start(bf16[96,640]{1,0:T(8,128)(2,1)} %get-tuple-element.66), channel_id=1, source_target_pairs={{0,32},{32,64},{64,96},{96,0},{1,33},{33,65},{65,97},{97,1},{2,34}... | collective-permute-start | bytes 368648 | tf_op jit(solution)/shard_map/ppermute | solution.py:277
  69.4 19.9 %collective-permute-start.9 = (bf16[96,640]{1,0:T(8,128)(2,1)}, bf16[96,640]{1,0:T(8,128)(2,1)S(1)}, u32[]{:S(2)}, u32[]{:S(2)}) collective-permute-start(bf16[96,640]{1,0:T(8,128)(2,1)} %get-tuple-element.81), channel_id=1, source_target_pairs={{0,64},{32,96},{64,0},{96,32},{1,65},{33,97},{65,1},{97,33},{2,66}... | collective-permute-start | bytes 368648 | tf_op jit(solution)/shard_map/ppermute | solution.py:277
  71.9 4.2 %copy-start.3 = (bf16[4,96,896]{2,1,0:T(8,128)(2,1)}, bf16[4,96,896]{2,1,0:T(8,128)(2,1)S(1)}, u32[]{:S(2)}) copy-start(bf16[4,96,896]{2,1,0:T(8,128)(2,1)S(1)} %collective-permute-done.2.refs_1_) | copy-start | bytes 2064388
  71.9 17.4 %collective-permute-start.10 = (bf16[96,640]{1,0:T(8,128)(2,1)}, bf16[96,640]{1,0:T(8,128)(2,1)S(1)}, u32[]{:S(2)}, u32[]{:S(2)}) collective-permute-start(bf16[96,640]{1,0:T(8,128)(2,1)} %get-tuple-element.82), channel_id=1, source_target_pairs={{0,96},{32,0},{64,32},{96,64},{1,97},{33,1},{65,33},{97,65},{2,98}... | collective-permute-start | bytes 368648 | tf_op jit(solution)/shard_map/ppermute | solution.py:277
  76.0 0.9 copy-start.4
  79.7 9.8 %collective-permute-start.6 = (bf16[96,896]{1,0:T(8,128)(2,1)}, bf16[96,896]{1,0:T(8,128)(2,1)S(1)}, u32[]{:S(2)}, u32[]{:S(2)}) collective-permute-start(bf16[96,896]{1,0:T(8,128)(2,1)} %get-tuple-element.76), channel_id=1, source_target_pairs={{0,128},{128,2},{2,130},{130,0},{1,129},{129,3},{3,131},{131,1},{4... | collective-permute-start | bytes 516104 | tf_op jit(solution)/shard_map/ppermute | solution.py:277
  81.2 10.1 %collective-permute-start.7 = (bf16[96,896]{1,0:T(8,128)(2,1)}, bf16[96,896]{1,0:T(8,128)(2,1)S(1)}, u32[]{:S(2)}, u32[]{:S(2)}) collective-permute-start(bf16[96,896]{1,0:T(8,128)(2,1)} %get-tuple-element.77), channel_id=1, source_target_pairs={{0,2},{128,130},{2,0},{130,128},{1,3},{129,131},{3,1},{131,129},{4... | collective-permute-start | bytes 516104 | tf_op jit(solution)/shard_map/ppermute | solution.py:277
  83.8 7.5 %collective-permute-start.8 = (bf16[96,896]{1,0:T(8,128)(2,1)}, bf16[96,896]{1,0:T(8,128)(2,1)S(1)}, u32[]{:S(2)}, u32[]{:S(2)}) collective-permute-start(bf16[96,896]{1,0:T(8,128)(2,1)} %get-tuple-element.78), channel_id=1, source_target_pairs={{0,130},{128,0},{2,128},{130,2},{1,131},{129,1},{3,129},{131,3},{4... | collective-permute-start | bytes 516104 | tf_op jit(solution)/shard_map/ppermute | solution.py:277
  85.7 10.5 %all-to-all-start.2 = ((bf16[16,48,128]{2,1,0:T(8,128)(2,1)}), bf16[16,48,128]{2,1,0:T(8,128)(2,1)S(1)}, u32[]{:S(2)}, u32[]{:S(2)}) async-start(bf16[16,48,128]{2,1,0:T(8,128)(2,1)} %broadcast_in_dim.6), calls=%async_computation.2 | async-start | bytes 393216 | tf_op jit(solution)/shard_map/all_to_all | solution.py:470

commit v11 on v9

--- a/solution.py
+++ b/solution.py
@@ -70,7 +70,7 @@
     gain = gain_ref[...].reshape(1, feat)
     shift = shift_ref[...].reshape(1, feat)
 
-    @pl.loop(0, side, unroll=4)
+    @pl.loop(0, side, unroll=16)
     def _(row):
         cells = pl.ds(pl.multiple_of(row * side, side), side)
         values = conv[cells, :]
@@ -129,7 +129,7 @@
     return jnp.asarray(np.eye(width, dtype=np.float32)[target], jnp.bfloat16)
 
 
-def front(core, image, taps, bias, gain, shift, w_up, b_row, cot, along_z, parts=4):
+def front(core, image, taps, bias, gain, shift, w_up, b_row, cot, along_z, parts=2):
     side, feat = image.shape[1], image.shape[3]
     cells = side * side
     hid = w_up.shape[1]

time: 124 us -> 123 us (level)
  Pallas kernels: 46.1 us -> 44.6 us
    pallas_call x1, Pallas kernels: 14.3 us -> 12.8 us  [front(): pl.pallas_call(front_kernel, name='front', in_specs=[pl.BlockSpec(memory_...]
where the time goes in v11:
time: 123 us; the launch traced here: 122 us
  Pallas kernels  44.6 us (36%)
  starting transfers between devices  33 us (27%)
  blocking collectives  26 us (21%)
  waiting for transfers between devices  12.8 us (10%)
  local copies, waits for them, and re-layouts  2.87 us (2%)
  other arithmetic  1.73 us (1%)
    all_to_all x1, blocking collectives, swap_pieces(): return lax.all_to_all(values, axes, 0, 0, tiled=True)  26 us
    pallas_call x1, Pallas kernels, back(): pl.pallas_call(back_kernel, name='back', grid=(feat // LANES,), in_specs=...  19.2 us
    all_to_all x3, starting transfers between devices, swap_pieces(): return lax.all_to_all(values, axes, 0, 0, tiled=True)  15.9 us
    ppermute x9, starting transfers between devices, to_owners(): lax.ppermute(piece, axes, [(named[i], named[(i + d) % 4]) for i in range(...  13.7 us
    pallas_call x1, Pallas kernels, front(): pl.pallas_call(front_kernel, name='front', in_specs=[pl.BlockSpec(memory_...  12.8 us
    all_to_all x3, waiting for transfers between devices, swap_pieces(): return lax.all_to_all(values, axes, 0, 0, tiled=True)  8.49 us
    pallas_call x1, Pallas kernels, product(): pl.pallas_call(product_kernel, name='product', in_specs=[pl.BlockSpec(mem...  5.49 us
    pallas_call x2, Pallas kernels, sum_pieces(): pl.pallas_call(sum_kernel, name='sum_pieces', out_shape=[jax.ShapeDtypeSt...  5.17 us
  transfers between devices with their start and end apart: 14, of which 6 were waited for; matrix products, arithmetic and copies ran while one was open for 2% of the time, Pallas kernels for 20%

profile of v11, /device:TPU:1, one launch (start us, length us, event | category | flops | bytes accessed | tf_op | source)
XLA Modules:
  0.0 121.8 jit_solution(6419294598518368124)
XLA Ops:
  0.6 12.8 %front.1 = (f32[256,1536]{1,0:T(8,128)}, f32[256,128]{1,0:T(8,128)}, bf16[4,2,2,96,256]{4,3,2,1,0:T(8,128)(2,1)}, bf16[256,1536]{1,0:T(8,128)(2,1)}, bf16[256,1536]{1,0:T(8,128)(2,1)}, /*index=5*/f32[1,3072]{1,0:T(1,128)}) custom-call(s32[1]{0:T(128)} %bitcast.core_ref, bf16[1,16,16,1536]{3,2,1,0:T(8,128)(2,1)} %image_ref.3, f32[49,1536]{1,0:T(8,128)} %taps_ref.3, ...), custom_call_target="tpu_custom_call" | custom-call | flops 1000 | bytes 1000 | tf_op jit(solution)/shard_map/front/pallas_call | solution.py:140
  13.4 3.3 %collective-permute-start.1 = (bf16[256,1536]{1,0:T(8,128)(2,1)}, bf16[256,1536]{1,0:T(8,128)(2,1)S(1)}, u32[]{:S(2)}, u32[]{:S(2)}) collective-permute-start(bf16[256,1536]{1,0:T(8,128)(2,1)} %get-tuple-element.48.away_ref), channel_id=1, source_target_pairs={{0,1},{1,0},{2,3},{3,2},{4,5},{5,4},{6,7},{7,6},{8,9},{9,8},{10,11... | collective-permute-start | bytes 2359304 | tf_op jit(solution)/shard_map/ppermute | solution.py:456
  16.8 0.1 collective-permute-start
  16.9 0.6 pad_add_fusion.place_ref
  17.5 1.4 %collective-permute-done.1.far_ref = bf16[256,1536]{1,0:T(8,128)(2,1)S(1)} collective-permute-done((bf16[256,1536]{1,0:T(8,128)(2,1)}, bf16[256,1536]{1,0:T(8,128)(2,1)S(1)}, u32[]{:S(2)}, u32[]{:S(2)}) %collective-permute-start.1) | collective-permute-done | bytes 786464 | tf_op jit(solution)/shard_map/ppermute | solution.py:456
  18.9 0.0 copy-start.1
  18.9 1.1 collective-permute-done
  20.0 0.0 copy-start.2
  20.0 0.0 copy-done.1
  20.0 0.9 copy-done.2
  21.0 5.5 %product.1 = (bf16[4,96,896]{2,1,0:T(8,128)(2,1)}, bf16[4,96,896]{2,1,0:T(8,128)(2,1)}, bf16[4,96,896]{2,1,0:T(8,128)(2,1)}, bf16[4,96,896]{2,1,0:T(8,128)(2,1)}, bf16[4,4,96,640]{3,2,1,0:T(8,128)(2,1)}) custom-call(s32[2]{0:T(128)} %pad_add_fusion.place_ref, bf16[4,4,96,256]{3,2,1,0:T(8,128)(2,1)} %bitcast.7, bf16[4,4,96,256]{3,2,1,0:T(8,128)(2,1)} %bitcast.8, ...), custom_call_target="tpu_custom_call" | custom-call | flops 1000 | bytes 1000 | tf_op jit(solution)/shard_map/product/pallas_call | solution.py:198
  26.5 3.6 %all-to-all-start = ((bf16[4,4,96,640]{3,2,1,0:T(8,128)(2,1)}), bf16[4,4,96,640]{3,2,1,0:T(8,128)(2,1)S(1)}, u32[]{:S(2)}, u32[]{:S(2)}) async-start(bf16[4,4,96,640]{3,2,1,0:T(8,128)(2,1)} %get-tuple-element.61), calls=%async_computation | async-start | bytes 3932160 | tf_op jit(solution)/shard_map/all_to_all | solution.py:435
  30.1 0.1 collective-permute-start.2
  30.2 2.4 %collective-permute-start.3 = (bf16[4,96,896]{2,1,0:T(8,128)(2,1)}, bf16[4,96,896]{2,1,0:T(8,128)(2,1)S(1)}, u32[]{:S(2)}, u32[]{:S(2)}) collective-permute-start(bf16[4,96,896]{2,1,0:T(8,128)(2,1)} %get-tuple-element.59), channel_id=1, source_target_pairs={{0,64},{32,96},{64,0},{96,32},{1,65},{33,97},{65,1},{97,33},{2,66}... | collective-permute-start | bytes 2064392 | tf_op jit(solution)/shard_map/ppermute | solution.py:242
  32.6 1.2 collective-permute-start.4
  33.8 19.2 %back.1 = (bf16[1,16,16,1536]{3,2,1,0:T(8,128)(2,1)}, bf16[12,64,128]{2,1,0:T(8,128)(2,1)}) custom-call(s32[1]{0:T(128)} %bitcast.core_ref, bf16[256,1536]{1,0:T(8,128)(2,1)} %get-tuple-element.48.away_ref, bf16[256,1536]{1,0:T(8,128)(2,1)} %get-tuple-element.49.near_ref, f32[256,128]{1,0:T(8,128)} %get-tuple-element.50.sigma_ref, f32[1536]{0:T(1024)} %gain_ref.3, ...), custom_call_target="tpu_custom_call" | custom-call | flops 1000 | bytes 1000 | tf_op jit(solution)/shard_map/back/pallas_call | solution.py:347
  53.0 1.7 %all-to-all-done.refs_0_ = bf16[4,4,96,640]{3,2,1,0:T(8,128)(2,1)S(1)} async-done(((bf16[4,4,96,640]{3,2,1,0:T(8,128)(2,1)}), bf16[4,4,96,640]{3,2,1,0:T(8,128)(2,1)S(1)}, u32[]{:S(2)}, u32[]{:S(2)}) %all-to-all-start) | async-done | bytes 1966112 | tf_op jit(solution)/shard_map/all_to_all | solution.py:435
  54.7 0.0 copy-start
  54.7 8.6 %all-to-all-start.1 = ((bf16[16,48,128]{2,1,0:T(8,128)(2,1)}), bf16[16,48,128]{2,1,0:T(8,128)(2,1)S(1)}, u32[]{:S(2)}, u32[]{:S(2)}) async-start(bf16[16,48,128]{2,1,0:T(8,128)(2,1)} %bitcast.9), calls=%async_computation.1 | async-start | bytes 393216 | tf_op jit(solution)/shard_map/all_to_all | solution.py:435
  63.3 0.0 copy-done
  63.3 2.4 %sum_pieces.2 = (bf16[96,640]{1,0:T(8,128)(2,1)}, bf16[96,640]{1,0:T(8,128)(2,1)}, bf16[96,640]{1,0:T(8,128)(2,1)}, bf16[96,640]{1,0:T(8,128)(2,1)}) custom-call(bf16[4,4,96,640]{3,2,1,0:T(8,128)(2,1)} %copy-done), custom_call_target="tpu_custom_call" | custom-call | flops 1000 | bytes 1000 | tf_op jit(solution)/shard_map/sum_pieces/pallas_call | solution.py:230
  65.7 0.0 copy-start.5
  65.7 1.2 %collective-permute-start.5 = (bf16[96,640]{1,0:T(8,128)(2,1)}, bf16[96,640]{1,0:T(8,128)(2,1)S(1)}, u32[]{:S(2)}, u32[]{:S(2)}) collective-permute-start(bf16[96,640]{1,0:T(8,128)(2,1)} %get-tuple-element.66), channel_id=1, source_target_pairs={{0,32},{32,64},{64,96},{96,0},{1,33},{33,65},{65,97},{97,1},{2,34}... | collective-permute-start | bytes 368648 | tf_op jit(solution)/shard_map/ppermute | solution.py:242
  67.0 2.5 %collective-permute-start.9 = (bf16[96,640]{1,0:T(8,128)(2,1)}, bf16[96,640]{1,0:T(8,128)(2,1)S(1)}, u32[]{:S(2)}, u32[]{:S(2)}) collective-permute-start(bf16[96,640]{1,0:T(8,128)(2,1)} %get-tuple-element.81), channel_id=1, source_target_pairs={{0,64},{32,96},{64,0},{96,32},{1,65},{33,97},{65,1},{97,33},{2,66}... | collective-permute-start | bytes 368648 | tf_op jit(solution)/shard_map/ppermute | solution.py:242
  69.4 0.0 collective-permute-done.2.refs_1_
  69.4 0.0 copy-start.3
  69.4 1.2 collective-permute-start.10
  70.6 3.0 %all-to-all-done.1 = bf16[16,48,128]{2,1,0:T(8,128)(2,1)S(1)} async-done(((bf16[16,48,128]{2,1,0:T(8,128)(2,1)}), bf16[16,48,128]{2,1,0:T(8,128)(2,1)S(1)}, u32[]{:S(2)}, u32[]{:S(2)}) %all-to-all-start.1) | async-done | bytes 196640 | tf_op jit(solution)/shard_map/all_to_all | solution.py:435
  73.7 0.0 collective-permute-done.3.refs_2_
  73.7 0.0 copy-start.4
  73.7 0.0 collective-permute-done.4.refs_3_
  73.7 0.0 collective-permute-done.5
  73.7 0.0 copy-done.3
  73.7 0.8 copy-done.4
  74.5 2.7 %sum_pieces.3 = (bf16[96,896]{1,0:T(8,128)(2,1)}, bf16[96,896]{1,0:T(8,128)(2,1)}, bf16[96,896]{1,0:T(8,128)(2,1)}, bf16[96,896]{1,0:T(8,128)(2,1)}) custom-call(bf16[4,96,896]{2,1,0:T(8,128)(2,1)} %get-tuple-element.71.refs_0_, bf16[4,96,896]{2,1,0:T(8,128)(2,1)} %copy-done.3, bf16[4,96,896]{2,1,0:T(8,128)(2,1)} %copy-done.4, ...), custom_call_target="tpu_custom_call" | custom-call | flops 1000 | bytes 1000 | tf_op jit(solution)/shard_map/sum_pieces/pallas_call | solution.py:230
  77.3 1.4 %collective-permute-start.6 = (bf16[96,896]{1,0:T(8,128)(2,1)}, bf16[96,896]{1,0:T(8,128)(2,1)S(1)}, u32[]{:S(2)}, u32[]{:S(2)}) collective-permute-start(bf16[96,896]{1,0:T(8,128)(2,1)} %get-tuple-element.76), channel_id=1, source_target_pairs={{0,128},{128,2},{2,130},{130,0},{1,129},{129,3},{3,131},{131,1},{4... | collective-permute-start | bytes 516104 | tf_op jit(solution)/shard_map/ppermute | solution.py:242
  78.7 2.5 %collective-permute-start.7 = (bf16[96,896]{1,0:T(8,128)(2,1)}, bf16[96,896]{1,0:T(8,128)(2,1)S(1)}, u32[]{:S(2)}, u32[]{:S(2)}) collective-permute-start(bf16[96,896]{1,0:T(8,128)(2,1)} %get-tuple-element.77), channel_id=1, source_target_pairs={{0,2},{128,130},{2,0},{130,128},{1,3},{129,131},{3,1},{131,129},{4... | collective-permute-start | bytes 516104 | tf_op jit(solution)/shard_map/ppermute | solution.py:242
  81.2 1.2 collective-permute-start.8
  82.4 0.7 broadcast_in_dim.6
  83.1 3.7 %all-to-all-start.2 = ((bf16[16,48,128]{2,1,0:T(8,128)(2,1)}), bf16[16,48,128]{2,1,0:T(8,128)(2,1)S(1)}, u32[]{:S(2)}, u32[]{:S(2)}) async-start(bf16[16,48,128]{2,1,0:T(8,128)(2,1)} %broadcast_in_dim.6), calls=%async_computation.2 | async-start | bytes 393216 | tf_op jit(solution)/shard_map/all_to_all | solution.py:435
  86.9 0.0 collective-permute-done.9
  86.9 0.0 collective-permute-done.10
  86.9 0.0 copy-done.5
  86.9 0.0 collective-permute-done.6
  86.9 1.8 %collective-permute-done.7 = bf16[96,896]{1,0:T(8,128)(2,1)S(1)} collective-permute-done((bf16[96,896]{1,0:T(8,128)(2,1)}, bf16[96,896]{1,0:T(8,128)(2,1)S(1)}, u32[]{:S(2)}, u32[]{:S(2)}) %collective-permute-start.7) | collective-permute-done | bytes 172064 | tf_op jit(solution)/shard_map/ppermute | solution.py:242
  88.7 0.0 collective-permute-done.8
  88.7 1.0 add_add_fusion
  89.7 0.4 convert_element_type.23
  90.1 3.7 %all-to-all-done.2 = bf16[16,48,128]{2,1,0:T(8,128)(2,1)S(1)} async-done(((bf16[16,48,128]{2,1,0:T(8,128)(2,1)}), bf16[16,48,128]{2,1,0:T(8,128)(2,1)S(1)}, u32[]{:S(2)}, u32[]{:S(2)}) %all-to-all-start.2) | async-done | bytes 196640 | tf_op jit(solution)/shard_map/all_to_all | solution.py:435
  93.9 26.0 %all_to_all.20.received_ref = bf16[16,120,128]{2,1,0:T(8,128)(2,1)} all-to-all(bf16[16,120,128]{2,1,0:T(8,128)(2,1)S(1)} %pad_maximum_fusion), channel_id=1, replica_groups=mesh['y_lo'=2,'x'=4,'z'=8,'y_hi'=2,'core'=2] {'z','core'}, dimensions={0} | all-to-all | bytes 983040 | tf_op jit(solution)/shard_map/all_to_all | solution.py:435
  119.9 1.9 %finish.1 = (f32[6,3072]{1,0:T(8,128)}, f32[3072]{0:T(1024)}, f32[1536]{0:T(1024)}, f32[1536]{0:T(1024)}, f32[49,1536]{1,0:T(8,128)}, /*index=5*/f32[1536]{0:T(1024)}) custom-call(bf16[16,120,128]{2,1,0:T(8,128)(2,1)} %all_to_all.20.received_ref), custom_call_target="tpu_custom_call" | custom-call | flops 1000 | bytes 1000 | tf_op jit(solution)/shard_map/finish/pallas_call | solution.py:418
  (7 shorter events, 0.2 us)
Async XLA Ops:
  13.4 5.5 %collective-permute-start.1 = (bf16[256,1536]{1,0:T(8,128)(2,1)}, bf16[256,1536]{1,0:T(8,128)(2,1)S(1)}, u32[]{:S(2)}, u32[]{:S(2)}) collective-permute-start(bf16[256,1536]{1,0:T(8,128)(2,1)} %get-tuple-element.48.away_ref), channel_id=1, source_target_pairs={{0,1},{1,0},{2,3},{3,2},{4,5},{5,4},{6,7},{7,6},{8,9},{9,8},{10,11... | collective-permute-start | bytes 2359304 | tf_op jit(solution)/shard_map/ppermute | solution.py:456
  16.8 3.2 %collective-permute-start = (bf16[4,2,2,96,256]{4,3,2,1,0:T(8,128)(2,1)}, bf16[4,2,2,96,256]{4,3,2,1,0:T(8,128)(2,1)S(1)}, u32[]{:S(2)}, u32[]{:S(2)}) collective-permute-start(bf16[4,2,2,96,256]{4,3,2,1,0:T(8,128)(2,1)} %get-tuple-element.52), channel_id=1, source_target_pairs={{0,1},{1,0},{2,3},{3,2},{4,5},{5,4},{6,7},{7,6},{8,9},{9,8},{10,11... | collective-permute-start | bytes 2359304 | tf_op jit(solution)/shard_map/ppermute | solution.py:457
  18.9 1.1 copy-start.1
  20.0 0.9 copy-start.2
  26.5 28.3 %all-to-all-start = ((bf16[4,4,96,640]{3,2,1,0:T(8,128)(2,1)}), bf16[4,4,96,640]{3,2,1,0:T(8,128)(2,1)S(1)}, u32[]{:S(2)}, u32[]{:S(2)}) async-start(bf16[4,4,96,640]{3,2,1,0:T(8,128)(2,1)} %get-tuple-element.61), calls=%async_computation | async-start | bytes 3932160 | tf_op jit(solution)/shard_map/all_to_all | solution.py:435
  30.1 39.3 %collective-permute-start.2 = (bf16[4,96,896]{2,1,0:T(8,128)(2,1)}, bf16[4,96,896]{2,1,0:T(8,128)(2,1)S(1)}, u32[]{:S(2)}, u32[]{:S(2)}) collective-permute-start(bf16[4,96,896]{2,1,0:T(8,128)(2,1)} %get-tuple-element.58), channel_id=1, source_target_pairs={{0,32},{32,64},{64,96},{96,0},{1,33},{33,65},{65,97},{97,1},{2,34}... | collective-permute-start | bytes 2064392 | tf_op jit(solution)/shard_map/ppermute | solution.py:242
  30.2 43.5 %collective-permute-start.3 = (bf16[4,96,896]{2,1,0:T(8,128)(2,1)}, bf16[4,96,896]{2,1,0:T(8,128)(2,1)S(1)}, u32[]{:S(2)}, u32[]{:S(2)}) collective-permute-start(bf16[4,96,896]{2,1,0:T(8,128)(2,1)} %get-tuple-element.59), channel_id=1, source_target_pairs={{0,64},{32,96},{64,0},{96,32},{1,65},{33,97},{65,1},{97,33},{2,66}... | collective-permute-start | bytes 2064392 | tf_op jit(solution)/shard_map/ppermute | solution.py:242
  32.6 41.1 %collective-permute-start.4 = (bf16[4,96,896]{2,1,0:T(8,128)(2,1)}, bf16[4,96,896]{2,1,0:T(8,128)(2,1)}, u32[]{:S(2)}, u32[]{:S(2)}) collective-permute-start(bf16[4,96,896]{2,1,0:T(8,128)(2,1)} %get-tuple-element.60), channel_id=1, source_target_pairs={{0,96},{32,0},{64,32},{96,64},{1,97},{33,1},{65,33},{97,65},{2,98}... | collective-permute-start | bytes 2064392 | tf_op jit(solution)/shard_map/ppermute | solution.py:242
  54.7 8.6 %copy-start = (bf16[4,4,96,640]{3,2,1,0:T(8,128)(2,1)}, bf16[4,4,96,640]{3,2,1,0:T(8,128)(2,1)S(1)}, u32[]{:S(2)}) copy-start(bf16[4,4,96,640]{3,2,1,0:T(8,128)(2,1)S(1)} %all-to-all-done.refs_0_) | copy-start | bytes 5898244
  54.7 18.9 %all-to-all-start.1 = ((bf16[16,48,128]{2,1,0:T(8,128)(2,1)}), bf16[16,48,128]{2,1,0:T(8,128)(2,1)S(1)}, u32[]{:S(2)}, u32[]{:S(2)}) async-start(bf16[16,48,128]{2,1,0:T(8,128)(2,1)} %bitcast.9), calls=%async_computation.1 | async-start | bytes 393216 | tf_op jit(solution)/shard_map/all_to_all | solution.py:435
  65.7 21.1 %copy-start.5 = (bf16[96,640]{1,0:T(8,128)(2,1)S(1)}, bf16[96,640]{1,0:T(8,128)(2,1)}, u32[]{:S(2)}) copy-start(bf16[96,640]{1,0:T(8,128)(2,1)} %get-tuple-element.79) | copy-start | bytes 368644
  65.7 7.9 %collective-permute-start.5 = (bf16[96,640]{1,0:T(8,128)(2,1)}, bf16[96,640]{1,0:T(8,128)(2,1)S(1)}, u32[]{:S(2)}, u32[]{:S(2)}) collective-permute-start(bf16[96,640]{1,0:T(8,128)(2,1)} %get-tuple-element.66), channel_id=1, source_target_pairs={{0,32},{32,64},{64,96},{96,0},{1,33},{33,65},{65,97},{97,1},{2,34}... | collective-permute-start | bytes 368648 | tf_op jit(solution)/shard_map/ppermute | solution.py:242
  67.0 19.9 %collective-permute-start.9 = (bf16[96,640]{1,0:T(8,128)(2,1)}, bf16[96,640]{1,0:T(8,128)(2,1)S(1)}, u32[]{:S(2)}, u32[]{:S(2)}) collective-permute-start(bf16[96,640]{1,0:T(8,128)(2,1)} %get-tuple-element.81), channel_id=1, source_target_pairs={{0,64},{32,96},{64,0},{96,32},{1,65},{33,97},{65,1},{97,33},{2,66}... | collective-permute-start | bytes 368648 | tf_op jit(solution)/shard_map/ppermute | solution.py:242
  69.4 4.3 %copy-start.3 = (bf16[4,96,896]{2,1,0:T(8,128)(2,1)}, bf16[4,96,896]{2,1,0:T(8,128)(2,1)S(1)}, u32[]{:S(2)}) copy-start(bf16[4,96,896]{2,1,0:T(8,128)(2,1)S(1)} %collective-permute-done.2.refs_1_) | copy-start | bytes 2064388
  69.4 17.4 %collective-permute-start.10 = (bf16[96,640]{1,0:T(8,128)(2,1)}, bf16[96,640]{1,0:T(8,128)(2,1)S(1)}, u32[]{:S(2)}, u32[]{:S(2)}) collective-permute-start(bf16[96,640]{1,0:T(8,128)(2,1)} %get-tuple-element.82), channel_id=1, source_target_pairs={{0,96},{32,0},{64,32},{96,64},{1,97},{33,1},{65,33},{97,65},{2,98}... | collective-permute-start | bytes 368648 | tf_op jit(solution)/shard_map/ppermute | solution.py:242
  73.7 0.9 copy-start.4
  77.3 9.7 %collective-permute-start.6 = (bf16[96,896]{1,0:T(8,128)(2,1)}, bf16[96,896]{1,0:T(8,128)(2,1)S(1)}, u32[]{:S(2)}, u32[]{:S(2)}) collective-permute-start(bf16[96,896]{1,0:T(8,128)(2,1)} %get-tuple-element.76), channel_id=1, source_target_pairs={{0,128},{128,2},{2,130},{130,0},{1,129},{129,3},{3,131},{131,1},{4... | collective-permute-start | bytes 516104 | tf_op jit(solution)/shard_map/ppermute | solution.py:242
  78.7 10.0 %collective-permute-start.7 = (bf16[96,896]{1,0:T(8,128)(2,1)}, bf16[96,896]{1,0:T(8,128)(2,1)S(1)}, u32[]{:S(2)}, u32[]{:S(2)}) collective-permute-start(bf16[96,896]{1,0:T(8,128)(2,1)} %get-tuple-element.77), channel_id=1, source_target_pairs={{0,2},{128,130},{2,0},{130,128},{1,3},{129,131},{3,1},{131,129},{4... | collective-permute-start | bytes 516104 | tf_op jit(solution)/shard_map/ppermute | solution.py:242
  81.2 7.5 %collective-permute-start.8 = (bf16[96,896]{1,0:T(8,128)(2,1)}, bf16[96,896]{1,0:T(8,128)(2,1)S(1)}, u32[]{:S(2)}, u32[]{:S(2)}) collective-permute-start(bf16[96,896]{1,0:T(8,128)(2,1)} %get-tuple-element.78), channel_id=1, source_target_pairs={{0,130},{128,0},{2,128},{130,2},{1,131},{129,1},{3,129},{131,3},{4... | collective-permute-start | bytes 516104 | tf_op jit(solution)/shard_map/ppermute | solution.py:242
  83.1 10.7 %all-to-all-start.2 = ((bf16[16,48,128]{2,1,0:T(8,128)(2,1)}), bf16[16,48,128]{2,1,0:T(8,128)(2,1)S(1)}, u32[]{:S(2)}, u32[]{:S(2)}) async-start(bf16[16,48,128]{2,1,0:T(8,128)(2,1)} %broadcast_in_dim.6), calls=%async_computation.2 | async-start | bytes 393216 | tf_op jit(solution)/shard_map/all_to_all | solution.py:435
